TPU v7x, 32 devices: a whole 2x2x4 slice. The times are simulated.
32 devices in a mesh: dp: 4 (over y, x), seq: 8 (over z, core).
Axes of the slice: x: 2, y: 2, z: 4, core: 2. Of those that a mesh axis runs over, the one named last changes fastest.
Arguments:
- patches: bfloat16 [8, 2304, 1280], P('dp', 'seq'), may hold values from -6 to 6
- ln1_gain: bfloat16 [1280], P('dp'), may hold values from 0.099609375 to 1.8984375
- ln1_bias: bfloat16 [1280], P('dp'), may hold values from -3 to 3
- qkv_weight: bfloat16 [1280, 3840], P('dp'), may hold values from -0.15625 to 0.15625
- q_bias: bfloat16 [1280], P('dp'), may hold values from -3 to 3
- v_bias: bfloat16 [1280], P('dp'), may hold values from -3 to 3
- proj_weight: bfloat16 [1280, 1280], P('dp'), may hold values from -6 to 6
- proj_bias: bfloat16 [1280], P('dp'), may hold values from -3 to 3
- ln2_gain: bfloat16 [1280], P('dp'), may hold values from 0.099609375 to 1.8984375
- ln2_bias: bfloat16 [1280], P('dp'), may hold values from -3 to 3
- fc1_weight: bfloat16 [1280, 5120], P('dp'), may hold values from -0.15625 to 0.15625
- fc1_bias: bfloat16 [5120], P('dp'), may hold values from -3 to 3
- fc2_weight: bfloat16 [5120, 1280], P('dp'), may hold values from -0.078125 to 0.078125
- fc2_bias: bfloat16 [1280], P('dp'), may hold values from -3 to 3
- rel_pos_h: bfloat16 [95, 80], replicated, may hold values from -0.5 to 0.5
- rel_pos_w: bfloat16 [95, 80], replicated, may hold values from -0.5 to 0.5
- cotangent: bfloat16 [8, 2304, 1280], P('dp', 'seq'), may hold values from -6 to 6
Outputs:
- output: bfloat16 [8, 2304, 1280], P('dp', 'seq')
- grad_patches: bfloat16 [8, 2304, 1280], P('dp', 'seq')
- grad_ln1_gain: float32 [1280], P('dp')
- grad_ln1_bias: float32 [1280], P('dp')
- grad_qkv_weight: float32 [1280, 3840], P('dp', 'seq')
- grad_q_bias: float32 [1280], P('dp')
- grad_v_bias: float32 [1280], P('dp')
- grad_proj_weight: float32 [1280, 1280], P('dp', 'seq')
- grad_proj_bias: float32 [1280], P('dp')
- grad_ln2_gain: float32 [1280], P('dp')
- grad_ln2_bias: float32 [1280], P('dp')
- grad_fc1_weight: float32 [1280, 5120], P('dp', 'seq')
- grad_fc1_bias: float32 [5120], P('dp')
- grad_fc2_weight: float32 [5120, 1280], P('dp', 'seq')
- grad_fc2_bias: float32 [1280], P('dp')
- grad_rel_pos_h: float32 [95, 80], replicated
- grad_rel_pos_w: float32 [95, 80], replicated
All inputs are finite; a program needn't handle non-finite values.
Results may differ from a plain program's by a relative error of at most 0.017.
Values may be sent and summed in bfloat16 or wider, within the bound.
A program may use at most 256 MiB of HBM per device.

v0:
```python
from functools import partial

import jax
import jax.numpy as jnp
from jax import lax
from jax.sharding import PartitionSpec as P

H = 16
HD = 80


EPSILON = 1e-06
HIGHEST = lax.Precision.HIGHEST
ROWS_DIMS = (((0,), (0,)), ((), ()))
COLS_DIMS = (((1,), (1,)), ((), ()))


def layer_norm(values, gain_vec, shift_vec):
    center = values - jnp.mean(values, -1, keepdims=True)
    spread = jnp.mean(center * center, -1, keepdims=True)
    return center * lax.rsqrt(spread + EPSILON) * gain_vec + shift_vec


def norm_back(values, gain_vec, upstream):

    def normalize(inputs_in, gains_in):
        return layer_norm(inputs_in, gains_in, 0.0)

    unused, pullback = jax.vjp(normalize, values, gain_vec)
    grad_values, grad_gain = pullback(upstream)
    return (grad_values, grad_gain, jnp.sum(upstream, 0))


def offsets(table):
    grid_side = (table.shape[0] + 1) // 2
    cube_shape = (grid_side, grid_side, table.shape[0])
    first_pos = lax.broadcasted_iota(jnp.int32, cube_shape, 0)
    second_pos = lax.broadcasted_iota(jnp.int32, cube_shape, 1)
    entry_pos = lax.broadcasted_iota(jnp.int32, cube_shape, 2)
    return (entry_pos == first_pos - second_pos + grid_side - 1).astype(jnp.float32)


def expand(table):
    return jnp.einsum("abr,rc->abc", offsets(table), table.astype(jnp.float32), precision=HIGHEST)


def block_size(seq_len):
    return seq_len // max(1, seq_len // 512)


def to_heads(flat, images):
    row_count = flat.shape[0] // images
    return (
        flat.reshape(images, row_count, H, HD)
        .transpose(0, 2, 1, 3)
        .reshape(images * H, row_count, HD)
    )


def from_heads(stacked, images):
    row_count = stacked.shape[1]
    return (
        stacked.reshape(images, H, row_count, HD)
        .transpose(0, 2, 1, 3)
        .reshape(images * row_count, H * HD)
    )


def score_block(query_block, key_rows, table_rows, table_w):
    block_rows, head_size = query_block.shape
    grid_side = table_w.shape[0]
    per_block = block_rows // grid_side
    scores = lax.dot_general(
        query_block, key_rows, COLS_DIMS, preferred_element_type=jnp.float32
    ) * head_size ** (-0.5)
    query_grid = query_block.astype(jnp.float32).reshape(per_block, grid_side, head_size)
    rel_rows = jnp.einsum("hwc,hkc->hwk", query_grid, table_rows, precision=HIGHEST)
    rel_cols = jnp.einsum("hwc,wkc->hwk", query_grid, table_w, precision=HIGHEST)
    scores = (
        scores.reshape(per_block, grid_side, grid_side, grid_side)
        + rel_rows[:, :, :, None]
        + rel_cols[:, :, None, :]
    )
    return (scores.reshape(block_rows, key_rows.shape[0]), query_grid)


def attend_pair(triple, table_h, table_w):
    query_rows, key_rows, value_rows = triple
    seq_len, head_size = query_rows.shape
    grid_side = table_w.shape[0]
    block_rows = block_size(seq_len)
    per_block = block_rows // grid_side

    def one_block(running, block_index):
        query_block = lax.dynamic_slice_in_dim(query_rows, block_index * block_rows, block_rows, 0)
        table_rows = lax.dynamic_slice_in_dim(table_h, block_index * per_block, per_block, 0)
        scores, query_grid = score_block(query_block, key_rows, table_rows, table_w)
        row_max = jnp.max(scores, -1, keepdims=True)
        exp_scores = jnp.exp(scores - row_max)
        row_total = jnp.sum(exp_scores, -1, keepdims=True)
        attn_probs = (exp_scores / row_total).astype(jnp.bfloat16)
        attended = jnp.dot(attn_probs, value_rows, preferred_element_type=jnp.float32).astype(
            jnp.bfloat16
        )
        return (running, (attended, (row_max + jnp.log(row_total))[:, 0]))

    unused, (attended, log_norm) = lax.scan(
        one_block, jnp.int32(0), jnp.arange(seq_len // block_rows, dtype=jnp.int32)
    )
    return (attended.reshape(seq_len, head_size), log_norm.reshape(seq_len))


def attend_back(bundle, table_h, table_w):
    query_rows, key_rows, value_rows, log_norm, grad_rows = bundle
    seq_len, head_size = query_rows.shape
    grid_side = table_w.shape[0]
    block_rows = block_size(seq_len)
    per_block = block_rows // grid_side
    score_scale = head_size ** (-0.5)

    def one_block(running, block_index):
        grad_keys, grad_values, grad_th, grad_tw = running
        first_row = block_index * block_rows
        first_grid = block_index * per_block
        query_block = lax.dynamic_slice_in_dim(query_rows, first_row, block_rows, 0)
        grad_block = lax.dynamic_slice_in_dim(grad_rows, first_row, block_rows, 0)
        norm_block = lax.dynamic_slice_in_dim(log_norm, first_row, block_rows, 0)
        table_rows = lax.dynamic_slice_in_dim(table_h, first_grid, per_block, 0)
        scores, query_grid = score_block(query_block, key_rows, table_rows, table_w)
        attn_probs = jnp.exp(scores - norm_block[:, None])
        grad_probs = lax.dot_general(
            grad_block, value_rows, COLS_DIMS, preferred_element_type=jnp.float32
        )
        row_inner = jnp.sum(attn_probs * grad_probs, -1, keepdims=True)
        grad_scores = (attn_probs * (grad_probs - row_inner)).astype(jnp.bfloat16)
        score_grid = grad_scores.astype(jnp.float32).reshape(
            per_block, grid_side, grid_side, grid_side
        )
        grad_rel_rows = jnp.sum(score_grid, 3)
        grad_rel_cols = jnp.sum(score_grid, 2)
        grad_query = (
            jnp.dot(grad_scores, key_rows, preferred_element_type=jnp.float32) * score_scale
        )
        rel_part = jnp.einsum(
            "hwk,hkc->hwc", grad_rel_rows, table_rows, precision=HIGHEST
        ) + jnp.einsum("hwk,wkc->hwc", grad_rel_cols, table_w, precision=HIGHEST)
        grad_query = grad_query + rel_part.reshape(block_rows, head_size)
        grad_keys = (
            grad_keys
            + lax.dot_general(
                grad_scores, query_block, ROWS_DIMS, preferred_element_type=jnp.float32
            )
            * score_scale
        )
        grad_values = grad_values + lax.dot_general(
            attn_probs.astype(jnp.bfloat16),
            grad_block,
            ROWS_DIMS,
            preferred_element_type=jnp.float32,
        )
        old_rows = lax.dynamic_slice_in_dim(grad_th, first_grid, per_block, 0)
        new_rows = old_rows + jnp.einsum(
            "hwk,hwc->hkc", grad_rel_rows, query_grid, precision=HIGHEST
        )
        grad_th = lax.dynamic_update_slice_in_dim(grad_th, new_rows, first_grid, 0)
        grad_tw = grad_tw + jnp.einsum("hwk,hwc->wkc", grad_rel_cols, query_grid, precision=HIGHEST)
        return ((grad_keys, grad_values, grad_th, grad_tw), grad_query.astype(jnp.bfloat16))

    starting = (
        jnp.zeros((seq_len, head_size), jnp.float32),
        jnp.zeros((seq_len, head_size), jnp.float32),
        jnp.zeros(table_h.shape, jnp.float32),
        jnp.zeros(table_w.shape, jnp.float32),
    )
    (grad_keys, grad_values, grad_th, grad_tw), grad_query = lax.scan(
        one_block, starting, jnp.arange(seq_len // block_rows, dtype=jnp.int32)
    )
    return (
        grad_query.reshape(seq_len, head_size),
        grad_keys.astype(jnp.bfloat16),
        grad_values.astype(jnp.bfloat16),
        grad_th,
        grad_tw,
    )


def on_device(
    patches,
    ln1_gain,
    ln1_bias,
    qkv_weight,
    q_bias,
    v_bias,
    proj_weight,
    proj_bias,
    ln2_gain,
    ln2_bias,
    fc1_weight,
    fc1_bias,
    fc2_weight,
    fc2_bias,
    rel_pos_h,
    rel_pos_w,
    cotangent,
):
    images, row_count, model_width = patches.shape
    gathered = (
        lax.all_gather(ln1_gain, "dp", axis=0, tiled=True),
        lax.all_gather(ln1_bias, "dp", axis=0, tiled=True),
        lax.all_gather(qkv_weight, "dp", axis=0, tiled=True),
        lax.all_gather(q_bias, "dp", axis=0, tiled=True),
        lax.all_gather(v_bias, "dp", axis=0, tiled=True),
        lax.all_gather(proj_weight, "dp", axis=0, tiled=True),
        lax.all_gather(proj_bias, "dp", axis=0, tiled=True),
        lax.all_gather(ln2_gain, "dp", axis=0, tiled=True),
        lax.all_gather(ln2_bias, "dp", axis=0, tiled=True),
        lax.all_gather(fc1_weight, "dp", axis=0, tiled=True),
        lax.all_gather(fc1_bias, "dp", axis=0, tiled=True),
        lax.all_gather(fc2_weight, "dp", axis=0, tiled=True),
        lax.all_gather(fc2_bias, "dp", axis=0, tiled=True),
    )
    (
        gain_one,
        shift_one,
        qkv_full,
        q_shift,
        v_shift,
        proj_full,
        proj_shift,
        gain_two,
        shift_two,
        fc1_full,
        fc1_shift,
        fc2_full,
        fc2_shift,
    ) = gathered
    inputs_f = patches.reshape(images * row_count, model_width).astype(jnp.float32)
    normed = layer_norm(
        inputs_f, gain_one.astype(jnp.float32), shift_one.astype(jnp.float32)
    ).astype(jnp.bfloat16)
    joined = jnp.dot(normed, qkv_full, preferred_element_type=jnp.float32)
    queries = (joined[:, :model_width] + q_shift.astype(jnp.float32)).astype(jnp.bfloat16)
    key_part = joined[:, model_width : 2 * model_width].astype(jnp.bfloat16)
    value_part = (joined[:, 2 * model_width :] + v_shift.astype(jnp.float32)).astype(jnp.bfloat16)
    head_q, head_k, head_v = (
        lax.all_to_all(to_heads(queries, images), "seq", split_axis=0, concat_axis=1, tiled=True),
        lax.all_to_all(to_heads(key_part, images), "seq", split_axis=0, concat_axis=1, tiled=True),
        lax.all_to_all(
            to_heads(value_part, images), "seq", split_axis=0, concat_axis=1, tiled=True
        ),
    )
    table_h = expand(rel_pos_h)
    table_w = expand(rel_pos_w)
    attended, log_norm = lax.map(
        partial(attend_pair, table_h=table_h, table_w=table_w), (head_q, head_k, head_v)
    )
    returned = lax.all_to_all(attended, "seq", split_axis=1, concat_axis=0, tiled=True)
    mixed_rows = from_heads(returned, images)
    middle = (
        inputs_f
        + jnp.dot(mixed_rows, proj_full, preferred_element_type=jnp.float32)
        + proj_shift.astype(jnp.float32)
    )
    normed_two = layer_norm(
        middle, gain_two.astype(jnp.float32), shift_two.astype(jnp.float32)
    ).astype(jnp.bfloat16)
    before_act = jnp.dot(
        normed_two, fc1_full, preferred_element_type=jnp.float32
    ) + fc1_shift.astype(jnp.float32)
    activated = jax.nn.gelu(before_act, approximate=False).astype(jnp.bfloat16)
    result = (
        middle
        + jnp.dot(activated, fc2_full, preferred_element_type=jnp.float32)
        + fc2_shift.astype(jnp.float32)
    )
    output = result.astype(jnp.bfloat16).reshape(images, row_count, model_width)
    qkv_back, proj_back, fc1_back, fc2_back, gain_one_back, gain_two_back = (
        lax.all_gather(qkv_weight, "dp", axis=0, tiled=True),
        lax.all_gather(proj_weight, "dp", axis=0, tiled=True),
        lax.all_gather(fc1_weight, "dp", axis=0, tiled=True),
        lax.all_gather(fc2_weight, "dp", axis=0, tiled=True),
        lax.all_gather(ln1_gain, "dp", axis=0, tiled=True),
        lax.all_gather(ln2_gain, "dp", axis=0, tiled=True),
    )
    grad_out = cotangent.reshape(images * row_count, model_width).astype(jnp.float32)
    grad_branch = grad_out.astype(jnp.bfloat16)
    grad_fc2 = lax.dot_general(
        activated, grad_branch, ROWS_DIMS, preferred_element_type=jnp.float32
    )
    grad_fc2_shift = jnp.sum(grad_branch.astype(jnp.float32), 0)
    grad_activated = lax.dot_general(
        grad_branch, fc2_back, COLS_DIMS, preferred_element_type=jnp.float32
    )
    unused, gelu_pull = jax.vjp(partial(jax.nn.gelu, approximate=False), before_act)
    grad_before = gelu_pull(grad_activated)[0].astype(jnp.bfloat16)
    grad_fc1 = lax.dot_general(
        normed_two, grad_before, ROWS_DIMS, preferred_element_type=jnp.float32
    )
    grad_fc1_shift = jnp.sum(grad_before.astype(jnp.float32), 0)
    grad_normed_two = lax.dot_general(
        grad_before, fc1_back, COLS_DIMS, preferred_element_type=jnp.float32
    )
    grad_middle_norm, grad_gain_two, grad_shift_two = norm_back(
        middle, gain_two_back.astype(jnp.float32), grad_normed_two
    )
    grad_middle = grad_out + grad_middle_norm
    grad_proj_in = grad_middle.astype(jnp.bfloat16)
    grad_proj = lax.dot_general(
        mixed_rows, grad_proj_in, ROWS_DIMS, preferred_element_type=jnp.float32
    )
    grad_proj_shift = jnp.sum(grad_proj_in.astype(jnp.float32), 0)
    grad_mixed = lax.dot_general(
        grad_proj_in, proj_back, COLS_DIMS, preferred_element_type=jnp.float32
    ).astype(jnp.bfloat16)
    grad_heads = lax.all_to_all(
        to_heads(grad_mixed, images), "seq", split_axis=0, concat_axis=1, tiled=True
    )

    def pair_back(running, bundle):
        grad_query, grad_keys, grad_values, grad_th, grad_tw = attend_back(bundle, table_h, table_w)
        return ((running[0] + grad_th, running[1] + grad_tw), (grad_query, grad_keys, grad_values))

    table_start = (jnp.zeros(table_h.shape, jnp.float32), jnp.zeros(table_w.shape, jnp.float32))
    (grad_table_h, grad_table_w), (pair_gq, pair_gk, pair_gv) = lax.scan(
        pair_back, table_start, (head_q, head_k, head_v, log_norm, grad_heads)
    )
    rows_gq, rows_gk, rows_gv = (
        lax.all_to_all(pair_gq, "seq", split_axis=1, concat_axis=0, tiled=True),
        lax.all_to_all(pair_gk, "seq", split_axis=1, concat_axis=0, tiled=True),
        lax.all_to_all(pair_gv, "seq", split_axis=1, concat_axis=0, tiled=True),
    )
    grad_queries = from_heads(rows_gq, images)
    grad_key_part = from_heads(rows_gk, images)
    grad_value_part = from_heads(rows_gv, images)
    grad_joined = jnp.concatenate([grad_queries, grad_key_part, grad_value_part], axis=1)
    grad_qkv = lax.dot_general(normed, grad_joined, ROWS_DIMS, preferred_element_type=jnp.float32)
    grad_q_shift = jnp.sum(grad_queries.astype(jnp.float32), 0)
    grad_v_shift = jnp.sum(grad_value_part.astype(jnp.float32), 0)
    grad_normed = lax.dot_general(
        grad_joined, qkv_back, COLS_DIMS, preferred_element_type=jnp.float32
    )
    grad_inputs_norm, grad_gain_one, grad_shift_one = norm_back(
        inputs_f, gain_one_back.astype(jnp.float32), grad_normed
    )
    grad_patches = (
        (grad_middle + grad_inputs_norm)
        .astype(jnp.bfloat16)
        .reshape(images, row_count, model_width)
    )
    grad_rel_h = jnp.einsum("abr,abc->rc", offsets(rel_pos_h), grad_table_h, precision=HIGHEST)
    grad_rel_w = jnp.einsum("abr,abc->rc", offsets(rel_pos_w), grad_table_w, precision=HIGHEST)
    matrix_sums = (
        lax.psum_scatter(
            grad_qkv.astype(jnp.bfloat16), "seq", scatter_dimension=1, tiled=True
        ).astype(jnp.float32),
        lax.psum_scatter(
            grad_proj.astype(jnp.bfloat16), "seq", scatter_dimension=1, tiled=True
        ).astype(jnp.float32),
        lax.psum_scatter(
            grad_fc1.astype(jnp.bfloat16), "seq", scatter_dimension=1, tiled=True
        ).astype(jnp.float32),
        lax.psum_scatter(
            grad_fc2.astype(jnp.bfloat16), "seq", scatter_dimension=1, tiled=True
        ).astype(jnp.float32),
    )
    vector_sums = (
        lax.psum(grad_gain_one.astype(jnp.bfloat16), "seq").astype(jnp.float32),
        lax.psum(grad_shift_one.astype(jnp.bfloat16), "seq").astype(jnp.float32),
        lax.psum(grad_q_shift.astype(jnp.bfloat16), "seq").astype(jnp.float32),
        lax.psum(grad_v_shift.astype(jnp.bfloat16), "seq").astype(jnp.float32),
        lax.psum(grad_proj_shift.astype(jnp.bfloat16), "seq").astype(jnp.float32),
        lax.psum(grad_gain_two.astype(jnp.bfloat16), "seq").astype(jnp.float32),
        lax.psum(grad_shift_two.astype(jnp.bfloat16), "seq").astype(jnp.float32),
        lax.psum(grad_fc1_shift.astype(jnp.bfloat16), "seq").astype(jnp.float32),
        lax.psum(grad_fc2_shift.astype(jnp.bfloat16), "seq").astype(jnp.float32),
    )
    owned = (
        lax.psum_scatter(
            matrix_sums[0].astype(jnp.bfloat16), "dp", scatter_dimension=0, tiled=True
        ).astype(jnp.float32),
        lax.psum_scatter(
            matrix_sums[1].astype(jnp.bfloat16), "dp", scatter_dimension=0, tiled=True
        ).astype(jnp.float32),
        lax.psum_scatter(
            matrix_sums[2].astype(jnp.bfloat16), "dp", scatter_dimension=0, tiled=True
        ).astype(jnp.float32),
        lax.psum_scatter(
            matrix_sums[3].astype(jnp.bfloat16), "dp", scatter_dimension=0, tiled=True
        ).astype(jnp.float32),
        lax.psum_scatter(
            vector_sums[0].astype(jnp.bfloat16), "dp", scatter_dimension=0, tiled=True
        ).astype(jnp.float32),
        lax.psum_scatter(
            vector_sums[1].astype(jnp.bfloat16), "dp", scatter_dimension=0, tiled=True
        ).astype(jnp.float32),
        lax.psum_scatter(
            vector_sums[2].astype(jnp.bfloat16), "dp", scatter_dimension=0, tiled=True
        ).astype(jnp.float32),
        lax.psum_scatter(
            vector_sums[3].astype(jnp.bfloat16), "dp", scatter_dimension=0, tiled=True
        ).astype(jnp.float32),
        lax.psum_scatter(
            vector_sums[4].astype(jnp.bfloat16), "dp", scatter_dimension=0, tiled=True
        ).astype(jnp.float32),
        lax.psum_scatter(
            vector_sums[5].astype(jnp.bfloat16), "dp", scatter_dimension=0, tiled=True
        ).astype(jnp.float32),
        lax.psum_scatter(
            vector_sums[6].astype(jnp.bfloat16), "dp", scatter_dimension=0, tiled=True
        ).astype(jnp.float32),
        lax.psum_scatter(
            vector_sums[7].astype(jnp.bfloat16), "dp", scatter_dimension=0, tiled=True
        ).astype(jnp.float32),
        lax.psum_scatter(
            vector_sums[8].astype(jnp.bfloat16), "dp", scatter_dimension=0, tiled=True
        ).astype(jnp.float32),
    )
    table_sums = lax.psum((grad_rel_h, grad_rel_w), ("dp", "seq"))
    return (
        output,
        grad_patches,
        owned[4],
        owned[5],
        owned[0],
        owned[6],
        owned[7],
        owned[1],
        owned[8],
        owned[9],
        owned[10],
        owned[2],
        owned[11],
        owned[3],
        owned[12],
        table_sums[0],
        table_sums[1],
    )


def solution(mesh):
    placed = (
        P("dp", "seq", None),
        P("dp"),
        P("dp"),
        P("dp", None),
        P("dp"),
        P("dp"),
        P("dp", None),
        P("dp"),
        P("dp"),
        P("dp"),
        P("dp", None),
        P("dp"),
        P("dp", None),
        P("dp"),
        P(),
        P(),
        P("dp", "seq", None),
    )
    return jax.shard_map(
        on_device,
        mesh=mesh,
        in_specs=placed,
        out_specs=(
            P("dp", "seq", None),
            P("dp", "seq", None),
            P("dp"),
            P("dp"),
            P("dp", "seq"),
            P("dp"),
            P("dp"),
            P("dp", "seq"),
            P("dp"),
            P("dp"),
            P("dp"),
            P("dp", "seq"),
            P("dp"),
            P("dp", "seq"),
            P("dp"),
            P(),
            P(),
        ),
        check_vma=False,
    )
```

profile of v0, /device:TPU:0, one launch (start us, length us, event | category | flops | bytes accessed | tf_op | source)
XLA Modules:
  0.0 3733.0 jit_solution(467111385809148290)
XLA Ops:
  13.0 18.7 all-reduce.20
  35.2 77.2 %all-gather.6.cloned.1.call-done = bf16[1280,3840]{1,0:T(8,128)(2,1)} async-done(((bf16[320,3840]{1,0:T(8,128)(2,1)}), bf16[1280,3840]{1,0:T(8,128)(2,1)}) %all-gather.6.cloned.1.call-update) | async-done | bytes 9830416 | tf_op jit(solution)/shard_map/all_gather | solution.py:210
  146.1 36.8 all-to-all-done
  195.1 38.5 %all-to-all-done.1 = bf16[32,288,80]{1,2,0:T(8,128)(2,1)} async-done(((bf16[32,288,80]{1,2,0:T(8,128)(2,1)}), bf16[32,288,80]{1,2,0:T(8,128)(2,1)}, u32[]{:S(2)}, u32[]{:S(2)}) %all-to-all-start.1) | async-done | bytes 1474592 | tf_op jit(solution)/shard_map/all_to_all | solution.py:247
  249.2 34.2 all-to-all-done.2
  287.8 850.9 %while.64 = (s32[]{:T(128)}, bf16[4,2304,80]{2,1,0:T(8,128)(2,1)}, f32[4,2304]{1,0:T(4,128)}, bf16[4,2304,80]{2,1,0:T(8,128)(2,1)}, bf16[4,2304,80]{2,1,0:T(8,12...) while((s32[]{:T(128)}, bf16[4,2304,80]{2,1,0:T(8,128)(2,1)}, ...), condition=%wide.region_7.8_spmd, body=%wide.region_2.7_spmd.sunk | while | flops 489746880 | bytes 65586248 | solution.py:254
  290.2 209.8 %while.67 = (s32[]{:T(128)}, bf16[4,576,80]{1,2,0:T(8,128)(2,1)S(1)}, f32[4,576]{1,0:T(4,128)S(1)}, s32[4]{0:T(128)S(1)}, bf16[2304,80]{1,0:T(8,128)(2,1)S(1)}, ...) while((s32[]{:T(128)}, ...), condition=%wide.region_6.6_spmd, body=%wide.region_3.5_spmd.sunk | while | flops 489746880 | bytes 61641484 | solution.py:107
  302.0 12.7 add.462
  324.8 12.3 add.465
  354.5 12.3 add.462
  376.9 12.3 add.465
  406.2 12.3 add.462
  428.6 12.3 add.465
  457.9 12.3 add.462
  480.3 12.3 add.465
  505.2 206.8 %while.67 = (s32[]{:T(128)}, bf16[4,576,80]{1,2,0:T(8,128)(2,1)S(1)}, f32[4,576]{1,0:T(4,128)S(1)}, s32[4]{0:T(128)S(1)}, bf16[2304,80]{1,0:T(8,128)(2,1)S(1)}, ...) while((s32[]{:T(128)}, ...), condition=%wide.region_6.6_spmd, body=%wide.region_3.5_spmd.sunk | while | flops 489746880 | bytes 61641484 | solution.py:107
  514.8 12.3 add.462
  537.2 12.3 add.465
  566.5 12.3 add.462
  588.9 12.3 add.465
  618.2 12.3 add.462
  640.6 12.3 add.465
  669.9 12.3 add.462
  692.3 12.3 add.465
  717.2 206.8 %while.67 = (s32[]{:T(128)}, bf16[4,576,80]{1,2,0:T(8,128)(2,1)S(1)}, f32[4,576]{1,0:T(4,128)S(1)}, s32[4]{0:T(128)S(1)}, bf16[2304,80]{1,0:T(8,128)(2,1)S(1)}, ...) while((s32[]{:T(128)}, ...), condition=%wide.region_6.6_spmd, body=%wide.region_3.5_spmd.sunk | while | flops 489746880 | bytes 61641484 | solution.py:107
  726.8 12.3 add.462
  749.2 12.3 add.465
  778.5 12.3 add.462
  800.9 12.3 add.465
  830.2 12.3 add.462
  881.9 12.3 add.462
  904.3 12.3 add.465
  929.2 206.8 %while.67 = (s32[]{:T(128)}, bf16[4,576,80]{1,2,0:T(8,128)(2,1)S(1)}, f32[4,576]{1,0:T(4,128)S(1)}, s32[4]{0:T(128)S(1)}, bf16[2304,80]{1,0:T(8,128)(2,1)S(1)}, ...) while((s32[]{:T(128)}, ...), condition=%wide.region_6.6_spmd, body=%wide.region_3.5_spmd.sunk | while | flops 489746880 | bytes 61641484 | solution.py:107
  938.8 12.3 add.462
  990.5 12.3 add.462
  1012.9 12.3 add.465
  1042.2 12.3 add.462
  1093.9 12.3 add.462
  1162.5 46.6 %all-to-all-done.3 = bf16[4,2304,80]{2,0,1:T(4,128)(2,1)S(1)} async-done(((bf16[4,2304,80]{2,0,1:T(4,128)(2,1)}), bf16[4,2304,80]{2,0,1:T(4,128)(2,1)S(1)}, u32[]{:S(2)}, u32[]{:S(2)}) %all-to-all-start.3) | async-done | bytes 1474592 | tf_op jit(solution)/shard_map/all_to_all | solution.py:257
  1229.5 14.6 fusion.52
  1244.1 39.8 %fusion.55 = (bf16[5120]{0:T(1024)(128)(2,1)}, bf16[576,5120]{1,0:T(8,128)(2,1)S(1)}, f32[576,5120]{1,0:T(8,128)}) fusion(f32[576,5120]{1,0:T(8,128)} %fusion.52, f32[5120]{0:T(1024)S(1)} %bitcast.308, bf16[576,1280]{1,0:T(8,128)(2,1)S(1)} %bitcast.290, bf16[5120,1280]{1,0:T(8,128)(2,1)} %all-gather.12.cloned.1.call-done), kind=kOutput, calls=%fused_computation.135 | convolution fusion | flops 7767976960 | bytes 44103680 | tf_op jit(solution)/shard_map/dot_general | solution.py:291
  1284.0 14.1 multiply_reduce_fusion.1
  1316.0 46.1 %all-to-all-done.4 = bf16[32,288,80]{1,2,0:T(8,128)(2,1)S(1)} async-done(((bf16[32,288,80]{1,2,0:T(8,128)(2,1)}), bf16[32,288,80]{1,2,0:T(8,128)(2,1)S(1)}, u32[]{:S(2)}, u32[]{:S(2)}) %all-to-all-start.4) | async-done | bytes 1474592 | tf_op jit(solution)/shard_map/all_to_all | solution.py:315
  1366.6 1615.6 %while.66 = (s32[]{:T(128)}, f32[48,48,80]{2,1,0:T(8,128)}, f32[48,48,80]{2,1,0:T(8,128)}, bf16[4,2304,80]{2,1,0:T(8,128)(2,1)}, bf16[4,2304,80]{1,2,0:T(8,128)(...) while((s32[]{:T(128)}, f32[48,48,80]{2,1,0:T(8,128)}, ...), condition=%wide.region_18.19_spmd.clone, body=%wide.region_12.18_spmd.clone.sunk | while | flops 1239431680 | bytes 191457536 | solution.py:324
  1376.5 388.0 %while.68 = (s32[]{:T(128)}, f32[2304,80]{0,1:T(8,128)}, f32[2304,80]{0,1:T(8,128)}, f32[48,48,80]{2,1,0:T(8,128)}, f32[48,48,80]{2,1,0:T(8,128)}, /*index=5*/bf...) while((s32[]{:T(128)}, f32[2304,80]{0,1:T(8,128)}, ...), condition=%wide.region_17.17_spmd.clone, body=%wide.region_13.16_spmd.clone.sunk | while | flops 1238325760 | bytes 172048112 | solution.py:175
  1779.7 388.0 %while.68 = (s32[]{:T(128)}, f32[2304,80]{0,1:T(8,128)}, f32[2304,80]{0,1:T(8,128)}, f32[48,48,80]{2,1,0:T(8,128)}, f32[48,48,80]{2,1,0:T(8,128)}, /*index=5*/bf...) while((s32[]{:T(128)}, f32[2304,80]{0,1:T(8,128)}, ...), condition=%wide.region_17.17_spmd.clone, body=%wide.region_13.16_spmd.clone.sunk | while | flops 1238325760 | bytes 172048112 | solution.py:175
  2183.6 388.0 %while.68 = (s32[]{:T(128)}, f32[2304,80]{0,1:T(8,128)}, f32[2304,80]{0,1:T(8,128)}, f32[48,48,80]{2,1,0:T(8,128)}, f32[48,48,80]{2,1,0:T(8,128)}, /*index=5*/bf...) while((s32[]{:T(128)}, f32[2304,80]{0,1:T(8,128)}, ...), condition=%wide.region_17.17_spmd.clone, body=%wide.region_13.16_spmd.clone.sunk | while | flops 1238325760 | bytes 172048112 | solution.py:175
  2587.6 388.0 %while.68 = (s32[]{:T(128)}, f32[2304,80]{0,1:T(8,128)}, f32[2304,80]{0,1:T(8,128)}, f32[48,48,80]{2,1,0:T(8,128)}, f32[48,48,80]{2,1,0:T(8,128)}, /*index=5*/bf...) while((s32[]{:T(128)}, f32[2304,80]{0,1:T(8,128)}, ...), condition=%wide.region_17.17_spmd.clone, body=%wide.region_13.16_spmd.clone.sunk | while | flops 1238325760 | bytes 172048112 | solution.py:175
  3002.5 49.8 %all-to-all-done.5 = bf16[4,2304,80]{2,0,1:T(4,128)(2,1)S(1)} async-done(((bf16[4,2304,80]{2,0,1:T(4,128)(2,1)}), bf16[4,2304,80]{2,0,1:T(4,128)(2,1)S(1)}, u32[]{:S(2)}, u32[]{:S(2)}) %all-to-all-start.5) | async-done | bytes 1474592 | tf_op jit(solution)/shard_map/all_to_all | solution.py:328
  3067.8 68.4 %all-to-all-done.6 = bf16[4,2304,80]{2,0,1:T(4,128)(2,1)} async-done(((bf16[4,2304,80]{2,0,1:T(4,128)(2,1)}), bf16[4,2304,80]{2,0,1:T(4,128)(2,1)}, u32[]{:S(2)}, u32[]{:S(2)}) %all-to-all-start.6) | async-done | bytes 1474592 | tf_op jit(solution)/shard_map/all_to_all | solution.py:329
  3164.6 30.7 all-to-all-done.7
  3225.0 17.3 convolution_convert_fusion.1
  3242.2 17.7 copy.178
  3272.2 13.0 convolution_convert_fusion
  3287.5 36.7 reduce-scatter.15.cloned.1.call-done
  3326.6 132.3 %reduce-scatter.29.cloned.1.call-done = bf16[640,1280]{1,0:T(8,128)(2,1)} async-done(((bf16[5120,1280]{1,0:T(8,128)(2,1)}), bf16[640,1280]{1,0:T(8,128)(2,1)}) %reduce-scatter.29.cloned.1.call-update) | async-done | bytes 1638416
  3468.5 41.1 %all-reduce.17 = (f32[95,80]{0,1:T(8,128)}, f32[95,80]{0,1:T(8,128)}) all-reduce(f32[95,80]{0,1:T(8,128)S(1)} %convolution_bitcast_fusion.3, f32[95,80]{0,1:T(8,128)S(1)} %convolution_bitcast_fusion.2), channel_id=1, replica_groups=mesh['dp'=4,'seq'=8] {'dp','seq'}, use_global_device_ids=true, to_apply=%region_56.57 | all-reduce | flops 15200 | bytes 121600 | tf_op jit(solution)/shard_map/psum | solution.py:418
  3509.7 15.3 fusion.54
  3524.9 69.9 %reduce-scatter.21.cloned.1.call-done = bf16[5120,160]{0,1:T(8,128)(2,1)} async-done(((bf16[5120,1280]{0,1:T(8,128)(2,1)}), bf16[5120,160]{0,1:T(8,128)(2,1)}) %reduce-scatter.21.cloned.1.call-update) | async-done | bytes 1638416 | tf_op jit(solution)/shard_map/reduce_scatter | solution.py:362
  3602.0 16.9 all-reduce.19
  3621.7 26.1 all-reduce.18
  3657.3 14.5 fusion.39
  3675.8 13.6 reduce-scatter.19.cloned.1.call-done
  3691.4 32.6 reduce-scatter.23.cloned.1.call-done
  (1218 shorter events, 2363.2 us)
Async XLA Ops:
  7.2 230.6 %copy-start = (bf16[95,80]{0,1:T(8,128)(2,1)S(1)}, bf16[95,80]{0,1:T(8,128)(2,1)}, u32[]{:S(2)}) copy-start(bf16[95,80]{0,1:T(8,128)(2,1)} %param.39) | copy-start | bytes 45604
  7.2 105.2 %all-gather.6.cloned.1.call-start = ((), (), s32[]{:S(2)}) async-start(), calls=%async_computation.16 | async-start | bytes 12288000 | tf_op jit(solution)/shard_map/all_gather | solution.py:210
  8.0 1214.3 %all-gather.8.cloned.1.call-start = ((), (), s32[]{:S(2)}) async-start(), calls=%async_computation.17 | async-start | bytes 4096000 | tf_op jit(solution)/shard_map/all_gather | solution.py:213
  8.8 1220.7 %all-gather.10.cloned.1.call-start = ((), (), s32[]{:S(2)}) async-start(), calls=%async_computation.18 | async-start | bytes 16384000 | tf_op jit(solution)/shard_map/all_gather | solution.py:217
  9.9 25.3 copy-start.47
  35.2 77.2 %copy-start.32 = (bf16[576,1280]{1,0:T(8,128)(2,1)}, bf16[576,1280]{1,0:T(8,128)(2,1)S(1)}, u32[]{:S(2)}) copy-start(bf16[576,1280]{1,0:T(8,128)(2,1)S(1)} %get-tuple-element.649) | copy-start | bytes 4423684
  131.8 51.1 %all-to-all-start = ((bf16[32,288,80]{1,2,0:T(8,128)(2,1)}), bf16[32,288,80]{1,2,0:T(8,128)(2,1)}, u32[]{:S(2)}, u32[]{:S(2)}) async-start(bf16[32,288,80]{1,2,0:T(8,128)(2,1)} %bitcast.302), calls=%async_computation | async-start | bytes 3932160 | tf_op jit(solution)/shard_map/all_to_all | solution.py:246
  182.8 50.8 %all-to-all-start.1 = ((bf16[32,288,80]{1,2,0:T(8,128)(2,1)}), bf16[32,288,80]{1,2,0:T(8,128)(2,1)}, u32[]{:S(2)}, u32[]{:S(2)}) async-start(bf16[32,288,80]{1,2,0:T(8,128)(2,1)} %bitcast.300), calls=%async_computation.1 | async-start | bytes 3932160 | tf_op jit(solution)/shard_map/all_to_all | solution.py:247
  233.6 49.8 %all-to-all-start.2 = ((bf16[32,288,80]{1,2,0:T(8,128)(2,1)}), bf16[32,288,80]{1,2,0:T(8,128)(2,1)S(1)}, u32[]{:S(2)}, u32[]{:S(2)}) async-start(bf16[32,288,80]{1,2,0:T(8,128)(2,1)} %bitcast.298), calls=%async_computation.2 | async-start | bytes 3932160 | tf_op jit(solution)/shard_map/all_to_all | solution.py:248
  237.2 1006.9 %all-gather.12.cloned.1.call-start = ((), (), s32[]{:S(2)}) async-start(), calls=%async_computation.19 | async-start | bytes 16384000 | tf_op jit(solution)/shard_map/all_gather | solution.py:219
  1150.7 58.4 %all-to-all-start.3 = ((bf16[4,2304,80]{2,0,1:T(4,128)(2,1)}), bf16[4,2304,80]{2,0,1:T(4,128)(2,1)S(1)}, u32[]{:S(2)}, u32[]{:S(2)}) async-start(bf16[4,2304,80]{2,0,1:T(4,128)(2,1)} %copy.138), calls=%async_computation.3 | async-start | bytes 4718592 | tf_op jit(solution)/shard_map/all_to_all | solution.py:257
  1154.5 75.0 %copy-start.58 = (f32[1280]{0:T(1024)}, f32[1280]{0:T(1024)S(1)}, u32[]{:S(2)}) copy-start(f32[1280]{0:T(1024)S(1)} %convert_element_type.215) | copy-start | bytes 15364
  1154.5 143.5 %copy-start.51 = (f32[1280]{0:T(1024)}, f32[1280]{0:T(1024)S(1)}, u32[]{:S(2)}) copy-start(f32[1280]{0:T(1024)S(1)} %convert_element_type.214) | copy-start | bytes 15364
  1162.5 81.6 %copy-start.37 = (f32[4,1,1280]{2,1,0:T(1,128)}, f32[4,1,1280]{2,1,0:T(1,128)S(1)}, u32[]{:S(2)}) copy-start(f32[4,1,1280]{2,1,0:T(1,128)S(1)} %convert_element_type.248) | copy-start | bytes 61444
  1213.1 9.3 copy-start.11
  1227.4 70.7 %copy-start.41 = (f32[576]{0:T(1024)}, f32[576]{0:T(1024)S(1)}, u32[]{:S(2)}) copy-start(f32[576]{0:T(1024)S(1)} %broadcast_multiply_fusion) | copy-start | bytes 6916
  1229.5 68.6 %copy-start.54 = (f32[576]{0:T(1024)}, f32[576]{0:T(1024)S(1)}, u32[]{:S(2)}) copy-start(f32[576]{0:T(1024)S(1)} %fusion.47) | copy-start | bytes 6916
  1229.5 14.6 copy-start.22
  1244.1 39.9 %copy-start.14 = (f32[576,1280]{1,0:T(8,128)S(1)}, f32[576,1280]{1,0:T(8,128)}, u32[]{:S(2)}) copy-start(f32[576,1280]{1,0:T(8,128)} %copy-done.13) | copy-start | bytes 8847364
  1284.0 14.1 copy-start.75
  1312.4 49.8 %all-to-all-start.4 = ((bf16[32,288,80]{1,2,0:T(8,128)(2,1)}), bf16[32,288,80]{1,2,0:T(8,128)(2,1)S(1)}, u32[]{:S(2)}, u32[]{:S(2)}) async-start(bf16[32,288,80]{1,2,0:T(8,128)(2,1)} %bitcast.303), calls=%async_computation.4 | async-start | bytes 3932160 | tf_op jit(solution)/shard_map/all_to_all | solution.py:315
  1426.2 7.8 slice-start.1
  1522.2 7.8 slice-start.1
  1619.5 7.8 slice-start.1
  1716.9 7.8 slice-start.1
  1829.4 7.8 slice-start.1
  1925.4 7.7 slice-start
  1925.4 7.8 slice-start.1
  2022.7 7.8 slice-start.1
  2120.1 7.8 slice-start.1
  2233.3 7.7 slice-start
  2233.3 7.8 slice-start.1
  2329.4 7.7 slice-start
  2329.4 7.8 slice-start.1
  2426.7 7.8 slice-start.1
  2524.0 7.8 slice-start.1
  2637.3 7.8 slice-start.1
  2733.3 7.7 slice-start
  2733.3 7.8 slice-start.1
  2830.7 7.8 slice-start.1
  2928.0 7.8 slice-start.1
  2994.1 58.2 %all-to-all-start.5 = ((bf16[4,2304,80]{2,0,1:T(4,128)(2,1)}), bf16[4,2304,80]{2,0,1:T(4,128)(2,1)S(1)}, u32[]{:S(2)}, u32[]{:S(2)}) async-start(bf16[4,2304,80]{2,0,1:T(4,128)(2,1)} %copy.151), calls=%async_computation.5 | async-start | bytes 4718592 | tf_op jit(solution)/shard_map/all_to_all | solution.py:328
  3052.3 10.8 copy-start.25
  3052.3 83.9 %all-to-all-start.6 = ((bf16[4,2304,80]{2,0,1:T(4,128)(2,1)}), bf16[4,2304,80]{2,0,1:T(4,128)(2,1)}, u32[]{:S(2)}, u32[]{:S(2)}) async-start(bf16[4,2304,80]{2,0,1:T(4,128)(2,1)} %copy.155), calls=%async_computation.6 | async-start | bytes 4718592 | tf_op jit(solution)/shard_map/all_to_all | solution.py:329
  3056.7 228.6 %reduce-scatter.17.cloned.1.call-start = ((), (), s32[]{:S(2)}) async-start(), calls=%async_computation.21 | async-start | bytes 3686400 | tf_op jit(solution)/shard_map/reduce_scatter | solution.py:356
  3136.2 59.1 %all-to-all-start.7 = ((bf16[4,2304,80]{2,0,1:T(4,128)(2,1)}), bf16[4,2304,80]{2,0,1:T(4,128)(2,1)}, u32[]{:S(2)}, u32[]{:S(2)}) async-start(bf16[4,2304,80]{2,0,1:T(4,128)(2,1)} %copy.159), calls=%async_computation.7 | async-start | bytes 4718592 | tf_op jit(solution)/shard_map/all_to_all | solution.py:330
  3140.6 183.6 %reduce-scatter.15.cloned.1.call-start = ((), (), s32[]{:S(2)}) async-start(), calls=%async_computation.20 | async-start | bytes 11059200 | tf_op jit(solution)/shard_map/reduce_scatter | solution.py:353
  3144.8 8.4 copy-start.19
  3199.3 8.5 copy-start.21
  3223.2 235.8 %reduce-scatter.29.cloned.1.call-start = ((), (), s32[]{:S(2)}) async-start(), calls=%async_computation.27 | async-start | bytes 14745600
  3260.0 334.9 %reduce-scatter.21.cloned.1.call-start = ((), (), s32[]{:S(2)}) async-start(), calls=%async_computation.23 | async-start | bytes 14745600 | tf_op jit(solution)/shard_map/reduce_scatter | solution.py:362
  3260.7 11.5 copy-start.23
  3285.2 386.5 %reduce-scatter.27.cloned.1.call-start = ((), (), s32[]{:S(2)}) async-start(), calls=%async_computation.26 | async-start | bytes 819200
  3287.4 386.1 %reduce-scatter.25.cloned.1.call-start = ((), (), s32[]{:S(2)}) async-start(), calls=%async_computation.25 | async-start | bytes 1638400
  3326.6 362.8 %reduce-scatter.19.cloned.1.call-start = ((), (), s32[]{:S(2)}) async-start(), calls=%async_computation.22 | async-start | bytes 2048000 | tf_op jit(solution)/shard_map/reduce_scatter | solution.py:384
  3462.6 47.1 %copy-start.40 = (f32[1280]{0:T(1024)S(1)}, f32[1280]{0:T(1024)}, u32[]{:S(2)}) copy-start(f32[1280]{0:T(1024)} %copy-done.39) | copy-start | bytes 15364
  3462.6 47.1 %copy-start.48 = (f32[576]{0:T(1024)S(1)}, f32[576]{0:T(1024)}, u32[]{:S(2)}) copy-start(f32[576]{0:T(1024)} %copy-done.47) | copy-start | bytes 6916
  3462.6 47.1 %copy-start.50 = (f32[576]{0:T(1024)S(1)}, f32[576]{0:T(1024)}, u32[]{:S(2)}) copy-start(f32[576]{0:T(1024)} %copy-done.49) | copy-start | bytes 6916
  3462.6 261.4 %reduce-scatter.23.cloned.1.call-start = ((), (), s32[]{:S(2)}) async-start(), calls=%async_computation.24 | async-start | bytes 2048000 | tf_op jit(solution)/shard_map/reduce_scatter | solution.py:387
  3509.7 15.3 copy-start.46
  3509.7 85.3 %copy-start.12 = (bf16[2,288,1280]{2,1,0:T(8,128)(2,1)S(1)}, bf16[2,288,1280]{2,1,0:T(8,128)(2,1)}, u32[]{:S(2)}) copy-start(bf16[2,288,1280]{2,1,0:T(8,128)(2,1)} %param.25) | copy-start | bytes 4423684
  3599.7 53.4 %copy-start.18 = (f32[576,1280]{1,0:T(8,128)S(1)}, f32[576,1280]{1,0:T(8,128)}, u32[]{:S(2)}) copy-start(f32[576,1280]{1,0:T(8,128)} %copy-done.17) | copy-start | bytes 8847364
  3599.7 53.4 %copy-start.44 = (f32[576]{0:T(1024)S(1)}, f32[576]{0:T(1024)}, u32[]{:S(2)}) copy-start(f32[576]{0:T(1024)} %copy-done.43) | copy-start | bytes 6916
  3657.3 68.6 %copy-start.1 = (bf16[95,80]{0,1:T(8,128)(2,1)S(1)}, bf16[95,80]{0,1:T(8,128)(2,1)}, u32[]{:S(2)}) copy-start(bf16[95,80]{0,1:T(8,128)(2,1)} %param.39) | copy-start | bytes 45604
  (133 other events, 429.6 us)
Sparse Core Ops, SparseCore 0:
  9.9 102.4 all-gather.5
  114.2 45.0 all-gather.7
  161.2 126.8 all-gather.9
  289.8 126.9 all-gather.11
  3063.3 75.9 reduce-scatter.16
  3223.3 100.8 reduce-scatter.14
  3326.4 132.4 reduce-scatter.28
  3461.3 133.5 reduce-scatter.20
  3598.3 23.8 reduce-scatter.26
  3625.3 29.3 reduce-scatter.24
  3658.0 31.3 reduce-scatter.18
  3692.5 31.3 reduce-scatter.22
where the time goes:
time: 3760 us; the launch traced here: 3730 us
  local copies, waits for them, and re-layouts  1750 us (47%)
  matrix products  834 us (22%)
  waiting for transfers between devices  716 us (19%)
  other arithmetic  222 us (6%)
  blocking collectives  111 us (3%)
  loops' own time  45.5 us (1%)
    add x128, local copies, waits for them, and re-layouts, score_block(): scores.reshape(per_block, grid_side, grid_side, grid_side)  1240 us
    dot_general x32, matrix products, score_block(): lax.dot_general(query_block, key_rows, COLS_DIMS, preferred_element_type=...  207 us
    reshape x16, local copies, waits for them, and re-layouts, one_block(): grad_scores.astype(jnp.float32)  173 us
    reduce_sum x16, other arithmetic, one_block(): grad_rel_cols = jnp.sum(score_grid, 2)  140 us
    unnamed x15, waiting for transfers between devices  135 us
    all_gather x1, waiting for transfers between devices, on_device(): lax.all_gather(qkv_weight, 'dp', axis=0, tiled=True)  77.2 us
  transfers between devices with their start and end apart: 20, of which 14 were waited for; matrix products, arithmetic and copies ran while one was open for 30% of the time, Pallas kernels for 0%

commit v1 on v0

v1 whole, which is shorter than its diff:
```python
import math
from functools import partial

import jax
import jax.numpy as jnp
from jax import lax
from jax.experimental import pallas as pl
from jax.experimental.pallas import tpu as pltpu
from jax.sharding import PartitionSpec as P

H = 16
HD = 80


EPSILON = 1e-06
ROWS_DIMS = (((0,), (0,)), ((), ()))
COLS_DIMS = (((1,), (1,)), ((), ()))


NT = (((1,), (1,)), ((), ()))
TN = (((0,), (0,)), ((), ()))
BF = jnp.bfloat16
F32 = jnp.float32
LOG2E = 1.4426950408889634


def dot(a, b, dims=(((1,), (0,)), ((), ()))):
    return lax.dot_general(a, b, dims, preferred_element_type=F32)


def hot_table(seq_len, side):
    token = lax.broadcasted_iota(jnp.int32, (seq_len, 256), 0)
    lane = lax.broadcasted_iota(jnp.int32, (seq_len, 256), 1)
    row_hit = (lane >= HD) & (token // side == lane - HD)
    col_hit = (lane >= HD + side) & (token % side == lane - HD - side)
    ones = (lane >= HD + 2 * side) & (lane < HD + 2 * side + 3)
    return (row_hit | col_hit | ones).astype(BF)


def flip_tables(rel_h, rel_w):
    entries = rel_h.shape[0]
    pad = ((0, 128 - entries), (0, 0))
    return jnp.concatenate([jnp.pad(rel_h[::-1], pad), jnp.pad(rel_w[::-1], pad)], 0)


def fwd_kernel(heads, side, tq, x_ref, hot_ref, f_ref, o_ref, qa_ref, kp, vp, osc):
    seq_len = x_ref.shape[0]
    lanes = heads * HD
    step = pl.program_id(0)
    factor = LOG2E / math.sqrt(HD)

    @pl.when(step == 0)
    def _():
        rows = seq_len // 9

        def prep(i, c):
            part = pl.ds(pl.multiple_of(i * rows, rows), rows)
            hot = hot_ref[part, :]
            for h in range(heads):
                kp[h, part, :] = hot
                kp[h, part, 0:HD] = x_ref[part, lanes + h * HD : lanes + (h + 1) * HD]
                vp[h, part, :] = jnp.ones((rows, 128), BF)
                vp[h, part, 0:HD] = x_ref[part, 2 * lanes + h * HD : 2 * lanes + (h + 1) * HD]
            return c

        lax.fori_loop(0, 9, prep, 0)

    base = pl.ds(pl.multiple_of(step * tq, tq), tq)
    groups = tq // side
    lane = lax.broadcasted_iota(jnp.int32, (tq, 128), 1)
    for h in range(heads):
        q = x_ref[base, h * HD : (h + 1) * HD]
        g = dot(q, f_ref[...], NT) * math.sqrt(HD)
        gh = [
            pltpu.roll(g[i * side : (i + 1) * side, :128], 33 + step * groups + i, axis=1)
            for i in range(groups)
        ]
        gw = [
            pltpu.roll(g[i * side : (i + 1) * side, 128:], 81, axis=1, stride=1, stride_axis=0)
            for i in range(groups)
        ]
        qa_ref[h, :, 0:128] = jnp.concatenate(gh, 0).astype(BF)
        qa_ref[h, :, 0:HD] = q
        qa_ref[h, :, 128:256] = jnp.where(lane < side, jnp.concatenate(gw, 0), 0.0).astype(BF)

    def one(h, c):
        s = dot(qa_ref[h], kp[h], NT)
        m = jnp.max(s, -1, keepdims=True)
        p = jnp.exp2((s - m) * factor).astype(BF)
        o = dot(p, vp[h])
        total = o[:, HD : HD + 1]
        osc[h] = o / total
        norm = m + jnp.log2(total) / factor
        hi = norm.astype(BF).astype(F32)
        mid = (norm - hi).astype(BF).astype(F32)
        low = norm - hi - mid
        old = qa_ref[h, :, 128:256].astype(F32)
        old = jnp.where(lane == side, -hi, old)
        old = jnp.where(lane == side + 1, -mid, old)
        old = jnp.where(lane == side + 2, -low, old)
        qa_ref[h, :, 128:256] = old.astype(BF)
        return c

    lax.fori_loop(0, heads, one, 0)
    for h in range(heads):
        o_ref[:, h * HD : (h + 1) * HD] = osc[h][:, 0:HD].astype(BF)


def attention_forward(x, hot, tables, side, tq=192):
    seq_len, width = x.shape
    heads = width // (3 * HD)
    return pl.pallas_call(
        partial(fwd_kernel, heads, side, tq),
        grid=(seq_len // tq,),
        in_specs=[
            pl.BlockSpec((seq_len, width), lambda i: (0, 0), pipeline_mode=pl.Buffered(1)),
            pl.BlockSpec((seq_len, 256), lambda i: (0, 0), pipeline_mode=pl.Buffered(1)),
            pl.BlockSpec((256, HD), lambda i: (0, 0), pipeline_mode=pl.Buffered(1)),
        ],
        out_specs=[
            pl.BlockSpec((tq, heads * HD), lambda i: (i, 0)),
            pl.BlockSpec((heads, tq, 256), lambda i: (0, i, 0)),
        ],
        out_shape=[
            jax.ShapeDtypeStruct((seq_len, heads * HD), BF),
            jax.ShapeDtypeStruct((heads, seq_len, 256), BF),
        ],
        scratch_shapes=[
            pltpu.VMEM((heads, seq_len, 256), BF),
            pltpu.VMEM((heads, seq_len, 128), BF),
            pltpu.VMEM((heads, tq, 128), F32),
        ],
        compiler_params=pltpu.CompilerParams(
            dimension_semantics=("arbitrary",), vmem_limit_bytes=60 << 20
        ),
        name="attention_forward",
    )(x, hot, tables)


def bwd_kernel(heads, side, tb, uc, x_ref, hot_ref, f_ref, qa_ref, o_ref, go_ref, dx_ref, gt_ref, kp, kt, vp, dop, dk, dv, dq):
    seq_len = x_ref.shape[0]
    lanes = heads * HD
    h = pl.program_id(0)
    step = pl.program_id(1)
    factor = LOG2E / math.sqrt(HD)
    scale = HD ** (-0.5)

    @pl.when((h == 0) & (step == 0))
    def _():
        gt_ref[...] = jnp.zeros_like(gt_ref)
        rows = seq_len // 9

        def prep(i, c):
            part = pl.ds(pl.multiple_of(i * rows, rows), rows)
            hot = hot_ref[part, :]
            lane = lax.broadcasted_iota(jnp.int32, (rows, 128), 1)
            for n in range(heads):
                kp[n, part, :] = hot
                kp[n, part, 0:HD] = x_ref[part, lanes + n * HD : lanes + (n + 1) * HD]
                vp[n, part, :] = jnp.ones((rows, 128), BF)
                vp[n, part, 0:HD] = x_ref[part, 2 * lanes + n * HD : 2 * lanes + (n + 1) * HD]
                go = go_ref[part, n * HD : (n + 1) * HD]
                inner = jnp.sum(
                    go.astype(F32) * o_ref[part, n * HD : (n + 1) * HD].astype(F32), -1, keepdims=True
                )
                hi = inner.astype(BF).astype(F32)
                low = inner - hi
                tail = jnp.where(lane == HD, -hi, jnp.where(lane == HD + 1, -low, 0.0))
                dop[n, part, :] = tail.astype(BF)
                dop[n, part, 0:HD] = go
                kt[n, :, part] = kp[n, part, :].T
            return c

        lax.fori_loop(0, 9, prep, 0)

    @pl.when(step == 0)
    def _():
        dk[h] = jnp.zeros_like(dk[h])
        dv[h] = jnp.zeros_like(dv[h])

    base = pl.ds(pl.multiple_of(step * tb, tb), tb)
    qa = qa_ref[0]
    do = dop[h, base, :]

    def one(j, acc):
        part = pl.ds(pl.multiple_of(j * uc, uc), uc)
        s = dot(kp[h, part, :], qa, NT)
        dp = dot(vp[h, part, :], do, NT)
        p = jnp.exp2(s * factor)
        ds = (p * dp).astype(BF)
        dv[h, part, :] += dot(p.astype(BF), do)
        dk[h, part, :] += dot(ds, qa[:, 0:128])
        return acc + dot(kt[h, :, part], ds)

    acc = lax.fori_loop(0, seq_len // uc, one, jnp.zeros((256, tb), F32), unroll=True)
    acc = acc.T
    lane = lax.broadcasted_iota(jnp.int32, (tb, 128), 1)
    groups = tb // side
    first = jnp.where(lane < HD, 0.0, acc[:, :128])
    second = jnp.where(lane < side, acc[:, 128:], 0.0)
    back_h = [
        pltpu.roll(first[i * side : (i + 1) * side], 256 - 33 - step * groups - i, axis=1)
        for i in range(groups)
    ]
    back_w = [
        unroll_w(second[i * side : (i + 1) * side], side) for i in range(groups)
    ]
    both = jnp.concatenate([jnp.concatenate(back_h, 0), jnp.concatenate(back_w, 0)], 1).astype(BF)
    rel = dot(both, f_ref[...])
    dq[h, base, :] = acc[:, :HD] * scale + rel
    gt_ref[...] += dot(both, qa[:, 0:128], TN)

    @pl.when((h == heads - 1) & (step == pl.num_programs(1) - 1))
    def _():
        rows = seq_len // 9

        def post(i, c):
            part = pl.ds(pl.multiple_of(i * rows, rows), rows)
            for n in range(heads):
                dx_ref[part, n * HD : (n + 1) * HD] = dq[n, part, :].astype(BF)
                dx_ref[part, lanes + n * HD : lanes + (n + 1) * HD] = (dk[n, part, 0:HD] * scale).astype(BF)
                dx_ref[part, 2 * lanes + n * HD : 2 * lanes + (n + 1) * HD] = dv[n, part, 0:HD].astype(BF)
            return c

        lax.fori_loop(0, 9, post, 0)


def unroll_w(val, side):
    out = val
    row = lax.broadcasted_iota(jnp.int32, val.shape, 0)
    shift = side - 1 - row
    bit = 1
    while bit < side:
        out = jnp.where((shift & bit) != 0, pltpu.roll(out, bit, axis=1), out)
        bit *= 2
    return out


def attention_backward(x, hot, tables, qa, o, go, side, tb=768, uc=256):
    seq_len, width = x.shape
    heads = width // (3 * HD)
    whole = lambda *shape: pl.BlockSpec(shape, lambda h, i: (0,) * len(shape), pipeline_mode=pl.Buffered(1))
    return pl.pallas_call(
        partial(bwd_kernel, heads, side, tb, uc),
        grid=(heads, seq_len // tb),
        in_specs=[
            whole(seq_len, width),
            whole(seq_len, 256),
            whole(256, HD),
            pl.BlockSpec((1, tb, 256), lambda h, i: (h, i, 0)),
            whole(seq_len, heads * HD),
            whole(seq_len, heads * HD),
        ],
        out_specs=[
            whole(seq_len, width),
            whole(256, 128),
        ],
        out_shape=[
            jax.ShapeDtypeStruct((seq_len, width), BF),
            jax.ShapeDtypeStruct((256, 128), F32),
        ],
        scratch_shapes=[
            pltpu.VMEM((heads, seq_len, 256), BF),
            pltpu.VMEM((heads, 256, seq_len), BF),
            pltpu.VMEM((heads, seq_len, 128), BF),
            pltpu.VMEM((heads, seq_len, 128), BF),
            pltpu.VMEM((heads, seq_len, 128), F32),
            pltpu.VMEM((heads, seq_len, 128), F32),
            pltpu.VMEM((heads, seq_len, HD), F32),
        ],
        compiler_params=pltpu.CompilerParams(
            dimension_semantics=("arbitrary", "arbitrary"), vmem_limit_bytes=63 << 20
        ),
        name="attention_backward",
    )(x, hot, tables, qa, o, go)


def layer_norm(values, gain_vec, shift_vec):
    center = values - jnp.mean(values, -1, keepdims=True)
    spread = jnp.mean(center * center, -1, keepdims=True)
    return center * lax.rsqrt(spread + EPSILON) * gain_vec + shift_vec


def norm_back(values, gain_vec, upstream):

    def normalize(inputs_in, gains_in):
        return layer_norm(inputs_in, gains_in, 0.0)

    unused, pullback = jax.vjp(normalize, values, gain_vec)
    grad_values, grad_gain = pullback(upstream)
    return (grad_values, grad_gain, jnp.sum(upstream, 0))


def to_heads(parts, images, ranks):
    group = ranks // images
    stacked = jnp.stack([p.reshape(images, -1, group, H * HD // group) for p in parts], 3)
    rows = stacked.shape[1]
    return stacked.transpose(0, 2, 1, 3, 4).reshape(ranks, rows, len(parts) * H * HD // group)


def from_heads(stacked, images, parts):
    ranks, rows, width = stacked.shape
    group = ranks // images
    split = stacked.reshape(images, group, rows, parts, width // parts)
    return split.transpose(0, 2, 3, 1, 4).reshape(images * rows, parts * H * HD)


def exchange(stacked):
    return lax.all_to_all(stacked, "seq", split_axis=0, concat_axis=0, tiled=True)


def on_device(
    patches,
    ln1_gain,
    ln1_bias,
    qkv_weight,
    q_bias,
    v_bias,
    proj_weight,
    proj_bias,
    ln2_gain,
    ln2_bias,
    fc1_weight,
    fc1_bias,
    fc2_weight,
    fc2_bias,
    rel_pos_h,
    rel_pos_w,
    cotangent,
):
    images, row_count, model_width = patches.shape
    gathered = (
        lax.all_gather(ln1_gain, "dp", axis=0, tiled=True),
        lax.all_gather(ln1_bias, "dp", axis=0, tiled=True),
        lax.all_gather(qkv_weight, "dp", axis=0, tiled=True),
        lax.all_gather(q_bias, "dp", axis=0, tiled=True),
        lax.all_gather(v_bias, "dp", axis=0, tiled=True),
        lax.all_gather(proj_weight, "dp", axis=0, tiled=True),
        lax.all_gather(proj_bias, "dp", axis=0, tiled=True),
        lax.all_gather(ln2_gain, "dp", axis=0, tiled=True),
        lax.all_gather(ln2_bias, "dp", axis=0, tiled=True),
        lax.all_gather(fc1_weight, "dp", axis=0, tiled=True),
        lax.all_gather(fc1_bias, "dp", axis=0, tiled=True),
        lax.all_gather(fc2_weight, "dp", axis=0, tiled=True),
        lax.all_gather(fc2_bias, "dp", axis=0, tiled=True),
    )
    (
        gain_one,
        shift_one,
        qkv_full,
        q_shift,
        v_shift,
        proj_full,
        proj_shift,
        gain_two,
        shift_two,
        fc1_full,
        fc1_shift,
        fc2_full,
        fc2_shift,
    ) = gathered
    inputs_f = patches.reshape(images * row_count, model_width).astype(jnp.float32)
    normed = layer_norm(
        inputs_f, gain_one.astype(jnp.float32), shift_one.astype(jnp.float32)
    ).astype(jnp.bfloat16)
    joined = jnp.dot(normed, qkv_full, preferred_element_type=jnp.float32)
    queries = (joined[:, :model_width] + q_shift.astype(jnp.float32)).astype(jnp.bfloat16)
    key_part = joined[:, model_width : 2 * model_width].astype(jnp.bfloat16)
    value_part = (joined[:, 2 * model_width :] + v_shift.astype(jnp.float32)).astype(jnp.bfloat16)
    ranks = lax.axis_size("seq")
    head_rows = exchange(to_heads((queries, key_part, value_part), images, ranks))
    seq_len = ranks * row_count
    head_rows = head_rows.reshape(seq_len, -1)
    side = (rel_pos_h.shape[0] + 1) // 2
    hot = hot_table(seq_len, side)
    tables = flip_tables(rel_pos_h, rel_pos_w)
    attended, query_aug = attention_forward(head_rows, hot, tables, side)
    mixed_rows = from_heads(exchange(attended.reshape(ranks, row_count, -1)), images, 1)
    middle = (
        inputs_f
        + jnp.dot(mixed_rows, proj_full, preferred_element_type=jnp.float32)
        + proj_shift.astype(jnp.float32)
    )
    normed_two = layer_norm(
        middle, gain_two.astype(jnp.float32), shift_two.astype(jnp.float32)
    ).astype(jnp.bfloat16)
    before_act = jnp.dot(
        normed_two, fc1_full, preferred_element_type=jnp.float32
    ) + fc1_shift.astype(jnp.float32)
    activated = jax.nn.gelu(before_act, approximate=False).astype(jnp.bfloat16)
    result = (
        middle
        + jnp.dot(activated, fc2_full, preferred_element_type=jnp.float32)
        + fc2_shift.astype(jnp.float32)
    )
    output = result.astype(jnp.bfloat16).reshape(images, row_count, model_width)
    qkv_back, proj_back, fc1_back, fc2_back = (qkv_full, proj_full, fc1_full, fc2_full)
    gain_one_back, gain_two_back = (gain_one, gain_two)
    grad_out = cotangent.reshape(images * row_count, model_width).astype(jnp.float32)
    grad_branch = grad_out.astype(jnp.bfloat16)
    grad_fc2 = lax.dot_general(
        activated, grad_branch, ROWS_DIMS, preferred_element_type=jnp.float32
    )
    grad_fc2_shift = jnp.sum(grad_branch.astype(jnp.float32), 0)
    grad_activated = lax.dot_general(
        grad_branch, fc2_back, COLS_DIMS, preferred_element_type=jnp.float32
    )
    unused, gelu_pull = jax.vjp(partial(jax.nn.gelu, approximate=False), before_act)
    grad_before = gelu_pull(grad_activated)[0].astype(jnp.bfloat16)
    grad_fc1 = lax.dot_general(
        normed_two, grad_before, ROWS_DIMS, preferred_element_type=jnp.float32
    )
    grad_fc1_shift = jnp.sum(grad_before.astype(jnp.float32), 0)
    grad_normed_two = lax.dot_general(
        grad_before, fc1_back, COLS_DIMS, preferred_element_type=jnp.float32
    )
    grad_middle_norm, grad_gain_two, grad_shift_two = norm_back(
        middle, gain_two_back.astype(jnp.float32), grad_normed_two
    )
    grad_middle = grad_out + grad_middle_norm
    grad_proj_in = grad_middle.astype(jnp.bfloat16)
    grad_proj = lax.dot_general(
        mixed_rows, grad_proj_in, ROWS_DIMS, preferred_element_type=jnp.float32
    )
    grad_proj_shift = jnp.sum(grad_proj_in.astype(jnp.float32), 0)
    grad_mixed = lax.dot_general(
        grad_proj_in, proj_back, COLS_DIMS, preferred_element_type=jnp.float32
    ).astype(jnp.bfloat16)
    grad_heads = exchange(to_heads((grad_mixed,), images, ranks)).reshape(seq_len, -1)
    grad_rows, grad_tables = attention_backward(
        head_rows, hot, tables, query_aug, attended, grad_heads, side
    )
    grad_joined = from_heads(exchange(grad_rows.reshape(ranks, row_count, -1)), images, 3)
    grad_queries = grad_joined[:, :model_width]
    grad_value_part = grad_joined[:, 2 * model_width :]
    grad_qkv = lax.dot_general(normed, grad_joined, ROWS_DIMS, preferred_element_type=jnp.float32)
    grad_q_shift = jnp.sum(grad_queries.astype(jnp.float32), 0)
    grad_v_shift = jnp.sum(grad_value_part.astype(jnp.float32), 0)
    grad_normed = lax.dot_general(
        grad_joined, qkv_back, COLS_DIMS, preferred_element_type=jnp.float32
    )
    grad_inputs_norm, grad_gain_one, grad_shift_one = norm_back(
        inputs_f, gain_one_back.astype(jnp.float32), grad_normed
    )
    grad_patches = (
        (grad_middle + grad_inputs_norm)
        .astype(jnp.bfloat16)
        .reshape(images, row_count, model_width)
    )
    entries = rel_pos_h.shape[0]
    grad_rel_h = grad_tables[:entries, :HD][::-1]
    grad_rel_w = grad_tables[128 : 128 + entries, :HD][::-1]
    matrix_sums = (
        lax.psum_scatter(
            grad_qkv.astype(jnp.bfloat16), "seq", scatter_dimension=1, tiled=True
        ).astype(jnp.float32),
        lax.psum_scatter(
            grad_proj.astype(jnp.bfloat16), "seq", scatter_dimension=1, tiled=True
        ).astype(jnp.float32),
        lax.psum_scatter(
            grad_fc1.astype(jnp.bfloat16), "seq", scatter_dimension=1, tiled=True
        ).astype(jnp.float32),
        lax.psum_scatter(
            grad_fc2.astype(jnp.bfloat16), "seq", scatter_dimension=1, tiled=True
        ).astype(jnp.float32),
    )
    vector_sums = (
        lax.psum(grad_gain_one.astype(jnp.bfloat16), "seq").astype(jnp.float32),
        lax.psum(grad_shift_one.astype(jnp.bfloat16), "seq").astype(jnp.float32),
        lax.psum(grad_q_shift.astype(jnp.bfloat16), "seq").astype(jnp.float32),
        lax.psum(grad_v_shift.astype(jnp.bfloat16), "seq").astype(jnp.float32),
        lax.psum(grad_proj_shift.astype(jnp.bfloat16), "seq").astype(jnp.float32),
        lax.psum(grad_gain_two.astype(jnp.bfloat16), "seq").astype(jnp.float32),
        lax.psum(grad_shift_two.astype(jnp.bfloat16), "seq").astype(jnp.float32),
        lax.psum(grad_fc1_shift.astype(jnp.bfloat16), "seq").astype(jnp.float32),
        lax.psum(grad_fc2_shift.astype(jnp.bfloat16), "seq").astype(jnp.float32),
    )
    owned = (
        lax.psum_scatter(
            matrix_sums[0].astype(jnp.bfloat16), "dp", scatter_dimension=0, tiled=True
        ).astype(jnp.float32),
        lax.psum_scatter(
            matrix_sums[1].astype(jnp.bfloat16), "dp", scatter_dimension=0, tiled=True
        ).astype(jnp.float32),
        lax.psum_scatter(
            matrix_sums[2].astype(jnp.bfloat16), "dp", scatter_dimension=0, tiled=True
        ).astype(jnp.float32),
        lax.psum_scatter(
            matrix_sums[3].astype(jnp.bfloat16), "dp", scatter_dimension=0, tiled=True
        ).astype(jnp.float32),
        lax.psum_scatter(
            vector_sums[0].astype(jnp.bfloat16), "dp", scatter_dimension=0, tiled=True
        ).astype(jnp.float32),
        lax.psum_scatter(
            vector_sums[1].astype(jnp.bfloat16), "dp", scatter_dimension=0, tiled=True
        ).astype(jnp.float32),
        lax.psum_scatter(
            vector_sums[2].astype(jnp.bfloat16), "dp", scatter_dimension=0, tiled=True
        ).astype(jnp.float32),
        lax.psum_scatter(
            vector_sums[3].astype(jnp.bfloat16), "dp", scatter_dimension=0, tiled=True
        ).astype(jnp.float32),
        lax.psum_scatter(
            vector_sums[4].astype(jnp.bfloat16), "dp", scatter_dimension=0, tiled=True
        ).astype(jnp.float32),
        lax.psum_scatter(
            vector_sums[5].astype(jnp.bfloat16), "dp", scatter_dimension=0, tiled=True
        ).astype(jnp.float32),
        lax.psum_scatter(
            vector_sums[6].astype(jnp.bfloat16), "dp", scatter_dimension=0, tiled=True
        ).astype(jnp.float32),
        lax.psum_scatter(
            vector_sums[7].astype(jnp.bfloat16), "dp", scatter_dimension=0, tiled=True
        ).astype(jnp.float32),
        lax.psum_scatter(
            vector_sums[8].astype(jnp.bfloat16), "dp", scatter_dimension=0, tiled=True
        ).astype(jnp.float32),
    )
    table_sums = lax.psum((grad_rel_h, grad_rel_w), ("dp", "seq"))
    return (
        output,
        grad_patches,
        owned[4],
        owned[5],
        owned[0],
        owned[6],
        owned[7],
        owned[1],
        owned[8],
        owned[9],
        owned[10],
        owned[2],
        owned[11],
        owned[3],
        owned[12],
        table_sums[0],
        table_sums[1],
    )


def solution(mesh):
    placed = (
        P("dp", "seq", None),
        P("dp"),
        P("dp"),
        P("dp", None),
        P("dp"),
        P("dp"),
        P("dp", None),
        P("dp"),
        P("dp"),
        P("dp"),
        P("dp", None),
        P("dp"),
        P("dp", None),
        P("dp"),
        P(),
        P(),
        P("dp", "seq", None),
    )
    return jax.shard_map(
        on_device,
        mesh=mesh,
        in_specs=placed,
        out_specs=(
            P("dp", "seq", None),
            P("dp", "seq", None),
            P("dp"),
            P("dp"),
            P("dp", "seq"),
            P("dp"),
            P("dp"),
            P("dp", "seq"),
            P("dp"),
            P("dp"),
            P("dp"),
            P("dp", "seq"),
            P("dp"),
            P("dp", "seq"),
            P("dp"),
            P(),
            P(),
        ),
        check_vma=False,
    )
```

time: 3760 us -> 1180 us (0.31)
  local copies, waits for them, and re-layouts: 1750 us -> 115 us
  matrix products: 834 us -> 161 us
  waiting for transfers between devices: 716 us -> 471 us
  other arithmetic: 222 us -> 49.1 us
  Pallas kernels: 0 us -> 159 us
  blocking collectives: 111 us -> 185 us
  loops' own time: 45.5 us -> 0 us
    add x144 -> x0, local copies, waits for them, and re-layouts: 1240 us -> none  [the longest x128 1240 us: score_block(): scores.reshape(per_block, grid_side, grid_side, grid_side)]
    dot_general x244 -> x0, matrix products: 674 us -> none  [the longest x32 207 us: score_block(): lax.dot_general(query_block, key_rows, COLS_DIMS, preferred_element_type=...]
    reshape x40 -> x3, local copies, waits for them, and re-layouts: 210 us -> 20.4 us  [the longest x2 12.6 us: from_heads(): return split.transpose(0, 2, 3, 1, 4).reshape(images * rows, parts * H * HD)]
    pallas_call x0 -> x2, Pallas kernels: none -> 159 us  [the longest x1 92 us: attention_backward(): pl.pallas_call(partial(bwd_kernel, heads, side, tb, uc), grid=(heads, seq...]
    reduce_sum x33 -> x0, other arithmetic: 155 us -> none  [the longest x16 140 us: one_block(): grad_rel_cols = jnp.sum(score_grid, 2)]
    unnamed x15, waiting for transfers between devices: 135 us -> 27.3 us
    while x235 -> x0, local copies, waits for them, and re-layouts: 101 us -> none
    all_to_all x0 -> x1, blocking collectives: none -> 75.8 us  [exchange(): lax.all_to_all(stacked, 'seq', split_axis=0, concat_axis=0, tiled=True)]
  transfers between devices with their start and end apart: 20 -> 15, of which waited for: 14 -> 7; matrix products, arithmetic and copies ran while one was open for 30% -> 22% of each run, Pallas kernels for 0% -> 14%
where the time goes in v1:
time: 1180 us; the launch traced here: 1170 us
  waiting for transfers between devices  471 us (40%)
  blocking collectives  185 us (16%)
  matrix products  161 us (14%)
  Pallas kernels  159 us (13%)
  local copies, waits for them, and re-layouts  115 us (10%)
  other arithmetic  49.1 us (4%)
  between operations  17.2 us (1%)
  starting transfers between devices  14.1 us (1%)
    all_to_all x3, waiting for transfers between devices, exchange(): lax.all_to_all(stacked, 'seq', split_axis=0, concat_axis=0, tiled=True)  312 us
    pallas_call x1, Pallas kernels, attention_backward(): pl.pallas_call(partial(bwd_kernel, heads, side, tb, uc), grid=(heads, seq...  92 us
    all_gather x1, waiting for transfers between devices, on_device(): lax.all_gather(qkv_weight, 'dp', axis=0, tiled=True)  77.4 us
    all_to_all x1, blocking collectives, exchange(): lax.all_to_all(stacked, 'seq', split_axis=0, concat_axis=0, tiled=True)  75.8 us
    pallas_call x1, Pallas kernels, attention_forward(): pl.pallas_call(partial(fwd_kernel, heads, side, tq), grid=(seq_len // tq,...  66.6 us
    reduce_scatter x1, waiting for transfers between devices, on_device(): lax.psum_scatter(grad_qkv.astype(jnp.bfloat16), 'seq', scatter_dimension=...  50.4 us
    psum x1, blocking collectives, on_device(): table_sums = lax.psum((grad_rel_h, grad_rel_w), ('dp', 'seq'))  39.9 us
    unnamed x116, local copies, waits for them, and re-layouts  39.9 us
  transfers between devices with their start and end apart: 15, of which 7 were waited for; matrix products, arithmetic and copies ran while one was open for 22% of the time, Pallas kernels for 14%

profile of v1, /device:TPU:0, one launch (start us, length us, event | category | flops | bytes accessed | tf_op | source)
XLA Modules:
  0.0 1170.9 jit_solution(7440116497457455185)
XLA Ops:
  13.1 18.2 %all-reduce.22 = (bf16[1280]{0:T(1024)(128)(2,1)S(1)}, bf16[1280]{0:T(1024)(128)(2,1)S(1)}, bf16[1280]{0:T(1024)(128)(2,1)S(1)}, bf16[1280]{0:T(1024)(128)(2,1)S...) all-reduce(bf16[1280]{0:T(1024)(128)(2,1)S(1)} %dynamic-update-slic, ...), channel_id=1, replica_groups=mesh['dp'=4,'seq'=8] {'dp'}, use_global_device_ids=true, to_apply=%add.3 | all-reduce | flops 8960 | bytes 35840
  33.0 2.0 bitcast_subtract_fusion
  35.0 77.4 %all-gather.6.cloned.1.call-done = bf16[1280,3840]{1,0:T(8,128)(2,1)} async-done(((bf16[320,3840]{1,0:T(8,128)(2,1)}), bf16[1280,3840]{1,0:T(8,128)(2,1)}) %all-gather.6.cloned.1.call-update) | async-done | bytes 9830416 | tf_op jit(solution)/shard_map/all_gather | solution.py:335
  112.5 9.3 fusion.17
  121.8 1.3 slice.43
  123.0 1.6 fusion.10
  124.7 3.0 stack_reshape.12
  127.7 4.1 copy.66
  131.8 4.4 stack_reshape.14
  136.2 5.2 copy.68
  141.4 4.4 stack_reshape.13
  145.9 5.1 copy.67
  151.0 5.8 pad_maximum_fusion
  156.8 7.9 copy.69
  164.7 4.9 all-to-all-start
  170.7 4.8 fusion.14.hot_ref
  175.4 99.4 %all-to-all-done = bf16[8,288,960]{2,1,0:T(8,128)(2,1)} async-done(((bf16[8,288,960]{2,1,0:T(8,128)(2,1)}), bf16[8,288,960]{2,1,0:T(8,128)(2,1)}, u32[]{:S(2)}, u32[]{:S(2)}) %all-to-all-start) | async-done | bytes 4423712 | tf_op jit(solution)/shard_map/all_to_all | solution.py:309
  274.8 66.6 %attention_forward.1 = (bf16[2304,320]{1,0:T(8,128)(2,1)}, bf16[4,2304,256]{2,1,0:T(8,128)(2,1)}) custom-call(bf16[2304,960]{1,0:T(8,128)(2,1)} %bitcast.4.x_ref, bf16[2304,256]{1,0:T(8,128)(2,1)} %fusion.14.hot_ref, bf16[256,80]{1,0:T(8,128)(2,1)} %fusion.23.f_ref), custom_call_target="tpu_custom_call" | custom-call | tf_op jit(solution)/shard_map/attention_forward/pallas_call | solution.py:112
  341.4 4.0 all-to-all-start.1
  345.5 8.2 all-gather
  353.7 33.6 %all-to-all-done.1 = bf16[8,288,320]{2,1,0:T(8,128)(2,1)S(1)} async-done(((bf16[8,288,320]{2,1,0:T(8,128)(2,1)}), bf16[8,288,320]{2,1,0:T(8,128)(2,1)S(1)}, u32[]{:S(2)}, u32[]{:S(2)}) %all-to-all-start.1) | async-done | bytes 1474592 | tf_op jit(solution)/shard_map/all_to_all | solution.py:309
  387.4 2.2 copy.72
  389.5 3.1 reshape.181
  392.7 4.7 fusion.42
  397.9 1.1 copy-done.6
  399.0 14.6 %fusion.33 = f32[576,5120]{1,0:T(8,128)} fusion(bf16[1280,5120]{1,0:T(8,128)(2,1)} %all-gather.10.cloned.1.call-done, f32[576,1280]{1,0:T(8,128)} %copy-done.6, f32[1280]{0:T(1024)S(1)} %convert_element_type.200, f32[1280]{0:T(1024)S(1)} %convert_element_type.199, f32[576]{0:T(1024)S(1)} %fusion.30, f32[576]{0:T(1024)S(1)} %broadcast_multiply_fusion), kind=kOutput, calls=%fused_computation.94 | convolution fusion | flops 7553433600 | bytes 27867648 | tf_op jit(solution)/shard_map/dot_general | solution.py:387
  413.6 3.4 all-gather.12.cloned.1.call-done
  417.0 38.7 %fusion.35 = (bf16[5120]{0:T(1024)(128)(2,1)S(1)}, bf16[576,5120]{1,0:T(8,128)(2,1)S(1)}, f32[576,5120]{1,0:T(8,128)}) fusion(f32[576,5120]{1,0:T(8,128)} %fusion.33, f32[5120]{0:T(1024)S(1)} %bitcast.74, bf16[576,1280]{1,0:T(8,128)(2,1)S(1)} %bitcast.63, bf16[5120,1280]{1,0:T(8,128)(2,1)} %all-gather.12.cloned.1.call-done), kind=kOutput, calls=%fused_computation.96 | convolution fusion | flops 7767976960 | bytes 44103680 | tf_op jit(solution)/shard_map/dot_general | solution.py:405
  455.6 13.9 %multiply_reduce_fusion = (bf16[1280]{0:T(1024)(128)(2,1)S(1)}, f32[576]{0:T(1024)S(1)}, bf16[1280]{0:T(1024)(128)(2,1)S(1)}, f32[576,1280]{1,0:T(8,128)S(1)}) fusion(f32[576,1280]{1,0:T(8,128)S(1)} %copy-done.7, f32[576]{0:T(1024)S(1)} %fusion.30, f32[576]{0:T(1024)S(1)} %broadcast_multiply_fusion, f32[1280]{0:T(1024)S(1)} %convert_element_type.199, ...), kind=kOutput, calls=%fused_computation.36 | convolution fusion | flops 7555642368 | bytes 24920832 | tf_op jit(solution)/shard_map/dot_general | solution.py:414
  470.9 1.0 copy-done.2
  472.9 4.2 convolution_convert_fusion.3
  477.1 16.6 %convolution_convert_fusion.1 = bf16[1280,5120]{1,0:T(8,128)(2,1)} fusion(bf16[576,5120]{1,0:T(8,128)(2,1)} %copy-done.38, f32[576,1280]{1,0:T(8,128)} %copy-done.6, f32[1280]{0:T(1024)S(1)} %convert_element_type.200, f32[1280]{0:T(1024)S(1)} %convert_element_type.199, f32[576]{0:T(1024)S(1)} %fusion.30, f32[576]{0:T(1024)S(1)} %broadcast_multiply_fusion), kind=kOutput, calls=%fused_computation.1 | convolution fusion | flops 7559987200 | bytes 21969408 | tf_op jit(solution)/shard_map/dot_general | solution.py:410
  493.7 17.8 %copy.83 = bf16[1280,5120]{0,1:T(8,128)(2,1)} copy(bf16[1280,5120]{1,0:T(8,128)(2,1)} %convolution_convert_fusion.1) | data formatting | bytes 26214400
  511.5 8.9 multiply_convert_fusion
  520.4 2.5 copy-done.9
  523.0 13.0 %convolution_convert_fusion = bf16[5120,1280]{0,1:T(8,128)(2,1)} fusion(bf16[576,5120]{1,0:T(8,128)(2,1)S(1)} %multiply_convert_fusion, bf16[576,1280]{1,0:T(8,128)(2,1)S(1)} %bitcast.64), kind=kOutput, calls=%fused_computation | convolution fusion | flops 7556300800 | bytes 20480000 | tf_op jit(solution)/shard_map/dot_general | solution.py:401
  536.0 5.1 convolution_convert_fusion.4
  541.2 3.4 stack_reshape.15
  544.8 75.8 %all_to_all.20 = bf16[8,288,320]{2,1,0:T(8,128)(2,1)} all-to-all(bf16[8,288,320]{2,1,0:T(8,128)(2,1)S(1)} %bitcast.69), channel_id=1, replica_groups=mesh['dp'=4,'seq'=8] {'seq'}, dimensions={0} | all-to-all | bytes 2949120 | tf_op jit(solution)/shard_map/all_to_all | solution.py:309
  620.6 92.0 %attention_backward.1 = (bf16[2304,960]{1,0:T(8,128)(2,1)}, f32[256,128]{1,0:T(8,128)}) custom-call(bf16[2304,960]{1,0:T(8,128)(2,1)} %bitcast.4.x_ref, bf16[2304,256]{1,0:T(8,128)(2,1)} %fusion.14.hot_ref, bf16[256,80]{1,0:T(8,128)(2,1)} %fusion.23.f_ref, bf16[4,2304,256]{2,1,0:T(8,128)(2,1)} %get-tuple-element.22.qa_ref, ...), custom_call_target="tpu_custom_call" | custom-call | tf_op jit(solution)/shard_map/attention_backward/pallas_call | solution.py:243
  712.6 4.7 all-to-all-start.3
  718.1 2.1 copy.81
  720.3 179.2 %all-to-all-done.3 = bf16[8,288,960]{2,1,0:T(8,128)(2,1)} async-done(((bf16[8,288,960]{2,1,0:T(8,128)(2,1)}), bf16[8,288,960]{2,1,0:T(8,128)(2,1)}, u32[]{:S(2)}, u32[]{:S(2)}) %all-to-all-start.3) | async-done | bytes 4423712 | tf_op jit(solution)/shard_map/all_to_all | solution.py:309
  899.4 8.2 copy.74
  907.7 13.1 %copy.75 = bf16[2,288,3,4,320]{4,3,2,1,0:T(4,128)(2,1)} copy(bf16[2,288,3,4,320]{1,4,2,3,0:T(8,128)(2,1)} %bitcast.62) | data formatting | bytes 8847360 | tf_op jit(solution)/shard_map/transpose | solution.py:305
  920.8 9.4 reshape.188
  930.2 13.7 %convolution_convert_fusion.2 = bf16[1280,3840]{0,1:T(8,128)(2,1)} fusion(bf16[576,1280]{1,0:T(8,128)(2,1)S(1)} %bitcast.73, bf16[576,3840]{1,0:T(8,128)(2,1)} %reshape.188), kind=kOutput, calls=%fused_computation.3 | convolution fusion | flops 5667225600 | bytes 15728640 | tf_op jit(solution)/shard_map/dot_general | solution.py:436
  944.0 3.6 copy.84
  949.7 39.9 %all-reduce.19 = (f32[95,80]{1,0:T(8,128)S(1)}, f32[95,80]{1,0:T(8,128)S(1)}) all-reduce(f32[95,80]{1,0:T(8,128)S(1)} %rev.14, f32[95,80]{1,0:T(8,128)S(1)} %rev.15), channel_id=1, replica_groups=mesh['dp'=4,'seq'=8] {'dp','seq'}, use_global_device_ids=true, to_apply=%region_43.44 | all-reduce | flops 15200 | bytes 121600 | tf_op jit(solution)/shard_map/psum | solution.py:519
  991.1 1.0 copy.82
  992.8 12.4 %fusion.34 = (bf16[1280]{0:T(1024)(128)(2,1)S(1)}, f32[576]{0:T(1024)S(1)}, bf16[1280]{0:T(1024)(128)(2,1)S(1)}, f32[576,1280]{1,0:T(8,128)S(1)}) fusion(f32[576,1280]{1,0:T(8,128)} %bitcast_subtract_fusion, f32[1280]{0:T(1024)S(1)} %copy-done.13, f32[576]{0:T(1024)S(1)} %copy-done.26, f32[576]{0:T(1024)S(1)} %copy-done.18, ...), kind=kOutput, calls=%fused_computation.95 | convolution fusion | flops 5668942848 | bytes 21644032 | tf_op jit(solution)/shard_map/dot_general | solution.py:439
  1005.2 2.3 add_add_fusion
  1007.6 2.2 reduce_sum.188
  1009.8 50.4 %reduce-scatter.15.cloned.1.call-done = bf16[1280,480]{0,1:T(8,128)(2,1)} async-done(((bf16[1280,3840]{0,1:T(8,128)(2,1)}), bf16[1280,480]{0,1:T(8,128)(2,1)}) %reduce-scatter.15.cloned.1.call-update) | async-done | bytes 1228816 | tf_op jit(solution)/shard_map/reduce_scatter | solution.py:454
  1060.1 2.5 copy.79
  1062.6 4.0 add_convert_fusion.2
  1066.6 2.7 slice_reduce_fusion
  1069.3 16.9 %all-reduce.21 = (bf16[1280]{0:T(1024)(128)(2,1)S(1)}, bf16[1280]{0:T(1024)(128)(2,1)S(1)}, bf16[1280]{0:T(1024)(128)(2,1)S(1)}, bf16[1280]{0:T(1024)(128)(2,1)S...) all-reduce(bf16[1280]{0:T(1024)(128)(2,1)S(1)} %dynamic-update-slic, ...), channel_id=1, replica_groups=mesh['dp'=4,'seq'=8] {'dp'}, use_global_device_ids=true, to_apply=%add.9 | all-reduce | flops 16640 | bytes 66560
  1087.0 26.2 %all-reduce.20 = (bf16[320]{0:T(512)(128)(2,1)S(1)}, bf16[320]{0:T(512)(128)(2,1)S(1)}, bf16[320]{0:T(512)(128)(2,1)S(1)}, bf16[320]{0:T(512)(128)(2,1)S(1)}, bf...) all-reduce(bf16[320]{0:T(512)(128)(2,1)S(1)} %dynamic-slice.9, ...), channel_id=1, replica_groups=mesh['dp'=4,'seq'=8] {'seq'}, use_global_device_ids=true, to_apply=%region_9.10 | all-reduce | flops 3840 | bytes 15360 | tf_op jit(solution)/shard_map/psum | solution.py:468
  1118.4 14.7 %fusion.8 = bf16[576,1280]{1,0:T(8,128)(2,1)} fusion(f32[576,1280]{1,0:T(8,128)S(1)} %copy-done.8, bf16[576,5120]{1,0:T(8,128)(2,1)} %copy-done.9, bf16[5120,1280]{1,0:T(8,128)(2,1)} %all-gather.12.cloned.1.call-done, f32[1280]{0:T(1024)S(1)} %convert_element_type.204), kind=kOutput, calls=%fused_computation.28 | convolution fusion | flops 7551959040 | bytes 23434240 | tf_op jit(solution)/shard_map/dot_general | solution.py:393
  1133.1 1.9 convert_element_type.229
  1135.1 1.9 convert_element_type.232
  1137.0 24.6 %reduce-scatter.25.cloned.1.call-done = bf16[320,480]{1,0:T(8,128)(2,1)} async-done(((bf16[1280,480]{1,0:T(8,128)(2,1)}), bf16[320,480]{1,0:T(8,128)(2,1)}) %reduce-scatter.25.cloned.1.call-update) | async-done | bytes 307216
  1161.6 1.2 copy.80
  (189 shorter events, 21.6 us)
Async XLA Ops:
  7.2 105.3 %all-gather.6.cloned.1.call-start = ((), (), s32[]{:S(2)}) async-start(), calls=%async_computation.12 | async-start | bytes 12288000 | tf_op jit(solution)/shard_map/all_gather | solution.py:335
  7.9 384.8 %all-gather.8.cloned.1.call-start = ((), (), s32[]{:S(2)}) async-start(), calls=%async_computation.13 | async-start | bytes 4096000 | tf_op jit(solution)/shard_map/all_gather | solution.py:338
  8.7 1.4 copy-start.29
  8.7 2.7 copy-start.30
  8.7 2.9 copy-start.31
  8.7 3.2 copy-start.32
  8.7 3.4 copy-start.33
  8.7 3.7 copy-start.34
  8.7 3.9 copy-start.35
  8.7 4.1 copy-start.36
  8.8 22.6 %copy-start = (bf16[2,288,1280]{2,1,0:T(8,128)(2,1)S(1)}, bf16[2,288,1280]{2,1,0:T(8,128)(2,1)}, u32[]{:S(2)}) copy-start(bf16[2,288,1280]{2,1,0:T(8,128)(2,1)} %param.17) | copy-start | bytes 4423684
  8.8 390.2 %all-gather.10.cloned.1.call-start = ((), (), s32[]{:S(2)}) async-start(), calls=%async_computation.14 | async-start | bytes 16384000 | tf_op jit(solution)/shard_map/all_gather | solution.py:342
  9.5 407.4 %all-gather.12.cloned.1.call-start = ((), (), s32[]{:S(2)}) async-start(), calls=%async_computation.15 | async-start | bytes 16384000 | tf_op jit(solution)/shard_map/all_gather | solution.py:344
  31.3 81.1 %copy-start.12 = (f32[1280]{0:T(1024)}, f32[1280]{0:T(1024)S(1)}, u32[]{:S(2)}) copy-start(f32[1280]{0:T(1024)S(1)} %convert_element_type.190) | copy-start | bytes 15364
  31.4 81.1 %copy-start.21 = (f32[1280]{0:T(1024)}, f32[1280]{0:T(1024)S(1)}, u32[]{:S(2)}) copy-start(f32[1280]{0:T(1024)S(1)} %convert_element_type.191) | copy-start | bytes 15364
  31.6 3.4 copy-start.15
  31.7 3.3 copy-start.17
  32.9 88.8 %copy-start.19 = (f32[576]{0:T(1024)}, f32[576]{0:T(1024)S(1)}, u32[]{:S(2)}) copy-start(f32[576]{0:T(1024)S(1)} %add.175) | copy-start | bytes 6916
  32.9 88.8 %copy-start.25 = (f32[576]{0:T(1024)}, f32[576]{0:T(1024)S(1)}, u32[]{:S(2)}) copy-start(f32[576]{0:T(1024)S(1)} %rsqrt.25) | copy-start | bytes 6916
  164.7 4.9 copy-start.23
  164.7 5.1 copy-start.24
  164.7 110.1 %all-to-all-start = ((bf16[8,288,960]{2,1,0:T(8,128)(2,1)}), bf16[8,288,960]{2,1,0:T(8,128)(2,1)}, u32[]{:S(2)}, u32[]{:S(2)}) async-start(bf16[8,288,960]{2,1,0:T(8,128)(2,1)} %copy.69), calls=%async_computation | async-start | bytes 9437184 | tf_op jit(solution)/shard_map/all_to_all | solution.py:309
  341.4 4.1 copy-start.28
  341.4 46.0 %all-to-all-start.1 = ((bf16[8,288,320]{2,1,0:T(8,128)(2,1)}), bf16[8,288,320]{2,1,0:T(8,128)(2,1)S(1)}, u32[]{:S(2)}, u32[]{:S(2)}) async-start(bf16[8,288,320]{2,1,0:T(8,128)(2,1)} %bitcast.65), calls=%async_computation.1 | async-start | bytes 3538944 | tf_op jit(solution)/shard_map/all_to_all | solution.py:309
  345.4 372.7 %reduce-scatter.17.cloned.1.call-start = ((), (), s32[]{:S(2)}) async-start(), calls=%async_computation.17 | async-start | bytes 3686400 | tf_op jit(solution)/shard_map/reduce_scatter | solution.py:457
  392.7 4.7 copy-start.10
  397.4 1.6 copy-start.6
  399.0 17.9 %copy-start.4 = (bf16[2,288,1280]{2,1,0:T(8,128)(2,1)S(1)}, bf16[2,288,1280]{2,1,0:T(8,128)(2,1)}, u32[]{:S(2)}) copy-start(bf16[2,288,1280]{2,1,0:T(8,128)(2,1)} %param.33) | copy-start | bytes 4423684
  416.9 38.7 %copy-start.7 = (f32[576,1280]{1,0:T(8,128)S(1)}, f32[576,1280]{1,0:T(8,128)}, u32[]{:S(2)}) copy-start(f32[576,1280]{1,0:T(8,128)} %copy-done.6) | copy-start | bytes 8847364
  455.6 13.9 %copy-start.38 = (bf16[576,5120]{1,0:T(8,128)(2,1)}, bf16[576,5120]{1,0:T(8,128)(2,1)S(1)}, u32[]{:S(2)}) copy-start(bf16[576,5120]{1,0:T(8,128)(2,1)S(1)} %get-tuple-element.130) | copy-start | bytes 17694724
  470.4 1.6 copy-start.2
  470.4 2.4 copy-start.11
  477.1 466.9 %reduce-scatter.29.cloned.1.call-start = ((), (), s32[]{:S(2)}) async-start(), calls=%async_computation.23 | async-start | bytes 14745600
  511.4 438.1 %reduce-scatter.21.cloned.1.call-start = ((), (), s32[]{:S(2)}) async-start(), calls=%async_computation.19 | async-start | bytes 14745600 | tf_op jit(solution)/shard_map/reduce_scatter | solution.py:463
  520.4 2.6 copy-start.9
  712.6 4.8 copy-start.1
  712.6 4.8 copy-start.13
  712.6 4.9 copy-start.16
  712.6 4.9 copy-start.22
  712.6 4.9 copy-start.27
  712.6 186.8 %all-to-all-start.3 = ((bf16[8,288,960]{2,1,0:T(8,128)(2,1)}), bf16[8,288,960]{2,1,0:T(8,128)(2,1)}, u32[]{:S(2)}, u32[]{:S(2)}) async-start(bf16[8,288,960]{2,1,0:T(8,128)(2,1)} %bitcast.70), calls=%async_computation.3 | async-start | bytes 9437184 | tf_op jit(solution)/shard_map/all_to_all | solution.py:309
  717.4 273.7 %reduce-scatter.27.cloned.1.call-start = ((), (), s32[]{:S(2)}) async-start(), calls=%async_computation.22 | async-start | bytes 819200
  720.2 339.9 %reduce-scatter.15.cloned.1.call-start = ((), (), s32[]{:S(2)}) async-start(), calls=%async_computation.16 | async-start | bytes 11059200 | tf_op jit(solution)/shard_map/reduce_scatter | solution.py:454
  943.9 3.8 copy-start.5
  943.9 189.2 %reduce-scatter.19.cloned.1.call-start = ((), (), s32[]{:S(2)}) async-start(), calls=%async_computation.18 | async-start | bytes 2048000 | tf_op jit(solution)/shard_map/reduce_scatter | solution.py:485
  944.0 5.3 copy-start.37
  947.6 2.0 copy-start.14
  947.6 45.2 %copy-start.18 = (f32[576]{0:T(1024)S(1)}, f32[576]{0:T(1024)}, u32[]{:S(2)}) copy-start(f32[576]{0:T(1024)} %copy-done.17) | copy-start | bytes 6916
  947.6 45.2 %copy-start.26 = (f32[576]{0:T(1024)S(1)}, f32[576]{0:T(1024)}, u32[]{:S(2)}) copy-start(f32[576]{0:T(1024)} %copy-done.25) | copy-start | bytes 6916
  947.7 187.4 %reduce-scatter.23.cloned.1.call-start = ((), (), s32[]{:S(2)}) async-start(), calls=%async_computation.20 | async-start | bytes 2048000 | tf_op jit(solution)/shard_map/reduce_scatter | solution.py:488
  949.6 212.0 %reduce-scatter.25.cloned.1.call-start = ((), (), s32[]{:S(2)}) async-start(), calls=%async_computation.21 | async-start | bytes 1638400
  992.8 12.4 %copy-start.20 = (f32[576]{0:T(1024)S(1)}, f32[576]{0:T(1024)}, u32[]{:S(2)}) copy-start(f32[576]{0:T(1024)} %copy-done.19) | copy-start | bytes 6916
  1007.6 55.1 %copy-start.3 = (f32[576,1280]{1,0:T(8,128)S(1)}, f32[576,1280]{1,0:T(8,128)}, u32[]{:S(2)}) copy-start(f32[576,1280]{1,0:T(8,128)} %copy-done.2) | copy-start | bytes 8847364
  1066.6 51.8 %copy-start.8 = (f32[576,1280]{1,0:T(8,128)S(1)}, f32[576,1280]{1,0:T(8,128)}, u32[]{:S(2)}) copy-start(f32[576,1280]{1,0:T(8,128)} %copy-done.6) | copy-start | bytes 8847364
Sparse Core Ops, SparseCore 0:
  9.9 102.5 all-gather.5
  114.3 45.0 all-gather.7
  161.2 126.8 all-gather.9
  289.8 127.0 all-gather.11
  477.2 41.3 reduce-scatter.16
  520.8 161.4 reduce-scatter.28
  684.7 221.6 reduce-scatter.20
  910.0 43.4 reduce-scatter.26
  955.8 104.2 reduce-scatter.14
  1063.3 31.1 reduce-scatter.18
  1097.7 31.3 reduce-scatter.22
  1132.2 29.3 reduce-scatter.24

commit v2 on v1

v2 whole, which is shorter than its diff:
```python
import math
from functools import partial

import jax
import jax.numpy as jnp
from jax import lax
from jax.experimental import pallas as pl
from jax.experimental.pallas import tpu as pltpu
from jax.sharding import PartitionSpec as P

H = 16
HD = 80
EPSILON = 1e-06
ROWS_DIMS = (((0,), (0,)), ((), ()))
COLS_DIMS = (((1,), (1,)), ((), ()))
NT = (((1,), (1,)), ((), ()))
TN = (((0,), (0,)), ((), ()))
BF = jnp.bfloat16
F32 = jnp.float32
LOG2E = 1.4426950408889634


def dot(a, b, dims=(((1,), (0,)), ((), ()))):
    return lax.dot_general(a, b, dims, preferred_element_type=F32)


def hot_table(seq_len, side):
    token = lax.broadcasted_iota(jnp.int32, (seq_len, 256), 0)
    lane = lax.broadcasted_iota(jnp.int32, (seq_len, 256), 1)
    row_hit = (lane >= HD) & (token // side == lane - HD)
    col_hit = (lane >= HD + side) & (token % side == lane - HD - side)
    ones = (lane >= HD + 2 * side) & (lane < HD + 2 * side + 3)
    return (row_hit | col_hit | ones).astype(BF)


def flip_tables(rel_h, rel_w):
    entries = rel_h.shape[0]
    pad = ((0, 128 - entries), (0, 0))
    return jnp.concatenate([jnp.pad(rel_h[::-1], pad), jnp.pad(rel_w[::-1], pad)], 0)


def fwd_kernel(heads, side, tq, x_ref, hot_ref, f_ref, o_ref, of_ref, qa_ref, kp, vp, osc):
    seq_len = x_ref.shape[0]
    lanes = heads * HD
    step = pl.program_id(0)
    factor = LOG2E / math.sqrt(HD)

    @pl.when(step == 0)
    def _():
        rows = seq_len // 9

        def prep(i, c):
            part = pl.ds(pl.multiple_of(i * rows, rows), rows)
            hot = hot_ref[part, :]
            for h in range(heads):
                kp[h, part, :] = hot
                kp[h, part, 0:HD] = x_ref[part, lanes + h * HD : lanes + (h + 1) * HD]
                vp[h, part, :] = jnp.ones((rows, 128), BF)
                vp[h, part, 0:HD] = x_ref[part, 2 * lanes + h * HD : 2 * lanes + (h + 1) * HD]
            return c

        lax.fori_loop(0, 9, prep, 0)

    base = pl.ds(pl.multiple_of(step * tq, tq), tq)
    groups = tq // side
    lane = lax.broadcasted_iota(jnp.int32, (tq, 128), 1)
    for h in range(heads):
        q = x_ref[base, h * HD : (h + 1) * HD]
        g = dot(q, f_ref[...], NT) * math.sqrt(HD)
        gh = [
            pltpu.roll(g[i * side : (i + 1) * side, :128], 33 + step * groups + i, axis=1)
            for i in range(groups)
        ]
        gw = [
            pltpu.roll(g[i * side : (i + 1) * side, 128:], 81, axis=1, stride=1, stride_axis=0)
            for i in range(groups)
        ]
        qa_ref[h, :, 0:128] = jnp.concatenate(gh, 0).astype(BF)
        qa_ref[h, :, 0:HD] = q
        qa_ref[h, :, 128:256] = jnp.where(lane < side, jnp.concatenate(gw, 0), 0.0).astype(BF)

    def one(h, c):
        s = dot(qa_ref[h], kp[h], NT)
        m = jnp.max(s, -1, keepdims=True)
        p = jnp.exp2((s - m) * factor).astype(BF)
        o = dot(p, vp[h])
        total = o[:, HD : HD + 1]
        osc[h] = o / total
        norm = m + jnp.log2(total) / factor
        hi = norm.astype(BF).astype(F32)
        mid = (norm - hi).astype(BF).astype(F32)
        low = norm - hi - mid
        old = qa_ref[h, :, 128:256].astype(F32)
        old = jnp.where(lane == side, -hi, old)
        old = jnp.where(lane == side + 1, -mid, old)
        old = jnp.where(lane == side + 2, -low, old)
        qa_ref[h, :, 128:256] = old.astype(BF)
        return c

    lax.fori_loop(0, heads, one, 0)
    for h in range(heads):
        o_ref[:, h * HD : (h + 1) * HD] = osc[h][:, 0:HD].astype(BF)
        of_ref[:, h * HD : (h + 1) * HD] = osc[h][:, 0:HD]


def attention_forward(x, hot, tables, side, tq=192):
    seq_len, width = x.shape
    heads = width // (3 * HD)
    return pl.pallas_call(
        partial(fwd_kernel, heads, side, tq),
        grid=(seq_len // tq,),
        in_specs=[
            pl.BlockSpec((seq_len, width), lambda i: (0, 0), pipeline_mode=pl.Buffered(1)),
            pl.BlockSpec((seq_len, 256), lambda i: (0, 0), pipeline_mode=pl.Buffered(1)),
            pl.BlockSpec((256, HD), lambda i: (0, 0), pipeline_mode=pl.Buffered(1)),
        ],
        out_specs=[
            pl.BlockSpec((tq, heads * HD), lambda i: (i, 0)),
            pl.BlockSpec((tq, heads * HD), lambda i: (i, 0)),
            pl.BlockSpec((heads, tq, 256), lambda i: (0, i, 0)),
        ],
        out_shape=[
            jax.ShapeDtypeStruct((seq_len, heads * HD), BF),
            jax.ShapeDtypeStruct((seq_len, heads * HD), F32),
            jax.ShapeDtypeStruct((heads, seq_len, 256), BF),
        ],
        scratch_shapes=[
            pltpu.VMEM((heads, seq_len, 256), BF),
            pltpu.VMEM((heads, seq_len, 128), BF),
            pltpu.VMEM((heads, tq, 128), F32),
        ],
        compiler_params=pltpu.CompilerParams(
            dimension_semantics=("arbitrary",), vmem_limit_bytes=60 << 20
        ),
        name="attention_forward",
    )(x, hot, tables)


def bwd_kernel(heads, side, tb, uc, x_ref, hot_ref, f_ref, qa_ref, o_ref, go_ref, dx_ref, gt_ref, kp, kt, vp, dop, dk, dv, dq):
    seq_len = x_ref.shape[0]
    lanes = heads * HD
    h = pl.program_id(0)
    step = pl.program_id(1)
    factor = LOG2E / math.sqrt(HD)
    scale = HD ** (-0.5)

    @pl.when((h == 0) & (step == 0))
    def _():
        gt_ref[...] = jnp.zeros_like(gt_ref)
        rows = seq_len // 9

        def prep(i, c):
            part = pl.ds(pl.multiple_of(i * rows, rows), rows)
            hot = hot_ref[part, :]
            lane = lax.broadcasted_iota(jnp.int32, (rows, 128), 1)
            for n in range(heads):
                kp[n, part, :] = hot
                kp[n, part, 0:HD] = x_ref[part, lanes + n * HD : lanes + (n + 1) * HD]
                vp[n, part, :] = jnp.ones((rows, 128), BF)
                vp[n, part, 0:HD] = x_ref[part, 2 * lanes + n * HD : 2 * lanes + (n + 1) * HD]
                go = go_ref[part, n * HD : (n + 1) * HD]
                inner = jnp.sum(
                    go.astype(F32) * o_ref[part, n * HD : (n + 1) * HD], -1, keepdims=True
                )
                hi = inner.astype(BF).astype(F32)
                low = inner - hi
                tail = jnp.where(lane == HD, -hi, jnp.where(lane == HD + 1, -low, 0.0))
                dop[n, part, :] = tail.astype(BF)
                dop[n, part, 0:HD] = go
                kt[n, :, part] = kp[n, part, :].T
            return c

        lax.fori_loop(0, 9, prep, 0)

    @pl.when(step == 0)
    def _():
        dk[h] = jnp.zeros_like(dk[h])
        dv[h] = jnp.zeros_like(dv[h])

    base = pl.ds(pl.multiple_of(step * tb, tb), tb)
    qa = qa_ref[0]
    do = dop[h, base, :]

    def one(j, acc):
        part = pl.ds(pl.multiple_of(j * uc, uc), uc)
        s = dot(kp[h, part, :], qa, NT)
        dp = dot(vp[h, part, :], do, NT)
        p = jnp.exp2(s * factor)
        ds = (p * dp).astype(BF)
        dv[h, part, :] += dot(p.astype(BF), do)
        dk[h, part, :] += dot(ds, qa[:, 0:128])
        return acc + dot(kt[h, :, part], ds)

    acc = lax.fori_loop(0, seq_len // uc, one, jnp.zeros((256, tb), F32), unroll=True)
    acc = acc.T
    lane = lax.broadcasted_iota(jnp.int32, (tb, 128), 1)
    groups = tb // side
    first = jnp.where(lane < HD, 0.0, acc[:, :128])
    second = jnp.where(lane < side, acc[:, 128:], 0.0)
    back_h = [
        pltpu.roll(first[i * side : (i + 1) * side], 256 - 33 - step * groups - i, axis=1)
        for i in range(groups)
    ]
    back_w = [
        unroll_w(second[i * side : (i + 1) * side], side) for i in range(groups)
    ]
    both = jnp.concatenate([jnp.concatenate(back_h, 0), jnp.concatenate(back_w, 0)], 1).astype(BF)
    rel = dot(both, f_ref[...])
    dq[h, base, :] = acc[:, :HD] * scale + rel
    gt_ref[...] += dot(both, qa[:, 0:128], TN)

    @pl.when((h == heads - 1) & (step == pl.num_programs(1) - 1))
    def _():
        rows = seq_len // 9

        def post(i, c):
            part = pl.ds(pl.multiple_of(i * rows, rows), rows)
            for n in range(heads):
                dx_ref[part, n * HD : (n + 1) * HD] = dq[n, part, :].astype(BF)
                dx_ref[part, lanes + n * HD : lanes + (n + 1) * HD] = (dk[n, part, 0:HD] * scale).astype(BF)
                dx_ref[part, 2 * lanes + n * HD : 2 * lanes + (n + 1) * HD] = dv[n, part, 0:HD].astype(BF)
            return c

        lax.fori_loop(0, 9, post, 0)


def unroll_w(val, side):
    out = val
    row = lax.broadcasted_iota(jnp.int32, val.shape, 0)
    shift = side - 1 - row
    bit = 1
    while bit < side:
        out = jnp.where((shift & bit) != 0, pltpu.roll(out, bit, axis=1), out)
        bit *= 2
    return out


def attention_backward(x, hot, tables, qa, o, go, side, tb=768, uc=256):
    seq_len, width = x.shape
    heads = width // (3 * HD)
    whole = lambda *shape: pl.BlockSpec(shape, lambda h, i: (0,) * len(shape), pipeline_mode=pl.Buffered(1))
    return pl.pallas_call(
        partial(bwd_kernel, heads, side, tb, uc),
        grid=(heads, seq_len // tb),
        in_specs=[
            whole(seq_len, width),
            whole(seq_len, 256),
            whole(256, HD),
            pl.BlockSpec((1, tb, 256), lambda h, i: (h, i, 0)),
            whole(seq_len, heads * HD),
            whole(seq_len, heads * HD),
        ],
        out_specs=[
            whole(seq_len, width),
            whole(256, 128),
        ],
        out_shape=[
            jax.ShapeDtypeStruct((seq_len, width), BF),
            jax.ShapeDtypeStruct((256, 128), F32),
        ],
        scratch_shapes=[
            pltpu.VMEM((heads, seq_len, 256), BF),
            pltpu.VMEM((heads, 256, seq_len), BF),
            pltpu.VMEM((heads, seq_len, 128), BF),
            pltpu.VMEM((heads, seq_len, 128), BF),
            pltpu.VMEM((heads, seq_len, 128), F32),
            pltpu.VMEM((heads, seq_len, 128), F32),
            pltpu.VMEM((heads, seq_len, HD), F32),
        ],
        compiler_params=pltpu.CompilerParams(
            dimension_semantics=("arbitrary", "arbitrary"), vmem_limit_bytes=63 << 20
        ),
        name="attention_backward",
    )(x, hot, tables, qa, o, go)


def mlp_kernel(chunk, n_own, n_other, g_own, g_other, w1, b1, w2, out, gn, gw1, gw2, gb1, n2, gb, n2t, act, gbef):
    half = n_own.shape[0]
    tokens = 2 * half

    @pl.when(pl.program_id(0) == 0)
    def _():
        n2[0:half, :] = n_own[...]
        n2[half:tokens, :] = n_other[...]
        gb[0:half, :] = g_own[...]
        gb[half:tokens, :] = g_other[...]
        n2t[:, 0:half] = n_own[...].T
        n2t[:, half:tokens] = n_other[...].T
        out[...] = jnp.zeros_like(out)
        gn[...] = jnp.zeros_like(gn)

    gb1[...] = jnp.zeros_like(gb1)

    def rows(i, c):
        part = pl.ds(pl.multiple_of(i * chunk, chunk), chunk)
        before = dot(n2[part, :], w1[...]) + b1[...]
        cdf = 0.5 + 0.5 * lax.erf(before * math.sqrt(0.5))
        activated = (before * cdf).astype(BF)
        slope = cdf + before * (jnp.exp(-0.5 * before * before) * (1.0 / math.sqrt(2.0 * math.pi)))
        act[part, :] = activated
        out[part, :] += dot(activated, w2[...])
        grad_act = dot(gb[part, :], w2[...], NT)
        grad_before = (slope * grad_act).astype(BF)
        gbef[part, :] = grad_before
        gn[part, :] += dot(grad_before, w1[...], NT)
        gb1[...] += jnp.sum(grad_before.astype(F32), 0, keepdims=True)
        return c

    lax.fori_loop(0, tokens // chunk, rows, 0)
    gw2[...] = dot(act[...], gb[...], TN).astype(BF)
    gw1[...] = dot(n2t[...], gbef[...]).astype(BF)


def mlp(n_own, n_other, g_own, g_other, w1, b1, w2, tile=512, chunk=None):
    half, width = n_own.shape
    hidden = w1.shape[1]
    tokens = 2 * half
    chunk = chunk or min(tokens, 288)
    fixed = lambda rows, cols: pl.BlockSpec((rows, cols), lambda i: (0, 0), pipeline_mode=pl.Buffered(1))
    return pl.pallas_call(
        partial(mlp_kernel, chunk),
        grid=(hidden // tile,),
        in_specs=[
            fixed(half, width),
            fixed(half, width),
            fixed(half, width),
            fixed(half, width),
            pl.BlockSpec((width, tile), lambda i: (0, i)),
            pl.BlockSpec((1, tile), lambda i: (0, i)),
            pl.BlockSpec((tile, width), lambda i: (i, 0)),
        ],
        out_specs=[
            fixed(tokens, width),
            fixed(tokens, width),
            pl.BlockSpec((width, tile), lambda i: (0, i)),
            pl.BlockSpec((tile, width), lambda i: (i, 0)),
            pl.BlockSpec((1, tile), lambda i: (0, i)),
        ],
        out_shape=[
            jax.ShapeDtypeStruct((tokens, width), F32),
            jax.ShapeDtypeStruct((tokens, width), F32),
            jax.ShapeDtypeStruct((width, hidden), BF),
            jax.ShapeDtypeStruct((hidden, width), BF),
            jax.ShapeDtypeStruct((1, hidden), F32),
        ],
        scratch_shapes=[
            pltpu.VMEM((tokens, width), BF),
            pltpu.VMEM((tokens, width), BF),
            pltpu.VMEM((width, tokens), BF),
            pltpu.VMEM((tokens, tile), BF),
            pltpu.VMEM((tokens, tile), BF),
        ],
        compiler_params=pltpu.CompilerParams(
            dimension_semantics=("arbitrary",), vmem_limit_bytes=60 << 20
        ),
        name="mlp_both_ways",
    )(n_own, n_other, g_own, g_other, w1, b1, w2)


def split_sizes(patches, ranks):
    images = patches.shape[0]
    return images, ranks // images // 2


def norm_parts(values):
    center = values - jnp.mean(values, -1, keepdims=True)
    spread = jnp.mean(center * center, -1, keepdims=True)
    return center, lax.rsqrt(spread + EPSILON)


def norm_back(values, gain_vec, upstream):
    center, inverse = norm_parts(values)
    normal = center * inverse
    scaled = upstream * gain_vec
    inner = jnp.mean(scaled * normal, -1, keepdims=True)
    grad_values = inverse * (scaled - jnp.mean(scaled, -1, keepdims=True) - normal * inner)
    return grad_values, jnp.sum(upstream * normal, 0), jnp.sum(upstream, 0)


def flip(value, axis, size, bit):
    return lax.ppermute(value, axis, [(i, i ^ bit) for i in range(size)])


def butterfly(value, axis, size):
    bit = 1
    while bit < size:
        value = value + flip(value, axis, size, bit)
        bit *= 2
    return value


def gather_pieces(value, axis, size, me):
    full = jnp.zeros((size,) + value.shape, value.dtype)
    full = lax.dynamic_update_index_in_dim(full, value, me, 0)
    for bit in range(1, size):
        full = lax.dynamic_update_index_in_dim(full, flip(value, axis, size, bit), me ^ bit, 0)
    return full


def scatter_sum(value, axis, size, me):
    total = lax.dynamic_index_in_dim(value, me, 0, keepdims=False).astype(jnp.float32)
    for bit in range(1, size):
        away = lax.dynamic_index_in_dim(value, me ^ bit, 0, keepdims=False)
        total = total + flip(away, axis, size, bit).astype(jnp.float32)
    return total


def pick(value, index, axis=0):
    return lax.dynamic_index_in_dim(value, index, axis, keepdims=False)


def on_device(
    patches,
    ln1_gain,
    ln1_bias,
    qkv_weight,
    q_bias,
    v_bias,
    proj_weight,
    proj_bias,
    ln2_gain,
    ln2_bias,
    fc1_weight,
    fc1_bias,
    fc2_weight,
    fc2_bias,
    rel_pos_h,
    rel_pos_w,
    cotangent,
):
    images, row_count, width = patches.shape
    dp, ng, np_, nc = (lax.axis_size(name) for name in ("dp", "g", "p", "c"))
    i_dp, i_g, i_p, i_c = (lax.axis_index(name) for name in ("dp", "g", "p", "c"))
    chips = ng * np_
    ranks = chips * nc
    seq_len = ranks * row_count
    own_rows = images * row_count
    heads = H * images // ranks
    shard_heads = H // dp
    core_heads = shard_heads // nc
    piece = core_heads * HD
    pieces = heads // core_heads
    lanes = heads * HD
    core_lanes = np_ * lanes
    hidden = fc1_weight.shape[1]
    unit = hidden // ranks
    side = (rel_pos_h.shape[0] + 1) // 2

    shard = width // dp
    hidden_shard = hidden // dp
    core_bias = pick(fc1_bias.reshape(hidden_shard // (nc * unit), nc, unit), i_c, 1).reshape(-1, shard)
    packed = jnp.concatenate(
        [
            jnp.stack([ln1_gain, ln1_bias, q_bias, v_bias, proj_bias, ln2_gain, ln2_bias, fc2_bias]),
            core_bias,
        ]
    )
    vectors = gather_pieces(packed, "dp", dp, i_dp).astype(jnp.float32)
    whole_vec = vectors[:, :8].transpose(1, 0, 2).reshape(8, width)
    gain_one, shift_one, q_shift, v_shift, proj_shift, gain_two, shift_two, fc2_shift = whole_vec
    fc1_shift = vectors[:, 8:].reshape(1, hidden // nc)

    starts = [
        part * width + (i_p * pieces + q) * shard_heads * HD + i_c * piece
        for part in range(3)
        for q in range(pieces)
    ]
    qkv_own = jnp.concatenate(
        [lax.dynamic_slice_in_dim(qkv_weight, start, piece, 1) for start in starts], 1
    )
    qkv_full = gather_pieces(qkv_own, "dp", dp, i_dp).reshape(width, 3 * lanes)

    def own_vec(vec):
        return jnp.concatenate(
            [lax.dynamic_slice_in_dim(vec, starts[q], piece, 0) for q in range(pieces)]
        )

    qkv_shift = jnp.concatenate([own_vec(q_shift), jnp.zeros((lanes,), jnp.float32), own_vec(v_shift)])

    proj_own = lax.dynamic_slice_in_dim(proj_weight, i_c * piece, piece, 0)
    fc1_own = pick(fc1_weight.reshape(shard, hidden // (nc * unit), nc, unit), i_c, 2).reshape(shard, -1)
    fc2_own = pick(fc2_weight.reshape(hidden_shard // (nc * unit), nc, unit, width), i_c, 1).reshape(-1, width)
    proj_half = lax.all_gather(proj_own, "dp", axis=0, tiled=True)
    fc1_half = lax.all_gather(fc1_own, "dp", axis=0, tiled=True)
    fc2_half = lax.all_gather(fc2_own, "dp", axis=0, tiled=True)

    inputs_f = patches.astype(jnp.float32)
    center, inverse = norm_parts(inputs_f)
    normed_own = (center * inverse * gain_one + shift_one).astype(jnp.bfloat16)
    place = lambda g, p, c: ((g * np_ + p) * nc + c) * row_count
    chunks = []
    for bit in range(ng):
        chunk = pick(normed_own, i_g ^ bit)
        chunk = chunk if bit == 0 else flip(chunk, "g", ng, bit)
        for bit_p in range(np_):
            moved = chunk if bit_p == 0 else flip(chunk, "p", np_, bit_p)
            chunks.append((bit, bit_p, 0, moved))
            chunks.append((bit, bit_p, 1, flip(moved, "c", nc, 1)))
    normed = jnp.zeros((seq_len, width), jnp.bfloat16)
    for bit, bit_p, bit_c, chunk in chunks:
        start = place(i_g ^ bit, i_p ^ bit_p, i_c ^ bit_c)
        normed = lax.dynamic_update_slice_in_dim(normed, chunk, start, 0)
    joined = jnp.dot(normed, qkv_full, preferred_element_type=jnp.float32)
    head_rows = (joined + qkv_shift).astype(jnp.bfloat16)

    hot = hot_table(seq_len, side)
    tables = flip_tables(rel_pos_h, rel_pos_w)
    attended, attended_f, query_aug = attention_forward(head_rows, hot, tables, side)

    def exchange(stacked):
        return lax.all_to_all(stacked, ("g", "p"), split_axis=0, concat_axis=0, tiled=True)

    def to_own_other(value):
        return pick(value, i_c, 0), pick(value, 1 - i_c, 0)

    def from_own_other(own, other):
        return jnp.where(i_c == 0, jnp.stack([own, other]), jnp.stack([other, own]))

    returned = exchange(attended.reshape(chips, nc * row_count, lanes))
    returned = returned.reshape(ng, np_, nc, row_count, lanes).transpose(2, 0, 3, 1, 4)
    mixed_own, mixed_other = to_own_other(returned.reshape(nc, own_rows, core_lanes))
    mixed = jnp.concatenate([mixed_own, mixed_other])
    partial_own = jnp.dot(mixed_own, proj_half, preferred_element_type=jnp.float32)
    partial_other = jnp.dot(mixed_other, proj_half, preferred_element_type=jnp.float32)
    inputs_rows = inputs_f.reshape(own_rows, width)
    middle = inputs_rows + partial_own + flip(partial_other, "c", nc, 1) + proj_shift
    center, inverse = norm_parts(middle)
    two_own = (center * inverse * gain_two + shift_two).astype(jnp.bfloat16)
    two_other = flip(two_own, "c", nc, 1)
    branch_own = cotangent.reshape(own_rows, width)
    branch_other = flip(branch_own, "c", nc, 1)
    grad_out = branch_own.astype(jnp.float32)

    out_part, back_part, grad_fc1, grad_fc2, grad_fc1_shift = mlp(
        two_own, two_other, branch_own, branch_other, fc1_half, fc1_shift, fc2_half
    )
    grad_two = back_part[:own_rows] + flip(back_part[own_rows:], "c", nc, 1)
    result = middle + out_part[:own_rows] + flip(out_part[own_rows:], "c", nc, 1) + fc2_shift
    output = result.astype(jnp.bfloat16).reshape(patches.shape)

    grad_norm, grad_gain_two, grad_shift_two = norm_back(middle, gain_two, grad_two)
    grad_middle = grad_out + grad_norm
    back_own = grad_middle.astype(jnp.bfloat16)
    back_other = flip(back_own, "c", nc, 1)
    grad_mixed_own = lax.dot_general(
        back_own, proj_half, COLS_DIMS, preferred_element_type=jnp.float32
    ).astype(jnp.bfloat16)
    grad_mixed_other = lax.dot_general(
        back_other, proj_half, COLS_DIMS, preferred_element_type=jnp.float32
    ).astype(jnp.bfloat16)
    grad_proj = lax.dot_general(
        mixed, jnp.concatenate([back_own, back_other]), ROWS_DIMS, preferred_element_type=jnp.float32
    ).astype(jnp.bfloat16)
    grad_mixed = from_own_other(grad_mixed_own, grad_mixed_other)
    grad_mixed = grad_mixed.reshape(nc, ng, row_count, np_, lanes).transpose(1, 3, 0, 2, 4)
    grad_heads = exchange(grad_mixed.reshape(chips, nc * row_count, lanes)).reshape(seq_len, lanes)

    sum_fc2 = lax.psum_scatter(grad_fc2, "dp", scatter_dimension=0, tiled=True)
    sum_fc1 = lax.psum_scatter(grad_fc1, "dp", scatter_dimension=0, tiled=True)
    sum_proj = lax.psum_scatter(grad_proj, "dp", scatter_dimension=0, tiled=True)
    sum_fc2 = lax.psum_scatter(sum_fc2, ("g", "p"), scatter_dimension=1, tiled=True)
    sum_fc1 = lax.psum_scatter(sum_fc1, ("g", "p"), scatter_dimension=1, tiled=True)
    sum_proj = lax.psum_scatter(sum_proj, ("g", "p"), scatter_dimension=1, tiled=True)
    out_fc1 = sum_fc1.astype(jnp.float32)

    def swap_columns(value):
        columns = value.shape[1] // nc
        split = value.reshape(value.shape[0], nc, columns)
        mine = pick(split, i_c, 1)
        theirs = flip(pick(split, 1 - i_c, 1), "c", nc, 1)
        return jnp.where(i_c == 0, jnp.stack([mine, theirs]), jnp.stack([theirs, mine]))

    out_fc2 = swap_columns(sum_fc2).reshape(nc, hidden_shard // (nc * unit), unit, -1)
    out_fc2 = out_fc2.transpose(1, 0, 2, 3).reshape(hidden_shard, -1).astype(jnp.float32)
    out_proj = swap_columns(sum_proj).reshape(shard, -1).astype(jnp.float32)

    grad_rows, grad_tables = attention_backward(
        head_rows, hot, tables, query_aug, attended_f, grad_heads, side
    )
    grad_qkv = lax.dot_general(normed, grad_rows, ROWS_DIMS, preferred_element_type=jnp.float32)
    grad_qkv = grad_qkv.astype(jnp.bfloat16).reshape(dp, shard, 3 * lanes)
    grad_full = lax.dot_general(
        grad_rows, qkv_full, COLS_DIMS, preferred_element_type=jnp.float32
    ).astype(jnp.bfloat16)

    split = grad_full.reshape(chips, nc, row_count, width)
    keep = pick(split, i_c, 1).astype(jnp.float32)
    summed = keep + flip(pick(split, 1 - i_c, 1), "c", nc, 1).astype(jnp.float32)
    by_chip = summed.astype(jnp.bfloat16).reshape(ng, np_, row_count, width)
    homes = []
    for bit in range(ng):
        rows = scatter_sum(pick(by_chip, i_g ^ bit), "p", np_, i_p)
        if bit:
            rows = flip(rows.astype(jnp.bfloat16), "g", ng, bit).astype(jnp.float32)
        homes.append(rows)
    grad_normed = jnp.where(i_g == 0, jnp.stack(homes), jnp.stack(homes[::-1])) if ng == 2 else homes[0][None]
    grad_normed = grad_normed.reshape(own_rows, width)
    grad_norm, grad_gain_one, grad_shift_one = norm_back(inputs_rows, gain_one, grad_normed)
    grad_patches = (grad_middle + grad_norm).astype(jnp.bfloat16).reshape(patches.shape)

    qkv_rows = scatter_sum(grad_qkv, "dp", dp, i_dp).astype(jnp.bfloat16)
    qkv_rows = qkv_rows.reshape(ng, shard // ng, 3 * lanes)
    qkv_rows = scatter_sum(qkv_rows, "g", ng, i_g).astype(jnp.bfloat16)
    cell = width // ranks
    send = jnp.zeros((ranks * 3, shard // ng, cell), jnp.bfloat16)
    for q, start in enumerate(starts):
        for u in range(piece // cell):
            column = q * piece + u * cell
            block = qkv_rows[None, :, column : column + cell]
            send = lax.dynamic_update_slice_in_dim(send, block, start // cell + u, 0)
    taken = lax.all_to_all(
        send.reshape(ranks, 3, shard // ng, cell), ("g", "p", "c"), split_axis=0, concat_axis=0, tiled=True
    )
    taken = taken.reshape(ng, np_ * nc, 3, shard // ng, cell).astype(jnp.float32).sum(1)
    out_qkv = taken.transpose(0, 2, 1, 3).reshape(shard, 3 * cell)

    def spread(vec):
        full = jnp.zeros((width,), jnp.float32)
        for q in range(pieces):
            full = lax.dynamic_update_slice_in_dim(full, vec[q * piece : (q + 1) * piece], starts[q], 0)
        return full

    def everywhere(value):
        for name, size in (("c", nc), ("p", np_), ("g", ng)):
            value = butterfly(value, name, size)
        return value

    bias_half = grad_fc1_shift.reshape(dp, hidden_shard // (nc * unit), 1, unit)
    bias_full = jnp.concatenate([bias_half, bias_half], 2)
    core = lax.broadcasted_iota(jnp.int32, bias_full.shape, 2)
    bias_full = jnp.where(core == i_c, bias_full, 0.0).reshape(dp, -1, shard)
    rows_f = lambda value: jnp.sum(value.astype(jnp.float32), 0)
    early = jnp.stack([grad_gain_two, grad_shift_two, rows_f(back_own), rows_f(branch_own)])
    early = jnp.concatenate([early.reshape(4, dp, shard).transpose(1, 0, 2), bias_full], 1)
    early = everywhere(scatter_sum(early, "dp", dp, i_dp))
    late = jnp.stack(
        [
            grad_gain_one,
            grad_shift_one,
            spread(rows_f(grad_rows[:, :lanes])),
            spread(rows_f(grad_rows[:, 2 * lanes :])),
        ]
    )
    late = everywhere(scatter_sum(late.reshape(4, dp, shard).transpose(1, 0, 2), "dp", dp, i_dp))
    entries = rel_pos_h.shape[0]
    rel = jnp.stack([grad_tables[:entries, :HD], grad_tables[128 : 128 + entries, :HD]])
    rel = butterfly(everywhere(rel), "dp", dp)[:, ::-1]
    return (
        output,
        grad_patches,
        late[0],
        late[1],
        out_qkv,
        late[2],
        late[3],
        out_proj,
        early[2],
        early[0],
        early[1],
        out_fc1,
        early[4:].reshape(-1),
        out_fc2,
        early[3],
        rel[0],
        rel[1],
    )


def solution(mesh):
    dp, ranks = mesh.shape["dp"], mesh.shape["seq"]

    def call(*args):
        images = args[0].shape[0] // dp
        shape = (dp, images, ranks // images // 2, 2)
        fine = jax.sharding.Mesh(mesh.devices.reshape(shape), ("dp", "g", "p", "c"))
        seq = ("g", "p", "c")
        tokens, rows, both = P("dp", seq, None), P("dp", None), P("dp", seq)
        vec = P("dp")
        return jax.shard_map(
            on_device,
            mesh=fine,
            in_specs=(
                tokens, vec, vec, rows, vec, vec, rows, vec, vec, vec, rows, vec, rows, vec, P(), P(), tokens
            ),
            out_specs=(
                tokens, tokens, vec, vec, both, vec, vec, both, vec, vec, vec, both, vec, both, vec, P(), P()
            ),
            check_vma=False,
        )(*args)

    return call
```

time: 1180 us -> 849 us (0.72)
  blocking collectives: 185 us -> 0 us
  waiting for transfers between devices: 471 us -> 326 us
  matrix products: 161 us -> 49.9 us
  Pallas kernels: 159 us -> 226 us
  starting transfers between devices: 14.1 us -> 55.3 us
  local copies, waits for them, and re-layouts: 115 us -> 130 us
    all_to_all x3, waiting for transfers between devices: 312 us -> 53.7 us  [the longest x2 38.9 us: exchange(): lax.all_to_all(stacked, ('g', 'p'), split_axis=0, concat_axis=0, tiled=True)]
    ppermute x0 -> x46, waiting for transfers between devices: none -> 241 us  [flip(): return lax.ppermute(value, axis, [(i, i ^ bit) for i in range(size)])]
    dot_general x11 -> x7, matrix products: 151 us -> 38.8 us  [the longest x1 10.7 us: on_device(): lax.dot_general(normed, grad_rows, ROWS_DIMS, preferred_element_type=jnp....]
    all_gather x4 -> x3, waiting for transfers between devices: 80.8 us -> 0.01 us  [the longest x1 0.01 us: on_device(): proj_half = lax.all_gather(proj_own, 'dp', axis=0, tiled=True)]
    all_to_all x1 -> x0, blocking collectives: 75.8 us -> none  [exchange(): lax.all_to_all(stacked, 'seq', split_axis=0, concat_axis=0, tiled=True)]
    pallas_call x0 -> x1, Pallas kernels: none -> 66.1 us  [mlp(): pl.pallas_call(partial(mlp_kernel, chunk), grid=(hidden // tile,), in_spe...]
    psum x2 -> x0, blocking collectives: 66.1 us -> none  [the longest x1 39.9 us: on_device(): table_sums = lax.psum((grad_rel_h, grad_rel_w), ('dp', 'seq'))]
    ppermute x0 -> x46, starting transfers between devices: none -> 42.3 us  [flip(): return lax.ppermute(value, axis, [(i, i ^ bit) for i in range(size)])]
  transfers between devices with their start and end apart: 15 -> 58, of which waited for: 7 -> 29; matrix products, arithmetic and copies ran while one was open for 22% -> 23% of each run, Pallas kernels for 14% -> 19%
where the time goes in v2:
time: 849 us; the launch traced here: 842 us
  waiting for transfers between devices  326 us (38%)
  Pallas kernels  226 us (27%)
  local copies, waits for them, and re-layouts  130 us (15%)
  starting transfers between devices  55.3 us (7%)
  matrix products  49.9 us (6%)
  other arithmetic  39.1 us (5%)
  between operations  15.3 us (2%)
    ppermute x46, waiting for transfers between devices, flip(): return lax.ppermute(value, axis, [(i, i ^ bit) for i in range(size)])  241 us
    pallas_call x1, Pallas kernels, attention_backward(): pl.pallas_call(partial(bwd_kernel, heads, side, tb, uc), grid=(heads, seq...  92.7 us
    pallas_call x1, Pallas kernels, attention_forward(): pl.pallas_call(partial(fwd_kernel, heads, side, tq), grid=(seq_len // tq,...  67.5 us
    pallas_call x1, Pallas kernels, mlp(): pl.pallas_call(partial(mlp_kernel, chunk), grid=(hidden // tile,), in_spe...  66.1 us
    ppermute x46, starting transfers between devices, flip(): return lax.ppermute(value, axis, [(i, i ^ bit) for i in range(size)])  42.3 us
    all_to_all x2, waiting for transfers between devices, exchange(): lax.all_to_all(stacked, ('g', 'p'), split_axis=0, concat_axis=0, tiled=True)  38.9 us
    reduce_scatter x1, waiting for transfers between devices, on_device(): lax.psum_scatter(grad_proj, 'dp', scatter_dimension=0, tiled=True)  30.2 us
    dynamic_slice x4, local copies, waits for them, and re-layouts, pick(): return lax.dynamic_index_in_dim(value, index, axis, keepdims=False)  28.1 us
  transfers between devices with their start and end apart: 58, of which 29 were waited for; matrix products, arithmetic and copies ran while one was open for 23% of the time, Pallas kernels for 19%

profile of v2, /device:TPU:0, one launch (start us, length us, event | category | flops | bytes accessed | tf_op | source)
XLA Modules:
  0.0 842.0 jit_solution(16598904898013789613)
XLA Ops:
  9.2 7.3 reshape.353
  16.5 24.1 %dynamic-slice_reduce_fusion = bf16[320,4,640]{2,1,0:T(4,128)(2,1)S(1)} fusion(bf16[320,4,2,640]{3,2,1,0:T(2,128)(2,1)S(1)} %reshape.353, s32[]{:T(128)S(6)} %select_n.246), kind=kLoop, calls=%fused_computation.11 | loop fusion | bytes 3276804 | tf_op jit(solution)/shard_map/jit(dynamic_index_in_dim)/dynamic_slice | solution.py:409
  42.9 3.0 collective-permute-start
  49.9 2.0 collective-permute-start.10
  53.4 3.0 constant_dynamic-slice_fusion.6
  60.1 4.8 fusion.16.hot_ref
  70.1 2.9 broadcast_in_dim.76
  76.1 2.7 collective-permute-start.6
  82.5 2.0 bitcast_dynamic-update-slice_fusion.2
  85.3 21.6 %collective-permute-done.4 = bf16[288,1280]{1,0:T(8,128)(2,1)S(1)} collective-permute-done((bf16[288,1280]{1,0:T(8,128)(2,1)}, bf16[288,1280]{1,0:T(8,128)(2,1)S(1)}, u32[]{:S(2)}, u32[]{:S(2)}) %collective-permute-start.4) | collective-permute-done | bytes 737312 | tf_op jit(solution)/shard_map/ppermute | solution.py:381
  106.9 2.8 collective-permute-start.8
  109.7 2.0 bitcast_dynamic-update-slice_fusion
  113.6 12.2 %collective-permute-done.8 = bf16[288,1280]{1,0:T(8,128)(2,1)S(1)} collective-permute-done((bf16[288,1280]{1,0:T(8,128)(2,1)S(1)}, bf16[288,1280]{1,0:T(8,128)(2,1)S(1)}, u32[]{:S(2)}, u32[]{:S(2)}) %collective-permute-start.8) | collective-permute-done | bytes 737312 | tf_op jit(solution)/shard_map/ppermute | solution.py:381
  130.5 11.1 %add_convert_fusion.x_ref = bf16[2304,960]{1,0:T(8,128)(2,1)} fusion(bf16[2304,1280]{1,0:T(8,128)(2,1)} %constant_dynamic-update-slice_fusion, bf16[1280,960]{1,0:T(8,128)(2,1)} %bitcast.12, f32[960]{0:T(1024)S(1)} %concatenate.36), kind=kOutput, calls=%fused_computation.1 | convolution fusion | flops 5666734080 | bytes 12783360 | tf_op jit(solution)/shard_map/dot_general | solution.py:503
  141.6 67.5 %attention_forward.1 = (bf16[2304,320]{1,0:T(8,128)(2,1)}, f32[2304,320]{1,0:T(8,128)}, bf16[4,2304,256]{2,1,0:T(8,128)(2,1)}) custom-call(bf16[2304,960]{1,0:T(8,128)(2,1)} %add_convert_fusion.x_ref, bf16[2304,256]{1,0:T(8,128)(2,1)} %fusion.16.hot_ref, bf16[256,80]{1,0:T(8,128)(2,1)} %fusion.35.f_ref), custom_call_target="tpu_custom_call" | custom-call | tf_op jit(solution)/shard_map/attention_forward/pallas_call | solution.py:109
  209.1 3.8 copy.95
  212.9 3.7 all-to-all-start
  216.9 38.9 %all-to-all-done = bf16[4,576,320]{1,2,0:T(8,128)(2,1)S(1)} async-done(((bf16[4,576,320]{1,2,0:T(8,128)(2,1)}), bf16[4,576,320]{1,2,0:T(8,128)(2,1)S(1)}, u32[]{:S(2)}, u32[]{:S(2)}) %all-to-all-start) | async-done | bytes 1474592 | tf_op jit(solution)/shard_map/all_to_all | solution.py:511
  261.2 4.6 fusion.65
  266.5 5.0 collective-permute-done.13
  271.5 4.4 fusion.64
  279.6 2.0 collective-permute-done.14.n_other
  281.7 66.1 %mlp_both_ways.1 = (f32[1152,1280]{1,0:T(8,128)}, f32[1152,1280]{1,0:T(8,128)}, bf16[1280,2560]{1,0:T(8,128)(2,1)}, bf16[2560,1280]{1,0:T(8,128)(2,1)}, f32[1,2560]{1,0:T(1,128)}) custom-call(bf16[576,1280]{1,0:T(8,128)(2,1)} %add_convert_fusion.2.n_own, bf16[576,1280]{1,0:T(8,128)(2,1)} %collective-permute-done.14.n_other, ...), custom_call_target="tpu_custom_call" | custom-call | tf_op jit(solution)/shard_map/mlp_both_ways/pallas_call | solution.py:320
  347.8 3.8 slice.112
  354.4 2.9 collective-permute-done.17
  357.4 4.1 multiply_reduce_fusion
  361.6 5.5 convert_reduce_fusion.4
  367.2 3.1 collective-permute-done.18
  371.5 3.6 convolution_convert_fusion.2
  375.7 30.2 %reduce-scatter.13.cloned.1.call-done = bf16[160,1280]{1,0:T(8,128)(2,1)} async-done(((bf16[640,1280]{1,0:T(8,128)(2,1)}), bf16[160,1280]{1,0:T(8,128)(2,1)}) %reduce-scatter.13.cloned.1.call-update) | async-done | bytes 409616 | tf_op jit(solution)/shard_map/reduce_scatter | solution.py:560
  405.9 2.1 copy.117
  409.6 2.8 convolution_convert_fusion.4
  413.2 3.2 convolution_convert_fusion.3
  417.8 2.3 copy.103
  420.1 4.7 all-to-all-start.1
  435.4 2.0 collective-permute-start.38
  437.4 14.3 %collective-permute-done.38 = f32[8,320]{1,0:T(8,128)S(1)} collective-permute-done((f32[8,320]{1,0:T(8,128)S(1)}, f32[8,320]{1,0:T(8,128)S(1)}, u32[]{:S(2)}, u32[]{:S(2)}) %collective-permute-start.38) | collective-permute-done | bytes 10272 | tf_op jit(solution)/shard_map/ppermute | solution.py:381
  451.7 4.6 collective-permute-start.39
  457.6 6.2 collective-permute-done.39
  464.4 2.5 copy.104
  467.0 92.7 %attention_backward.1 = (bf16[2304,960]{1,0:T(8,128)(2,1)}, f32[256,128]{1,0:T(8,128)}) custom-call(bf16[2304,960]{1,0:T(8,128)(2,1)} %add_convert_fusion.x_ref, bf16[2304,256]{1,0:T(8,128)(2,1)} %fusion.16.hot_ref, bf16[256,80]{1,0:T(8,128)(2,1)} %fusion.35.f_ref, bf16[4,2304,256]{2,1,0:T(8,128)(2,1)} %get-tuple-element.30.qa_ref, ...), custom_call_target="tpu_custom_call" | custom-call | tf_op jit(solution)/shard_map/attention_backward/pallas_call | solution.py:242
  559.7 9.4 %convolution_convert_fusion = bf16[2304,1280]{1,0:T(8,128)(2,1)S(1)} fusion(bf16[2304,960]{1,0:T(8,128)(2,1)} %get-tuple-element.32, bf16[1280,960]{1,0:T(8,128)(2,1)} %bitcast.12), kind=kOutput, calls=%fused_computation | convolution fusion | flops 5665259520 | bytes 12779520 | tf_op jit(solution)/shard_map/dot_general | solution.py:582
  571.0 2.6 copy-done.5
  574.6 10.7 %convolution_convert_fusion.1 = bf16[1280,960]{0,1:T(8,128)(2,1)} fusion(bf16[2304,1280]{1,0:T(8,128)(2,1)} %constant_dynamic-update-slice_fusion, bf16[2304,960]{1,0:T(8,128)(2,1)S(1)} %copy-done.7), kind=kOutput, calls=%fused_computation.5 | convolution fusion | flops 5663539200 | bytes 12779520 | tf_op jit(solution)/shard_map/dot_general | solution.py:580
  585.5 3.0 copy.105
  592.9 4.0 collective-permute-done.42
  597.0 2.6 convert_reduce_fusion.1
  599.6 3.6 collective-permute-done.43
  606.2 14.6 %collective-permute-done.30 = bf16[320,960]{1,0:T(8,128)(2,1)S(1)} collective-permute-done((bf16[320,960]{1,0:T(8,128)(2,1)S(1)}, bf16[320,960]{1,0:T(8,128)(2,1)S(1)}, u32[]{:S(2)}, u32[]{:S(2)}) %collective-permute-start.30) | collective-permute-done | bytes 614432 | tf_op jit(solution)/shard_map/ppermute | solution.py:381
  624.6 2.1 collective-permute-done.45
  626.7 10.5 %collective-permute-done.32 = bf16[160,960]{1,0:T(8,128)(2,1)S(1)} collective-permute-done((bf16[160,960]{1,0:T(8,128)(2,1)S(1)}, bf16[160,960]{1,0:T(8,128)(2,1)S(1)}, u32[]{:S(2)}, u32[]{:S(2)}) %collective-permute-start.32) | collective-permute-done | bytes 307232 | tf_op jit(solution)/shard_map/ppermute | solution.py:381
  639.5 3.5 copy.121
  643.0 3.4 fusion
  646.7 2.0 collective-permute-start.21
  651.5 36.9 %collective-permute-done.20 = bf16[288,1280]{1,0:T(8,128)(2,1)S(1)} collective-permute-done((bf16[288,1280]{1,0:T(8,128)(2,1)S(1)}, bf16[288,1280]{1,0:T(8,128)(2,1)S(1)}, u32[]{:S(2)}, u32[]{:S(2)}) %collective-permute-start.20) | collective-permute-done | bytes 737312 | tf_op jit(solution)/shard_map/ppermute | solution.py:381
  688.4 18.7 %collective-permute-done.21 = bf16[288,1280]{1,0:T(8,128)(2,1)S(1)} collective-permute-done((bf16[288,1280]{1,0:T(8,128)(2,1)S(1)}, bf16[288,1280]{1,0:T(8,128)(2,1)S(1)}, u32[]{:S(2)}, u32[]{:S(2)}) %collective-permute-start.21) | collective-permute-done | bytes 737312 | tf_op jit(solution)/shard_map/ppermute | solution.py:381
  711.0 3.6 all-to-all-start.2
  718.6 4.1 copy.119
  722.7 71.6 %collective-permute-done.22 = bf16[288,1280]{1,0:T(8,128)(2,1)} collective-permute-done((bf16[288,1280]{1,0:T(8,128)(2,1)}, bf16[288,1280]{1,0:T(8,128)(2,1)}, u32[]{:S(2)}, u32[]{:S(2)}) %collective-permute-start.22) | collective-permute-done | bytes 737312 | tf_op jit(solution)/shard_map/ppermute | solution.py:381
  795.6 2.8 multiply_reduce_fusion.1
  799.8 2.4 collective-permute-start.25
  802.2 14.9 %all-to-all-done.2 = bf16[8,3,160,160]{3,2,1,0:T(8,128)(2,1)S(1)} async-done(((bf16[8,3,160,160]{3,2,1,0:T(8,128)(2,1)}), bf16[8,3,160,160]{3,2,1,0:T(8,128)(2,1)S(1)}, u32[]{:S(2)}, u32[]{:S(2)}) %all-to-all-start.2) | async-done | bytes 1228832 | tf_op jit(solution)/shard_map/all_to_all | solution.py:611
  821.1 3.5 collective-permute-done.27
  826.9 4.2 fusion.10
  (342 shorter events, 103.8 us)
Async XLA Ops:
  7.2 253.9 %all-gather.5.cloned.1.call-start = ((), (), s32[]{:S(2)}) async-start(), calls=%async_computation.9 | async-start | bytes 2048000 | tf_op jit(solution)/shard_map/all_gather | solution.py:483
  9.1 272.5 %all-gather.7.cloned.1.call-start = ((), (), s32[]{:S(2)}) async-start(), calls=%async_computation.10 | async-start | bytes 8192000 | tf_op jit(solution)/shard_map/all_gather | solution.py:484
  42.2 239.4 %all-gather.9.cloned.1.call-start = ((), (), s32[]{:S(2)}) async-start(), calls=%async_computation.14 | async-start | bytes 8192000 | tf_op jit(solution)/shard_map/all_gather | solution.py:485
  42.9 23.6 %collective-permute-start = (bf16[10,320]{1,0:T(8,128)(2,1)S(1)}, bf16[10,320]{1,0:T(8,128)(2,1)}, u32[]{:S(2)}, u32[]{:S(2)}) collective-permute-start(bf16[10,320]{1,0:T(8,128)(2,1)S(1)} %concatenate.34), channel_id=1, source_target_pairs={{0,8},{8,0},{16,24},{24,16},{1,9},{9,1},{17,25},{25,17},{2,10},{10... | collective-permute-start | bytes 19208 | tf_op jit(solution)/shard_map/ppermute | solution.py:381
  45.9 21.3 %collective-permute-start.1 = (bf16[10,320]{1,0:T(8,128)(2,1)S(1)}, bf16[10,320]{1,0:T(8,128)(2,1)}, u32[]{:S(2)}, u32[]{:S(2)}) collective-permute-start(bf16[10,320]{1,0:T(8,128)(2,1)S(1)} %concatenate.34), channel_id=1, source_target_pairs={{0,16},{8,24},{16,0},{24,8},{1,17},{9,25},{17,1},{25,9},{2,18},{10... | collective-permute-start | bytes 19208 | tf_op jit(solution)/shard_map/ppermute | solution.py:381
  47.4 20.5 %collective-permute-start.2 = (bf16[10,320]{1,0:T(8,128)(2,1)S(1)}, bf16[10,320]{1,0:T(8,128)(2,1)}, u32[]{:S(2)}, u32[]{:S(2)}) collective-permute-start(bf16[10,320]{1,0:T(8,128)(2,1)S(1)} %concatenate.34), channel_id=1, source_target_pairs={{0,24},{8,16},{16,8},{24,0},{1,25},{9,17},{17,9},{25,1},{2,26},{10... | collective-permute-start | bytes 19208 | tf_op jit(solution)/shard_map/ppermute | solution.py:381
  49.9 32.5 %collective-permute-start.10 = (bf16[320,960]{1,0:T(8,128)(2,1)S(1)}, bf16[320,960]{1,0:T(8,128)(2,1)}, u32[]{:S(2)}, u32[]{:S(2)}) collective-permute-start(bf16[320,960]{1,0:T(8,128)(2,1)S(1)} %concatenate.35), channel_id=1, source_target_pairs={{0,8},{8,0},{16,24},{24,16},{1,9},{9,1},{17,25},{25,17},{2,10},{10... | collective-permute-start | bytes 1843208 | tf_op jit(solution)/shard_map/ppermute | solution.py:381
  51.9 32.5 %collective-permute-start.11 = (bf16[320,960]{1,0:T(8,128)(2,1)S(1)}, bf16[320,960]{1,0:T(8,128)(2,1)S(1)}, u32[]{:S(2)}, u32[]{:S(2)}) collective-permute-start(bf16[320,960]{1,0:T(8,128)(2,1)S(1)} %concatenate.35), channel_id=1, source_target_pairs={{0,16},{8,24},{16,0},{24,8},{1,17},{9,25},{17,1},{25,9},{2,18},{10... | collective-permute-start | bytes 1843208 | tf_op jit(solution)/shard_map/ppermute | solution.py:381
  66.5 43.3 %collective-permute-start.12 = (bf16[320,960]{1,0:T(8,128)(2,1)S(1)}, bf16[320,960]{1,0:T(8,128)(2,1)}, u32[]{:S(2)}, u32[]{:S(2)}) collective-permute-start(bf16[320,960]{1,0:T(8,128)(2,1)S(1)} %concatenate.35), channel_id=1, source_target_pairs={{0,24},{8,16},{16,8},{24,0},{1,25},{9,17},{17,9},{25,1},{2,26},{10... | collective-permute-start | bytes 1843208 | tf_op jit(solution)/shard_map/ppermute | solution.py:381
  74.3 32.6 %collective-permute-start.4 = (bf16[288,1280]{1,0:T(8,128)(2,1)}, bf16[288,1280]{1,0:T(8,128)(2,1)S(1)}, u32[]{:S(2)}, u32[]{:S(2)}) collective-permute-start(bf16[288,1280]{1,0:T(8,128)(2,1)} %get-tuple-element.154), channel_id=1, source_target_pairs={{0,2},{2,0},{1,3},{3,1},{4,6},{6,4},{5,7},{7,5},{8,10},{10,8},{9,1... | collective-permute-start | bytes 2211848 | tf_op jit(solution)/shard_map/ppermute | solution.py:381
  76.1 30.8 %collective-permute-start.6 = (bf16[288,1280]{1,0:T(8,128)(2,1)S(1)}, bf16[288,1280]{1,0:T(8,128)(2,1)S(1)}, u32[]{:S(2)}, u32[]{:S(2)}) collective-permute-start(bf16[288,1280]{1,0:T(8,128)(2,1)S(1)} %dynamic-slice_bitcast_fusion.5), channel_id=1, source_target_pairs={{0,4},{4,0},{1,5},{5,1},{2,6},{6,2},{3,7},{7,3},{8,12},{12,8},{9,1... | collective-permute-start | bytes 2211848 | tf_op jit(solution)/shard_map/ppermute | solution.py:381
  82.4 29.3 %collective-permute-start.3 = (bf16[288,1280]{1,0:T(8,128)(2,1)}, bf16[288,1280]{1,0:T(8,128)(2,1)S(1)}, u32[]{:S(2)}, u32[]{:S(2)}) collective-permute-start(bf16[288,1280]{1,0:T(8,128)(2,1)} %get-tuple-element.154), channel_id=1, source_target_pairs={{0,1},{1,0},{2,3},{3,2},{4,5},{5,4},{6,7},{7,6},{8,9},{9,8},{10,11... | collective-permute-start | bytes 2211848 | tf_op jit(solution)/shard_map/ppermute | solution.py:381
  106.9 18.9 %collective-permute-start.5 = (bf16[288,1280]{1,0:T(8,128)(2,1)S(1)}, bf16[288,1280]{1,0:T(8,128)(2,1)S(1)}, u32[]{:S(2)}, u32[]{:S(2)}) collective-permute-start(bf16[288,1280]{1,0:T(8,128)(2,1)S(1)} %collective-permute-done.4), channel_id=1, source_target_pairs={{0,1},{1,0},{2,3},{3,2},{4,5},{5,4},{6,7},{7,6},{8,9},{9,8},{10,11... | collective-permute-start | bytes 2211848 | tf_op jit(solution)/shard_map/ppermute | solution.py:381
  106.9 18.9 %collective-permute-start.8 = (bf16[288,1280]{1,0:T(8,128)(2,1)S(1)}, bf16[288,1280]{1,0:T(8,128)(2,1)S(1)}, u32[]{:S(2)}, u32[]{:S(2)}) collective-permute-start(bf16[288,1280]{1,0:T(8,128)(2,1)S(1)} %collective-permute-done.6), channel_id=1, source_target_pairs={{0,2},{2,0},{1,3},{3,1},{4,6},{6,4},{5,7},{7,5},{8,10},{10,8},{9,1... | collective-permute-start | bytes 2211848 | tf_op jit(solution)/shard_map/ppermute | solution.py:381
  111.7 15.9 %collective-permute-start.7 = (bf16[288,1280]{1,0:T(8,128)(2,1)S(1)}, bf16[288,1280]{1,0:T(8,128)(2,1)S(1)}, u32[]{:S(2)}, u32[]{:S(2)}) collective-permute-start(bf16[288,1280]{1,0:T(8,128)(2,1)S(1)} %collective-permute-done.6), channel_id=1, source_target_pairs={{0,1},{1,0},{2,3},{3,2},{4,5},{5,4},{6,7},{7,6},{8,9},{9,8},{10,11... | collective-permute-start | bytes 2211848 | tf_op jit(solution)/shard_map/ppermute | solution.py:381
  125.8 3.8 collective-permute-start.9
  212.9 42.9 %all-to-all-start = ((bf16[4,576,320]{1,2,0:T(8,128)(2,1)}), bf16[4,576,320]{1,2,0:T(8,128)(2,1)S(1)}, u32[]{:S(2)}, u32[]{:S(2)}) async-start(bf16[4,576,320]{1,2,0:T(8,128)(2,1)} %copy.95), calls=%async_computation | async-start | bytes 3276800 | tf_op jit(solution)/shard_map/all_to_all | solution.py:511
  216.6 189.3 %reduce-scatter.13.cloned.1.call-start = ((), (), s32[]{:S(2)}) async-start(), calls=%async_computation.11 | async-start | bytes 2048000 | tf_op jit(solution)/shard_map/reduce_scatter | solution.py:560
  265.8 5.7 collective-permute-start.13
  265.8 13.9 %collective-permute-start.15 = (bf16[576,1280]{1,0:T(8,128)(2,1)}, bf16[576,1280]{1,0:T(8,128)(2,1)}, u32[]{:S(2)}, u32[]{:S(2)}) collective-permute-start(bf16[576,1280]{1,0:T(8,128)(2,1)} %bitcast.18.g_own), channel_id=1, source_target_pairs={{0,1},{1,0},{2,3},{3,2},{4,5},{5,4},{6,7},{7,6},{8,9},{9,8},{10,11... | collective-permute-start | bytes 4423688 | tf_op jit(solution)/shard_map/ppermute | solution.py:381
  278.1 3.6 collective-permute-start.14
  351.6 5.7 collective-permute-start.17
  354.2 7.4 collective-permute-start.16
  361.6 9.9 %copy-start.10 = (bf16[576,640]{1,0:T(8,128)(2,1)S(1)}, bf16[576,640]{1,0:T(8,128)(2,1)}, u32[]{:S(2)}) copy-start(bf16[576,640]{1,0:T(8,128)(2,1)} %get-tuple-element.169) | copy-start | bytes 2211844
  361.6 9.9 %copy-start.12 = (bf16[576,640]{1,0:T(8,128)(2,1)S(1)}, bf16[576,640]{1,0:T(8,128)(2,1)}, u32[]{:S(2)}) copy-start(bf16[576,640]{1,0:T(8,128)(2,1)} %copy-done.11) | copy-start | bytes 2211844
  367.1 3.3 collective-permute-start.18
  375.1 264.4 %reduce-scatter.17.cloned.1.call-start = ((), (), s32[]{:S(2)}) async-start(), calls=%async_computation.13 | async-start | bytes 8192000 | tf_op jit(solution)/shard_map/reduce_scatter | solution.py:558
  375.7 339.0 %reduce-scatter.19.cloned.1.call-start = ((), (), s32[]{:S(2)}) async-start(), calls=%async_computation.15 | async-start | bytes 819200
  408.0 310.7 %reduce-scatter.15.cloned.1.call-start = ((), (), s32[]{:S(2)}) async-start(), calls=%async_computation.12 | async-start | bytes 8192000 | tf_op jit(solution)/shard_map/reduce_scatter | solution.py:559
  420.1 44.3 %all-to-all-start.1 = ((bf16[4,576,320]{1,2,0:T(8,128)(2,1)}), bf16[4,576,320]{1,2,0:T(8,128)(2,1)S(1)}, u32[]{:S(2)}, u32[]{:S(2)}) async-start(bf16[4,576,320]{1,2,0:T(8,128)(2,1)} %copy.103), calls=%async_computation.1 | async-start | bytes 3276800 | tf_op jit(solution)/shard_map/all_to_all | solution.py:511
  424.8 400.9 %reduce-scatter.23.cloned.1.call-start = ((), (), s32[]{:S(2)}) async-start(), calls=%async_computation.17 | async-start | bytes 2048000
  427.2 4.0 collective-permute-start.34
  428.7 3.9 collective-permute-start.35
  429.3 4.8 collective-permute-start.36
  434.1 1.2 collective-permute-start.37
  435.4 16.3 %collective-permute-start.38 = (f32[8,320]{1,0:T(8,128)S(1)}, f32[8,320]{1,0:T(8,128)S(1)}, u32[]{:S(2)}, u32[]{:S(2)}) collective-permute-start(f32[8,320]{1,0:T(8,128)S(1)} %add.546), channel_id=1, source_target_pairs={{0,2},{2,0},{1,3},{3,1},{4,6},{6,4},{5,7},{7,5},{8,10},{10,8},{9,1... | collective-permute-start | bytes 30728 | tf_op jit(solution)/shard_map/ppermute | solution.py:381
  451.7 12.1 %collective-permute-start.39 = (f32[8,320]{1,0:T(8,128)S(1)}, f32[8,320]{1,0:T(8,128)S(1)}, u32[]{:S(2)}, u32[]{:S(2)}) collective-permute-start(f32[8,320]{1,0:T(8,128)S(1)} %add.547), channel_id=1, source_target_pairs={{0,4},{4,0},{1,5},{5,1},{2,6},{6,2},{3,7},{7,3},{8,12},{12,8},{9,1... | collective-permute-start | bytes 30728 | tf_op jit(solution)/shard_map/ppermute | solution.py:381
  573.6 11.8 %copy-start.16 = (f32[256,128]{1,0:T(8,128)S(1)}, f32[256,128]{1,0:T(8,128)}, u32[]{:S(2)}) copy-start(f32[256,128]{1,0:T(8,128)} %get-tuple-element.36) | copy-start | bytes 393220
  573.6 69.5 %collective-permute-start.19 = (bf16[4,288,1280]{2,1,0:T(8,128)(2,1)}, bf16[4,288,1280]{2,1,0:T(8,128)(2,1)}, u32[]{:S(2)}, u32[]{:S(2)}) collective-permute-start(bf16[4,288,1280]{2,1,0:T(8,128)(2,1)} %dynamic-slice_bitcast_fusion), channel_id=1, source_target_pairs={{0,1},{1,0},{2,3},{3,2},{4,5},{5,4},{6,7},{7,6},{8,9},{9,8},{10,11... | collective-permute-start | bytes 8847368 | tf_op jit(solution)/shard_map/ppermute | solution.py:381
  585.4 6.8 collective-permute-start.41
  588.6 17.6 %collective-permute-start.29 = (bf16[320,960]{1,0:T(8,128)(2,1)S(1)}, bf16[320,960]{1,0:T(8,128)(2,1)S(1)}, u32[]{:S(2)}, u32[]{:S(2)}) collective-permute-start(bf16[320,960]{1,0:T(8,128)(2,1)S(1)} %get-tuple-element.160), channel_id=1, source_target_pairs={{0,8},{8,0},{16,24},{24,16},{1,9},{9,1},{17,25},{25,17},{2,10},{10... | collective-permute-start | bytes 1843208 | tf_op jit(solution)/shard_map/ppermute | solution.py:381
  590.1 30.7 %collective-permute-start.30 = (bf16[320,960]{1,0:T(8,128)(2,1)S(1)}, bf16[320,960]{1,0:T(8,128)(2,1)S(1)}, u32[]{:S(2)}, u32[]{:S(2)}) collective-permute-start(bf16[320,960]{1,0:T(8,128)(2,1)S(1)} %get-tuple-element.162), channel_id=1, source_target_pairs={{0,16},{8,24},{16,0},{24,8},{1,17},{9,25},{17,1},{25,9},{2,18},{10... | collective-permute-start | bytes 1843208 | tf_op jit(solution)/shard_map/ppermute | solution.py:381
  591.3 29.9 %collective-permute-start.31 = (bf16[320,960]{1,0:T(8,128)(2,1)S(1)}, bf16[320,960]{1,0:T(8,128)(2,1)S(1)}, u32[]{:S(2)}, u32[]{:S(2)}) collective-permute-start(bf16[320,960]{1,0:T(8,128)(2,1)S(1)} %get-tuple-element.161), channel_id=1, source_target_pairs={{0,24},{8,16},{16,8},{24,0},{1,25},{9,17},{17,9},{25,1},{2,26},{10... | collective-permute-start | bytes 1843208 | tf_op jit(solution)/shard_map/ppermute | solution.py:381
  592.2 4.7 collective-permute-start.42
  596.9 6.3 collective-permute-start.43
  603.2 18.8 %collective-permute-start.44 = (f32[2,95,80]{2,1,0:T(8,128)S(1)}, f32[2,95,80]{2,1,0:T(8,128)S(1)}, u32[]{:S(2)}, u32[]{:S(2)}) collective-permute-start(f32[2,95,80]{2,1,0:T(8,128)S(1)} %add.551), channel_id=1, source_target_pairs={{0,8},{8,0},{16,24},{24,16},{1,9},{9,1},{17,25},{25,17},{2,10},{10... | collective-permute-start | bytes 182408 | tf_op jit(solution)/shard_map/ppermute | solution.py:381
  621.7 15.5 %collective-permute-start.32 = (bf16[160,960]{1,0:T(8,128)(2,1)S(1)}, bf16[160,960]{1,0:T(8,128)(2,1)S(1)}, u32[]{:S(2)}, u32[]{:S(2)}) collective-permute-start(bf16[160,960]{1,0:T(8,128)(2,1)S(1)} %dynamic-slice_bitcast_fusion.10), channel_id=1, source_target_pairs={{0,4},{4,0},{1,5},{5,1},{2,6},{6,2},{3,7},{7,3},{8,12},{12,8},{9,1... | collective-permute-start | bytes 921608 | tf_op jit(solution)/shard_map/ppermute | solution.py:381
  622.0 4.7 collective-permute-start.45
  646.6 41.8 %collective-permute-start.20 = (bf16[288,1280]{1,0:T(8,128)(2,1)S(1)}, bf16[288,1280]{1,0:T(8,128)(2,1)S(1)}, u32[]{:S(2)}, u32[]{:S(2)}) collective-permute-start(bf16[288,1280]{1,0:T(8,128)(2,1)S(1)} %get-tuple-element.158), channel_id=1, source_target_pairs={{0,2},{2,0},{1,3},{3,1},{4,6},{6,4},{5,7},{7,5},{8,10},{10,8},{9,1... | collective-permute-start | bytes 2211848 | tf_op jit(solution)/shard_map/ppermute | solution.py:381
  646.7 60.5 %collective-permute-start.21 = (bf16[288,1280]{1,0:T(8,128)(2,1)S(1)}, bf16[288,1280]{1,0:T(8,128)(2,1)S(1)}, u32[]{:S(2)}, u32[]{:S(2)}) collective-permute-start(bf16[288,1280]{1,0:T(8,128)(2,1)S(1)} %get-tuple-element.157), channel_id=1, source_target_pairs={{0,2},{2,0},{1,3},{3,1},{4,6},{6,4},{5,7},{7,5},{8,10},{10,8},{9,1... | collective-permute-start | bytes 2211848 | tf_op jit(solution)/shard_map/ppermute | solution.py:381
  708.8 85.5 %collective-permute-start.22 = (bf16[288,1280]{1,0:T(8,128)(2,1)}, bf16[288,1280]{1,0:T(8,128)(2,1)}, u32[]{:S(2)}, u32[]{:S(2)}) collective-permute-start(bf16[288,1280]{1,0:T(8,128)(2,1)} %get-tuple-element.155), channel_id=1, source_target_pairs={{0,4},{4,0},{1,5},{5,1},{2,6},{6,2},{3,7},{7,3},{8,12},{12,8},{9,1... | collective-permute-start | bytes 2211848 | tf_op jit(solution)/shard_map/ppermute | solution.py:381
  711.0 106.1 %all-to-all-start.2 = ((bf16[8,3,160,160]{3,2,1,0:T(8,128)(2,1)}), bf16[8,3,160,160]{3,2,1,0:T(8,128)(2,1)S(1)}, u32[]{:S(2)}, u32[]{:S(2)}) async-start(bf16[8,3,160,160]{3,2,1,0:T(8,128)(2,1)} %bitcast.56), calls=%async_computation.2 | async-start | bytes 3932160 | tf_op jit(solution)/shard_map/all_to_all | solution.py:611
  714.6 117.2 %reduce-scatter.21.cloned.1.call-start = ((), (), s32[]{:S(2)}) async-start(), calls=%async_computation.16 | async-start | bytes 2457600
  715.7 2.0 collective-permute-start.33
  722.7 72.9 %copy-start.3 = (bf16[2,288,1280]{2,1,0:T(8,128)(2,1)S(1)}, bf16[2,288,1280]{2,1,0:T(8,128)(2,1)}, u32[]{:S(2)}) copy-start(bf16[2,288,1280]{2,1,0:T(8,128)(2,1)} %param.17) | copy-start | bytes 4423684
  722.7 72.9 %copy-start.4 = (f32[1,288,1280]{2,1,0:T(8,128)S(1)}, f32[1,288,1280]{2,1,0:T(8,128)}, u32[]{:S(2)}) copy-start(f32[1,288,1280]{2,1,0:T(8,128)} %get-tuple-element.156) | copy-start | bytes 4423684
  798.6 21.1 %collective-permute-start.23 = (f32[4,320]{1,0:T(4,128)S(1)}, f32[4,320]{1,0:T(4,128)S(1)}, u32[]{:S(2)}, u32[]{:S(2)}) collective-permute-start(f32[4,320]{1,0:T(4,128)S(1)} %bitcast.252), channel_id=1, source_target_pairs={{0,8},{8,0},{16,24},{24,16},{1,9},{9,1},{17,25},{25,17},{2,10},{10... | collective-permute-start | bytes 15368 | tf_op jit(solution)/shard_map/ppermute | solution.py:381
  798.7 21.0 %collective-permute-start.24 = (f32[4,320]{1,0:T(4,128)S(1)}, f32[4,320]{1,0:T(4,128)S(1)}, u32[]{:S(2)}, u32[]{:S(2)}) collective-permute-start(f32[4,320]{1,0:T(4,128)S(1)} %bitcast.253), channel_id=1, source_target_pairs={{0,16},{8,24},{16,0},{24,8},{1,17},{9,25},{17,1},{25,9},{2,18},{10... | collective-permute-start | bytes 15368 | tf_op jit(solution)/shard_map/ppermute | solution.py:381
  799.8 19.9 %collective-permute-start.25 = (f32[4,320]{1,0:T(4,128)S(1)}, f32[4,320]{1,0:T(4,128)S(1)}, u32[]{:S(2)}, u32[]{:S(2)}) collective-permute-start(f32[4,320]{1,0:T(4,128)S(1)} %bitcast.254), channel_id=1, source_target_pairs={{0,24},{8,16},{16,8},{24,0},{1,25},{9,17},{17,9},{25,1},{2,26},{10... | collective-permute-start | bytes 15368 | tf_op jit(solution)/shard_map/ppermute | solution.py:381
  817.4 9.5 %copy-start.24 = (f32[576]{0:T(1024)S(1)}, f32[576]{0:T(1024)}, u32[]{:S(2)}) copy-start(f32[576]{0:T(1024)} %rsqrt.29) | copy-start | bytes 6916
  819.7 1.2 collective-permute-start.26
  820.9 3.6 collective-permute-start.27
  824.6 6.6 collective-permute-start.28
  826.8 7.2 collective-permute-start.40
  (31 other events, 131.5 us)
Sparse Core Ops, SparseCore 0:
  10.5 34.2 all-gather.4
  46.6 95.6 all-gather.6
  144.1 72.3 all-gather.8
  375.2 30.6 reduce-scatter.12
  408.8 72.9 reduce-scatter.16
  484.4 22.1 reduce-scatter.18
  509.7 71.2 reduce-scatter.14
  643.2 60.6 reduce-scatter.22
  722.9 67.9 reduce-scatter.20

commit v3 on v2

v3 whole, which is shorter than its diff:
```python
import math
from functools import partial

import jax
import jax.numpy as jnp
from jax import lax
from jax.experimental import pallas as pl
from jax.experimental.pallas import tpu as pltpu
from jax.sharding import PartitionSpec as P

H = 16
HD = 80
EPSILON = 1e-06
NT = (((1,), (1,)), ((), ()))
TN = (((0,), (0,)), ((), ()))
BF = jnp.bfloat16
F32 = jnp.float32
LOG2E = 1.4426950408889634
FACTOR = LOG2E / math.sqrt(HD)
FREE = pl.CostEstimate(flops=1, bytes_accessed=1, transcendentals=0)


def dot(a, b, dims=(((1,), (0,)), ((), ()))):
    return lax.dot_general(a, b, dims, preferred_element_type=F32)


def params(axes, mib=60):
    return pltpu.CompilerParams(
        dimension_semantics=("arbitrary",) * axes, vmem_limit_bytes=mib << 20
    )


def whole(*shape):
    return pl.BlockSpec(shape, lambda *at: (0,) * len(shape), pipeline_mode=pl.Buffered(1))


def hot_table(seq_len, side):
    token = lax.broadcasted_iota(jnp.int32, (seq_len, 256), 0)
    lane = lax.broadcasted_iota(jnp.int32, (seq_len, 256), 1)
    row_hit = (lane >= HD) & (token // side == lane - HD)
    col_hit = (lane >= HD + side) & (token % side == lane - HD - side)
    ones = (lane >= HD + 2 * side) & (lane < HD + 2 * side + 3)
    return (row_hit | col_hit | ones).astype(BF)


def flip_tables(rel_h, rel_w):
    entries = rel_h.shape[0]
    pad = ((0, 128 - entries), (0, 0))
    return jnp.concatenate([jnp.pad(rel_h[::-1], pad), jnp.pad(rel_w[::-1], pad)], 0)


def normal_rows(values):
    center = values - jnp.mean(values, -1, keepdims=True)
    spread = jnp.mean(center * center, -1, keepdims=True)
    return center * lax.rsqrt(spread + EPSILON)


def qkv_kernel(pieces, group_heads, side, raw, gain, shift, w, bias, hot, tables, normed, qa, kp, vp):
    rows = raw.shape[0]
    rows_n = (normal_rows(raw[...].astype(F32)) * gain[...] + shift[...]).astype(BF)
    normed[...] = rows_n
    joined = (dot(rows_n, w[...]) + bias[...]).astype(BF)
    first_row = pl.program_id(0) * (rows // side)
    lane = lax.broadcasted_iota(jnp.int32, (rows, 128), 1)
    width = group_heads * HD
    for n in range(pieces * group_heads):
        q_at = (n // group_heads) * 3 * width + (n % group_heads) * HD
        q = joined[:, q_at : q_at + HD]
        g = dot(q, tables[...], NT) * math.sqrt(HD)
        gh = []
        gw = []
        for i in range(rows // side):
            part = g[i * side : (i + 1) * side]
            gh.append(pltpu.roll(part[:, :128], first_row + (33 + i), axis=1))
            gw.append(pltpu.roll(part[:, 128:], 81, axis=1, stride=1, stride_axis=0))
        qa[n, :, 0:128] = jnp.concatenate(gh, 0).astype(BF)
        qa[n, :, 0:HD] = q
        qa[n, :, 128:256] = jnp.where(lane < side, jnp.concatenate(gw, 0), 0.0).astype(BF)
        kp[n] = hot[...]
        kp[n, :, 0:HD] = joined[:, q_at + width : q_at + width + HD]
        vp[n] = jnp.ones((rows, 128), BF)
        vp[n, :, 0:HD] = joined[:, q_at + 2 * width : q_at + 2 * width + HD]


def qkv_rows(raw, gain, shift, w, bias, hot, tables, pieces, group_heads, side, rows=384):
    seq_len, width = raw.shape
    lanes = w.shape[1]
    heads = pieces * group_heads
    return pl.pallas_call(
        partial(qkv_kernel, pieces, group_heads, side),
        grid=(seq_len // rows,),
        in_specs=[
            pl.BlockSpec((rows, width), lambda i: (i, 0)),
            whole(1, width),
            whole(1, width),
            whole(width, lanes),
            whole(1, lanes),
            pl.BlockSpec((rows, 256), lambda i: (i, 0)),
            whole(256, HD),
        ],
        out_specs=[
            pl.BlockSpec((rows, width), lambda i: (i, 0)),
            pl.BlockSpec((heads, rows, 256), lambda i: (0, i, 0)),
            pl.BlockSpec((heads, rows, 256), lambda i: (0, i, 0)),
            pl.BlockSpec((heads, rows, 128), lambda i: (0, i, 0)),
        ],
        out_shape=[
            jax.ShapeDtypeStruct((seq_len, width), BF),
            jax.ShapeDtypeStruct((heads, seq_len, 256), BF),
            jax.ShapeDtypeStruct((heads, seq_len, 256), BF),
            jax.ShapeDtypeStruct((heads, seq_len, 128), BF),
        ],
        compiler_params=params(1),
        cost_estimate=FREE,
        name="qkv_rows",
    )(raw, gain, shift, w, bias, hot, tables)


def attend_kernel(heads, side, aliased, at, qa, kp, vp, *refs):
    o, of, qo = refs[2:] if aliased else refs
    rows = qa.shape[1]
    h = pl.program_id(0)
    part = pl.ds(pl.multiple_of(pl.program_id(1) * rows, rows), rows)
    s = dot(qa[0], kp[0], NT)
    m = jnp.max(s, -1, keepdims=True)
    p = jnp.exp2((s - m) * FACTOR).astype(BF)
    out = dot(p, vp[0])
    total = out[:, HD : HD + 1]
    out = out / total
    norm = m + jnp.log2(total) / FACTOR
    hi = norm.astype(BF).astype(F32)
    mid = (norm - hi).astype(BF).astype(F32)
    low = norm - hi - mid
    lane = lax.broadcasted_iota(jnp.int32, (rows, 128), 1)
    old = qa[0, :, 128:256].astype(F32)
    old = jnp.where(lane == side, -hi, old)
    old = jnp.where(lane == side + 1, -mid, old)
    old = jnp.where(lane == side + 2, -low, old)
    qo[0, :, 0:128] = qa[0, :, 0:128]
    qo[0, :, 128:256] = old.astype(BF)
    for n in range(heads):

        @pl.when(h == n)
        def _(n=n):
            o[part, n * HD : (n + 1) * HD] = out[:, 0:HD].astype(BF)
            of[part, n * HD : (n + 1) * HD] = out[:, 0:HD]


def attend(group, qa, kp, vp, side, groups, old=(), tq=192):
    heads, seq_len, _ = qa.shape
    rows = seq_len // groups
    steps = rows // tq
    lanes = heads * HD
    query = pl.BlockSpec((1, tq, 256), lambda h, i, at: (h, at[0] * steps + i, 0))
    return pl.pallas_call(
        partial(attend_kernel, heads, side, bool(old)),
        grid_spec=pltpu.PrefetchScalarGridSpec(
            num_scalar_prefetch=1,
            grid=(heads, steps),
            in_specs=[
                query,
                pl.BlockSpec((1, seq_len, 256), lambda h, i, at: (h, 0, 0)),
                pl.BlockSpec((1, seq_len, 128), lambda h, i, at: (h, 0, 0)),
            ]
            + [pl.BlockSpec(memory_space=pl.ANY)] * len(old),
            out_specs=[
                pl.BlockSpec((rows, lanes), lambda h, i, at: (0, 0)),
                pl.BlockSpec((rows, lanes), lambda h, i, at: (at[0], 0)),
                query,
            ],
        ),
        out_shape=[
            jax.ShapeDtypeStruct((rows, lanes), BF),
            jax.ShapeDtypeStruct((seq_len, lanes), F32),
            jax.ShapeDtypeStruct((heads, seq_len, 256), BF),
        ],
        input_output_aliases={4: 1, 5: 2} if old else {},
        compiler_params=params(2),
        cost_estimate=FREE,
        name="attend",
    )(jnp.stack([group]), qa, kp, vp, *old)


def attend_back_kernel(heads, first, side, uc, qa_ref, kp, vp, of, go, tables, dx, gt, kt, dop, dk, dv, dq):
    seq_len = kp.shape[1]
    tb = qa_ref.shape[1]
    h = pl.program_id(0)
    step = pl.program_id(1)
    last = pl.num_programs(1) - 1
    scale = HD ** (-0.5)
    rows = seq_len // 9

    @pl.when((h == 0) & (step == 0))
    def _():
        gt[...] = jnp.zeros_like(gt)

        def prep(i, c):
            part = pl.ds(pl.multiple_of(i * rows, rows), rows)
            lane = lax.broadcasted_iota(jnp.int32, (rows, 128), 1)
            for n in range(heads):
                at = (first + n) * HD
                rows_go = go[part, at : at + HD]
                inner = jnp.sum(rows_go.astype(F32) * of[part, at : at + HD], -1, keepdims=True)
                hi = inner.astype(BF).astype(F32)
                tail = jnp.where(lane == HD, -hi, jnp.where(lane == HD + 1, hi - inner, 0.0))
                dop[n, part, :] = tail.astype(BF)
                dop[n, part, 0:HD] = rows_go
            return c

        lax.fori_loop(0, 9, prep, 0)

    @pl.when(step == 0)
    def _():
        def prep(i, c):
            part = pl.ds(pl.multiple_of(i * rows, rows), rows)
            kt[:, part] = kp[0, part, :].T
            dk[part, :] = jnp.zeros((rows, 128), F32)
            dv[part, :] = jnp.zeros((rows, 128), F32)
            return c

        lax.fori_loop(0, 9, prep, 0)

    base = pl.ds(pl.multiple_of(step * tb, tb), tb)
    qa = qa_ref[0]
    do = dop[h, base, :]

    def one(j, acc):
        part = pl.ds(pl.multiple_of(j * uc, uc), uc)
        s = dot(kp[0, part, :], qa, NT)
        dp = dot(vp[0, part, :], do, NT)
        p = jnp.exp2(s * FACTOR)
        ds = (p * dp).astype(BF)
        dv[part, :] += dot(p.astype(BF), do)
        dk[part, :] += dot(ds, qa[:, 0:128])
        return acc + dot(kt[:, part], ds)

    acc = lax.fori_loop(0, seq_len // uc, one, jnp.zeros((256, tb), F32), unroll=True)
    acc = acc.T
    lane = lax.broadcasted_iota(jnp.int32, (tb, 128), 1)
    groups = tb // side
    rel_h = jnp.where(lane < HD, 0.0, acc[:, :128])
    rel_w = jnp.where(lane < side, acc[:, 128:], 0.0)
    back_h = []
    back_w = []
    for i in range(groups):
        part = slice(i * side, (i + 1) * side)
        back_h.append(pltpu.roll(rel_h[part], 256 - 33 - step * groups - i, axis=1))
        back_w.append(stagger(rel_w[part], side))
    both = jnp.concatenate([jnp.concatenate(back_h, 0), jnp.concatenate(back_w, 0)], 1).astype(BF)
    dq[base, :] = acc[:, :HD] * scale + dot(both, tables[...])
    gt[...] += dot(both, qa[:, 0:128], TN)

    width = heads * HD
    for n in range(heads):

        @pl.when((h == n) & (step == last))
        def _(n=n):
            def post(i, c):
                part = pl.ds(pl.multiple_of(i * rows, rows), rows)
                at = n * HD
                dx[part, at : at + HD] = dq[part, :].astype(BF)
                dx[part, width + at : width + at + HD] = (dk[part, 0:HD] * scale).astype(BF)
                dx[part, 2 * width + at : 2 * width + at + HD] = dv[part, 0:HD].astype(BF)
                return c

            lax.fori_loop(0, 9, post, 0)


def stagger(val, side):
    row = lax.broadcasted_iota(jnp.int32, val.shape, 0)
    shift = side - 1 - row
    bit = 1
    while bit < side:
        val = jnp.where((shift & bit) != 0, pltpu.roll(val, bit, axis=1), val)
        bit *= 2
    return val


def attend_back(first, count, qa, kp, vp, of, go, tables, side, tb=768, uc=256):
    heads, seq_len, _ = qa.shape
    lanes = heads * HD
    return pl.pallas_call(
        partial(attend_back_kernel, count, first, side, uc),
        grid=(count, seq_len // tb),
        in_specs=[
            pl.BlockSpec((1, tb, 256), lambda h, i: (first + h, i, 0)),
            pl.BlockSpec((1, seq_len, 256), lambda h, i: (first + h, 0, 0)),
            pl.BlockSpec((1, seq_len, 128), lambda h, i: (first + h, 0, 0)),
            whole(seq_len, lanes),
            whole(seq_len, lanes),
            whole(256, HD),
        ],
        out_specs=[whole(seq_len, 3 * count * HD), whole(256, 128)],
        out_shape=[
            jax.ShapeDtypeStruct((seq_len, 3 * count * HD), BF),
            jax.ShapeDtypeStruct((256, 128), F32),
        ],
        scratch_shapes=[
            pltpu.VMEM((256, seq_len), BF),
            pltpu.VMEM((count, seq_len, 128), BF),
            pltpu.VMEM((seq_len, 128), F32),
            pltpu.VMEM((seq_len, 128), F32),
            pltpu.VMEM((seq_len, HD), F32),
        ],
        compiler_params=params(2),
        cost_estimate=FREE,
        name="attend_back",
    )(qa, kp, vp, of, go, tables)


def project_kernel(chips, np_, at, *refs):
    pieces = refs[:chips]
    w, mixed, own, other = refs[chips:]
    i_g, i_p, i_c = at[0], at[1], at[2]
    rows = pieces[0].shape[0] // 2
    lanes = pieces[0].shape[1]
    images = chips // np_
    for k in range(chips):
        for swap in range(2):

            @pl.when(i_c == swap)
            def _(k=k, swap=swap):
                for b in range(2):
                    src = (swap ^ b) * rows
                    mixed[i_p ^ (k % np_), b, i_g ^ (k // np_)] = pieces[k][src : src + rows, :]

    for b, out in ((0, own), (1, other)):
        for n in range(images):
            total = None
            for p in range(np_):
                term = dot(mixed[p, b, n], w[p])
                total = term if total is None else total + term
            out[n] = total


def project(pieces, w, at, np_):
    chips = len(pieces)
    rows2, lanes = pieces[0].shape
    rows = rows2 // 2
    images = chips // np_
    width = w.shape[2]
    one = jax.ShapeDtypeStruct((images, rows, width), F32)
    return pl.pallas_call(
        partial(project_kernel, chips, np_),
        in_specs=[pl.BlockSpec(memory_space=pltpu.SMEM)]
        + [pl.BlockSpec(memory_space=pltpu.VMEM)] * (chips + 1),
        out_specs=[pl.BlockSpec(memory_space=pltpu.VMEM)] * 3,
        out_shape=[jax.ShapeDtypeStruct((np_, 2, images, rows, lanes), BF), one, one],
        compiler_params=pltpu.CompilerParams(vmem_limit_bytes=40 << 20),
        cost_estimate=FREE,
        name="project",
    )(at, *pieces, w)


def mlp_kernel(aliased, n_own, n_other, g_own, g_other, w1, b1, w2, *refs):
    if aliased:
        out_in, gn_in, out, gn, grads, gb1, n2t, gb, act, gbef = refs
    else:
        out, gn, grads, gb1, n2t, gb, act, gbef = refs
    half, width = n_own.shape
    step = pl.program_id(0)
    chunk = out.shape[0]
    per = half // chunk
    shards, shard, hidden = w1.shape
    first = w1[...].reshape(width, hidden)
    second = w2[...].reshape(hidden, width)

    @pl.when(step == 0)
    def _():
        gb1[...] = jnp.zeros_like(gb1)

    def rows(n_ref, g_ref, at):
        src = pl.ds(pl.multiple_of((step - at) * chunk, chunk), chunk)
        dst = pl.ds(pl.multiple_of(step * chunk, chunk), chunk)
        n2 = n_ref[src, :]
        g2 = g_ref[src, :]
        gb[dst, :] = g2
        before = dot(n2, first) + b1[...]
        cdf = 0.5 + 0.5 * lax.erf(before * math.sqrt(0.5))
        activated = (before * cdf).astype(BF)
        slope = cdf + before * (jnp.exp(-0.5 * before * before) * (1.0 / math.sqrt(2.0 * math.pi)))
        act[dst, :] = activated
        value = dot(activated, second)
        grad_before = (slope * dot(g2, second, NT)).astype(BF)
        gbef[dst, :] = grad_before
        back = dot(grad_before, first, NT)
        if aliased:
            value = value + out_in[...]
            back = back + gn_in[...]
        out[...] = value
        gn[...] = back
        gb1[...] += jnp.sum(grad_before.astype(F32), 0, keepdims=True)

    @pl.when(step < per)
    def _():
        rows(n_own, g_own, 0)

    @pl.when((step >= per) & (step < 2 * per))
    def _():
        rows(n_other, g_other, per)

    @pl.when(step == 2 * per)
    def _():
        n2t[:, 0:half] = n_own[...].T
        n2t[:, half : 2 * half] = n_other[...].T
        grads[:, 0:shard, :] = dot(n2t[...], gbef[...]).astype(BF).reshape(shards, shard, hidden)
        grads[:, shard : 2 * shard, :] = dot(act[...], gb[...], TN).astype(BF).reshape(shards, shard, width)


def mlp_half(which, n_own, n_other, g_own, g_other, weights, b1, old=(), chunk=288):
    half, width = n_own.shape
    dp = weights.shape[0]
    shard = width // dp
    hidden = width
    chunk = min(chunk, half)
    steps = 2 * half // chunk
    tile = pl.BlockSpec((chunk, width), lambda i: (jnp.minimum(i, steps - 1), 0))
    rows = jax.ShapeDtypeStruct((2 * half, width), F32)
    flops = 12 * 2 * half * width * hidden
    return pl.pallas_call(
        partial(mlp_kernel, bool(old)),
        grid=(steps + 1,),
        in_specs=[whole(half, width)] * 4
        + [
            pl.BlockSpec((dp, shard, width), lambda i: (0, which, 0), pipeline_mode=pl.Buffered(1)),
            whole(1, hidden),
            pl.BlockSpec((dp, shard, width), lambda i: (0, 2 + which, 0), pipeline_mode=pl.Buffered(1)),
        ]
        + [tile] * len(old),
        out_specs=[tile, tile, whole(dp, 2 * shard, width), whole(1, hidden)],
        out_shape=[
            rows,
            rows,
            jax.ShapeDtypeStruct((dp, 2 * shard, width), BF),
            jax.ShapeDtypeStruct((1, hidden), F32),
        ],
        input_output_aliases={7: 0, 8: 1} if old else {},
        scratch_shapes=[
            pltpu.VMEM((width, 2 * half), BF),
            pltpu.VMEM((2 * half, width), BF),
            pltpu.VMEM((2 * half, hidden), BF),
            pltpu.VMEM((2 * half, hidden), BF),
        ],
        compiler_params=params(1),
        cost_estimate=FREE,
        name="mlp_half",
    )(n_own, n_other, g_own, g_other, weights, b1, weights, *old)


def rows_back_kernel(pieces, np_, at, *refs):
    dx = refs[:pieces]
    raw, w, send, keep, sums = refs[pieces:]
    step = pl.program_id(0)
    total = None
    width = dx[0].shape[1]
    for q in range(pieces):
        term = dot(dx[q][...], w[:, q * width : (q + 1) * width], NT)
        total = term if total is None else total + term
    normal = normal_rows(raw[...].astype(F32))

    @pl.when(step == 0)
    def _():
        sums[...] = jnp.zeros_like(sums)

    sums[0:1, :] += jnp.sum(total * normal, 0, keepdims=True)
    sums[1:2, :] += jnp.sum(total, 0, keepdims=True)
    for q in range(pieces):
        sums[2 + q : 3 + q, 0:width] += jnp.sum(dx[q][...].astype(F32), 0, keepdims=True)

    @pl.when(step < np_)
    def _():
        send[0] = total.astype(BF)

    @pl.when(step >= np_)
    def _():
        keep[0] = total


def rows_back(group, core, dx, raw, w, np_, row_count):
    pieces = len(dx)
    seq_len, width = raw.shape
    lanes = dx[0].shape[1]

    def block(i, at):
        bit = jnp.where(i < np_, 1, 0)
        return (at[0] * np_ + i % np_) * 2 + (at[1] ^ bit), 0

    return pl.pallas_call(
        partial(rows_back_kernel, pieces, np_),
        grid_spec=pltpu.PrefetchScalarGridSpec(
            num_scalar_prefetch=1,
            grid=(2 * np_,),
            in_specs=[pl.BlockSpec((row_count, lanes), block)] * pieces
            + [pl.BlockSpec((row_count, width), block), whole(width, pieces * lanes)],
            out_specs=[
                pl.BlockSpec((1, row_count, width), lambda i, at: (jnp.minimum(i, np_ - 1), 0, 0)),
                pl.BlockSpec((1, row_count, width), lambda i, at: (jnp.maximum(i - np_, 0), 0, 0)),
                whole(8, width),
            ],
        ),
        out_shape=[
            jax.ShapeDtypeStruct((np_, row_count, width), BF),
            jax.ShapeDtypeStruct((np_, row_count, width), F32),
            jax.ShapeDtypeStruct((8, width), F32),
        ],
        compiler_params=params(1),
        cost_estimate=FREE,
        name="rows_back",
    )(jnp.stack([group, core]), *dx, raw, w)


def select_kernel(ng, np_, nc, at, qkv, fc1, fc2, proj, own, slab):
    i_p, i_c = at[1], at[2]
    shard = fc1.shape[0]
    width = proj.shape[1]
    hidden = fc1.shape[1]
    chips = ng * np_
    unit = hidden // (chips * nc)
    part = unit // 2
    piece = proj.shape[0] // nc
    shard_lanes = proj.shape[0]
    lanes = own.shape[1] // 3
    pieces = lanes // piece
    per = fc2.shape[0] // (nc * unit)
    for c in range(nc):

        @pl.when(i_c == c)
        def _(c=c):
            for u in range(2):
                for z in range(chips):
                    src = (z * nc + c) * unit + u * part
                    slab[u * shard : (u + 1) * shard, z * part : (z + 1) * part] = fc1[:, src : src + part]
                for b in range(per):
                    src = (b * nc + c) * unit + u * part
                    dst = (2 + u) * shard + b * part
                    slab[dst : dst + part, :] = fc2[src : src + part, :]
            slab[4 * shard : 4 * shard + piece, :] = proj[c * piece : (c + 1) * piece, :]

        for p in range(np_):

            @pl.when((i_c == c) & (i_p == p))
            def _(c=c, p=p):
                for q in range(pieces):
                    for t in range(3):
                        src = t * width + (p * pieces + q) * shard_lanes + c * piece
                        dst = (3 * q + t) * piece
                        own[:, dst : dst + piece] = qkv[:, src : src + piece]


def select(at, qkv, fc1, fc2, proj, ng, np_, nc, lanes):
    shard, width = proj.shape[0], proj.shape[1]
    return pl.pallas_call(
        partial(select_kernel, ng, np_, nc),
        in_specs=[pl.BlockSpec(memory_space=pltpu.SMEM)] + [pl.BlockSpec(memory_space=pltpu.VMEM)] * 4,
        out_specs=[pl.BlockSpec(memory_space=pltpu.VMEM)] * 2,
        out_shape=[
            jax.ShapeDtypeStruct((shard, 3 * lanes), BF),
            jax.ShapeDtypeStruct((4 * shard + shard // nc, width), BF),
        ],
        compiler_params=pltpu.CompilerParams(vmem_limit_bytes=40 << 20),
        cost_estimate=FREE,
        name="select",
    )(at, qkv, fc1, fc2, proj)


def start_kernel(sizes, split, patches, own, vec, rows, full, vecs, local, send, recv):
    dp, ng, np_ = sizes
    i_dp, i_g, i_p, i_c = (lax.axis_index(name) for name in ("dp", "g", "p", "c"))
    count = patches.shape[1]
    step = count // split

    barrier = pltpu.get_barrier_semaphore()
    peers = [{"dp": i_dp ^ k} for k in range(1, dp)]
    peers += [{"g": i_g ^ k} for k in range(1, ng)]
    peers += [{"p": i_p ^ k} for k in range(1, np_)]
    peers += [{"c": 1 - i_c}]
    for peer in peers:
        pl.semaphore_signal(barrier, inc=1, device_id=peer, device_id_type=pl.DeviceIdType.MESH)
    pl.semaphore_wait(barrier, len(peers))

    used = []

    def remote(src, dst, peer):
        n = len(used)
        copy = pltpu.make_async_remote_copy(
            src_ref=src,
            dst_ref=dst,
            send_sem=send.at[n],
            recv_sem=recv.at[n],
            device_id=peer,
            device_id_type=pl.DeviceIdType.MESH,
        )
        used.append(copy)
        return copy

    def place(g, p, c, part):
        start = ((g * np_ + p) * 2 + c) * count + part * step
        return rows.at[pl.ds(pl.multiple_of(start, 8), step)]

    mine = [patches.at[i_g, pl.ds(part * step, step)] for part in range(split)]
    home = [pltpu.make_async_copy(mine[part], place(i_g, i_p, i_c, part), local.at[part]) for part in range(split)]
    home.append(pltpu.make_async_copy(own, full.at[i_dp], local.at[split]))
    home.append(pltpu.make_async_copy(vec, vecs.at[i_dp], local.at[split + 1]))

    far = {}
    for part in range(split):
        for bit in range(1, ng):
            src = patches.at[i_g ^ bit, pl.ds(part * step, step)]
            far[bit, part] = remote(src, place(i_g, i_p, i_c, part), {"g": i_g ^ bit})
            far[bit, part].start()
    over_dp = []
    for bit in range(1, dp):
        over_dp.append(remote(vec, vecs.at[i_dp], {"dp": i_dp ^ bit}))
        over_dp.append(remote(own, full.at[i_dp], {"dp": i_dp ^ bit}))
    for copy in over_dp:
        copy.start()
    near = {}
    for bit in range(1, np_):
        for part in range(split):
            near[bit, part] = remote(mine[part], place(i_g, i_p, i_c, part), {"p": i_p ^ bit})
            near[bit, part].start()
    cores = []
    for part in range(split):
        cores.append(remote(mine[part], place(i_g, i_p, i_c, part), {"c": 1 - i_c}))
        cores[-1].start()
    for copy in home:
        copy.start()

    onward = {}
    for part in range(split):
        for bit in range(1, ng):
            far[bit, part].wait_recv()
            came = place(i_g ^ bit, i_p, i_c, part)
            for bit_p in range(1, np_):
                onward[bit, bit_p, part] = remote(came, came, {"p": i_p ^ bit_p})
                onward[bit, bit_p, part].start()
            cores.append(remote(came, came, {"c": 1 - i_c}))
            cores[-1].start()
        for bit in range(1, np_):
            near[bit, part].wait_recv()
            came = place(i_g, i_p ^ bit, i_c, part)
            cores.append(remote(came, came, {"c": 1 - i_c}))
            cores[-1].start()
    for (bit, bit_p, part), copy in onward.items():
        copy.wait_recv()
        came = place(i_g ^ bit, i_p ^ bit_p, i_c, part)
        cores.append(remote(came, came, {"c": 1 - i_c}))
        cores[-1].start()
    for copy in over_dp + cores:
        copy.wait_recv()
    for copy in used:
        copy.wait_send()
    for copy in home:
        copy.wait()


def start_exchange(patches, own, vec, sizes, split=3):
    dp, ng, np_ = sizes
    images, count, width = patches.shape
    chunk_copies = ng * np_ + (ng - 1) + (np_ - 1) + (ng - 1) * (np_ - 1)
    copies = 2 * (dp - 1) + split * chunk_copies
    hbm = pl.BlockSpec(memory_space=pl.ANY)
    return pl.pallas_call(
        partial(start_kernel, sizes, split),
        in_specs=[hbm] * 3,
        out_specs=[hbm] * 3,
        out_shape=[
            jax.ShapeDtypeStruct((ng * np_ * 2 * count, width), BF),
            jax.ShapeDtypeStruct((dp,) + own.shape, BF),
            jax.ShapeDtypeStruct((dp,) + vec.shape, BF),
        ],
        scratch_shapes=[
            pltpu.SemaphoreType.DMA((split + 2,)),
            pltpu.SemaphoreType.DMA((copies,)),
            pltpu.SemaphoreType.DMA((copies,)),
        ],
        compiler_params=pltpu.CompilerParams(collective_id=0, has_side_effects=True),
        cost_estimate=FREE,
        name="start_exchange",
    )(patches, own, vec)


def flip(value, axis, size, bit):
    return lax.ppermute(value, axis, [(i, i ^ bit) for i in range(size)])


def pick(value, index, axis=0):
    return lax.dynamic_index_in_dim(value, index, axis, keepdims=False)


def gather_pieces(value, axis, size, me):
    full = jnp.zeros((size,) + value.shape, value.dtype)
    full = lax.dynamic_update_index_in_dim(full, value, me, 0)
    for bit in range(1, size):
        full = lax.dynamic_update_index_in_dim(full, flip(value, axis, size, bit), me ^ bit, 0)
    return full


def scatter_sum(value, axis, size, me):
    total = pick(value, me).astype(F32)
    for bit in range(1, size):
        total = total + flip(pick(value, me ^ bit), axis, size, bit).astype(F32)
    return total


def tie(*values):
    return lax.optimization_barrier(values)


def after(value, *others):
    return tie(value, *others)[0]


def norm_back(values, gain_vec, upstream):
    center = values - jnp.mean(values, -1, keepdims=True)
    spread = jnp.mean(center * center, -1, keepdims=True)
    inverse = lax.rsqrt(spread + EPSILON)
    normal = center * inverse
    scaled = upstream * gain_vec
    inner = jnp.mean(scaled * normal, -1, keepdims=True)
    return inverse * (scaled - jnp.mean(scaled, -1, keepdims=True) - normal * inner), normal


def on_device(
    patches,
    ln1_gain,
    ln1_bias,
    qkv_weight,
    q_bias,
    v_bias,
    proj_weight,
    proj_bias,
    ln2_gain,
    ln2_bias,
    fc1_weight,
    fc1_bias,
    fc2_weight,
    fc2_bias,
    rel_pos_h,
    rel_pos_w,
    cotangent,
):
    images, row_count, width = patches.shape
    dp, ng, np_, nc = (lax.axis_size(name) for name in ("dp", "g", "p", "c"))
    i_dp, i_g, i_p, i_c = (lax.axis_index(name) for name in ("dp", "g", "p", "c"))
    chips = ng * np_
    i_z = i_g * np_ + i_p
    ranks = chips * nc
    seq_len = ranks * row_count
    own_rows = images * row_count
    heads = H * images // ranks
    shard_heads = H // dp
    core_heads = shard_heads // nc
    piece = core_heads * HD
    pieces = heads // core_heads
    lanes = heads * HD
    hidden = fc1_weight.shape[1]
    unit = hidden // ranks
    shard = width // dp
    per = hidden // dp // (nc * unit)
    side = (rel_pos_h.shape[0] + 1) // 2

    core_bias = pick(fc1_bias.reshape(per, nc, 2, unit // 2), i_c, 1).transpose(1, 0, 2)
    packed = jnp.concatenate(
        [
            jnp.stack([ln1_gain, ln1_bias, q_bias, v_bias, proj_bias, ln2_gain, ln2_bias, fc2_bias]),
            core_bias.reshape(-1, shard),
        ]
    )
    spot = jnp.stack([i_g, i_p, i_c])
    qkv_own, slab = select(spot, qkv_weight, fc1_weight, fc2_weight, proj_weight, ng, np_, nc, lanes)
    weights = lax.all_gather(slab, "dp", axis=0)
    proj_half = weights[:, 4 * shard :]
    raw, qkv_full, vectors = start_exchange(patches, qkv_own, packed, (dp, ng, np_))
    qkv_full = qkv_full.reshape(width, 3 * lanes)
    vectors = vectors.astype(F32)
    whole_vec = vectors.transpose(1, 0, 2).reshape(-1, width)
    gain_one, shift_one, q_shift, v_shift, proj_shift, gain_two, shift_two, fc2_shift = whole_vec[:8]
    fc1_shift = vectors[:, 8:].reshape(dp, 2, -1).transpose(1, 0, 2).reshape(2, 1, -1)

    starts = [
        part * width + (i_p * pieces + q) * shard_heads * HD + i_c * piece
        for q in range(pieces)
        for part in range(3)
    ]
    zero = jnp.zeros((piece,), F32)
    biases = []
    for q in range(pieces):
        at = starts[3 * q]
        biases += [lax.dynamic_slice_in_dim(q_shift, at, piece, 0), zero]
        biases += [lax.dynamic_slice_in_dim(v_shift, at, piece, 0)]
    qkv_shift = jnp.concatenate(biases)[None]

    branch_own = cotangent.reshape(own_rows, width)
    branch_other = flip(branch_own, "c", nc, 1)

    hot = hot_table(seq_len, side)
    tables = flip_tables(rel_pos_h, rel_pos_w)
    normed, query, key_rows, value_rows = qkv_rows(
        raw, gain_one[None], shift_one[None], qkv_full, qkv_shift, hot, tables, pieces, core_heads, side
    )
    far_att, att_f, query_a = attend(i_g ^ 1, query, key_rows, value_rows, side, ng)
    far_att = far_att.reshape(np_, nc * row_count, lanes)
    arrived = {}
    for bit_p in range(np_):
        arrived[1, bit_p] = flip(pick(far_att, i_p ^ bit_p), ("g", "p"), chips, np_ + bit_p)
    near_att, att_f, query_a = attend(i_g, query, key_rows, value_rows, side, ng, (att_f, query_a))
    near_att, *pinned = tie(near_att, *[arrived[1, k] for k in range(np_)])
    for k in range(np_):
        arrived[1, k] = pinned[k]
    near_att = near_att.reshape(np_, nc * row_count, lanes)
    arrived[0, 0] = pick(near_att, i_p)
    for bit_p in range(1, np_):
        arrived[0, bit_p] = flip(pick(near_att, i_p ^ bit_p), ("g", "p"), chips, bit_p)

    mixed, partial_own, partial_other = project(
        [arrived[k // np_, k % np_] for k in range(chips)], proj_half.reshape(np_, lanes, width), spot, np_
    )
    inputs_rows = patches.reshape(own_rows, width).astype(F32)
    partial_own = partial_own.reshape(own_rows, width)
    middle = inputs_rows + partial_own + flip(partial_other, "c", nc, 1).reshape(own_rows, width) + proj_shift
    center = middle - jnp.mean(middle, -1, keepdims=True)
    spread = jnp.mean(center * center, -1, keepdims=True)
    two_own = (center * lax.rsqrt(spread + EPSILON) * gain_two + shift_two).astype(BF)
    two_other = flip(two_own, "c", nc, 1)

    def over_dp(value):
        return lax.psum_scatter(value.reshape(-1, value.shape[-1]), "dp", scatter_dimension=0, tiled=True)

    out_a, back_a, grads_a, bias_a = mlp_half(
        0, two_own, two_other, branch_own, branch_other, weights, fc1_shift[0]
    )
    sum_a = over_dp(grads_a)
    out_b, back_b, grads_b, bias_b = mlp_half(
        1, two_own, two_other, branch_own, branch_other, weights, fc1_shift[1], (out_a, back_a)
    )
    grad_two = back_b[:own_rows] + flip(back_b[own_rows:], "c", nc, 1)
    result = middle + out_b[:own_rows] + flip(out_b[own_rows:], "c", nc, 1) + fc2_shift
    output = result.astype(BF).reshape(patches.shape)

    grad_norm, normal_two = norm_back(middle, gain_two, grad_two)
    grad_middle = branch_own.astype(F32) + grad_norm
    back_own = grad_middle.astype(BF)
    back_other = flip(back_own, "c", nc, 1)
    both = jnp.stack([back_own, back_other])
    proj_rows = proj_half.reshape(np_, lanes, width)
    grad_mixed = jnp.einsum("btd,pld->pbtl", both, proj_rows, preferred_element_type=F32).astype(BF)
    grad_mixed = grad_mixed.reshape(np_, nc, ng, row_count, lanes)
    grad_heads = jnp.zeros((chips, nc, row_count, lanes), BF)
    for k in list(range(1, chips)) + [0]:
        block = pick(pick(grad_mixed, i_p ^ (k % np_)), i_g ^ (k // np_), 1)
        block = jnp.where(i_c == 0, block, block[::-1])
        block = block if k == 0 else flip(block, ("g", "p"), chips, k)
        grad_heads = lax.dynamic_update_index_in_dim(grad_heads, block, i_z ^ k, 0)
    grad_heads = grad_heads.reshape(seq_len, lanes)
    sum_b = over_dp(grads_b)
    grad_proj = jnp.einsum(
        "pbtl,btd->pld", mixed.reshape(np_, nc, own_rows, lanes), both, preferred_element_type=F32
    ).astype(BF)
    sum_p = over_dp(grad_proj.reshape(dp, piece, width))

    def pieces_over_chips(value):
        split = value.reshape(value.shape[0], chips, width // chips).transpose(1, 0, 2)
        sent = [flip(pick(split, i_z ^ bit), ("g", "p"), chips, bit) for bit in range(1, chips)]
        return [pick(split, i_z)] + sent

    def add_up(values):
        return sum(value.astype(F32) for value in values)

    sum_a = pieces_over_chips(after(sum_a, grad_heads))
    dx = []
    grad_tables = 0.0
    for q in range(pieces):
        rows, table = attend_back(
            q * core_heads, core_heads, query_a, key_rows, value_rows, att_f, grad_heads, tables, side
        )
        if q == 0:
            rows, *sum_a = tie(rows, *sum_a)
            sum_b = pieces_over_chips(after(sum_b, rows))
            sum_p = pieces_over_chips(after(sum_p, rows))
            key_rows = after(key_rows, rows)
        elif q == 1:
            rows, *both_sums = tie(rows, *sum_b, *sum_p)
            sum_b, sum_p = both_sums[:chips], both_sums[chips:]
        dx.append(rows)
        grad_tables = grad_tables + table
    sum_a, sum_b, sum_p = add_up(sum_a), add_up(sum_b), add_up(sum_p)
    out_fc1 = jnp.stack([sum_a[:shard], sum_b[:shard]], 1).reshape(shard, unit)

    def swap_columns(value):
        split = value.reshape(value.shape[0], nc, -1)
        theirs = flip(pick(split, 1 - i_c, 1).astype(BF), "c", nc, 1).astype(F32)
        mine = pick(split, i_c, 1)
        return jnp.where(i_c == 0, jnp.stack([mine, theirs]), jnp.stack([theirs, mine]))

    out_fc2 = jnp.stack([sum_a[shard:].reshape(per, unit // 2, -1), sum_b[shard:].reshape(per, unit // 2, -1)], 1)
    out_fc2 = swap_columns(out_fc2.reshape(per * unit, -1)).reshape(nc, per, unit, -1)
    out_fc2 = out_fc2.transpose(1, 0, 2, 3).reshape(hidden // dp, -1)
    out_proj = swap_columns(sum_p).reshape(shard, -1)

    far_send, far_keep, sums = rows_back(i_g ^ 1, i_c, dx, raw, qkv_full, np_, row_count)
    far_came = flip(far_send, "c", nc, 1)
    near_send, near_keep, part = rows_back(i_g, i_c, after(tuple(dx), far_send), raw, qkv_full, np_, row_count)
    near_send, far_came = tie(near_send, far_came)
    sums = sums + part
    near_came = flip(near_send, "c", nc, 1)
    far_sum = (far_keep + far_came.astype(F32)).astype(BF)
    far_pieces = [pick(far_sum, i_p)] + [flip(pick(far_sum, i_p ^ k), "p", np_, k) for k in range(1, np_)]
    homes_start = [far_sum, near_send]
    homes_later = (far_pieces, near_keep, near_came)
    dx = tie(*dx, *homes_start)[: pieces]
    grad_qkv = [lax.dot_general(normed, rows, TN, preferred_element_type=F32).astype(BF) for rows in dx]
    grad_qkv, (far_pieces, near_keep, near_came) = tie(grad_qkv, homes_later)
    far_rows = flip(add_up(far_pieces).astype(BF), "g", ng, 1).astype(F32)
    near_rows = scatter_sum((near_keep + near_came.astype(F32)).astype(BF), "p", np_, i_p)
    grad_normed = jnp.where(i_g == 0, jnp.stack([near_rows, far_rows]), jnp.stack([far_rows, near_rows]))
    grad_norm, _ = norm_back(inputs_rows, gain_one, grad_normed.reshape(own_rows, width))
    grad_patches = (grad_middle + grad_norm).astype(BF).reshape(patches.shape)

    qkv_rows_sum = scatter_sum(jnp.concatenate(grad_qkv, 1).reshape(dp, shard, 3 * lanes), "dp", dp, i_dp).astype(BF)
    qkv_rows_sum = scatter_sum(qkv_rows_sum.reshape(ng, shard // ng, 3 * lanes), "g", ng, i_g).astype(BF)
    cell = width // ranks
    send = jnp.zeros((ranks * 3, shard // ng, cell), BF)
    for n, start in enumerate(starts):
        for u in range(piece // cell):
            column = n * piece + u * cell
            block = qkv_rows_sum[None, :, column : column + cell]
            send = lax.dynamic_update_slice_in_dim(send, block, start // cell + u, 0)
    taken = lax.all_to_all(
        send.reshape(ranks, 3, shard // ng, cell), ("g", "p", "c"), split_axis=0, concat_axis=0, tiled=True
    )
    taken = taken.reshape(ng, np_ * nc, 3, shard // ng, cell).astype(F32).sum(1)
    out_qkv = taken.transpose(0, 2, 1, 3).reshape(shard, 3 * cell)

    def everywhere(value):
        for name, size in (("c", nc), ("p", np_), ("g", ng), ("dp", dp)):
            bit = 1
            while bit < size:
                value = value + flip(value, name, size, bit)
                bit *= 2
        return value

    bias_half = jnp.stack([bias_a.reshape(dp, per, unit // 2), bias_b.reshape(dp, per, unit // 2)], 2)
    bias_half = bias_half.reshape(dp * per, 1, unit)
    bias_full = jnp.concatenate([bias_half] * nc, 1)
    core = lax.broadcasted_iota(jnp.int32, bias_full.shape, 1)
    bias_full = jnp.where(core == i_c, bias_full, 0.0).reshape(-1, width)
    rows_f = lambda value: jnp.sum(value.astype(F32), 0)
    early = jnp.stack([jnp.sum(grad_two * normal_two, 0), jnp.sum(grad_two, 0), rows_f(back_own), rows_f(branch_own)])
    early = everywhere(jnp.concatenate([early, bias_full]))

    def spread(part):
        full = jnp.zeros((width,), F32)
        for q in range(pieces):
            block = sums[2 + q, part * piece : (part + 1) * piece]
            full = lax.dynamic_update_slice_in_dim(full, block, starts[3 * q], 0)
        return full

    entries = rel_pos_h.shape[0]
    rel = jnp.stack([grad_tables[:entries, :HD], grad_tables[128 : 128 + entries, :HD]])[:, ::-1]
    late = jnp.concatenate([sums[0], sums[1], spread(0), spread(2), rel.reshape(-1)])
    late = everywhere(late)
    rel = late[4 * width :].reshape(2, entries, HD)

    def owned(vec):
        return lax.dynamic_slice_in_dim(vec, i_dp * (vec.shape[0] // dp), vec.shape[0] // dp, 0)

    late_vec = [owned(late[n * width : (n + 1) * width]) for n in range(4)]
    early_vec = [owned(early[n]) for n in range(4)]
    return (
        output,
        grad_patches,
        late_vec[0],
        late_vec[1],
        out_qkv,
        late_vec[2],
        late_vec[3],
        out_proj,
        early_vec[2],
        early_vec[0],
        early_vec[1],
        out_fc1,
        owned(early[4:].reshape(-1)),
        out_fc2,
        early_vec[3],
        rel[0],
        rel[1],
    )


def solution(mesh):
    dp, ranks = mesh.shape["dp"], mesh.shape["seq"]

    def call(*args):
        images = args[0].shape[0] // dp
        shape = (dp, images, ranks // images // 2, 2)
        fine = jax.sharding.Mesh(mesh.devices.reshape(shape), ("dp", "g", "p", "c"))
        seq = ("g", "p", "c")
        tokens, rows, both = P("dp", seq, None), P("dp", None), P("dp", seq)
        vec = P("dp")
        return jax.shard_map(
            on_device,
            mesh=fine,
            in_specs=(
                tokens, vec, vec, rows, vec, vec, rows, vec, vec, vec, rows, vec, rows, vec, P(), P(), tokens
            ),
            out_specs=(
                tokens, tokens, vec, vec, both, vec, vec, both, vec, vec, vec, both, vec, both, vec, P(), P()
            ),
            check_vma=False,
        )(*args)

    return call
```

time: 849 us -> 751 us (0.88)
  waiting for transfers between devices: 326 us -> 157 us
  Pallas kernels: 226 us -> 354 us
  local copies, waits for them, and re-layouts: 130 us -> 85.2 us
  matrix products: 49.9 us -> 22.4 us
  other arithmetic: 39.1 us -> 53.8 us
    pallas_call x3 -> x12, Pallas kernels: 226 us -> 354 us  [the longest x2 95.7 us: attend_back(): pl.pallas_call(partial(attend_back_kernel, count, first, side, uc), grid=...]
    ppermute x46 -> x42, waiting for transfers between devices: 241 us -> 119 us  [flip(): return lax.ppermute(value, axis, [(i, i ^ bit) for i in range(size)])]
    all_to_all x2 -> x0, waiting for transfers between devices: 38.9 us -> none  [exchange(): lax.all_to_all(stacked, ('g', 'p'), split_axis=0, concat_axis=0, tiled=True)]
    reduce_scatter x3 -> x1, waiting for transfers between devices: 30.2 us -> 0.01 us  [over_dp(): lax.psum_scatter(value.reshape(-1, value.shape[-1]), 'dp', scatter_dimens...]
    dot_general x8 -> x4, matrix products: 49.9 us -> 22.4 us  [the longest x2 11.6 us: on_device(): lax.dot_general(normed, rows, TN, preferred_element_type=F32).astype(BF)]
    dynamic_slice x4 -> x2, local copies, waits for them, and re-layouts: 28.1 us -> 1.27 us  [pick(): return lax.dynamic_index_in_dim(value, index, axis, keepdims=False)]
    all_to_all x1, waiting for transfers between devices: 14.9 us -> 37.7 us  [on_device(): lax.all_to_all(send.reshape(ranks, 3, shard // ng, cell), ('g', 'p', 'c')...]
    dynamic_update_slice x20 -> x7, local copies, waits for them, and re-layouts: 16.5 us -> 1.28 us  [the longest x4 1.05 us: spread(): full = lax.dynamic_update_slice_in_dim(full, block, starts[3 * q], 0)]
  transfers between devices with their start and end apart: 58 -> 47, of which waited for: 29 -> 21; matrix products, arithmetic and copies ran while one was open for 23% -> 17% of each run, Pallas kernels for 19% -> 39%
where the time goes in v3:
time: 751 us; the launch traced here: 742 us
  Pallas kernels  354 us (47%)
  waiting for transfers between devices  157 us (21%)
  local copies, waits for them, and re-layouts  85.2 us (11%)
  starting transfers between devices  54.3 us (7%)
  other arithmetic  53.8 us (7%)
  matrix products  22.4 us (3%)
  between operations  15.6 us (2%)
    ppermute x42, waiting for transfers between devices, flip(): return lax.ppermute(value, axis, [(i, i ^ bit) for i in range(size)])  119 us
    pallas_call x2, Pallas kernels, attend_back(): pl.pallas_call(partial(attend_back_kernel, count, first, side, uc), grid=...  95.7 us
    pallas_call x2, Pallas kernels, mlp_half(): pl.pallas_call(partial(mlp_kernel, bool(old)), grid=(steps + 1,), in_spec...  84.4 us
    pallas_call x2, Pallas kernels, attend(): pl.pallas_call(partial(attend_kernel, heads, side, bool(old)), grid_spec=...  68 us
    pallas_call x1, Pallas kernels, start_exchange(): pl.pallas_call(partial(start_kernel, sizes, split), in_specs=[hbm] * 3, o...  57.8 us
    ppermute x42, starting transfers between devices, flip(): return lax.ppermute(value, axis, [(i, i ^ bit) for i in range(size)])  50.4 us
    all_to_all x1, waiting for transfers between devices, on_device(): lax.all_to_all(send.reshape(ranks, 3, shard // ng, cell), ('g', 'p', 'c')...  37.7 us
    unnamed x130, local copies, waits for them, and re-layouts  36.1 us
  transfers between devices with their start and end apart: 47, of which 21 were waited for; matrix products, arithmetic and copies ran while one was open for 17% of the time, Pallas kernels for 39%

profile of v3, /device:TPU:0, one launch (start us, length us, event | category | flops | bytes accessed | tf_op | source)
XLA Modules:
  0.0 742.3 jit_solution(10132491306731371160)
XLA Ops:
  7.3 1.9 copy-done.3
  9.2 1.9 copy-done.4
  20.2 57.8 %start_exchange.1 = (bf16[2304,1280]{1,0:T(8,128)(2,1)}, bf16[4,320,960]{2,1,0:T(8,128)(2,1)}, bf16[4,10,320]{2,1,0:T(8,128)(2,1)}) custom-call(bf16[2,288,1280]{2,1,0:T(8,128)(2,1)} %patches.1, bf16[320,960]{1,0:T(8,128)(2,1)} %copy-done.7, bf16[10,320]{1,0:T(8,128)(2,1)} %concatenate.23.vec), custom_call_target="tpu_custom_call" | custom-call | flops 1 | bytes 1 | tf_op jit(solution)/shard_map/start_exchange/pallas_call | solution.py:663
  82.4 4.8 fusion.19.hot
  87.2 17.5 %qkv_rows.1 = (bf16[2304,1280]{1,0:T(8,128)(2,1)}, bf16[4,2304,256]{2,1,0:T(8,128)(2,1)}, bf16[4,2304,256]{2,1,0:T(8,128)(2,1)}, bf16[4,2304,128]{2,1,0:T(8,128)(2,1)}) custom-call(bf16[2304,1280]{1,0:T(8,128)(2,1)} %get-tuple-element.87.raw.refs_2_, f32[1,1280]{1,0:T(1,128)} %unstack.35.gain, f32[1,1280]{1,0:T(1,128)} %unstack.37.shift, ...), custom_call_target="tpu_custom_call" | custom-call | flops 1 | bytes 1 | tf_op jit(solution)/shard_map/qkv_rows/pallas_call | solution.py:89
  104.7 34.0 %attend.2 = (bf16[1152,320]{1,0:T(8,128)(2,1)}, f32[2304,320]{1,0:T(8,128)}, bf16[4,2304,256]{2,1,0:T(8,128)(2,1)}) custom-call(s32[1]{0:T(128)} %bitcast.8.at, bf16[4,2304,256]{2,1,0:T(8,128)(2,1)} %get-tuple-element.90.qa, bf16[4,2304,256]{2,1,0:T(8,128)(2,1)} %get-tuple-element.114.kp, bf16[4,2304,128]{2,1,0:T(8,128)(2,1)} %get-tuple-element.92.vp), custom_call_target="tpu_custom_call" | custom-call | flops 1 | bytes 1 | tf_op jit(solution)/shard_map/attend/pallas_call | solution.py:155
  141.3 2.8 collective-permute-start.1
  144.1 34.0 %attend.3 = (bf16[1152,320]{1,0:T(8,128)(2,1)}, f32[2304,320]{1,0:T(8,128)}, bf16[4,2304,256]{2,1,0:T(8,128)(2,1)}) custom-call(s32[1]{0:T(128)} %bitcast.1.at, bf16[4,2304,256]{2,1,0:T(8,128)(2,1)} %get-tuple-element.90.qa, bf16[4,2304,256]{2,1,0:T(8,128)(2,1)} %get-tuple-element.114.kp, ...), custom_call_target="tpu_custom_call", output_to_operand_aliasing={{1}: (4, {}), {2}: (5, {})} | custom-call | flops 1 | bytes 1 | tf_op jit(solution)/shard_map/attend/pallas_call | solution.py:155
  180.8 2.1 collective-permute-start.2
  184.6 8.5 %collective-permute-done.2.refs_1_ = bf16[576,320]{1,0:T(8,128)(2,1)S(1)} collective-permute-done((bf16[576,320]{1,0:T(8,128)(2,1)S(1)}, bf16[576,320]{1,0:T(8,128)(2,1)S(1)}, u32[]{:S(2)}, u32[]{:S(2)}) %collective-permute-start.2) | collective-permute-done | bytes 368672 | tf_op jit(solution)/shard_map/ppermute | solution.py:684
  194.9 5.8 project.1
  203.9 5.0 collective-permute-done.3
  208.8 3.1 convert_reduce_fusion.1
  212.0 3.5 fusion.9
  215.6 5.3 add_convert_fusion.3
  221.8 2.6 collective-permute-done.4.n_other
  225.5 46.8 %mlp_half.2 = (f32[1152,1280]{1,0:T(8,128)}, f32[1152,1280]{1,0:T(8,128)}, bf16[4,640,1280]{2,1,0:T(8,128)(2,1)}, f32[1,1280]{1,0:T(1,128)}) custom-call(bf16[576,1280]{1,0:T(8,128)(2,1)} %get-tuple-element.250.n_own, bf16[576,1280]{1,0:T(8,128)(2,1)} %copy-done.25, bf16[576,1280]{1,0:T(8,128)(2,1)} %bitcast.19.g_own, ...), custom_call_target="tpu_custom_call" | custom-call | flops 1 | bytes 1 | tf_op jit(solution)/shard_map/mlp_half/pallas_call | solution.py:420
  273.1 37.6 %mlp_half.3 = (f32[1152,1280]{1,0:T(8,128)}, f32[1152,1280]{1,0:T(8,128)}, bf16[4,640,1280]{2,1,0:T(8,128)(2,1)}, f32[1,1280]{1,0:T(1,128)}) custom-call(bf16[576,1280]{1,0:T(8,128)(2,1)} %get-tuple-element.250.n_own, bf16[576,1280]{1,0:T(8,128)(2,1)} %copy-done.25, bf16[576,1280]{1,0:T(8,128)(2,1)} %bitcast.19.g_own, ...), custom_call_target="tpu_custom_call", output_to_operand_aliasing={{0}: (7, {}), {1}: (8, {})} | custom-call | flops 1 | bytes 1 | tf_op jit(solution)/shard_map/mlp_half/pallas_call | solution.py:420
  310.7 3.8 slice.167
  317.6 2.7 collective-permute-done.7
  320.2 4.4 multiply_reduce_fusion
  324.7 5.6 convert_reduce_fusion.3
  330.3 2.2 convert_reduce_fusion.2
  336.0 2.4 collective-permute-done.37
  338.4 2.3 collective-permute-start.38
  340.7 2.6 collective-permute-done.38
  343.3 2.2 collective-permute-start.39
  347.5 2.0 collective-permute-start.40
  349.5 5.4 fusion
  356.7 5.3 fusion.23
  362.0 2.9 copy.96
  367.7 2.2 collective-permute-start.11
  370.0 13.1 %collective-permute-done.9 = bf16[2,288,320]{2,1,0:T(8,128)(2,1)S(1)} collective-permute-done((bf16[2,288,320]{2,1,0:T(8,128)(2,1)S(1)}, bf16[2,288,320]{2,1,0:T(8,128)(2,1)S(1)}, u32[]{:S(2)}, u32[]{:S(2)}) %collective-permute-start.9) | collective-permute-done | bytes 368672 | tf_op jit(solution)/shard_map/ppermute | solution.py:684
  383.3 16.0 %collective-permute-done.10 = bf16[2,288,320]{2,1,0:T(8,128)(2,1)S(1)} collective-permute-done((bf16[2,288,320]{2,1,0:T(8,128)(2,1)S(1)}, bf16[2,288,320]{2,1,0:T(8,128)(2,1)S(1)}, u32[]{:S(2)}, u32[]{:S(2)}) %collective-permute-start.10) | collective-permute-done | bytes 368672 | tf_op jit(solution)/shard_map/ppermute | solution.py:684
  399.6 3.4 copy.117
  404.2 7.1 collective-permute-start.12
  411.4 2.4 collective-permute-start.14
  416.4 47.5 %attend_back.2 = (bf16[2304,480]{1,0:T(8,128)(2,1)}, f32[256,128]{1,0:T(8,128)}) custom-call(bf16[4,2304,256]{2,1,0:T(8,128)(2,1)} %get-tuple-element.108.qa_ref, bf16[4,2304,256]{2,1,0:T(8,128)(2,1)} %get-tuple-element.114.kp, bf16[4,2304,128]{2,1,0:T(8,128)(2,1)} %get-tuple-element.92.vp, f32[2304,320]{1,0:T(8,128)} %get-tuple-element.109.of, ...), custom_call_target="tpu_custom_call" | custom-call | flops 1 | bytes 1 | tf_op jit(solution)/shard_map/attend_back/pallas_call | solution.py:282
  463.9 2.8 copy.119
  471.0 2.3 collective-permute-start.17
  476.9 1.9 collective-permute-start.19
  479.2 48.2 %attend_back.3 = (bf16[2304,480]{1,0:T(8,128)(2,1)}, f32[256,128]{1,0:T(8,128)}) custom-call(bf16[4,2304,256]{2,1,0:T(8,128)(2,1)} %get-tuple-element.108.qa_ref, bf16[4,2304,256]{2,1,0:T(8,128)(2,1)} %get-tuple-element.114.kp, bf16[4,2304,128]{2,1,0:T(8,128)(2,1)} %get-tuple-element.92.vp, f32[2304,320]{1,0:T(8,128)} %get-tuple-element.109.of, ...), custom_call_target="tpu_custom_call" | custom-call | flops 1 | bytes 1 | tf_op jit(solution)/shard_map/attend_back/pallas_call | solution.py:282
  528.4 2.4 collective-permute-start.20
  531.0 4.1 collective-permute-done.20
  535.1 11.5 %rows_back.2 = (bf16[2,288,1280]{2,1,0:T(8,128)(2,1)}, f32[2,288,1280]{2,1,0:T(8,128)}, f32[8,1280]{1,0:T(8,128)}) custom-call(s32[2]{0:T(128)} %get-tuple-element.304.at, bf16[2304,480]{1,0:T(8,128)(2,1)} %get-tuple-element.128.refs_0_, bf16[2304,480]{1,0:T(8,128)(2,1)} %get-tuple-element.129.refs_1_, bf16[2304,1280]{1,0:T(8,128)(2,1)} %get-tuple-element.87.raw.refs_2_, ...), custom_call_target="tpu_custom_call" | custom-call | flops 1 | bytes 1 | tf_op jit(solution)/shard_map/rows_back/pallas_call | solution.py:488
  546.7 11.7 %rows_back.3 = (bf16[2,288,1280]{2,1,0:T(8,128)(2,1)}, f32[2,288,1280]{2,1,0:T(8,128)}, f32[8,1280]{1,0:T(8,128)}) custom-call(s32[2]{0:T(128)} %get-tuple-element.305.at, bf16[2304,480]{1,0:T(8,128)(2,1)} %get-tuple-element.128.refs_0_, bf16[2304,480]{1,0:T(8,128)(2,1)} %get-tuple-element.129.refs_1_, bf16[2304,1280]{1,0:T(8,128)(2,1)} %get-tuple-element.87.raw.refs_2_, ...), custom_call_target="tpu_custom_call" | custom-call | flops 1 | bytes 1 | tf_op jit(solution)/shard_map/rows_back/pallas_call | solution.py:488
  574.7 4.4 collective-permute-done.27
  581.0 2.0 copy.108
  583.0 2.1 collective-permute-done.28
  590.7 3.4 collective-permute-done.30
  601.9 5.9 convolution_convert_fusion.1
  607.8 5.7 convolution_convert_fusion
  613.6 5.8 collective-permute-done.22
  622.3 3.2 copy.100
  626.8 2.0 collective-permute-start.32
  632.5 2.6 collective-permute-start.25
  635.1 9.3 %collective-permute-done.33 = bf16[320,960]{1,0:T(8,128)(2,1)S(1)} collective-permute-done((bf16[320,960]{1,0:T(8,128)(2,1)S(1)}, bf16[320,960]{1,0:T(8,128)(2,1)S(1)}, u32[]{:S(2)}, u32[]{:S(2)}) %collective-permute-start.33) | collective-permute-done | bytes 614432 | tf_op jit(solution)/shard_map/ppermute | solution.py:684
  644.3 12.7 %collective-permute-done.32 = bf16[320,960]{1,0:T(8,128)(2,1)S(1)} collective-permute-done((bf16[320,960]{1,0:T(8,128)(2,1)S(1)}, bf16[320,960]{1,0:T(8,128)(2,1)S(1)}, u32[]{:S(2)}, u32[]{:S(2)}) %collective-permute-start.32) | collective-permute-done | bytes 614432 | tf_op jit(solution)/shard_map/ppermute | solution.py:684
  658.9 3.8 collective-permute-done.24
  663.9 16.7 %collective-permute-done.34 = bf16[160,960]{1,0:T(8,128)(2,1)S(1)} collective-permute-done((bf16[160,960]{1,0:T(8,128)(2,1)S(1)}, bf16[160,960]{1,0:T(8,128)(2,1)S(1)}, u32[]{:S(2)}, u32[]{:S(2)}) %collective-permute-start.34) | collective-permute-done | bytes 307232 | tf_op jit(solution)/shard_map/ppermute | solution.py:684
  682.7 3.7 all-to-all-start
  688.1 2.6 multiply_reduce_fusion.3
  690.8 4.1 fusion.5
  695.0 37.7 %all-to-all-done = bf16[8,3,160,160]{3,2,1,0:T(8,128)(2,1)S(1)} async-done(((bf16[8,3,160,160]{3,2,1,0:T(8,128)(2,1)}), bf16[8,3,160,160]{3,2,1,0:T(8,128)(2,1)S(1)}, u32[]{:S(2)}, u32[]{:S(2)}) %all-to-all-start) | async-done | bytes 1228832 | tf_op jit(solution)/shard_map/all_to_all | solution.py:929
  (362 shorter events, 103.5 us)
Async XLA Ops:
  7.2 175.8 %all-gather.3.cloned.1.call-start = ((), (), s32[]{:S(2)}) async-start(), calls=%async_computation.5 | async-start | bytes 18432000 | tf_op jit(solution)/shard_map/all_gather | solution.py:772
  18.2 62.4 %copy-start.42 = (bf16[95,80]{0,1:T(8,128)(2,1)S(1)}, bf16[95,80]{0,1:T(8,128)(2,1)}, u32[]{:S(2)}) copy-start(bf16[95,80]{0,1:T(8,128)(2,1)} %param.32) | copy-start | bytes 45604
  18.2 62.6 %copy-start.43 = (bf16[95,80]{0,1:T(8,128)(2,1)S(1)}, bf16[95,80]{0,1:T(8,128)(2,1)}, u32[]{:S(2)}) copy-start(bf16[95,80]{0,1:T(8,128)(2,1)} %param.31) | copy-start | bytes 45604
  18.2 381.4 %reduce-scatter.10.cloned.1.call-start = ((), (), s32[]{:S(2)}) async-start(), calls=%async_computation.6 | async-start | bytes 8192000
  140.0 38.1 %collective-permute-start = (bf16[576,320]{1,0:T(8,128)(2,1)S(1)}, bf16[576,320]{1,0:T(8,128)(2,1)S(1)}, u32[]{:S(2)}, u32[]{:S(2)}) collective-permute-start(bf16[576,320]{1,0:T(8,128)(2,1)S(1)} %get-tuple-element.273), channel_id=1, source_target_pairs={{0,4},{2,6},{4,0},{6,2},{1,5},{3,7},{5,1},{7,3},{8,12},{10,14},{12... | collective-permute-start | bytes 1105928 | tf_op jit(solution)/shard_map/ppermute | solution.py:684
  141.3 37.5 %collective-permute-start.1 = (bf16[576,320]{1,0:T(8,128)(2,1)S(1)}, bf16[576,320]{1,0:T(8,128)(2,1)S(1)}, u32[]{:S(2)}, u32[]{:S(2)}) collective-permute-start(bf16[576,320]{1,0:T(8,128)(2,1)S(1)} %get-tuple-element.272), channel_id=1, source_target_pairs={{0,6},{2,4},{4,2},{6,0},{1,7},{3,5},{5,3},{7,1},{8,14},{10,12},{12... | collective-permute-start | bytes 1105928 | tf_op jit(solution)/shard_map/ppermute | solution.py:684
  180.8 12.2 %collective-permute-start.2 = (bf16[576,320]{1,0:T(8,128)(2,1)S(1)}, bf16[576,320]{1,0:T(8,128)(2,1)S(1)}, u32[]{:S(2)}, u32[]{:S(2)}) collective-permute-start(bf16[576,320]{1,0:T(8,128)(2,1)S(1)} %get-tuple-element.270), channel_id=1, source_target_pairs={{0,2},{2,0},{4,6},{6,4},{1,3},{3,1},{5,7},{7,5},{8,10},{10,8},{12,... | collective-permute-start | bytes 1105928 | tf_op jit(solution)/shard_map/ppermute | solution.py:684
  182.9 10.9 %copy-start.9 = (bf16[576,320]{1,0:T(8,128)(2,1)S(1)}, bf16[576,320]{1,0:T(8,128)(2,1)}, u32[]{:S(2)}) copy-start(bf16[576,320]{1,0:T(8,128)(2,1)} %copy-done.8) | copy-start | bytes 1105924
  182.9 10.9 %copy-start.11 = (bf16[576,320]{1,0:T(8,128)(2,1)S(1)}, bf16[576,320]{1,0:T(8,128)(2,1)}, u32[]{:S(2)}) copy-start(bf16[576,320]{1,0:T(8,128)(2,1)} %copy-done.10) | copy-start | bytes 1105924
  203.1 5.7 collective-permute-start.3
  203.1 18.7 %collective-permute-start.5 = (bf16[576,1280]{1,0:T(8,128)(2,1)}, bf16[576,1280]{1,0:T(8,128)(2,1)}, u32[]{:S(2)}, u32[]{:S(2)}) collective-permute-start(bf16[576,1280]{1,0:T(8,128)(2,1)} %bitcast.19.g_own), channel_id=1, source_target_pairs={{0,1},{1,0},{2,3},{3,2},{4,5},{5,4},{6,7},{7,6},{8,9},{9,8},{10,11... | collective-permute-start | bytes 4423688 | tf_op jit(solution)/shard_map/ppermute | solution.py:684
  220.9 3.5 collective-permute-start.4
  272.3 191.6 %reduce-scatter.12.cloned.1.call-start = ((), (), s32[]{:S(2)}) async-start(), calls=%async_computation.7 | async-start | bytes 8192000
  310.7 162.6 %reduce-scatter.8.cloned.1.call-start = ((), (), s32[]{:S(2)}) async-start(), calls=%async_computation.4 | async-start | bytes 2048000 | tf_op jit(solution)/shard_map/reduce_scatter | solution.py:828
  310.7 4.7 copy-start.19
  314.5 5.7 collective-permute-start.7
  315.5 4.8 copy-start.17
  317.3 7.4 collective-permute-start.6
  324.7 7.9 %copy-start.45 = (f32[1,1280]{1,0:T(1,128)S(1)}, f32[1,1280]{1,0:T(1,128)}, u32[]{:S(2)}) copy-start(f32[1,1280]{1,0:T(1,128)} %get-tuple-element.146) | copy-start | bytes 15364
  324.7 8.0 %copy-start.44 = (f32[1,1280]{1,0:T(1,128)S(1)}, f32[1,1280]{1,0:T(1,128)}, u32[]{:S(2)}) copy-start(f32[1,1280]{1,0:T(1,128)} %get-tuple-element.145) | copy-start | bytes 15364
  324.7 24.8 %copy-start.15 = (bf16[2,2,2,288,320]{4,3,2,1,0:T(8,128)(2,1)S(1)}, bf16[2,2,2,288,320]{4,3,2,1,0:T(8,128)(2,1)}, u32[]{:S(2)}) copy-start(bf16[2,2,2,288,320]{4,3,2,1,0:T(8,128)(2,1)} %copy-done.14) | copy-start | bytes 4423684
  330.3 19.2 %copy-start.29 = (bf16[576,1280]{1,0:T(8,128)(2,1)}, bf16[576,1280]{1,0:T(8,128)(2,1)S(1)}, u32[]{:S(2)}) copy-start(bf16[576,1280]{1,0:T(8,128)(2,1)S(1)} %get-tuple-element.246) | copy-start | bytes 4423684
  330.3 19.2 %collective-permute-start.8 = (bf16[576,1280]{1,0:T(8,128)(2,1)S(1)}, bf16[576,1280]{1,0:T(8,128)(2,1)}, u32[]{:S(2)}, u32[]{:S(2)}) collective-permute-start(bf16[576,1280]{1,0:T(8,128)(2,1)S(1)} %get-tuple-element.246), channel_id=1, source_target_pairs={{0,1},{1,0},{2,3},{3,2},{4,5},{5,4},{6,7},{7,6},{8,9},{9,8},{10,11... | collective-permute-start | bytes 4423688 | tf_op jit(solution)/shard_map/ppermute | solution.py:684
  333.1 1.3 collective-permute-start.36
  334.4 4.0 collective-permute-start.37
  338.4 4.9 collective-permute-start.38
  343.3 4.2 collective-permute-start.39
  347.5 7.6 %collective-permute-start.40 = (f32[8,1280]{1,0:T(8,128)S(1)}, f32[8,1280]{1,0:T(8,128)}, u32[]{:S(2)}, u32[]{:S(2)}) collective-permute-start(f32[8,1280]{1,0:T(8,128)S(1)} %add.465), channel_id=1, source_target_pairs={{0,16},{8,24},{16,0},{24,8},{1,17},{9,25},{17,1},{25,9},{2,18},{10... | collective-permute-start | bytes 122888 | tf_op jit(solution)/shard_map/ppermute | solution.py:684
  349.5 7.1 copy-start.1
  365.2 17.8 %collective-permute-start.9 = (bf16[2,288,320]{2,1,0:T(8,128)(2,1)S(1)}, bf16[2,288,320]{2,1,0:T(8,128)(2,1)S(1)}, u32[]{:S(2)}, u32[]{:S(2)}) collective-permute-start(bf16[2,288,320]{2,1,0:T(8,128)(2,1)S(1)} %reverse_select_fusion.3), channel_id=1, source_target_pairs={{0,2},{2,0},{4,6},{6,4},{1,3},{3,1},{5,7},{7,5},{8,10},{10,8},{12,... | collective-permute-start | bytes 1105928 | tf_op jit(solution)/shard_map/ppermute | solution.py:684
  367.0 32.3 %collective-permute-start.10 = (bf16[2,288,320]{2,1,0:T(8,128)(2,1)S(1)}, bf16[2,288,320]{2,1,0:T(8,128)(2,1)S(1)}, u32[]{:S(2)}, u32[]{:S(2)}) collective-permute-start(bf16[2,288,320]{2,1,0:T(8,128)(2,1)S(1)} %reverse_select_fusion.2), channel_id=1, source_target_pairs={{0,4},{2,6},{4,0},{6,2},{1,5},{3,7},{5,1},{7,3},{8,12},{10,14},{12... | collective-permute-start | bytes 1105928 | tf_op jit(solution)/shard_map/ppermute | solution.py:684
  367.7 31.6 %collective-permute-start.11 = (bf16[2,288,320]{2,1,0:T(8,128)(2,1)S(1)}, bf16[2,288,320]{2,1,0:T(8,128)(2,1)S(1)}, u32[]{:S(2)}, u32[]{:S(2)}) collective-permute-start(bf16[2,288,320]{2,1,0:T(8,128)(2,1)S(1)} %reverse_select_fusion.1), channel_id=1, source_target_pairs={{0,6},{2,4},{4,2},{6,0},{1,7},{3,5},{5,3},{7,1},{8,14},{10,12},{12... | collective-permute-start | bytes 1105928 | tf_op jit(solution)/shard_map/ppermute | solution.py:684
  404.2 62.5 %collective-permute-start.12 = (bf16[640,320]{0,1:T(8,128)(2,1)}, bf16[640,320]{0,1:T(8,128)(2,1)S(1)}, u32[]{:S(2)}, u32[]{:S(2)}) collective-permute-start(bf16[640,320]{0,1:T(8,128)(2,1)} %get-tuple-element.266), channel_id=1, source_target_pairs={{0,2},{2,0},{4,6},{6,4},{1,3},{3,1},{5,7},{7,5},{8,10},{10,8},{12,... | collective-permute-start | bytes 1228808 | tf_op jit(solution)/shard_map/ppermute | solution.py:684
  411.4 55.4 %collective-permute-start.13 = (bf16[640,320]{0,1:T(8,128)(2,1)}, bf16[640,320]{0,1:T(8,128)(2,1)S(1)}, u32[]{:S(2)}, u32[]{:S(2)}) collective-permute-start(bf16[640,320]{0,1:T(8,128)(2,1)} %get-tuple-element.265), channel_id=1, source_target_pairs={{0,4},{2,6},{4,0},{6,2},{1,5},{3,7},{5,1},{7,3},{8,12},{10,14},{12... | collective-permute-start | bytes 1228808 | tf_op jit(solution)/shard_map/ppermute | solution.py:684
  411.4 55.5 %collective-permute-start.14 = (bf16[640,320]{0,1:T(8,128)(2,1)}, bf16[640,320]{0,1:T(8,128)(2,1)S(1)}, u32[]{:S(2)}, u32[]{:S(2)}) collective-permute-start(bf16[640,320]{0,1:T(8,128)(2,1)} %get-tuple-element.264), channel_id=1, source_target_pairs={{0,6},{2,4},{4,2},{6,0},{1,7},{3,5},{5,3},{7,1},{8,14},{10,12},{12... | collective-permute-start | bytes 1228808 | tf_op jit(solution)/shard_map/ppermute | solution.py:684
  467.9 10.9 %copy-start.28 = (bf16[640,320]{0,1:T(8,128)(2,1)S(1)}, bf16[640,320]{0,1:T(8,128)(2,1)}, u32[]{:S(2)}) copy-start(bf16[640,320]{0,1:T(8,128)(2,1)} %get-tuple-element.147) | copy-start | bytes 1228804
  468.9 66.2 %collective-permute-start.15 = (bf16[640,320]{0,1:T(8,128)(2,1)}, bf16[640,320]{0,1:T(8,128)(2,1)S(1)}, u32[]{:S(2)}, u32[]{:S(2)}) collective-permute-start(bf16[640,320]{0,1:T(8,128)(2,1)} %get-tuple-element.262), channel_id=1, source_target_pairs={{0,2},{2,0},{4,6},{6,4},{1,3},{3,1},{5,7},{7,5},{8,10},{10,8},{12,... | collective-permute-start | bytes 1228808 | tf_op jit(solution)/shard_map/ppermute | solution.py:684
  470.0 65.1 %collective-permute-start.16 = (bf16[640,320]{0,1:T(8,128)(2,1)}, bf16[640,320]{0,1:T(8,128)(2,1)S(1)}, u32[]{:S(2)}, u32[]{:S(2)}) collective-permute-start(bf16[640,320]{0,1:T(8,128)(2,1)} %get-tuple-element.261), channel_id=1, source_target_pairs={{0,4},{2,6},{4,0},{6,2},{1,5},{3,7},{5,1},{7,3},{8,12},{10,14},{12... | collective-permute-start | bytes 1228808 | tf_op jit(solution)/shard_map/ppermute | solution.py:684
  471.0 64.1 %collective-permute-start.17 = (bf16[640,320]{0,1:T(8,128)(2,1)}, bf16[640,320]{0,1:T(8,128)(2,1)S(1)}, u32[]{:S(2)}, u32[]{:S(2)}) collective-permute-start(bf16[640,320]{0,1:T(8,128)(2,1)} %get-tuple-element.260), channel_id=1, source_target_pairs={{0,6},{2,4},{4,2},{6,0},{1,7},{3,5},{5,3},{7,1},{8,14},{10,12},{12... | collective-permute-start | bytes 1228808 | tf_op jit(solution)/shard_map/ppermute | solution.py:684
  476.0 52.4 %collective-permute-start.18 = (bf16[160,320]{1,0:T(8,128)(2,1)S(1)}, bf16[160,320]{1,0:T(8,128)(2,1)S(1)}, u32[]{:S(2)}, u32[]{:S(2)}) collective-permute-start(bf16[160,320]{1,0:T(8,128)(2,1)S(1)} %bitcast.281), channel_id=1, source_target_pairs={{0,2},{2,0},{4,6},{6,4},{1,3},{3,1},{5,7},{7,5},{8,10},{10,8},{12,... | collective-permute-start | bytes 307208 | tf_op jit(solution)/shard_map/ppermute | solution.py:684
  476.9 54.1 %collective-permute-start.19 = (bf16[160,320]{1,0:T(8,128)(2,1)}, bf16[160,320]{1,0:T(8,128)(2,1)S(1)}, u32[]{:S(2)}, u32[]{:S(2)}) collective-permute-start(bf16[160,320]{1,0:T(8,128)(2,1)} %bitcast.241), channel_id=1, source_target_pairs={{0,4},{2,6},{4,0},{6,2},{1,5},{3,7},{5,1},{7,3},{8,12},{10,14},{12... | collective-permute-start | bytes 307208 | tf_op jit(solution)/shard_map/ppermute | solution.py:684
  479.2 48.2 %copy-start.40 = (f32[256,128]{1,0:T(8,128)S(1)}, f32[256,128]{1,0:T(8,128)}, u32[]{:S(2)}) copy-start(f32[256,128]{1,0:T(8,128)} %get-tuple-element.137) | copy-start | bytes 393220
  528.4 6.7 collective-permute-start.20
  546.7 51.8 %collective-permute-start.21 = (bf16[2,288,1280]{2,1,0:T(8,128)(2,1)}, bf16[2,288,1280]{2,1,0:T(8,128)(2,1)}, u32[]{:S(2)}, u32[]{:S(2)}) collective-permute-start(bf16[2,288,1280]{2,1,0:T(8,128)(2,1)} %get-tuple-element.122), channel_id=1, source_target_pairs={{0,1},{1,0},{2,3},{3,2},{4,5},{5,4},{6,7},{7,6},{8,9},{9,8},{10,11... | collective-permute-start | bytes 4423688 | tf_op jit(solution)/shard_map/ppermute | solution.py:684
  546.7 11.7 %copy-start.41 = (f32[8,1280]{1,0:T(8,128)S(1)}, f32[8,1280]{1,0:T(8,128)}, u32[]{:S(2)}) copy-start(f32[8,1280]{1,0:T(8,128)} %get-tuple-element.135) | copy-start | bytes 122884
  566.3 7.4 collective-permute-start.26
  571.6 3.1 collective-permute-start.35
  573.2 13.6 %collective-permute-start.41 = (bf16[640,160]{0,1:T(8,128)(2,1)}, bf16[640,160]{0,1:T(8,128)(2,1)}, u32[]{:S(2)}, u32[]{:S(2)}) collective-permute-start(bf16[640,160]{0,1:T(8,128)(2,1)} %fusion.33), channel_id=1, source_target_pairs={{0,1},{1,0},{2,3},{3,2},{4,5},{5,4},{6,7},{7,6},{8,9},{9,8},{10,11... | collective-permute-start | bytes 614408 | tf_op jit(solution)/shard_map/ppermute | solution.py:684
  574.6 4.5 collective-permute-start.27
  579.1 6.0 collective-permute-start.28
  581.0 17.4 %copy-start.27 = (f32[2,288,1280]{2,1,0:T(8,128)S(1)}, f32[2,288,1280]{2,1,0:T(8,128)}, u32[]{:S(2)}) copy-start(f32[2,288,1280]{2,1,0:T(8,128)} %get-tuple-element.121) | copy-start | bytes 8847364
  585.1 4.5 collective-permute-start.29
  589.6 4.5 collective-permute-start.30
  600.4 19.0 %collective-permute-start.23 = (bf16[2,288,1280]{2,1,0:T(8,128)(2,1)S(1)}, bf16[2,288,1280]{2,1,0:T(8,128)(2,1)S(1)}, u32[]{:S(2)}, u32[]{:S(2)}) collective-permute-start(bf16[2,288,1280]{2,1,0:T(8,128)(2,1)S(1)} %copy-done.55), channel_id=1, source_target_pairs={{0,1},{1,0},{2,3},{3,2},{4,5},{5,4},{6,7},{7,6},{8,9},{9,8},{10,11... | collective-permute-start | bytes 4423688 | tf_op jit(solution)/shard_map/ppermute | solution.py:684
  600.4 18.9 %collective-permute-start.22 = (bf16[288,1280]{1,0:T(8,128)(2,1)S(1)}, bf16[288,1280]{1,0:T(8,128)(2,1)S(1)}, u32[]{:S(2)}, u32[]{:S(2)}) collective-permute-start(bf16[288,1280]{1,0:T(8,128)(2,1)S(1)} %get-tuple-element.268), channel_id=1, source_target_pairs={{0,2},{2,0},{1,3},{3,1},{4,6},{6,4},{5,7},{7,5},{8,10},{10,8},{9,1... | collective-permute-start | bytes 2211848 | tf_op jit(solution)/shard_map/ppermute | solution.py:684
  601.9 5.9 copy-start.22
  625.7 18.6 %collective-permute-start.33 = (bf16[320,960]{1,0:T(8,128)(2,1)S(1)}, bf16[320,960]{1,0:T(8,128)(2,1)S(1)}, u32[]{:S(2)}, u32[]{:S(2)}) collective-permute-start(bf16[320,960]{1,0:T(8,128)(2,1)S(1)} %get-tuple-element.254), channel_id=1, source_target_pairs={{0,24},{8,16},{16,8},{24,0},{1,25},{9,17},{17,9},{25,1},{2,26},{10... | collective-permute-start | bytes 1843208 | tf_op jit(solution)/shard_map/ppermute | solution.py:684
  626.8 30.2 %collective-permute-start.32 = (bf16[320,960]{1,0:T(8,128)(2,1)S(1)}, bf16[320,960]{1,0:T(8,128)(2,1)S(1)}, u32[]{:S(2)}, u32[]{:S(2)}) collective-permute-start(bf16[320,960]{1,0:T(8,128)(2,1)S(1)} %get-tuple-element.255), channel_id=1, source_target_pairs={{0,16},{8,24},{16,0},{24,8},{1,17},{9,25},{17,1},{25,9},{2,18},{10... | collective-permute-start | bytes 1843208 | tf_op jit(solution)/shard_map/ppermute | solution.py:684
  628.8 28.2 %collective-permute-start.31 = (bf16[320,960]{1,0:T(8,128)(2,1)S(1)}, bf16[320,960]{1,0:T(8,128)(2,1)S(1)}, u32[]{:S(2)}, u32[]{:S(2)}) collective-permute-start(bf16[320,960]{1,0:T(8,128)(2,1)S(1)} %get-tuple-element.253), channel_id=1, source_target_pairs={{0,8},{8,0},{16,24},{24,16},{1,9},{9,1},{17,25},{25,17},{2,10},{10... | collective-permute-start | bytes 1843208 | tf_op jit(solution)/shard_map/ppermute | solution.py:684
  631.1 31.6 %collective-permute-start.24 = (bf16[288,1280]{1,0:T(8,128)(2,1)S(1)}, bf16[288,1280]{1,0:T(8,128)(2,1)S(1)}, u32[]{:S(2)}, u32[]{:S(2)}) collective-permute-start(bf16[288,1280]{1,0:T(8,128)(2,1)S(1)} %dynamic-slice_bitcast_fusion), channel_id=1, source_target_pairs={{0,2},{2,0},{1,3},{3,1},{4,6},{6,4},{5,7},{7,5},{8,10},{10,8},{9,1... | collective-permute-start | bytes 2211848 | tf_op jit(solution)/shard_map/ppermute | solution.py:684
  632.5 54.0 %collective-permute-start.25 = (bf16[288,1280]{1,0:T(8,128)(2,1)}, bf16[288,1280]{1,0:T(8,128)(2,1)}, u32[]{:S(2)}, u32[]{:S(2)}) collective-permute-start(bf16[288,1280]{1,0:T(8,128)(2,1)} %add_convert_fusion.4), channel_id=1, source_target_pairs={{0,4},{4,0},{1,5},{5,1},{2,6},{6,2},{3,7},{7,3},{8,12},{12,8},{9,1... | collective-permute-start | bytes 2211848 | tf_op jit(solution)/shard_map/ppermute | solution.py:684
  657.5 23.2 %collective-permute-start.34 = (bf16[160,960]{1,0:T(8,128)(2,1)S(1)}, bf16[160,960]{1,0:T(8,128)(2,1)S(1)}, u32[]{:S(2)}, u32[]{:S(2)}) collective-permute-start(bf16[160,960]{1,0:T(8,128)(2,1)S(1)} %dynamic-slice_bitcast_fusion.23), channel_id=1, source_target_pairs={{0,4},{4,0},{1,5},{5,1},{2,6},{6,2},{3,7},{7,3},{8,12},{12,8},{9,1... | collective-permute-start | bytes 921608 | tf_op jit(solution)/shard_map/ppermute | solution.py:684
  682.7 5.1 copy-start.16
  682.7 50.0 %all-to-all-start = ((bf16[8,3,160,160]{3,2,1,0:T(8,128)(2,1)}), bf16[8,3,160,160]{3,2,1,0:T(8,128)(2,1)S(1)}, u32[]{:S(2)}, u32[]{:S(2)}) async-start(bf16[8,3,160,160]{3,2,1,0:T(8,128)(2,1)} %bitcast.260), calls=%async_computation.1 | async-start | bytes 3932160 | tf_op jit(solution)/shard_map/all_to_all | solution.py:929
  (39 other events, 63.4 us)
Sparse Core Ops, SparseCore 0:
  18.3 162.3 all-gather.2
  272.5 72.0 reduce-scatter.9
  347.6 72.3 reduce-scatter.11
  422.9 31.3 reduce-scatter.7

commit v4 on v3

v4 whole, which is shorter than its diff:
```python
import math
from functools import partial

import jax
import jax.numpy as jnp
from jax import lax
from jax.experimental import pallas as pl
from jax.experimental.pallas import tpu as pltpu
from jax.sharding import PartitionSpec as P

H = 16
HD = 80
EPSILON = 1e-06
NT = (((1,), (1,)), ((), ()))
TN = (((0,), (0,)), ((), ()))
BF = jnp.bfloat16
F32 = jnp.float32
LOG2E = 1.4426950408889634
FACTOR = LOG2E / math.sqrt(HD)
FREE = pl.CostEstimate(flops=1, bytes_accessed=1, transcendentals=0)


def busy(gflops):
    return pl.CostEstimate(flops=gflops * 10**9, bytes_accessed=1, transcendentals=0)


def dot(a, b, dims=(((1,), (0,)), ((), ()))):
    return lax.dot_general(a, b, dims, preferred_element_type=F32)


def params(axes, mib=60):
    return pltpu.CompilerParams(
        dimension_semantics=("arbitrary",) * axes, vmem_limit_bytes=mib << 20
    )


def whole(*shape):
    return pl.BlockSpec(shape, lambda *at: (0,) * len(shape), pipeline_mode=pl.Buffered(1))


def flip_tables(rel_h, rel_w):
    entries = rel_h.shape[0]
    pad = ((0, 128 - entries), (0, 0))
    return jnp.concatenate([jnp.pad(rel_h[::-1], pad), jnp.pad(rel_w[::-1], pad)], 0)


def normal_rows(values):
    center = values - jnp.mean(values, -1, keepdims=True)
    spread = jnp.mean(center * center, -1, keepdims=True)
    return center * lax.rsqrt(spread + EPSILON)


def qkv_kernel(pieces, group_heads, side, raw, gain, shift, w, bias, tables, normed, qa, kp, vp):
    rows = raw.shape[0]
    rows_n = (normal_rows(raw[...].astype(F32)) * gain[...] + shift[...]).astype(BF)
    normed[...] = rows_n
    joined = (dot(rows_n, w[...]) + bias[...]).astype(BF)
    first_row = pl.program_id(0) * (rows // side)
    lane = lax.broadcasted_iota(jnp.int32, (rows, 128), 1)
    group_lane = lax.broadcasted_iota(jnp.int32, (side, 128), 1)
    group_row = lax.broadcasted_iota(jnp.int32, (side, 128), 0)
    col_hot = (group_lane == group_row) | ((group_lane >= side) & (group_lane < side + 3))
    col_hot = jnp.where(col_hot, 1.0, 0.0).astype(BF)
    hot = []
    for i in range(rows // side):
        hot.append(jnp.where(group_lane == first_row + (HD + i), 1.0, 0.0).astype(BF))
    row_hot = jnp.concatenate(hot, 0)
    col_hot = jnp.concatenate([col_hot] * (rows // side), 0)
    width = group_heads * HD
    for n in range(pieces * group_heads):
        q_at = (n // group_heads) * 3 * width + (n % group_heads) * HD
        q = joined[:, q_at : q_at + HD]
        g = dot(q, tables[...], NT) * math.sqrt(HD)
        gh = []
        gw = []
        for i in range(rows // side):
            part = g[i * side : (i + 1) * side]
            gh.append(pltpu.roll(part[:, :128], first_row + (33 + i), axis=1))
            gw.append(pltpu.roll(part[:, 128:], 81, axis=1, stride=1, stride_axis=0))
        qa[n, :, 0:128] = jnp.concatenate(gh, 0).astype(BF)
        qa[n, :, 0:HD] = q
        qa[n, :, 128:256] = jnp.where(lane < side, jnp.concatenate(gw, 0), 0.0).astype(BF)
        kp[n, :, 0:128] = row_hot
        kp[n, :, 128:256] = col_hot
        kp[n, :, 0:HD] = joined[:, q_at + width : q_at + width + HD]
        vp[n] = jnp.ones((rows, 128), BF)
        vp[n, :, 0:HD] = joined[:, q_at + 2 * width : q_at + 2 * width + HD]


def qkv_rows(raw, gain, shift, w, bias, tables, pieces, group_heads, side, rows=384):
    seq_len, width = raw.shape
    lanes = w.shape[1]
    heads = pieces * group_heads
    return pl.pallas_call(
        partial(qkv_kernel, pieces, group_heads, side),
        grid=(seq_len // rows,),
        in_specs=[
            pl.BlockSpec((rows, width), lambda i: (i, 0)),
            whole(1, width),
            whole(1, width),
            whole(width, lanes),
            whole(1, lanes),
            whole(256, HD),
        ],
        out_specs=[
            pl.BlockSpec((rows, width), lambda i: (i, 0)),
            pl.BlockSpec((heads, rows, 256), lambda i: (0, i, 0)),
            pl.BlockSpec((heads, rows, 256), lambda i: (0, i, 0)),
            pl.BlockSpec((heads, rows, 128), lambda i: (0, i, 0)),
        ],
        out_shape=[
            jax.ShapeDtypeStruct((seq_len, width), BF),
            jax.ShapeDtypeStruct((heads, seq_len, 256), BF),
            jax.ShapeDtypeStruct((heads, seq_len, 256), BF),
            jax.ShapeDtypeStruct((heads, seq_len, 128), BF),
        ],
        compiler_params=params(1),
        cost_estimate=FREE,
        name="qkv_rows",
    )(raw, gain, shift, w, bias, tables)


def attend_kernel(heads, side, aliased, sub, at, qa, kp, vp, *refs):
    o, of, qo = refs[2:] if aliased else refs
    rows = qa.shape[1]
    h = pl.program_id(0)
    base = pl.multiple_of(pl.program_id(1) * rows, rows)
    lane = lax.broadcasted_iota(jnp.int32, (sub, 128), 1)
    count = rows // sub
    scores = [dot(qa[0, 0:sub, :], kp[0], NT)]
    outs = []
    for n in range(count):
        part = slice(n * sub, (n + 1) * sub)
        if n + 1 < count:
            scores.append(dot(qa[0, (n + 1) * sub : (n + 2) * sub, :], kp[0], NT))
        s = scores[n]
        m = jnp.max(s, -1, keepdims=True)
        p = jnp.exp2(s * FACTOR - m * FACTOR).astype(BF)
        out = dot(p, vp[0])
        total = out[:, HD : HD + 1]
        out = out / total
        norm = m + jnp.log2(total) / FACTOR
        hi = norm.astype(BF).astype(F32)
        mid = (norm - hi).astype(BF).astype(F32)
        low = norm - hi - mid
        old = qa[0, part, 128:256].astype(F32)
        old = jnp.where(lane == side, -hi, old)
        old = jnp.where(lane == side + 1, -mid, old)
        old = jnp.where(lane == side + 2, -low, old)
        qo[0, part, 0:128] = qa[0, part, 0:128]
        qo[0, part, 128:256] = old.astype(BF)
        outs.append(out)
    out = jnp.concatenate(outs, 0)
    part = pl.ds(base, rows)
    for n in range(heads):

        @pl.when(h == n)
        def _(n=n):
            o[part, n * HD : (n + 1) * HD] = out[:, 0:HD].astype(BF)
            of[part, n * HD : (n + 1) * HD] = out[:, 0:HD]


def attend(group, qa, kp, vp, side, groups, old=(), tq=1152, sub=576):
    heads, seq_len, _ = qa.shape
    rows = seq_len // groups
    steps = rows // tq
    lanes = heads * HD
    query = pl.BlockSpec((1, tq, 256), lambda h, i, at: (h, at[0] * steps + i, 0))
    return pl.pallas_call(
        partial(attend_kernel, heads, side, bool(old), sub),
        grid_spec=pltpu.PrefetchScalarGridSpec(
            num_scalar_prefetch=1,
            grid=(heads, steps),
            in_specs=[
                query,
                pl.BlockSpec((1, seq_len, 256), lambda h, i, at: (h, 0, 0)),
                pl.BlockSpec((1, seq_len, 128), lambda h, i, at: (h, 0, 0)),
            ]
            + [pl.BlockSpec(memory_space=pl.ANY)] * len(old),
            out_specs=[
                pl.BlockSpec((rows, lanes), lambda h, i, at: (0, 0)),
                pl.BlockSpec((rows, lanes), lambda h, i, at: (at[0], 0)),
                query,
            ],
        ),
        out_shape=[
            jax.ShapeDtypeStruct((rows, lanes), BF),
            jax.ShapeDtypeStruct((seq_len, lanes), F32),
            jax.ShapeDtypeStruct((heads, seq_len, 256), BF),
        ],
        input_output_aliases={4: 1, 5: 2} if old else {},
        compiler_params=params(2),
        cost_estimate=busy(20),
        name="attend",
    )(jnp.stack([group]), qa, kp, vp, *old)


def attend_back_kernel(heads, first, side, uc, qa_ref, kp, vp, of, go, tables, dx, gt, kt, dop, dk, dv, dq):
    seq_len = kp.shape[1]
    tb = qa_ref.shape[1]
    h = pl.program_id(0)
    step = pl.program_id(1)
    last = pl.num_programs(1) - 1
    scale = HD ** (-0.5)
    rows = seq_len // 9

    @pl.when((h == 0) & (step == 0))
    def _():
        gt[...] = jnp.zeros_like(gt)

        def prep(i, c):
            part = pl.ds(pl.multiple_of(i * rows, rows), rows)
            lane = lax.broadcasted_iota(jnp.int32, (rows, 128), 1)
            for n in range(heads):
                at = (first + n) * HD
                rows_go = go[part, at : at + HD]
                inner = jnp.sum(rows_go.astype(F32) * of[part, at : at + HD], -1, keepdims=True)
                hi = inner.astype(BF).astype(F32)
                tail = jnp.where(lane == HD, -hi, jnp.where(lane == HD + 1, hi - inner, 0.0))
                dop[n, part, :] = tail.astype(BF)
                dop[n, part, 0:HD] = rows_go
            return c

        lax.fori_loop(0, 9, prep, 0)

    @pl.when(step == 0)
    def _():
        def prep(i, c):
            part = pl.ds(pl.multiple_of(i * rows, rows), rows)
            kt[:, part] = kp[0, part, :].T[0 : HD + 2 * side]
            dk[part, :] = jnp.zeros((rows, 128), F32)
            dv[part, :] = jnp.zeros((rows, 128), F32)
            return c

        lax.fori_loop(0, 9, prep, 0)

    base = pl.ds(pl.multiple_of(step * tb, tb), tb)
    qa = qa_ref[0]
    do = dop[h, base, :]

    def scores(j):
        part = slice(j * uc, (j + 1) * uc)
        return dot(kp[0, part, :], qa, NT), dot(vp[0, part, :], do, NT)

    acc = None
    count = seq_len // uc
    ahead = scores(0)
    for j in range(count):
        s, dp = ahead
        if j + 1 < count:
            ahead = scores(j + 1)
        part = slice(j * uc, (j + 1) * uc)
        p = jnp.exp2(s * FACTOR)
        ds = (p * dp).astype(BF)
        dv[part, :] += dot(p.astype(BF), do)
        dk[part, :] += dot(ds, qa[:, 0:128])
        term = dot(kt[:, part], ds)
        acc = term if acc is None else acc + term
    acc = jnp.concatenate([acc, jnp.zeros((256 - HD - 2 * side, tb), F32)], 0).T
    lane = lax.broadcasted_iota(jnp.int32, (tb, 128), 1)
    groups = tb // side
    rel_h = jnp.where(lane < HD, 0.0, acc[:, :128])
    rel_w = jnp.where(lane < side, acc[:, 128:], 0.0)
    back_h = []
    back_w = []
    for i in range(groups):
        part = slice(i * side, (i + 1) * side)
        back_h.append(pltpu.roll(rel_h[part], 256 - 33 - step * groups - i, axis=1))
        back_w.append(stagger(rel_w[part], side))
    both = jnp.concatenate([jnp.concatenate(back_h, 0), jnp.concatenate(back_w, 0)], 1).astype(BF)
    dq[base, :] = acc[:, :HD] * scale + dot(both, tables[...])
    gt[...] += dot(both, qa[:, 0:128], TN)

    width = heads * HD
    for n in range(heads):

        @pl.when((h == n) & (step == last))
        def _(n=n):
            def post(i, c):
                part = pl.ds(pl.multiple_of(i * rows, rows), rows)
                at = n * HD
                dx[part, at : at + HD] = dq[part, :].astype(BF)
                dx[part, width + at : width + at + HD] = (dk[part, 0:HD] * scale).astype(BF)
                dx[part, 2 * width + at : 2 * width + at + HD] = dv[part, 0:HD].astype(BF)
                return c

            lax.fori_loop(0, 9, post, 0)


def stagger(val, side):
    row = lax.broadcasted_iota(jnp.int32, val.shape, 0)
    shift = side - 1 - row
    bit = 1
    while bit < side:
        val = jnp.where((shift & bit) != 0, pltpu.roll(val, bit, axis=1), val)
        bit *= 2
    return val


def attend_back(first, count, qa, kp, vp, of, go, tables, side, tb=768, uc=256):
    heads, seq_len, _ = qa.shape
    lanes = heads * HD
    return pl.pallas_call(
        partial(attend_back_kernel, count, first, side, uc),
        grid=(count, seq_len // tb),
        in_specs=[
            pl.BlockSpec((1, tb, 256), lambda h, i: (first + h, i, 0)),
            pl.BlockSpec((1, seq_len, 256), lambda h, i: (first + h, 0, 0)),
            pl.BlockSpec((1, seq_len, 128), lambda h, i: (first + h, 0, 0)),
            whole(seq_len, lanes),
            whole(seq_len, lanes),
            whole(256, HD),
        ],
        out_specs=[whole(seq_len, 3 * count * HD), whole(256, 128)],
        out_shape=[
            jax.ShapeDtypeStruct((seq_len, 3 * count * HD), BF),
            jax.ShapeDtypeStruct((256, 128), F32),
        ],
        scratch_shapes=[
            pltpu.VMEM((HD + 2 * side, seq_len), BF),
            pltpu.VMEM((count, seq_len, 128), BF),
            pltpu.VMEM((seq_len, 128), F32),
            pltpu.VMEM((seq_len, 128), F32),
            pltpu.VMEM((seq_len, HD), F32),
        ],
        compiler_params=params(2),
        cost_estimate=busy(50),
        name="attend_back",
    )(qa, kp, vp, of, go, tables)


def mlp_kernel(aliased, per, n_own, n_other, g_own, g_other, w1, b1, w2, *refs):
    if aliased:
        out_in, gn_in, out, gn, grads, gb1, n2, gb, act, gbef = refs
    else:
        out, gn, grads, gb1, n2, gb, act, gbef = refs
    step = pl.program_id(0)
    chunk = out.shape[0]
    shards, shard, hidden = w1.shape
    width = n_own.shape[1]
    steps = 2 * per

    @pl.when(step == 0)
    def _():
        gb1[...] = jnp.zeros_like(gb1)

    @pl.when(step < steps)
    def _():
        first = w1[...].reshape(width, hidden)
        second = w2[...].reshape(hidden, width)
        dst = pl.ds(pl.multiple_of(step * chunk, chunk), chunk)
        mine = step < per
        n2[dst, :] = jnp.where(mine, n_own[...], n_other[...])
        gb[dst, :] = jnp.where(mine, g_own[...], g_other[...])
        before = dot(n2[dst, :], first) + b1[...]
        grad_act = dot(gb[dst, :], second, NT)
        cdf = 0.5 + 0.5 * lax.erf(before * math.sqrt(0.5))
        act[dst, :] = (before * cdf).astype(BF)
        slope = cdf + before * (jnp.exp(-0.5 * before * before) * (1.0 / math.sqrt(2.0 * math.pi)))
        grad_before = slope * grad_act
        gbef[dst, :] = grad_before.astype(BF)
        gb1[...] += jnp.sum(gbef[dst, :].astype(F32), 0, keepdims=True)
        value = dot(act[dst, :], second)
        back = dot(gbef[dst, :], first, NT)
        if aliased:
            value = value + out_in[...]
            back = back + gn_in[...]
        out[...] = value
        gn[...] = back

    for j in range(shards):

        @pl.when(step == steps + j)
        def _(j=j):
            rows = slice(j * shard, (j + 1) * shard)
            grads[0, 0:shard, :] = dot(n2[:, rows], gbef[...], TN).astype(BF)
            grads[0, shard : 2 * shard, :] = dot(act[:, rows], gb[...], TN).astype(BF)


def mlp_half(n_own, n_other, g_own, g_other, weights, b1, old=(), chunk=288):
    half, width = n_own.shape
    dp = weights.shape[0]
    shard = width // dp
    hidden = width
    chunk = min(chunk, half)
    per = half // chunk
    steps = 2 * per
    tile = pl.BlockSpec((chunk, width), lambda i: (jnp.minimum(i, steps - 1), 0))
    own = pl.BlockSpec((chunk, width), lambda i: (jnp.minimum(i, per - 1), 0))
    other = pl.BlockSpec((chunk, width), lambda i: (jnp.clip(i - per, 0, per - 1), 0))
    rows = jax.ShapeDtypeStruct((2 * half, width), F32)
    return pl.pallas_call(
        partial(mlp_kernel, bool(old), per),
        grid=(steps + dp,),
        in_specs=[own, other, own, other]
        + [
            pl.BlockSpec((dp, shard, width), lambda i: (0, 0, 0), pipeline_mode=pl.Buffered(1)),
            whole(1, hidden),
            pl.BlockSpec((dp, shard, width), lambda i: (0, 1, 0), pipeline_mode=pl.Buffered(1)),
        ]
        + [tile] * len(old),
        out_specs=[
            tile,
            tile,
            pl.BlockSpec((1, 2 * shard, width), lambda i: (jnp.maximum(i - steps, 0), 0, 0)),
            whole(1, hidden),
        ],
        out_shape=[
            rows,
            rows,
            jax.ShapeDtypeStruct((dp, 2 * shard, width), BF),
            jax.ShapeDtypeStruct((1, hidden), F32),
        ],
        input_output_aliases={7: 0, 8: 1} if old else {},
        scratch_shapes=[pltpu.VMEM((2 * half, width), BF)] * 4,
        compiler_params=params(1, 63),
        cost_estimate=busy(35),
        name="mlp_half",
    )(n_own, n_other, g_own, g_other, weights, b1, weights, *old)


def select_kernel(ng, np_, nc, at, qkv, fc1, fc2, proj, own, *slabs):
    i_p, i_c = at[1], at[2]
    shard = fc1.shape[0]
    width = proj.shape[1]
    hidden = fc1.shape[1]
    chips = ng * np_
    unit = hidden // (chips * nc)
    part = unit // 2
    piece = proj.shape[0] // nc
    shard_lanes = proj.shape[0]
    lanes = own.shape[1] // 3
    pieces = lanes // piece
    per = fc2.shape[0] // (nc * unit)
    for c in range(nc):

        @pl.when(i_c == c)
        def _(c=c):
            for u in range(2):
                for z in range(chips):
                    src = (z * nc + c) * unit + u * part
                    slabs[u][0:shard, z * part : (z + 1) * part] = fc1[:, src : src + part]
                for b in range(per):
                    src = (b * nc + c) * unit + u * part
                    dst = shard + b * part
                    slabs[u][dst : dst + part, :] = fc2[src : src + part, :]
            slabs[0][2 * shard : 2 * shard + piece, :] = proj[c * piece : (c + 1) * piece, :]

        for p in range(np_):

            @pl.when((i_c == c) & (i_p == p))
            def _(c=c, p=p):
                for q in range(pieces):
                    for t in range(3):
                        src = t * width + (p * pieces + q) * shard_lanes + c * piece
                        dst = (3 * q + t) * piece
                        own[:, dst : dst + piece] = qkv[:, src : src + piece]


def select(at, qkv, fc1, fc2, proj, ng, np_, nc, lanes):
    shard, width = proj.shape[0], proj.shape[1]
    return pl.pallas_call(
        partial(select_kernel, ng, np_, nc),
        in_specs=[pl.BlockSpec(memory_space=pltpu.SMEM)] + [pl.BlockSpec(memory_space=pltpu.VMEM)] * 4,
        out_specs=[pl.BlockSpec(memory_space=pltpu.VMEM)] * 3,
        out_shape=[
            jax.ShapeDtypeStruct((shard, 3 * lanes), BF),
            jax.ShapeDtypeStruct((2 * shard + shard // nc, width), BF),
            jax.ShapeDtypeStruct((2 * shard, width), BF),
        ],
        compiler_params=pltpu.CompilerParams(vmem_limit_bytes=40 << 20),
        cost_estimate=FREE,
        name="select",
    )(at, qkv, fc1, fc2, proj)


def start_kernel(sizes, split, patches, own, vec, rows, full, vecs, local, send, recv):
    dp, ng, np_ = sizes
    i_dp, i_g, i_p, i_c = (lax.axis_index(name) for name in ("dp", "g", "p", "c"))
    count = patches.shape[1]
    step = count // split

    barrier = pltpu.get_barrier_semaphore()
    peers = [{"dp": i_dp ^ k} for k in range(1, dp)]
    peers += [{"g": i_g ^ k} for k in range(1, ng)]
    peers += [{"p": i_p ^ k} for k in range(1, np_)]
    peers += [{"c": 1 - i_c}]
    for peer in peers:
        pl.semaphore_signal(barrier, inc=1, device_id=peer, device_id_type=pl.DeviceIdType.MESH)
    pl.semaphore_wait(barrier, len(peers))

    used = []

    def remote(src, dst, peer):
        n = len(used)
        copy = pltpu.make_async_remote_copy(
            src_ref=src,
            dst_ref=dst,
            send_sem=send.at[n],
            recv_sem=recv.at[n],
            device_id=peer,
            device_id_type=pl.DeviceIdType.MESH,
        )
        used.append(copy)
        return copy

    def place(g, p, c, part):
        start = ((g * np_ + p) * 2 + c) * count + part * step
        return rows.at[pl.ds(pl.multiple_of(start, 8), step)]

    mine = [patches.at[i_g, pl.ds(part * step, step)] for part in range(split)]
    home = [pltpu.make_async_copy(mine[part], place(i_g, i_p, i_c, part), local.at[part]) for part in range(split)]
    home.append(pltpu.make_async_copy(own, full.at[i_dp], local.at[split]))
    home.append(pltpu.make_async_copy(vec, vecs.at[i_dp], local.at[split + 1]))

    far = {}
    for part in range(split):
        for bit in range(1, ng):
            src = patches.at[i_g ^ bit, pl.ds(part * step, step)]
            far[bit, part] = remote(src, place(i_g, i_p, i_c, part), {"g": i_g ^ bit})
            far[bit, part].start()
    over_dp = []
    for bit in range(1, dp):
        over_dp.append(remote(vec, vecs.at[i_dp], {"dp": i_dp ^ bit}))
        over_dp.append(remote(own, full.at[i_dp], {"dp": i_dp ^ bit}))
    for copy in over_dp:
        copy.start()
    near = {}
    for bit in range(1, np_):
        for part in range(split):
            near[bit, part] = remote(mine[part], place(i_g, i_p, i_c, part), {"p": i_p ^ bit})
            near[bit, part].start()
    cores = []
    for part in range(split):
        cores.append(remote(mine[part], place(i_g, i_p, i_c, part), {"c": 1 - i_c}))
        cores[-1].start()
    for copy in home:
        copy.start()

    onward = {}
    for part in range(split):
        for bit in range(1, ng):
            far[bit, part].wait_recv()
            came = place(i_g ^ bit, i_p, i_c, part)
            for bit_p in range(1, np_):
                onward[bit, bit_p, part] = remote(came, came, {"p": i_p ^ bit_p})
                onward[bit, bit_p, part].start()
            cores.append(remote(came, came, {"c": 1 - i_c}))
            cores[-1].start()
        for bit in range(1, np_):
            near[bit, part].wait_recv()
            came = place(i_g, i_p ^ bit, i_c, part)
            cores.append(remote(came, came, {"c": 1 - i_c}))
            cores[-1].start()
    for (bit, bit_p, part), copy in onward.items():
        copy.wait_recv()
        came = place(i_g ^ bit, i_p ^ bit_p, i_c, part)
        cores.append(remote(came, came, {"c": 1 - i_c}))
        cores[-1].start()
    for copy in over_dp + cores:
        copy.wait_recv()
    for copy in used:
        copy.wait_send()
    for copy in home:
        copy.wait()


def start_exchange(patches, own, vec, sizes, split=3):
    dp, ng, np_ = sizes
    images, count, width = patches.shape
    chunk_copies = ng * np_ + (ng - 1) + (np_ - 1) + (ng - 1) * (np_ - 1)
    copies = 2 * (dp - 1) + split * chunk_copies
    hbm = pl.BlockSpec(memory_space=pl.ANY)
    return pl.pallas_call(
        partial(start_kernel, sizes, split),
        in_specs=[hbm] * 3,
        out_specs=[hbm] * 3,
        out_shape=[
            jax.ShapeDtypeStruct((ng * np_ * 2 * count, width), BF),
            jax.ShapeDtypeStruct((dp,) + own.shape, BF),
            jax.ShapeDtypeStruct((dp,) + vec.shape, BF),
        ],
        scratch_shapes=[
            pltpu.SemaphoreType.DMA((split + 2,)),
            pltpu.SemaphoreType.DMA((copies,)),
            pltpu.SemaphoreType.DMA((copies,)),
        ],
        compiler_params=pltpu.CompilerParams(collective_id=0, has_side_effects=True),
        cost_estimate=FREE,
        name="start_exchange",
    )(patches, own, vec)


def rows_back_kernel(pieces, *refs):
    dx = refs[:pieces]
    raw, w, out, sums = refs[pieces:]
    total = None
    width = dx[0].shape[1]
    for q in range(pieces):
        term = dot(dx[q][...], w[:, q * width : (q + 1) * width], NT)
        total = term if total is None else total + term
    normal = normal_rows(raw[...].astype(F32))

    @pl.when(pl.program_id(0) == 0)
    def _():
        sums[...] = jnp.zeros_like(sums)

    sums[0:1, :] += jnp.sum(total * normal, 0, keepdims=True)
    sums[1:2, :] += jnp.sum(total, 0, keepdims=True)
    for q in range(pieces):
        sums[2 + q : 3 + q, 0:width] += jnp.sum(dx[q][...].astype(F32), 0, keepdims=True)
    out[...] = total.astype(BF)


def rows_back(dx, raw, w, rows=384):
    pieces = len(dx)
    seq_len, width = raw.shape
    lanes = dx[0].shape[1]
    block = lambda cols: pl.BlockSpec((rows, cols), lambda i: (i, 0))
    return pl.pallas_call(
        partial(rows_back_kernel, pieces),
        grid=(seq_len // rows,),
        in_specs=[block(lanes)] * pieces + [block(width), whole(width, pieces * lanes)],
        out_specs=[block(width), whole(8, width)],
        out_shape=[jax.ShapeDtypeStruct((seq_len, width), BF), jax.ShapeDtypeStruct((8, width), F32)],
        compiler_params=params(1),
        cost_estimate=busy(15),
        name="rows_back",
    )(*dx, raw, w)


class Links:
    def __init__(self, send, recv):
        self.send, self.recv, self.copies = send, recv, []

    def __call__(self, src, dst, peer):
        n = len(self.copies)
        copy = pltpu.make_async_remote_copy(
            src_ref=src,
            dst_ref=dst,
            send_sem=self.send.at[n],
            recv_sem=self.recv.at[n],
            device_id=peer,
            device_id_type=pl.DeviceIdType.MESH,
        )
        copy.start()
        self.copies.append(copy)
        return copy

    def drain(self):
        for copy in self.copies:
            copy.wait_send()


def meet(peers):
    barrier = pltpu.get_barrier_semaphore()
    for peer in peers:
        pl.semaphore_signal(barrier, inc=1, device_id=peer, device_id_type=pl.DeviceIdType.MESH)
    pl.semaphore_wait(barrier, len(peers))


def finish_kernel(sizes, split, pieces, part_w, vec_block, *refs):
    dp, ng, np_ = sizes
    chips = ng * np_
    rows_in, vec, inputs, grad_mid, gain = refs[:5]
    grads = refs[5 : 5 + pieces]
    parts_a, parts_b, parts_p = (refs[5 + pieces + n * chips : 5 + pieces + (n + 1) * chips] for n in range(3))
    (home, owned, total, out_fc1, out_fc2, out_proj, keep, came, pair, far, slabs, cells, taken, by_dp, by_chip, by_core,
     give, got, give_p, got_p, sem, send, recv, cell_send, cell_recv) = refs[5 + pieces + 3 * chips :]
    i_dp, i_g, i_p, i_c = (lax.axis_index(name) for name in ("dp", "g", "p", "c"))
    count = keep.shape[1]
    step = count // split
    ranks = chips * 2
    shard = owned.shape[0]
    cell = owned.shape[1] // 3
    i_s = (i_g * np_ + i_p) * 2 + i_c

    peers = [{"dp": i_dp ^ k} for k in range(1, dp)]
    for k in range(1, ranks):
        bit_g, bit_p, bit_c = k // (np_ * 2), (k // 2) % np_, k % 2
        peers.append({"g": i_g ^ bit_g, "p": i_p ^ bit_p, "c": i_c ^ bit_c})
    meet(peers)
    link = Links(send, recv)

    order = list(range(np_, chips)) + list(range(np_))
    z_of = lambda k: (i_g ^ (k // np_)) * np_ + (i_p ^ (k % np_))
    part_rows = lambda part: pl.ds(part * step, step)

    def rows_at(k, c, part):
        start = (z_of(k) * 2 + c) * count + part * step
        return rows_in.at[pl.ds(pl.multiple_of(start, 8), step)]

    block = vec_block
    rest = vec.shape[0] - dp * block

    def vec_rows(j):
        return vec.at[pl.ds(pl.multiple_of(j * block, 8), block)]

    by_dp[i_dp, 0:block] = vec[pl.ds(pl.multiple_of(i_dp * block, 8), block), :]
    by_dp[i_dp, block : block + rest] = vec[dp * block : dp * block + rest, :]
    vec_dp = []
    for bit in range(1, dp):
        peer = {"dp": i_dp ^ bit}
        vec_dp.append(link(vec_rows(i_dp ^ bit), by_dp.at[i_dp, pl.ds(0, block)], peer))
        vec_dp.append(link(vec.at[pl.ds(dp * block, rest)], by_dp.at[i_dp, pl.ds(block, rest)], peer))

    loads = {}
    from_core = {}
    n = 0
    for k in order:
        for part in range(split):
            loads[k, part] = pltpu.make_async_copy(rows_at(k, i_c, part), keep.at[k, part_rows(part)], sem.at[n])
            loads[k, part].start()
            n += 1
            from_core[k, part] = link(rows_at(k, 1 - i_c, part), came.at[k, part_rows(part)], {"c": 1 - i_c})
    from_dp = []
    own_slab = []
    for q in range(pieces):
        src = grads[q].at[pl.ds(pl.multiple_of(i_dp * shard, 8), shard)]
        own_slab.append(pltpu.make_async_copy(src, slabs.at[0, q], sem.at[n]))
        own_slab[-1].start()
        n += 1
    for bit in range(1, dp):
        for q in range(pieces):
            src = grads[q].at[pl.ds(pl.multiple_of((i_dp ^ bit) * shard, 8), shard)]
            from_dp.append(link(src, slabs.at[bit, q], {"dp": i_dp ^ bit}))

    def sum_of(ref, count):
        value = ref[0]
        for n in range(1, count):
            value = value + ref[n]
        return value

    i_z = i_g * np_ + i_p
    vec_late = []

    def vec_over_chips():
        for copy in vec_dp:
            copy.wait_recv()
        by_chip[i_z] = sum_of(by_dp, dp)
        for k in range(1, chips):
            peer = {"g": i_g ^ (k // np_), "p": i_p ^ (k % np_)}
            vec_late.append(link(by_chip.at[i_z], by_chip.at[i_z], peer))

    def vec_over_cores():
        for copy in vec_late:
            copy.wait_recv()
        by_core[i_c] = sum_of(by_chip, chips)
        vec_late.append(link(by_core.at[i_c], by_core.at[i_c], {"c": 1 - i_c}))

    def collected(parts):
        value = parts[0][...].astype(F32)
        for ref in parts[1:]:
            value = value + ref[...].astype(F32)
        return value

    def halves(value, there, swaps):
        cols = value.shape[1] // 2
        mine = jnp.where(i_c == 0, value[:, :cols], value[:, cols:])
        there[...] = jnp.where(i_c == 0, value[:, cols:], value[:, :cols]).astype(BF)
        return mine

    fc_rows = shard
    hidden_rows = give.shape[1]
    swaps = []
    part_lanes = parts_a[0].shape[1]
    per_rows = out_fc1.shape[1] // 2
    blocks = hidden_rows // per_rows

    def place_fc2(u, core, value):
        for b in range(blocks):
            start = ((b * 2 + core) * 2 + u) * per_rows
            at = pl.ds(pl.multiple_of(start, 8), per_rows)
            out_fc2[at, :] = value[b * per_rows : (b + 1) * per_rows, :]

    def place_proj(core, value):
        rows_p = value.shape[0]
        out_proj[pl.ds(pl.multiple_of(core * rows_p, 8), rows_p), :] = value

    def collect():
        for u, parts in ((0, parts_a), (1, parts_b)):
            value = collected(parts)
            out_fc1[:, u * per_rows : (u + 1) * per_rows] = value[0:fc_rows]
            place_fc2(u, i_c, halves(value[fc_rows:], give.at[u], swaps))
            swaps.append(link(give.at[u], got.at[u], {"c": 1 - i_c}))
        place_proj(i_c, halves(collected(parts_p), give_p, swaps))
        swaps.append(link(give_p, got_p, {"c": 1 - i_c}))

    def swapped():
        for copy in swaps:
            copy.wait_recv()
        for u in range(2):
            place_fc2(u, 1 - i_c, got[u].astype(F32))
        place_proj(1 - i_c, got_p[...].astype(F32))

    def add(k, part):
        loads[k, part].wait()
        from_core[k, part].wait_recv()
        at = part_rows(part)
        keep[k, at, :] = (keep[k, at, :].astype(F32) + came[k, at, :].astype(F32)).astype(BF)

    collect()
    from_pair = {}
    for n, k in enumerate(order):
        if n == len(order) // 2:
            vec_over_chips()
        for part in range(split):
            add(k, part)
            bit_p = k % np_
            if bit_p:
                at = part_rows(part)
                dst = pair.at[k // np_, bit_p, at]
                from_pair[k // np_, bit_p, part] = link(keep.at[k, at], dst, {"p": i_p ^ bit_p})

    def over_pair(bit_g, part):
        at = part_rows(part)
        value = keep[bit_g * np_, at, :].astype(F32)
        for bit_p in range(1, np_):
            from_pair[bit_g, bit_p, part].wait_recv()
            value = value + pair[bit_g, bit_p, at, :].astype(F32)
        return value

    from_far = {}
    for part in range(split):
        at = part_rows(part)
        for bit_g in range(1, ng):
            pair[bit_g, 0, at, :] = over_pair(bit_g, part).astype(BF)
            from_far[bit_g, part] = link(pair.at[bit_g, 0, at], far.at[bit_g, at], {"g": i_g ^ bit_g})

    def arrived(image, at, value):
        grad, _ = norm_back(inputs[image, at, :].astype(F32), gain[...], value)
        home[image, at, :] = (grad_mid[image, at, :] + grad).astype(BF)

    for copy in own_slab:
        copy.wait()
    for copy in from_dp:
        copy.wait_recv()
    width = part_w * 3
    shard_lanes = grads[0].shape[0] // dp
    group_lanes = part_w
    cell_n = 0
    waits = []
    for q in range(pieces):
        value = slabs[0, q].astype(F32)
        for bit in range(1, dp):
            value = value + slabs[bit, q].astype(F32)
        value = value.astype(BF)
        for t in range(3):
            for u in range(part_w // cell):
                lane = t * part_w + u * cell
                cells[cell_n] = value[:, lane : lane + cell]
                start = (i_p * pieces + q) * (shard_lanes // cell) + i_c * (part_w // cell) + u
                unit = t * (dp * (shard_lanes // cell)) + start
                owner = unit // 3
                slot = unit % 3
                dst = taken.at[i_g, slot]
                o_c = owner % 2
                o_p = (owner // 2) % np_
                o_g = owner // (2 * np_)

                @pl.when(owner == i_s)
                def _(cell_n=cell_n, dst=dst, slot=slot):
                    pltpu.make_async_copy(cells.at[cell_n], dst, cell_recv.at[i_g * 3 + slot]).start()

                @pl.when(owner != i_s)
                def _(cell_n=cell_n, dst=dst, slot=slot, o_g=o_g, o_p=o_p, o_c=o_c):
                    pltpu.make_async_remote_copy(
                        src_ref=cells.at[cell_n],
                        dst_ref=dst,
                        send_sem=cell_send.at[cell_n],
                        recv_sem=cell_recv.at[i_g * 3 + slot],
                        device_id={"g": o_g, "p": o_p, "c": o_c},
                        device_id_type=pl.DeviceIdType.MESH,
                    ).start()

                waits.append((cell_n, owner))
                cell_n += 1
    for part in range(split):
        arrived(i_g, part_rows(part), over_pair(0, part))

    vec_over_cores()
    swapped()
    vec_late[-1].wait_recv()
    total[...] = sum_of(by_core, 2)

    for part in range(split):
        at = part_rows(part)
        for bit_g in range(1, ng):
            from_far[bit_g, part].wait_recv()
            arrived(i_g ^ bit_g, at, far[bit_g, at, :].astype(F32))
    for slot in range(3):
        value = None
        for g in range(ng):
            pltpu.make_async_copy(cells.at[0], taken.at[g, slot], cell_recv.at[g * 3 + slot]).wait()
            term = taken[g, slot].astype(F32)
            value = term if value is None else value + term
        owned[:, slot * cell : (slot + 1) * cell] = value
    for cell_n, owner in waits:

        @pl.when(owner != i_s)
        def _(cell_n=cell_n):
            pltpu.make_async_copy(cells.at[cell_n], cells.at[cell_n], cell_send.at[cell_n]).wait()

    link.drain()


def finish(rows_in, vec, vec_block, inputs, grad_mid, gain, grads, parts, sizes, part_w, split=3):
    count = inputs.shape[1]
    dp, ng, np_ = sizes
    chips = ng * np_
    pieces = len(grads)
    width = rows_in.shape[1]
    shard = grads[0].shape[0] // dp
    cell = width // (chips * 2)
    total_cells = pieces * 3 * (part_w // cell)
    parts_a, parts_b, parts_p = parts
    lanes = parts_a[0].shape[1]
    hidden_rows = parts_a[0].shape[0] - shard
    piece_rows = parts_p[0].shape[0]
    own_vec = vec.shape[0] - (dp - 1) * vec_block
    copies = split * (chips + ng * (np_ - 1) + ng - 1) + (dp - 1) * pieces + 2 * (dp - 1) + chips + 3
    hbm = pl.BlockSpec(memory_space=pl.ANY)
    vmem = pl.BlockSpec(memory_space=pltpu.VMEM)
    return pl.pallas_call(
        partial(finish_kernel, sizes, split, pieces, part_w, vec_block),
        in_specs=[hbm] + [vmem] * 4 + [hbm] * pieces + [vmem] * (3 * chips),
        out_specs=[vmem] * 6,
        out_shape=[
            jax.ShapeDtypeStruct((ng, count, width), BF),
            jax.ShapeDtypeStruct((shard, 3 * cell), F32),
            jax.ShapeDtypeStruct((own_vec, 128), F32),
            jax.ShapeDtypeStruct((shard, 2 * lanes), F32),
            jax.ShapeDtypeStruct((4 * hidden_rows, lanes // 2), F32),
            jax.ShapeDtypeStruct((2 * piece_rows, lanes // 2), F32),
        ],
        scratch_shapes=[
            pltpu.VMEM((chips, count, width), BF),
            pltpu.VMEM((chips, count, width), BF),
            pltpu.VMEM((ng, np_, count, width), BF),
            pltpu.VMEM((ng, count, width), BF),
            pltpu.VMEM((dp, pieces, shard, 3 * part_w), BF),
            pltpu.VMEM((total_cells, shard, cell), BF),
            pltpu.VMEM((ng, 3, shard, cell), BF),
            pltpu.VMEM((dp, own_vec, 128), F32),
            pltpu.VMEM((chips, own_vec, 128), F32),
            pltpu.VMEM((2, own_vec, 128), F32),
            pltpu.VMEM((2, hidden_rows, lanes // 2), BF),
            pltpu.VMEM((2, hidden_rows, lanes // 2), BF),
            pltpu.VMEM((piece_rows, lanes // 2), BF),
            pltpu.VMEM((piece_rows, lanes // 2), BF),
            pltpu.SemaphoreType.DMA((split * chips + pieces,)),
            pltpu.SemaphoreType.DMA((copies,)),
            pltpu.SemaphoreType.DMA((copies,)),
            pltpu.SemaphoreType.DMA((total_cells,)),
            pltpu.SemaphoreType.DMA((3 * ng,)),
        ],
        compiler_params=pltpu.CompilerParams(collective_id=1, has_side_effects=True, vmem_limit_bytes=56 << 20),
        cost_estimate=FREE,
        name="finish",
    )(rows_in, vec, inputs, grad_mid, gain, *grads, *parts_a, *parts_b, *parts_p)


def places():
    return tuple(lax.axis_index(name) for name in ("dp", "g", "p", "c"))


def middle_kernel(sizes, near, *refs):
    dp, ng, np_ = sizes
    far = refs[:np_]
    (w, patches, bias, gain, shift, mid, two_own, two_other, mixed,
     pieces, mine, away, came, sem, send, recv) = refs[np_:]
    i_dp, i_g, i_p, i_c = places()
    rows = patches.shape[1]
    core = {"c": 1 - i_c}
    meet([core] + [{"p": i_p ^ k} for k in range(1, np_)])
    link = Links(send, recv)
    here = pltpu.make_async_copy(near.at[i_p], pieces.at[0], sem.at[0])
    here.start()
    arrive = [link(near.at[i_p ^ k], pieces.at[k], {"p": i_p ^ k}) for k in range(1, np_)]

    def split(piece, p, image):
        for swap in range(2):

            @pl.when(i_c == swap)
            def _(swap=swap):
                for b in range(2):
                    mixed[p, b, image] = piece[(swap ^ b) * rows : ((swap ^ b) + 1) * rows, :]

    def product(b, image):
        total = None
        for p in range(np_):
            term = dot(mixed[p, b, image], w[p])
            total = term if total is None else total + term
        return total

    other = []
    for bit in (1, 0):
        image = i_g ^ bit
        if bit:
            for k in range(np_):
                split(far[k], i_p ^ k, image)
        else:
            here.wait()
            for copy in arrive:
                copy.wait_recv()
            for k in range(np_):
                split(pieces.at[k], i_p ^ k, image)
        away[image] = product(1, image)
        other.append(link(away.at[image], came.at[image], core))
        mine[image] = product(0, image)
    back = []
    for bit in (1, 0):
        image = i_g ^ bit
        other[1 - bit].wait_recv()
        value = patches[image].astype(F32) + mine[image] + came[image] + bias[...]
        mid[image] = value
        two_own[image] = (normal_rows(value) * gain[...] + shift[...]).astype(BF)
        back.append(link(two_own.at[image], two_other.at[image], core))
    for copy in back:
        copy.wait_recv()
    link.drain()


def middle_rows(near, far, w, patches, bias, gain, shift, sizes):
    dp, ng, np_ = sizes
    images, rows, width = patches.shape
    lanes = near.shape[2]
    vmem = pl.BlockSpec(memory_space=pltpu.VMEM)
    copies = np_ - 1 + 2 * images
    own = jax.ShapeDtypeStruct((images, rows, width), BF)
    return pl.pallas_call(
        partial(middle_kernel, sizes),
        in_specs=[pl.BlockSpec(memory_space=pl.ANY)] + [vmem] * (len(far) + 5),
        out_specs=[vmem] * 4,
        out_shape=[
            jax.ShapeDtypeStruct((images, rows, width), F32),
            own,
            own,
            jax.ShapeDtypeStruct((np_, 2, images, rows, lanes), BF),
        ],
        scratch_shapes=[
            pltpu.VMEM((np_, 2 * rows, lanes), BF),
            pltpu.VMEM((images, rows, width), F32),
            pltpu.VMEM((images, rows, width), F32),
            pltpu.VMEM((images, rows, width), F32),
            pltpu.SemaphoreType.DMA((1,)),
            pltpu.SemaphoreType.DMA((copies,)),
            pltpu.SemaphoreType.DMA((copies,)),
        ],
        compiler_params=pltpu.CompilerParams(collective_id=2, has_side_effects=True, vmem_limit_bytes=48 << 20),
        cost_estimate=FREE,
        name="middle_rows",
    )(near, *far, w, patches, bias, gain, shift)


def norm_back(values, gain, upstream):
    center = values - jnp.mean(values, -1, keepdims=True)
    spread = jnp.mean(center * center, -1, keepdims=True)
    inverse = lax.rsqrt(spread + EPSILON)
    normal = center * inverse
    scaled = upstream * gain
    inner = jnp.mean(scaled * normal, -1, keepdims=True)
    return inverse * (scaled - jnp.mean(scaled, -1, keepdims=True) - normal * inner), normal


def turn_kernel(sizes, mid, gn, out, branch, gain, shift, w, mixed, output, grad_mid, heads, grad_proj, sums,
                back_own, back_other, gn_own, gn_came, out_own, out_came, stage, sem, send, recv):
    dp, ng, np_ = sizes
    i_dp, i_g, i_p, i_c = places()
    images, rows, width = mid.shape
    i_z = i_g * np_ + i_p
    core = {"c": 1 - i_c}
    peers = [core]
    for k in range(1, ng * np_):
        peers.append({"g": i_g ^ (k // np_), "p": i_p ^ (k % np_)})
    meet(peers)
    link = Links(send, recv)
    turns = [i_g ^ 1, i_g]

    def half(ref, b, image):
        start = (b * images + image) * rows
        return ref.at[pl.ds(pl.multiple_of(start, 8), rows)]

    loads = []
    crossed = []
    for n, image in enumerate(turns):
        crossed.append(link(half(gn, 1, image), gn_came.at[image], core))
        loads.append(pltpu.make_async_copy(half(gn, 0, image), gn_own.at[image], sem.at[n]))
        loads[-1].start()
    locals_ = []
    sums[...] = jnp.zeros_like(sums)

    def give(n, b):
        image = turns[n]
        source = (back_own if b == 0 else back_other)[image]
        for k in range(np_):
            slot = (n * np_ + k) * 2 + b
            stage[slot] = dot(source, w[i_p ^ k], NT).astype(BF)
            start = (i_z * 2 + (i_c ^ b)) * rows
            dst = heads.at[pl.ds(pl.multiple_of(start, 8), rows)]
            if n == 1 and k == 0:
                locals_.append(pltpu.make_async_copy(stage.at[slot], dst, sem.at[2 * images + b]))
                locals_[-1].start()
            else:
                arrivals.append(link(stage.at[slot], dst, {"g": image, "p": i_p ^ k}))

    arrivals = []
    others = []
    for n, image in enumerate(turns):
        loads[n].wait()
        crossed[n].wait_recv()
        grad_two = gn_own[image] + gn_came[image]
        grad_out = branch[image].astype(F32)
        grad_norm, normal = norm_back(mid[image], gain[...], grad_two)
        grad = grad_out + grad_norm
        grad_mid[image] = grad
        back_own[image] = grad.astype(BF)
        others.append(link(back_own.at[image], back_other.at[image], core))
        sums[0:1, :] += jnp.sum(grad_two * normal, 0, keepdims=True)
        sums[1:2, :] += jnp.sum(grad_two, 0, keepdims=True)
        sums[2:3, :] += jnp.sum(back_own[image].astype(F32), 0, keepdims=True)
        sums[3:4, :] += jnp.sum(grad_out, 0, keepdims=True)
        give(n, 0)
    outs = []
    for n, image in enumerate(turns):
        others[n].wait_recv()
        give(n, 1)
        outs.append(link(half(out, 1, image), out_came.at[image], core))
        loads.append(pltpu.make_async_copy(half(out, 0, image), out_own.at[image], sem.at[images + n]))
        loads[-1].start()
    for p in range(np_):
        total = None
        for b, source in ((0, back_own), (1, back_other)):
            for image in range(images):
                term = dot(mixed[p, b, image], source[image], TN)
                total = term if total is None else total + term
        grad_proj[p] = total.astype(BF)
    for n, image in enumerate(turns):
        loads[images + n].wait()
        outs[n].wait_recv()
        value = mid[image] + out_own[image] + out_came[image] + shift[...]
        output[image] = value.astype(BF)
    for copy in locals_:
        copy.wait()
    for copy in arrivals:
        copy.wait_recv()
    link.drain()


def turn(mid, gn, out, branch, gain, shift, w, mixed, sizes):
    dp, ng, np_ = sizes
    images, rows, width = mid.shape
    lanes = w.shape[1]
    chips = ng * np_
    vmem = pl.BlockSpec(memory_space=pltpu.VMEM)
    hbm = pl.BlockSpec(memory_space=pl.ANY)
    copies = 3 * images + 2 * (chips - 1)
    own = (images, rows, width)
    return pl.pallas_call(
        partial(turn_kernel, sizes),
        in_specs=[vmem, hbm, hbm] + [vmem] * 5,
        out_specs=[vmem, vmem, hbm, vmem, vmem],
        out_shape=[
            jax.ShapeDtypeStruct(own, BF),
            jax.ShapeDtypeStruct(own, F32),
            jax.ShapeDtypeStruct((chips * 2 * rows, lanes), BF),
            jax.ShapeDtypeStruct((np_, lanes, width), BF),
            jax.ShapeDtypeStruct((8, width), F32),
        ],
        scratch_shapes=[
            pltpu.VMEM(own, BF),
            pltpu.VMEM(own, BF),
            pltpu.VMEM(own, F32),
            pltpu.VMEM(own, F32),
            pltpu.VMEM(own, F32),
            pltpu.VMEM(own, F32),
            pltpu.VMEM((chips * 2, rows, lanes), BF),
            pltpu.SemaphoreType.DMA((2 * images + 2,)),
            pltpu.SemaphoreType.DMA((copies,)),
            pltpu.SemaphoreType.DMA((copies,)),
        ],
        compiler_params=pltpu.CompilerParams(collective_id=3, has_side_effects=True, vmem_limit_bytes=56 << 20),
        cost_estimate=FREE,
        name="turn",
    )(mid, gn, out, branch, gain, shift, w, mixed)


def flip(value, axis, size, bit):
    return lax.ppermute(value, axis, [(i, i ^ bit) for i in range(size)])


def pick(value, index, axis=0):
    return lax.dynamic_index_in_dim(value, index, axis, keepdims=False)


def gather_pieces(value, axis, size, me):
    full = jnp.zeros((size,) + value.shape, value.dtype)
    full = lax.dynamic_update_index_in_dim(full, value, me, 0)
    for bit in range(1, size):
        full = lax.dynamic_update_index_in_dim(full, flip(value, axis, size, bit), me ^ bit, 0)
    return full


def scatter_sum(value, axis, size, me):
    total = pick(value, me).astype(F32)
    for bit in range(1, size):
        total = total + flip(pick(value, me ^ bit), axis, size, bit).astype(F32)
    return total


def tie(*values):
    return lax.optimization_barrier(values)


def after(value, *others):
    return tie(value, *others)[0]


def on_device(
    patches,
    ln1_gain,
    ln1_bias,
    qkv_weight,
    q_bias,
    v_bias,
    proj_weight,
    proj_bias,
    ln2_gain,
    ln2_bias,
    fc1_weight,
    fc1_bias,
    fc2_weight,
    fc2_bias,
    rel_pos_h,
    rel_pos_w,
    cotangent,
):
    images, row_count, width = patches.shape
    dp, ng, np_, nc = (lax.axis_size(name) for name in ("dp", "g", "p", "c"))
    i_dp, i_g, i_p, i_c = (lax.axis_index(name) for name in ("dp", "g", "p", "c"))
    chips = ng * np_
    i_z = i_g * np_ + i_p
    ranks = chips * nc
    seq_len = ranks * row_count
    own_rows = images * row_count
    heads = H * images // ranks
    shard_heads = H // dp
    core_heads = shard_heads // nc
    piece = core_heads * HD
    pieces = heads // core_heads
    lanes = heads * HD
    hidden = fc1_weight.shape[1]
    unit = hidden // ranks
    shard = width // dp
    per = hidden // dp // (nc * unit)
    side = (rel_pos_h.shape[0] + 1) // 2

    core_bias = pick(fc1_bias.reshape(per, nc, 2, unit // 2), i_c, 1).transpose(1, 0, 2)
    packed = jnp.concatenate(
        [
            jnp.stack([ln1_gain, ln1_bias, q_bias, v_bias, proj_bias, ln2_gain, ln2_bias, fc2_bias]),
            core_bias.reshape(-1, shard),
        ]
    )
    spot = jnp.stack([i_g, i_p, i_c])
    qkv_own, slab_a, slab_b = select(spot, qkv_weight, fc1_weight, fc2_weight, proj_weight, ng, np_, nc, lanes)
    weights_a = lax.all_gather(slab_a, "dp", axis=0)
    weights_b = lax.all_gather(slab_b, "dp", axis=0)
    proj_half = weights_a[:, 2 * shard :]
    raw, qkv_full, vectors = start_exchange(patches, qkv_own, packed, (dp, ng, np_))
    qkv_full = qkv_full.reshape(width, 3 * lanes)
    vectors = vectors.astype(F32)
    whole_vec = vectors.transpose(1, 0, 2).reshape(-1, width)
    gain_one, shift_one, q_shift, v_shift, proj_shift, gain_two, shift_two, fc2_shift = whole_vec[:8]
    fc1_shift = vectors[:, 8:].reshape(dp, 2, -1).transpose(1, 0, 2).reshape(2, 1, -1)

    starts = [
        part * width + (i_p * pieces + q) * shard_heads * HD + i_c * piece
        for q in range(pieces)
        for part in range(3)
    ]
    zero = jnp.zeros((piece,), F32)
    biases = []
    for q in range(pieces):
        at = starts[3 * q]
        biases += [lax.dynamic_slice_in_dim(q_shift, at, piece, 0), zero]
        biases += [lax.dynamic_slice_in_dim(v_shift, at, piece, 0)]
    qkv_shift = jnp.concatenate(biases)[None]

    branch_own = cotangent.reshape(own_rows, width)
    branch_other = flip(branch_own, "c", nc, 1)

    tables = flip_tables(rel_pos_h, rel_pos_w)
    normed, query, key_rows, value_rows = qkv_rows(
        raw, gain_one[None], shift_one[None], qkv_full, qkv_shift, tables, pieces, core_heads, side
    )
    far_att, att_f, query_a = attend(i_g ^ 1, query, key_rows, value_rows, side, ng)
    far_att = far_att.reshape(np_, nc * row_count, lanes)
    arrived = {}
    for bit_p in range(np_):
        arrived[1, bit_p] = flip(pick(far_att, i_p ^ bit_p), ("g", "p"), chips, np_ + bit_p)
    near_att, att_f, query_a = attend(i_g, query, key_rows, value_rows, side, ng, (att_f, query_a))
    near_att, *pinned = tie(near_att, *[arrived[1, k] for k in range(np_)])
    for k in range(np_):
        arrived[1, k] = pinned[k]
    near_att = near_att.reshape(np_, nc * row_count, lanes)
    proj_rows = proj_half.reshape(np_, lanes, width)
    sizes = (dp, ng, np_)
    middle, two_own, two_other, mixed = middle_rows(
        near_att,
        [arrived[1, k] for k in range(np_)],
        proj_rows,
        patches,
        proj_shift[None],
        gain_two[None],
        shift_two[None],
        sizes,
    )
    two_own, two_other = two_own.reshape(own_rows, width), two_other.reshape(own_rows, width)

    def over_dp(value):
        return lax.psum_scatter(value.reshape(-1, value.shape[-1]), "dp", scatter_dimension=0, tiled=True)

    out_a, back_a, grads_a, bias_a = mlp_half(
        two_own, two_other, branch_own, branch_other, weights_a, fc1_shift[0]
    )
    sum_a = over_dp(grads_a)
    out_b, back_b, grads_b, bias_b = mlp_half(
        two_own, two_other, branch_own, branch_other, weights_b, fc1_shift[1], (out_a, back_a)
    )
    output, grad_middle, grad_heads, grad_proj, early = turn(
        middle, back_b, out_b, cotangent, gain_two[None], fc2_shift[None], proj_rows, mixed, sizes
    )
    sum_b = over_dp(grads_b)
    sum_p = over_dp(grad_proj.reshape(dp, piece, width))

    def pieces_over_chips(value):
        split = value.reshape(value.shape[0], chips, width // chips).transpose(1, 0, 2)
        sent = [flip(pick(split, i_z ^ bit), ("g", "p"), chips, bit) for bit in range(1, chips)]
        return [pick(split, i_z)] + sent

    grad_heads, sum_a = tie(grad_heads, sum_a)
    sum_a = pieces_over_chips(sum_a)
    dx = []
    grad_tables = 0.0
    for q in range(pieces):
        rows, table = attend_back(
            q * core_heads, core_heads, query_a, key_rows, value_rows, att_f, grad_heads, tables, side
        )
        if q == 0:
            rows, *sum_a = tie(rows, *sum_a)
            sum_b = pieces_over_chips(after(sum_b, rows))
            key_rows = after(key_rows, rows)
        elif q == 1:
            rows, *sum_b = tie(rows, *sum_b)
        dx.append(rows)
        grad_tables = grad_tables + table
    dx[-1], sum_p = tie(dx[-1], sum_p)
    sum_p = pieces_over_chips(sum_p)

    grad_rows, sums = rows_back(dx, raw, qkv_full)
    grad_qkv = [lax.dot_general(normed, rows, TN, preferred_element_type=F32).astype(BF) for rows in dx]

    def spread(part):
        full = jnp.zeros((width,), F32)
        for q in range(pieces):
            block = sums[2 + q, part * piece : (part + 1) * piece]
            full = lax.dynamic_update_slice_in_dim(full, block, starts[3 * q], 0)
        return full

    entries = rel_pos_h.shape[0]
    rel = jnp.stack([grad_tables[:entries, :HD], grad_tables[128 : 128 + entries, :HD]])[:, ::-1]
    bias_half = jnp.stack([bias_a.reshape(dp, per, unit // 2), bias_b.reshape(dp, per, unit // 2)], 2)
    bias_half = bias_half.reshape(dp * per, 1, unit)
    bias_full = jnp.concatenate([bias_half] * nc, 1)
    core = lax.broadcasted_iota(jnp.int32, bias_full.shape, 1)
    bias_full = jnp.where(core == i_c, bias_full, 0.0).reshape(dp, -1)
    eight = jnp.concatenate([jnp.stack([sums[0], sums[1], spread(0), spread(2)]), early[:4]])
    vectors = jnp.concatenate([eight.reshape(8, dp, shard).transpose(1, 0, 2).reshape(dp, -1), bias_full], 1)
    block = -(-vectors.shape[1] // 1024) * 8
    vectors = jnp.pad(vectors, ((0, 0), (0, block * 128 - vectors.shape[1])))
    rel = rel.reshape(-1)
    vectors = jnp.concatenate([vectors.reshape(-1), jnp.pad(rel, (0, -rel.shape[0] % 1024))]).reshape(-1, 128)
    grad_patches, out_qkv, vectors, out_fc1, out_fc2, out_proj = finish(
        grad_rows,
        vectors,
        block,
        patches,
        grad_middle,
        gain_one[None],
        grad_qkv,
        (sum_a, sum_b, sum_p),
        sizes,
        piece,
    )
    rel = vectors[block:].reshape(-1)[: 2 * entries * HD].reshape(2, entries, HD)
    flat = vectors[:block].reshape(-1)
    vec = [flat[n * shard : (n + 1) * shard] for n in range(8)]
    fc1_vec = flat[8 * shard : 8 * shard + hidden // dp]
    return (
        output,
        grad_patches,
        vec[0],
        vec[1],
        out_qkv,
        vec[2],
        vec[3],
        out_proj,
        vec[6],
        vec[4],
        vec[5],
        out_fc1,
        fc1_vec,
        out_fc2,
        vec[7],
        rel[0],
        rel[1],
    )


def solution(mesh):
    dp, ranks = mesh.shape["dp"], mesh.shape["seq"]

    def call(*args):
        images = args[0].shape[0] // dp
        shape = (dp, images, ranks // images // 2, 2)
        fine = jax.sharding.Mesh(mesh.devices.reshape(shape), ("dp", "g", "p", "c"))
        seq = ("g", "p", "c")
        tokens, rows, both = P("dp", seq, None), P("dp", None), P("dp", seq)
        vec = P("dp")
        return jax.shard_map(
            on_device,
            mesh=fine,
            in_specs=(
                tokens, vec, vec, rows, vec, vec, rows, vec, vec, vec, rows, vec, rows, vec, P(), P(), tokens
            ),
            out_specs=(
                tokens, tokens, vec, vec, both, vec, vec, both, vec, vec, vec, both, vec, both, vec, P(), P()
            ),
            check_vma=False,
        )(*args)

    return call
```

time: 751 us -> 590 us (0.79)
  waiting for transfers between devices: 157 us -> 14.4 us
  Pallas kernels: 354 us -> 458 us
  other arithmetic: 53.8 us -> 2.34 us
  starting transfers between devices: 54.3 us -> 20.3 us
  local copies, waits for them, and re-layouts: 85.2 us -> 57.7 us
  matrix products: 22.4 us -> 13.1 us
    ppermute x42 -> x12, waiting for transfers between devices: 119 us -> 13.6 us  [flip(): return lax.ppermute(value, axis, [(i, i ^ bit) for i in range(size)])]
    pallas_call x7 -> x8, Pallas kernels: 181 us -> 284 us  [the longest x1 79.4 us: finish(): pl.pallas_call(partial(finish_kernel, sizes, split, pieces, part_w, vec_b...]
    all_to_all x1 -> x0, waiting for transfers between devices: 37.7 us -> none  [on_device(): lax.all_to_all(send.reshape(ranks, 3, shard // ng, cell), ('g', 'p', 'c')...]
    ppermute x42 -> x12, starting transfers between devices: 50.4 us -> 19.9 us  [flip(): return lax.ppermute(value, axis, [(i, i ^ bit) for i in range(size)])]
    reduce_sum x7 -> x0, other arithmetic: 21.7 us -> none  [the longest x2 7.78 us: on_device(): rows_f = lambda value: jnp.sum(value.astype(F32), 0)]
    convert_element_type x8 -> x0, other arithmetic: 19.4 us -> none  [the longest x1 5.32 us: on_device(): (center * lax.rsqrt(spread + EPSILON) * gain_two + shift_two).astype(BF)]
    unnamed x130 -> x87, local copies, waits for them, and re-layouts: 36.1 us -> 21 us
    dot_general x2 -> x0, matrix products: 10.8 us -> none  [the longest x1 5.43 us: on_device(): jnp.einsum('pbtl,btd->pld', mixed.reshape(np_, nc, own_rows, lanes), both...]
  transfers between devices with their start and end apart: 47 -> 17, of which waited for: 21 -> 3; matrix products, arithmetic and copies ran while one was open for 17% -> 6% of each run, Pallas kernels for 39% -> 62%
where the time goes in v4:
time: 590 us; the launch traced here: 581 us
  Pallas kernels  458 us (78%)
  local copies, waits for them, and re-layouts  57.7 us (10%)
  starting transfers between devices  20.3 us (3%)
  between operations  15 us (3%)
  waiting for transfers between devices  14.4 us (2%)
  matrix products  13.1 us (2%)
    pallas_call x2, Pallas kernels, attend_back(): pl.pallas_call(partial(attend_back_kernel, count, first, side, uc), grid=...  95.1 us
    pallas_call x1, Pallas kernels, finish(): pl.pallas_call(partial(finish_kernel, sizes, split, pieces, part_w, vec_b...  79.4 us
    pallas_call x2, Pallas kernels, mlp_half(): pl.pallas_call(partial(mlp_kernel, bool(old), per), grid=(steps + dp,), i...  68.4 us
    pallas_call x1, Pallas kernels, start_exchange(): pl.pallas_call(partial(start_kernel, sizes, split), in_specs=[hbm] * 3, o...  58.3 us
    pallas_call x1, Pallas kernels, turn(): pl.pallas_call(partial(turn_kernel, sizes), in_specs=[vmem, hbm, hbm] + [...  48.9 us
    pallas_call x2, Pallas kernels, attend(): pl.pallas_call(partial(attend_kernel, heads, side, bool(old), sub), grid_...  39.3 us
    pallas_call x1, Pallas kernels, middle_rows(): pl.pallas_call(partial(middle_kernel, sizes), in_specs=[pl.BlockSpec(memo...  30.9 us
    unnamed x87, local copies, waits for them, and re-layouts  21 us
  transfers between devices with their start and end apart: 17, of which 3 were waited for; matrix products, arithmetic and copies ran while one was open for 6% of the time, Pallas kernels for 62%

profile of v4, /device:TPU:0, one launch (start us, length us, event | category | flops | bytes accessed | tf_op | source)
XLA Modules:
  0.0 581.2 jit_solution(14149597947008057945)
XLA Ops:
  7.3 1.9 copy-done.1
  9.2 1.9 copy-done.2
  11.2 1.7 copy-done.3
  12.9 1.1 copy-done.5
  14.0 3.2 select.23
  17.2 0.8 copy-done.6
  19.3 1.2 concatenate.24.vec
  20.5 58.3 %start_exchange.1 = (bf16[2304,1280]{1,0:T(8,128)(2,1)}, bf16[4,320,960]{2,1,0:T(8,128)(2,1)}, bf16[4,10,320]{2,1,0:T(8,128)(2,1)}) custom-call(bf16[2,288,1280]{2,1,0:T(8,128)(2,1)} %refs_2_.1, bf16[320,960]{1,0:T(8,128)(2,1)} %copy-done.6, bf16[10,320]{1,0:T(8,128)(2,1)} %concatenate.24.vec), custom_call_target="tpu_custom_call" | custom-call | flops 1 | bytes 1 | tf_op jit(solution)/shard_map/start_exchange/pallas_call | solution.py:574
  78.8 0.8 fusion.7
  83.1 18.2 %qkv_rows.1 = (bf16[2304,1280]{1,0:T(8,128)(2,1)}, bf16[4,2304,256]{2,1,0:T(8,128)(2,1)}, bf16[4,2304,256]{2,1,0:T(8,128)(2,1)}, bf16[4,2304,128]{2,1,0:T(8,128)(2,1)}) custom-call(bf16[2304,1280]{1,0:T(8,128)(2,1)} %get-tuple-element.82.raw.refs_2_, f32[1,1280]{1,0:T(1,128)} %unstack.43.gain.refs_4_, f32[1,1280]{1,0:T(1,128)} %unstack.45.shift, ...), custom_call_target="tpu_custom_call" | custom-call | flops 1 | bytes 1 | tf_op jit(solution)/shard_map/qkv_rows/pallas_call | solution.py:94
  101.3 19.5 %attend.2 = (bf16[1152,320]{1,0:T(8,128)(2,1)}, f32[2304,320]{1,0:T(8,128)}, bf16[4,2304,256]{2,1,0:T(8,128)(2,1)}) custom-call(s32[1]{0:T(128)} %bitcast.7.at, bf16[4,2304,256]{2,1,0:T(8,128)(2,1)} %get-tuple-element.85.qa, bf16[4,2304,256]{2,1,0:T(8,128)(2,1)} %get-tuple-element.114.kp, bf16[4,2304,128]{2,1,0:T(8,128)(2,1)} %get-tuple-element.87.vp), custom_call_target="tpu_custom_call" | custom-call | flops 20000000000 | bytes 1 | tf_op jit(solution)/shard_map/attend/pallas_call | solution.py:169
  120.8 2.1 dynamic-slice_bitcast_fusion
  122.9 2.2 collective-permute-start
  125.1 1.9 collective-permute-start.1
  127.0 19.7 %attend.3 = (bf16[1152,320]{1,0:T(8,128)(2,1)}, f32[2304,320]{1,0:T(8,128)}, bf16[4,2304,256]{2,1,0:T(8,128)(2,1)}) custom-call(s32[1]{0:T(128)} %bitcast.at, bf16[4,2304,256]{2,1,0:T(8,128)(2,1)} %get-tuple-element.85.qa, bf16[4,2304,256]{2,1,0:T(8,128)(2,1)} %get-tuple-element.114.kp, ...), custom_call_target="tpu_custom_call", output_to_operand_aliasing={{1}: (4, {}), {2}: (5, {})} | custom-call | flops 20000000000 | bytes 1 | tf_op jit(solution)/shard_map/attend/pallas_call | solution.py:169
  147.7 7.5 %collective-permute-done.refs_0_ = bf16[576,320]{1,0:T(8,128)(2,1)S(1)} collective-permute-done((bf16[576,320]{1,0:T(8,128)(2,1)}, bf16[576,320]{1,0:T(8,128)(2,1)S(1)}, u32[]{:S(2)}, u32[]{:S(2)}) %collective-permute-start) | collective-permute-done | bytes 368672 | tf_op jit(solution)/shard_map/ppermute | solution.py:1189
  155.3 2.7 slice.139
  158.0 30.9 %middle_rows.1 = (f32[2,288,1280]{2,1,0:T(8,128)}, bf16[2,288,1280]{2,1,0:T(8,128)(2,1)S(1)}, bf16[2,288,1280]{2,1,0:T(8,128)(2,1)S(1)}, bf16[2,2,2,288,320]{4,3,2,1,0:T(8,128)(2,1)}) custom-call(bf16[2,576,320]{2,1,0:T(8,128)(2,1)S(1)} %bitcast.74, bf16[576,320]{1,0:T(8,128)(2,1)S(1)} %collective-permute-done.refs_0_, ...), custom_call_target="tpu_custom_call" | custom-call | flops 1 | bytes 1 | tf_op jit(solution)/shard_map/middle_rows/pallas_call | solution.py:1031
  189.0 1.1 copy-done.8
  190.1 1.1 copy-done.9
  191.2 33.2 %mlp_half.2 = (f32[1152,1280]{1,0:T(8,128)}, f32[1152,1280]{1,0:T(8,128)}, bf16[4,640,1280]{2,1,0:T(8,128)(2,1)}, f32[1,1280]{1,0:T(1,128)}) custom-call(bf16[576,1280]{1,0:T(8,128)(2,1)} %bitcast.75, bf16[576,1280]{1,0:T(8,128)(2,1)} %bitcast.77, bf16[576,1280]{1,0:T(8,128)(2,1)} %bitcast.16.g_own, bf16[576,1280]{1,0:T(8,128)(2,1)} %collective-permute-done.2.g_other, ...), custom_call_target="tpu_custom_call" | custom-call | flops 35000000512 | bytes 1 | tf_op jit(solution)/shard_map/mlp_half/pallas_call | solution.py:392
  225.2 35.1 %mlp_half.3 = (f32[1152,1280]{1,0:T(8,128)}, f32[1152,1280]{1,0:T(8,128)}, bf16[4,640,1280]{2,1,0:T(8,128)(2,1)}, f32[1,1280]{1,0:T(1,128)}) custom-call(bf16[576,1280]{1,0:T(8,128)(2,1)} %bitcast.76, bf16[576,1280]{1,0:T(8,128)(2,1)} %bitcast.78, bf16[576,1280]{1,0:T(8,128)(2,1)} %bitcast.16.g_own, ...), custom_call_target="tpu_custom_call", output_to_operand_aliasing={{0}: (7, {}), {1}: (8, {})} | custom-call | flops 35000000512 | bytes 1 | tf_op jit(solution)/shard_map/mlp_half/pallas_call | solution.py:392
  261.4 48.9 %turn.1 = (bf16[2,288,1280]{2,1,0:T(8,128)(2,1)}, f32[2,288,1280]{2,1,0:T(8,128)}, bf16[2304,320]{1,0:T(8,128)(2,1)}, bf16[2,320,1280]{2,1,0:T(8,128)(2,1)}, f32[8,1280]{1,0:T(8,128)}) custom-call(f32[2,288,1280]{2,1,0:T(8,128)} %get-tuple-element.96.mid, f32[1152,1280]{1,0:T(8,128)} %get-tuple-element.102.gn, f32[1152,1280]{1,0:T(8,128)} %get-tuple-element.103.out, ...), custom_call_target="tpu_custom_call" | custom-call | flops 1 | bytes 1 | tf_op jit(solution)/shard_map/turn/pallas_call | solution.py:1159
  310.3 0.8 slice.121
  311.5 3.4 copy.131
  315.1 1.0 copy.113
  316.1 5.2 collective-permute-start.3
  321.7 1.0 copy.115
  322.7 2.3 collective-permute-start.5
  325.0 47.1 %attend_back.2 = (bf16[2304,480]{1,0:T(8,128)(2,1)}, f32[256,128]{1,0:T(8,128)}) custom-call(bf16[4,2304,256]{2,1,0:T(8,128)(2,1)} %get-tuple-element.106.qa_ref, bf16[4,2304,256]{2,1,0:T(8,128)(2,1)} %get-tuple-element.114.kp, bf16[4,2304,128]{2,1,0:T(8,128)(2,1)} %get-tuple-element.87.vp, f32[2304,320]{1,0:T(8,128)} %get-tuple-element.107.of, ...), custom_call_target="tpu_custom_call" | custom-call | flops 49999998976 | bytes 1 | tf_op jit(solution)/shard_map/attend_back/pallas_call | solution.py:303
  372.1 1.0 copy.112
  373.1 2.8 copy.133
  376.0 0.8 copy-done.14
  376.9 1.0 copy.118
  377.9 1.2 collective-permute-start.6
  379.4 1.0 collective-permute-start.7
  380.4 1.0 copy.120
  381.4 2.3 collective-permute-start.8
  383.6 48.0 %attend_back.3 = (bf16[2304,480]{1,0:T(8,128)(2,1)}, f32[256,128]{1,0:T(8,128)}) custom-call(bf16[4,2304,256]{2,1,0:T(8,128)(2,1)} %get-tuple-element.106.qa_ref, bf16[4,2304,256]{2,1,0:T(8,128)(2,1)} %get-tuple-element.114.kp, bf16[4,2304,128]{2,1,0:T(8,128)(2,1)} %get-tuple-element.87.vp, f32[2304,320]{1,0:T(8,128)} %get-tuple-element.107.of, ...), custom_call_target="tpu_custom_call" | custom-call | flops 49999998976 | bytes 1 | tf_op jit(solution)/shard_map/attend_back/pallas_call | solution.py:303
  431.7 6.5 %convolution_convert_fusion.1 = bf16[1280,480]{0,1:T(8,128)(2,1)S(1)} fusion(bf16[2304,1280]{1,0:T(8,128)(2,1)} %get-tuple-element.129, bf16[2304,480]{1,0:T(8,128)(2,1)} %get-tuple-element.113.refs_0_), kind=kOutput, calls=%fused_computation.1 | convolution fusion | flops 2831769600 | bytes 9338880 | tf_op jit(solution)/shard_map/dot_general | solution.py:1362
  438.2 1.0 copy.117
  439.2 1.5 copy.124.refs_5_
  441.2 6.6 %convolution_convert_fusion = bf16[1280,480]{0,1:T(8,128)(2,1)S(1)} fusion(bf16[2304,1280]{1,0:T(8,128)(2,1)} %get-tuple-element.129, bf16[2304,480]{1,0:T(8,128)(2,1)} %get-tuple-element.120.refs_1_), kind=kOutput, calls=%fused_computation | convolution fusion | flops 2831769600 | bytes 9338880 | tf_op jit(solution)/shard_map/dot_general | solution.py:1362
  447.8 16.8 %rows_back.1 = (bf16[2304,1280]{1,0:T(8,128)(2,1)}, f32[8,1280]{1,0:T(8,128)}) custom-call(bf16[2304,480]{1,0:T(8,128)(2,1)} %get-tuple-element.113.refs_0_, bf16[2304,480]{1,0:T(8,128)(2,1)} %get-tuple-element.120.refs_1_, bf16[2304,1280]{1,0:T(8,128)(2,1)} %get-tuple-element.82.raw.refs_2_, bf16[1280,960]{1,0:T(8,128)(2,1)} %bitcast.86), custom_call_target="tpu_custom_call" | custom-call | flops 15000000512 | bytes 1 | tf_op jit(solution)/shard_map/rows_back/pallas_call | solution.py:620
  464.6 0.9 fusion.8
  465.5 0.8 slice.116
  466.3 1.5 copy.125.refs_6_
  469.4 1.0 constant_dynamic-slice_fusion
  470.6 2.7 collective-permute-start.11
  473.4 0.9 collective-permute-start.9
  475.5 5.1 collective-permute-done.10.refs_17_
  480.6 1.0 collective-permute-done.9.refs_16_
  482.2 79.4 %finish.1 = (bf16[2,288,1280]{2,1,0:T(8,128)(2,1)}, f32[320,480]{1,0:T(8,128)}, f32[152,128]{1,0:T(8,128)}, f32[320,640]{1,0:T(8,128)}, f32[1280,160]{1,0:T(8,128)}, /*index=5*/f32[320,160]{1,0:T(8,128)}) custom-call(bf16[2304,1280]{1,0:T(8,128)(2,1)} %get-tuple-element.121.refs_0_, f32[248,128]{1,0:T(8,128)} %fusion.2.refs_1_, ...), custom_call_target="tpu_custom_call" | custom-call | flops 1 | bytes 1 | tf_op jit(solution)/shard_map/finish/pallas_call | solution.py:924
  561.6 1.0 slice.135
  562.6 0.7 slice_bitcast_fusion.2
  563.3 1.3 slice_bitcast_fusion.4
  564.6 2.6 copy.127
  567.3 0.7 copy.128
  568.0 0.7 copy.129
  568.7 0.8 copy.126
  570.3 1.1 copy.161
  571.4 1.1 copy.162
  572.5 0.8 copy.163
  573.3 0.9 copy.164
  (164 shorter events, 13.6 us)
Async XLA Ops:
  7.2 148.1 %all-gather.5.cloned.1.call-start = ((), (), s32[]{:S(2)}) async-start(), calls=%async_computation.4 | async-start | bytes 10240000 | tf_op jit(solution)/shard_map/all_gather | solution.py:1267
  7.3 1.9 copy-start.1
  9.2 1.9 copy-start.2
  11.2 1.7 copy-start.3
  12.9 1.1 copy-start.5
  17.2 0.8 copy-start.6
  18.1 0.9 copy-start.27
  18.1 1.0 copy-start.28
  18.1 1.0 copy-start.29
  18.1 1.0 copy-start.30
  18.1 1.1 copy-start.31
  18.1 1.1 copy-start.32
  18.1 1.1 copy-start.33
  18.1 1.1 copy-start.34
  18.1 1.1 copy-start.35
  18.2 63.2 %copy-start.23 = (bf16[95,80]{0,1:T(8,128)(2,1)S(1)}, bf16[95,80]{0,1:T(8,128)(2,1)}, u32[]{:S(2)}) copy-start(bf16[95,80]{0,1:T(8,128)(2,1)} %param.32) | copy-start | bytes 45604
  18.2 63.3 %copy-start.24 = (bf16[95,80]{0,1:T(8,128)(2,1)S(1)}, bf16[95,80]{0,1:T(8,128)(2,1)}, u32[]{:S(2)}) copy-start(bf16[95,80]{0,1:T(8,128)(2,1)} %param.31) | copy-start | bytes 45604
  18.2 207.0 %all-gather.7.cloned.1.call-start = ((), (), s32[]{:S(2)}) async-start(), calls=%async_computation.5 | async-start | bytes 8192000 | tf_op jit(solution)/shard_map/all_gather | solution.py:1268
  18.9 292.6 %reduce-scatter.10.cloned.1.call-start = ((), (), s32[]{:S(2)}) async-start(), calls=%async_computation.6 | async-start | bytes 8192000
  122.9 32.3 %collective-permute-start = (bf16[576,320]{1,0:T(8,128)(2,1)}, bf16[576,320]{1,0:T(8,128)(2,1)S(1)}, u32[]{:S(2)}, u32[]{:S(2)}) collective-permute-start(bf16[576,320]{1,0:T(8,128)(2,1)} %get-tuple-element.249), channel_id=1, source_target_pairs={{0,4},{2,6},{4,0},{6,2},{1,5},{3,7},{5,1},{7,3},{8,12},{10,14},{12... | collective-permute-start | bytes 1105928 | tf_op jit(solution)/shard_map/ppermute | solution.py:1189
  125.1 30.1 %collective-permute-start.1 = (bf16[576,320]{1,0:T(8,128)(2,1)}, bf16[576,320]{1,0:T(8,128)(2,1)S(1)}, u32[]{:S(2)}, u32[]{:S(2)}) collective-permute-start(bf16[576,320]{1,0:T(8,128)(2,1)} %get-tuple-element.248), channel_id=1, source_target_pairs={{0,6},{2,4},{4,2},{6,0},{1,7},{3,5},{5,3},{7,1},{8,14},{10,12},{12... | collective-permute-start | bytes 1105928 | tf_op jit(solution)/shard_map/ppermute | solution.py:1189
  127.0 64.2 %collective-permute-start.2 = (bf16[576,1280]{1,0:T(8,128)(2,1)}, bf16[576,1280]{1,0:T(8,128)(2,1)}, u32[]{:S(2)}, u32[]{:S(2)}) collective-permute-start(bf16[576,1280]{1,0:T(8,128)(2,1)} %bitcast.16.g_own), channel_id=1, source_target_pairs={{0,1},{1,0},{2,3},{3,2},{4,5},{5,4},{6,7},{7,6},{8,9},{9,8},{10,11... | collective-permute-start | bytes 4423688 | tf_op jit(solution)/shard_map/ppermute | solution.py:1189
  146.7 11.3 %copy-start = (bf16[2,288,1280]{2,1,0:T(8,128)(2,1)S(1)}, bf16[2,288,1280]{2,1,0:T(8,128)(2,1)}, u32[]{:S(2)}) copy-start(bf16[2,288,1280]{2,1,0:T(8,128)(2,1)} %refs_2_.1) | copy-start | bytes 4423684
  146.7 11.3 %copy-start.4 = (bf16[1152,320]{1,0:T(8,128)(2,1)S(1)}, bf16[1152,320]{1,0:T(8,128)(2,1)}, u32[]{:S(2)}) copy-start(bf16[1152,320]{1,0:T(8,128)(2,1)} %get-tuple-element.92) | copy-start | bytes 2211844
  146.8 42.1 %copy-start.7 = (f32[1,1280]{1,0:T(1,128)}, f32[1,1280]{1,0:T(1,128)S(1)}, u32[]{:S(2)}) copy-start(f32[1,1280]{1,0:T(1,128)S(1)} %unstack.53.refs_5_.gain) | copy-start | bytes 15364
  189.0 1.1 copy-start.8
  190.1 1.1 copy-start.9
  224.5 148.6 %reduce-scatter.12.cloned.1.call-start = ((), (), s32[]{:S(2)}) async-start(), calls=%async_computation.7 | async-start | bytes 8192000
  260.3 180.9 %reduce-scatter.8.cloned.1.call-start = ((), (), s32[]{:S(2)}) async-start(), calls=%async_computation.3 | async-start | bytes 2048000 | tf_op jit(solution)/shard_map/reduce_scatter | solution.py:1322
  261.4 49.7 %copy-start.26 = (f32[1,1280]{1,0:T(1,128)S(1)}, f32[1,1280]{1,0:T(1,128)}, u32[]{:S(2)}) copy-start(f32[1,1280]{1,0:T(1,128)} %get-tuple-element.125) | copy-start | bytes 15364
  261.4 49.8 %copy-start.25 = (f32[1,1280]{1,0:T(1,128)S(1)}, f32[1,1280]{1,0:T(1,128)}, u32[]{:S(2)}) copy-start(f32[1,1280]{1,0:T(1,128)} %get-tuple-element.124) | copy-start | bytes 15364
  316.1 59.9 %collective-permute-start.3 = (bf16[640,320]{1,0:T(8,128)(2,1)}, bf16[640,320]{1,0:T(8,128)(2,1)}, u32[]{:S(2)}, u32[]{:S(2)}) collective-permute-start(bf16[640,320]{1,0:T(8,128)(2,1)} %bitcast.22), channel_id=1, source_target_pairs={{0,2},{2,0},{4,6},{6,4},{1,3},{3,1},{5,7},{7,5},{8,10},{10,8},{12,... | collective-permute-start | bytes 1228808 | tf_op jit(solution)/shard_map/ppermute | solution.py:1189
  321.6 54.4 %collective-permute-start.4 = (bf16[640,320]{1,0:T(8,128)(2,1)S(1)}, bf16[640,320]{1,0:T(8,128)(2,1)}, u32[]{:S(2)}, u32[]{:S(2)}) collective-permute-start(bf16[640,320]{1,0:T(8,128)(2,1)S(1)} %bitcast.93), channel_id=1, source_target_pairs={{0,4},{2,6},{4,0},{6,2},{1,5},{3,7},{5,1},{7,3},{8,12},{10,14},{12... | collective-permute-start | bytes 1228808 | tf_op jit(solution)/shard_map/ppermute | solution.py:1189
  322.7 53.3 %collective-permute-start.5 = (bf16[640,320]{1,0:T(8,128)(2,1)}, bf16[640,320]{1,0:T(8,128)(2,1)S(1)}, u32[]{:S(2)}, u32[]{:S(2)}) collective-permute-start(bf16[640,320]{1,0:T(8,128)(2,1)} %bitcast.24), channel_id=1, source_target_pairs={{0,6},{2,4},{4,2},{6,0},{1,7},{3,5},{5,3},{7,1},{8,14},{10,12},{12... | collective-permute-start | bytes 1228808 | tf_op jit(solution)/shard_map/ppermute | solution.py:1189
  376.0 0.8 copy-start.14
  377.9 63.2 %collective-permute-start.6 = (bf16[640,320]{1,0:T(8,128)(2,1)}, bf16[640,320]{1,0:T(8,128)(2,1)}, u32[]{:S(2)}, u32[]{:S(2)}) collective-permute-start(bf16[640,320]{1,0:T(8,128)(2,1)} %bitcast.28), channel_id=1, source_target_pairs={{0,2},{2,0},{4,6},{6,4},{1,3},{3,1},{5,7},{7,5},{8,10},{10,8},{12,... | collective-permute-start | bytes 1228808 | tf_op jit(solution)/shard_map/ppermute | solution.py:1189
  379.4 61.7 %collective-permute-start.7 = (bf16[640,320]{1,0:T(8,128)(2,1)S(1)}, bf16[640,320]{1,0:T(8,128)(2,1)}, u32[]{:S(2)}, u32[]{:S(2)}) collective-permute-start(bf16[640,320]{1,0:T(8,128)(2,1)S(1)} %bitcast.92), channel_id=1, source_target_pairs={{0,4},{2,6},{4,0},{6,2},{1,5},{3,7},{5,1},{7,3},{8,12},{10,14},{12... | collective-permute-start | bytes 1228808 | tf_op jit(solution)/shard_map/ppermute | solution.py:1189
  381.4 59.8 %collective-permute-start.8 = (bf16[640,320]{1,0:T(8,128)(2,1)}, bf16[640,320]{1,0:T(8,128)(2,1)S(1)}, u32[]{:S(2)}, u32[]{:S(2)}) collective-permute-start(bf16[640,320]{1,0:T(8,128)(2,1)} %bitcast.30), channel_id=1, source_target_pairs={{0,6},{2,4},{4,2},{6,0},{1,7},{3,5},{5,3},{7,1},{8,14},{10,12},{12... | collective-permute-start | bytes 1228808 | tf_op jit(solution)/shard_map/ppermute | solution.py:1189
  438.2 2.5 copy-start.18
  438.2 2.5 copy-start.19
  441.2 6.7 %copy-start.15 = (bf16[640,320]{1,0:T(8,128)(2,1)}, bf16[640,320]{1,0:T(8,128)(2,1)S(1)}, u32[]{:S(2)}) copy-start(bf16[640,320]{1,0:T(8,128)(2,1)S(1)} %collective-permute-done.8.refs_14_) | copy-start | bytes 1228804
  464.6 4.2 copy-start.16
  470.5 10.1 %collective-permute-start.10 = (bf16[160,320]{1,0:T(8,128)(2,1)S(1)}, bf16[160,320]{1,0:T(8,128)(2,1)S(1)}, u32[]{:S(2)}, u32[]{:S(2)}) collective-permute-start(bf16[160,320]{1,0:T(8,128)(2,1)S(1)} %bitcast.99), channel_id=1, source_target_pairs={{0,4},{2,6},{4,0},{6,2},{1,5},{3,7},{5,1},{7,3},{8,12},{10,14},{12... | collective-permute-start | bytes 307208 | tf_op jit(solution)/shard_map/ppermute | solution.py:1189
  470.6 10.0 %collective-permute-start.11 = (bf16[160,320]{1,0:T(8,128)(2,1)S(1)}, bf16[160,320]{1,0:T(8,128)(2,1)S(1)}, u32[]{:S(2)}, u32[]{:S(2)}) collective-permute-start(bf16[160,320]{1,0:T(8,128)(2,1)S(1)} %bitcast.100), channel_id=1, source_target_pairs={{0,6},{2,4},{4,2},{6,0},{1,7},{3,5},{5,3},{7,1},{8,14},{10,12},{12... | collective-permute-start | bytes 307208 | tf_op jit(solution)/shard_map/ppermute | solution.py:1189
  473.4 8.2 %collective-permute-start.9 = (bf16[160,320]{1,0:T(8,128)(2,1)S(1)}, bf16[160,320]{1,0:T(8,128)(2,1)S(1)}, u32[]{:S(2)}, u32[]{:S(2)}) collective-permute-start(bf16[160,320]{1,0:T(8,128)(2,1)S(1)} %bitcast.101), channel_id=1, source_target_pairs={{0,2},{2,0},{4,6},{6,4},{1,3},{3,1},{5,7},{7,5},{8,10},{10,8},{12,... | collective-permute-start | bytes 307208 | tf_op jit(solution)/shard_map/ppermute | solution.py:1189
  480.6 1.0 copy-start.20
  480.6 1.0 copy-start.21
  481.6 0.6 copy-start.22
  561.6 7.1 %copy-start.17 = (f32[320,160]{1,0:T(8,128)S(1)}, f32[320,160]{1,0:T(8,128)}, u32[]{:S(2)}) copy-start(f32[320,160]{1,0:T(8,128)} %get-tuple-element.220) | copy-start | bytes 614404
  561.6 8.6 %copy-start.10 = (bf16[2,288,1280]{2,1,0:T(8,128)(2,1)S(1)}, bf16[2,288,1280]{2,1,0:T(8,128)(2,1)}, u32[]{:S(2)}) copy-start(bf16[2,288,1280]{2,1,0:T(8,128)(2,1)} %get-tuple-element.295) | copy-start | bytes 4423684
  567.2 4.2 copy-start.11
  570.3 2.2 copy-start.13
  571.4 2.0 copy-start.12
Sparse Core Ops, SparseCore 0:
  18.3 109.8 all-gather.4
  130.0 72.3 all-gather.6
  224.6 69.9 reduce-scatter.9
  297.5 72.3 reduce-scatter.11
  372.8 31.3 reduce-scatter.7

commit v5 on v4

--- a/solution.py
+++ b/solution.py
@@ -591,44 +591,6 @@
     )(patches, own, vec)
 
 
-def rows_back_kernel(pieces, *refs):
-    dx = refs[:pieces]
-    raw, w, out, sums = refs[pieces:]
-    total = None
-    width = dx[0].shape[1]
-    for q in range(pieces):
-        term = dot(dx[q][...], w[:, q * width : (q + 1) * width], NT)
-        total = term if total is None else total + term
-    normal = normal_rows(raw[...].astype(F32))
-
-    @pl.when(pl.program_id(0) == 0)
-    def _():
-        sums[...] = jnp.zeros_like(sums)
-
-    sums[0:1, :] += jnp.sum(total * normal, 0, keepdims=True)
-    sums[1:2, :] += jnp.sum(total, 0, keepdims=True)
-    for q in range(pieces):
-        sums[2 + q : 3 + q, 0:width] += jnp.sum(dx[q][...].astype(F32), 0, keepdims=True)
-    out[...] = total.astype(BF)
-
-
-def rows_back(dx, raw, w, rows=384):
-    pieces = len(dx)
-    seq_len, width = raw.shape
-    lanes = dx[0].shape[1]
-    block = lambda cols: pl.BlockSpec((rows, cols), lambda i: (i, 0))
-    return pl.pallas_call(
-        partial(rows_back_kernel, pieces),
-        grid=(seq_len // rows,),
-        in_specs=[block(lanes)] * pieces + [block(width), whole(width, pieces * lanes)],
-        out_specs=[block(width), whole(8, width)],
-        out_shape=[jax.ShapeDtypeStruct((seq_len, width), BF), jax.ShapeDtypeStruct((8, width), F32)],
-        compiler_params=params(1),
-        cost_estimate=busy(15),
-        name="rows_back",
-    )(*dx, raw, w)
-
-
 class Links:
     def __init__(self, send, recv):
         self.send, self.recv, self.copies = send, recv, []
@@ -659,158 +621,99 @@
     pl.semaphore_wait(barrier, len(peers))
 
 
-def finish_kernel(sizes, split, pieces, part_w, vec_block, *refs):
+def finish_kernel(sizes, split, pieces, part_w, *refs):
     dp, ng, np_ = sizes
     chips = ng * np_
-    rows_in, vec, inputs, grad_mid, gain = refs[:5]
-    grads = refs[5 : 5 + pieces]
-    parts_a, parts_b, parts_p = (refs[5 + pieces + n * chips : 5 + pieces + (n + 1) * chips] for n in range(3))
-    (home, owned, total, out_fc1, out_fc2, out_proj, keep, came, pair, far, slabs, cells, taken, by_dp, by_chip, by_core,
-     give, got, give_p, got_p, sem, send, recv, cell_send, cell_recv) = refs[5 + pieces + 3 * chips :]
-    i_dp, i_g, i_p, i_c = (lax.axis_index(name) for name in ("dp", "g", "p", "c"))
-    count = keep.shape[1]
+    ranks = chips * 2
+    raw, normed = refs[:2]
+    dx = refs[2 : 2 + pieces]
+    tables = refs[2 + pieces : 2 + 2 * pieces]
+    refs = refs[2 + 2 * pieces :]
+    w, inputs, grad_mid, gain, early, proj_in = refs[:6]
+    parts_a, parts_b = refs[6 : 6 + chips], refs[6 + chips : 6 + 2 * chips]
+    (home, owned, out_vec, out_tab, out_fc1, out_fc2, out_proj,
+     dx_all, norm_all, dx_ring, raw_ring, keep, away, came, pair, far, slab_out, slabs, cells, taken,
+     sums, lane_sums, vec, vec_out, vec_dp, vec_z, vec_c, tab, tab_dp, tab_z, tab_c, tab_all,
+     give, got, give_p, got_p, proj_out, proj_got, sem, send, recv, cell_send, cell_recv) = refs[6 + 2 * chips :]
+    i_dp, i_g, i_p, i_c = places()
+    i_z = i_g * np_ + i_p
+    i_s = i_z * 2 + i_c
+    count, width = keep.shape[1], keep.shape[2]
     step = count // split
-    ranks = chips * 2
     shard = owned.shape[0]
     cell = owned.shape[1] // 3
-    i_s = (i_g * np_ + i_p) * 2 + i_c
-
+    lanes = dx_all.shape[2]
+    core = {"c": 1 - i_c}
+    chip_peer = lambda k: {"g": i_g ^ (k // np_), "p": i_p ^ (k % np_)}
     peers = [{"dp": i_dp ^ k} for k in range(1, dp)]
     for k in range(1, ranks):
-        bit_g, bit_p, bit_c = k // (np_ * 2), (k // 2) % np_, k % 2
-        peers.append({"g": i_g ^ bit_g, "p": i_p ^ bit_p, "c": i_c ^ bit_c})
+        peers.append({"g": i_g ^ (k // (np_ * 2)), "p": i_p ^ ((k // 2) % np_), "c": i_c ^ (k % 2)})
     meet(peers)
     link = Links(send, recv)
 
-    order = list(range(np_, chips)) + list(range(np_))
     z_of = lambda k: (i_g ^ (k // np_)) * np_ + (i_p ^ (k % np_))
     part_rows = lambda part: pl.ds(part * step, step)
-
-    def rows_at(k, c, part):
-        start = (z_of(k) * 2 + c) * count + part * step
-        return rows_in.at[pl.ds(pl.multiple_of(start, 8), step)]
-
-    block = vec_block
-    rest = vec.shape[0] - dp * block
-
-    def vec_rows(j):
-        return vec.at[pl.ds(pl.multiple_of(j * block, 8), block)]
-
-    by_dp[i_dp, 0:block] = vec[pl.ds(pl.multiple_of(i_dp * block, 8), block), :]
-    by_dp[i_dp, block : block + rest] = vec[dp * block : dp * block + rest, :]
-    vec_dp = []
-    for bit in range(1, dp):
-        peer = {"dp": i_dp ^ bit}
-        vec_dp.append(link(vec_rows(i_dp ^ bit), by_dp.at[i_dp, pl.ds(0, block)], peer))
-        vec_dp.append(link(vec.at[pl.ds(dp * block, rest)], by_dp.at[i_dp, pl.ds(block, rest)], peer))
-
+    far_slots, near_slots = list(range(np_, chips)), list(range(np_))
+    jobs = [(k, b) for group in (far_slots, near_slots) for b in (1, 0) for k in group]
     loads = {}
+
+    def load(n):
+        if n < len(jobs):
+            k, b = jobs[n]
+            start = (z_of(k) * 2 + (i_c ^ b)) * count
+            at = pl.ds(pl.multiple_of(start, 8), count)
+            slot = n % 2
+            loads[n] = [pltpu.make_async_copy(raw.at[at], raw_ring.at[slot], sem.at[slot * (1 + pieces)])]
+            for q in range(pieces):
+                loads[n].append(
+                    pltpu.make_async_copy(dx[q].at[at], dx_ring.at[slot, q], sem.at[slot * (1 + pieces) + 1 + q])
+                )
+            for copy in loads[n]:
+                copy.start()
+
+    load(0)
+    load(1)
+    whole_loads = [pltpu.make_async_copy(normed, norm_all, sem.at[2 * (1 + pieces)])]
+    for q in range(pieces):
+        whole_loads.append(pltpu.make_async_copy(dx[q], dx_all.at[q], sem.at[2 * (1 + pieces) + 1 + q]))
+    for copy in whole_loads:
+        copy.start()
+    sums[...] = jnp.zeros_like(sums)
+    lane_sums[...] = jnp.zeros_like(lane_sums)
     from_core = {}
-    n = 0
-    for k in order:
-        for part in range(split):
-            loads[k, part] = pltpu.make_async_copy(rows_at(k, i_c, part), keep.at[k, part_rows(part)], sem.at[n])
-            loads[k, part].start()
-            n += 1
-            from_core[k, part] = link(rows_at(k, 1 - i_c, part), came.at[k, part_rows(part)], {"c": 1 - i_c})
-    from_dp = []
-    own_slab = []
-    for q in range(pieces):
-        src = grads[q].at[pl.ds(pl.multiple_of(i_dp * shard, 8), shard)]
-        own_slab.append(pltpu.make_async_copy(src, slabs.at[0, q], sem.at[n]))
-        own_slab[-1].start()
-        n += 1
-    for bit in range(1, dp):
+
+    def rows(n):
+        k, b = jobs[n]
+        slot = n % 2
+        for copy in loads[n]:
+            copy.wait()
+        normal = normal_rows(raw_ring[slot].astype(F32))
+        total = None
         for q in range(pieces):
-            src = grads[q].at[pl.ds(pl.multiple_of((i_dp ^ bit) * shard, 8), shard)]
-            from_dp.append(link(src, slabs.at[bit, q], {"dp": i_dp ^ bit}))
-
-    def sum_of(ref, count):
-        value = ref[0]
-        for n in range(1, count):
-            value = value + ref[n]
-        return value
-
-    i_z = i_g * np_ + i_p
-    vec_late = []
-
-    def vec_over_chips():
-        for copy in vec_dp:
-            copy.wait_recv()
-        by_chip[i_z] = sum_of(by_dp, dp)
-        for k in range(1, chips):
-            peer = {"g": i_g ^ (k // np_), "p": i_p ^ (k % np_)}
-            vec_late.append(link(by_chip.at[i_z], by_chip.at[i_z], peer))
-
-    def vec_over_cores():
-        for copy in vec_late:
-            copy.wait_recv()
-        by_core[i_c] = sum_of(by_chip, chips)
-        vec_late.append(link(by_core.at[i_c], by_core.at[i_c], {"c": 1 - i_c}))
-
-    def collected(parts):
-        value = parts[0][...].astype(F32)
-        for ref in parts[1:]:
-            value = value + ref[...].astype(F32)
-        return value
-
-    def halves(value, there, swaps):
-        cols = value.shape[1] // 2
-        mine = jnp.where(i_c == 0, value[:, :cols], value[:, cols:])
-        there[...] = jnp.where(i_c == 0, value[:, cols:], value[:, :cols]).astype(BF)
-        return mine
-
-    fc_rows = shard
-    hidden_rows = give.shape[1]
-    swaps = []
-    part_lanes = parts_a[0].shape[1]
-    per_rows = out_fc1.shape[1] // 2
-    blocks = hidden_rows // per_rows
-
-    def place_fc2(u, core, value):
-        for b in range(blocks):
-            start = ((b * 2 + core) * 2 + u) * per_rows
-            at = pl.ds(pl.multiple_of(start, 8), per_rows)
-            out_fc2[at, :] = value[b * per_rows : (b + 1) * per_rows, :]
-
-    def place_proj(core, value):
-        rows_p = value.shape[0]
-        out_proj[pl.ds(pl.multiple_of(core * rows_p, 8), rows_p), :] = value
-
-    def collect():
-        for u, parts in ((0, parts_a), (1, parts_b)):
-            value = collected(parts)
-            out_fc1[:, u * per_rows : (u + 1) * per_rows] = value[0:fc_rows]
-            place_fc2(u, i_c, halves(value[fc_rows:], give.at[u], swaps))
-            swaps.append(link(give.at[u], got.at[u], {"c": 1 - i_c}))
-        place_proj(i_c, halves(collected(parts_p), give_p, swaps))
-        swaps.append(link(give_p, got_p, {"c": 1 - i_c}))
-
-    def swapped():
-        for copy in swaps:
-            copy.wait_recv()
-        for u in range(2):
-            place_fc2(u, 1 - i_c, got[u].astype(F32))
-        place_proj(1 - i_c, got_p[...].astype(F32))
-
-    def add(k, part):
-        loads[k, part].wait()
-        from_core[k, part].wait_recv()
-        at = part_rows(part)
-        keep[k, at, :] = (keep[k, at, :].astype(F32) + came[k, at, :].astype(F32)).astype(BF)
-
-    collect()
+            value = dx_ring[slot, q]
+            term = dot(value, w[:, q * lanes : (q + 1) * lanes], NT)
+            total = term if total is None else total + term
+            lane_sums[q : q + 1, :] += jnp.sum(value.astype(F32), 0, keepdims=True)
+        sums[0:1, :] += jnp.sum(total * normal, 0, keepdims=True)
+        sums[1:2, :] += jnp.sum(total, 0, keepdims=True)
+        if b:
+            away[k] = total.astype(BF)
+            from_core[k] = link(away.at[k], came.at[k], core)
+        else:
+            keep[k] = total.astype(BF)
+        load(n + 2)
+
     from_pair = {}
-    for n, k in enumerate(order):
-        if n == len(order) // 2:
-            vec_over_chips()
-        for part in range(split):
-            add(k, part)
-            bit_p = k % np_
-            if bit_p:
+
+    def over_cores(slots):
+        for k in slots:
+            from_core[k].wait_recv()
+            for part in range(split):
                 at = part_rows(part)
-                dst = pair.at[k // np_, bit_p, at]
-                from_pair[k // np_, bit_p, part] = link(keep.at[k, at], dst, {"p": i_p ^ bit_p})
+                keep[k, at, :] = (keep[k, at, :].astype(F32) + came[k, at, :].astype(F32)).astype(BF)
+                if k % np_:
+                    dst = pair.at[k // np_, k % np_, at]
+                    from_pair[k // np_, k % np_, part] = link(keep.at[k, at], dst, {"p": i_p ^ (k % np_)})
 
     def over_pair(bit_g, part):
         at = part_rows(part)
@@ -820,37 +723,122 @@
             value = value + pair[bit_g, bit_p, at, :].astype(F32)
         return value
 
+    half = len(far_slots) * 2
+    for n in range(half):
+        rows(n)
+
+    part_lanes = parts_a[0].shape[1]
+    for z in range(chips):
+        proj_out[z] = proj_in[:, z * part_lanes : (z + 1) * part_lanes]
+    from_chip = [link(proj_out.at[z_of(k)], proj_got.at[k], chip_peer(k)) for k in range(1, chips)]
+    over_cores(far_slots)
+
+    for copy in whole_loads:
+        copy.wait()
+    for j in range(dp):
+        for q in range(pieces):
+            slab_out[j, q] = dot(norm_all[:, j * shard : (j + 1) * shard], dx_all[q], TN).astype(BF)
+    from_dp = [link(slab_out.at[i_dp ^ bit], slabs.at[bit], {"dp": i_dp ^ bit}) for bit in range(1, dp)]
+
     from_far = {}
     for part in range(split):
         at = part_rows(part)
         for bit_g in range(1, ng):
             pair[bit_g, 0, at, :] = over_pair(bit_g, part).astype(BF)
             from_far[bit_g, part] = link(pair.at[bit_g, 0, at], far.at[bit_g, at], {"g": i_g ^ bit_g})
-
-    def arrived(image, at, value):
-        grad, _ = norm_back(inputs[image, at, :].astype(F32), gain[...], value)
-        home[image, at, :] = (grad_mid[image, at, :] + grad).astype(BF)
-
-    for copy in own_slab:
-        copy.wait()
+    for n in range(half, len(jobs)):
+        rows(n)
+
+    vec[...] = jnp.zeros_like(vec)
+    vec[0:2, :] = sums[0:2, :]
+    vec[4:12, :] = early[...]
+    for p in range(np_):
+        for c in range(2):
+
+            @pl.when((i_p == p) & (i_c == c))
+            def _(p=p, c=c):
+                for q in range(pieces):
+                    at = (p * pieces + q) * shard + c * part_w
+                    vec[2:3, at : at + part_w] = lane_sums[q : q + 1, 0:part_w]
+                    vec[3:4, at : at + part_w] = lane_sums[q : q + 1, 2 * part_w : 3 * part_w]
+
+    table = tables[0][...]
+    for ref in tables[1:]:
+        table = table + ref[...]
+    tab[...] = table
+    tab_rows = tab.shape[0] // dp
+    tab_at = lambda j: pl.ds(pl.multiple_of(j * tab_rows, 8), tab_rows)
+    for j in range(dp):
+        vec_out[j] = vec[:, j * shard : (j + 1) * shard]
+    vec_dp[i_dp] = vec_out[i_dp]
+    tab_dp[i_dp] = tab[tab_at(i_dp), :]
+    small = []
+    for bit in range(1, dp):
+        small.append(link(vec_out.at[i_dp ^ bit], vec_dp.at[i_dp], {"dp": i_dp ^ bit}))
+        small.append(link(tab.at[tab_at(i_dp ^ bit)], tab_dp.at[i_dp], {"dp": i_dp ^ bit}))
+
+    def sum_of(ref, n):
+        value = ref[0]
+        for i in range(1, n):
+            value = value + ref[i]
+        return value
+
+    over_cores(near_slots)
+    for copy in small:
+        copy.wait_recv()
+    vec_z[i_z] = sum_of(vec_dp, dp)
+    tab_z[i_z] = sum_of(tab_dp, dp)
+    small = []
+    for k in range(1, chips):
+        small.append(link(vec_z.at[i_z], vec_z.at[i_z], chip_peer(k)))
+        small.append(link(tab_z.at[i_z], tab_z.at[i_z], chip_peer(k)))
+
+    hidden_rows = give.shape[1]
+    per_rows = part_lanes
+    swaps = []
+
+    def halves(value, there):
+        cols = value.shape[1] // 2
+        mine = jnp.where(i_c == 0, value[:, :cols], value[:, cols:])
+        there[...] = jnp.where(i_c == 0, value[:, cols:], value[:, :cols]).astype(BF)
+        return mine
+
+    def place_fc2(u, c, value):
+        for b in range(hidden_rows // per_rows):
+            start = ((b * 2 + c) * 2 + u) * per_rows
+            out_fc2[pl.ds(pl.multiple_of(start, 8), per_rows), :] = value[b * per_rows : (b + 1) * per_rows, :]
+
+    def place_proj(c, value):
+        out_proj[pl.ds(pl.multiple_of(c * value.shape[0], 8), value.shape[0]), :] = value
+
+    for u, parts in ((0, parts_a), (1, parts_b)):
+        value = parts[0][...].astype(F32)
+        for ref in parts[1:]:
+            value = value + ref[...].astype(F32)
+        out_fc1[:, u * per_rows : (u + 1) * per_rows] = value[0:shard]
+        place_fc2(u, i_c, halves(value[shard:], give.at[u]))
+        swaps.append(link(give.at[u], got.at[u], core))
+    value = proj_out[i_z].astype(F32)
+    for k in range(1, chips):
+        from_chip[k - 1].wait_recv()
+        value = value + proj_got[k].astype(F32)
+    place_proj(i_c, halves(value, give_p))
+    swaps.append(link(give_p, got_p, core))
+
     for copy in from_dp:
         copy.wait_recv()
-    width = part_w * 3
-    shard_lanes = grads[0].shape[0] // dp
-    group_lanes = part_w
-    cell_n = 0
-    waits = []
+    sent_cells = []
     for q in range(pieces):
-        value = slabs[0, q].astype(F32)
+        value = slab_out[i_dp, q].astype(F32)
         for bit in range(1, dp):
             value = value + slabs[bit, q].astype(F32)
         value = value.astype(BF)
         for t in range(3):
             for u in range(part_w // cell):
+                n = len(sent_cells)
                 lane = t * part_w + u * cell
-                cells[cell_n] = value[:, lane : lane + cell]
-                start = (i_p * pieces + q) * (shard_lanes // cell) + i_c * (part_w // cell) + u
-                unit = t * (dp * (shard_lanes // cell)) + start
+                cells[n] = value[:, lane : lane + cell]
+                unit = (t * width + (i_p * pieces + q) * shard + i_c * part_w) // cell + u
                 owner = unit // 3
                 slot = unit % 3
                 dst = taken.at[i_g, slot]
@@ -859,30 +847,43 @@
                 o_g = owner // (2 * np_)
 
                 @pl.when(owner == i_s)
-                def _(cell_n=cell_n, dst=dst, slot=slot):
-                    pltpu.make_async_copy(cells.at[cell_n], dst, cell_recv.at[i_g * 3 + slot]).start()
+                def _(n=n, dst=dst, slot=slot):
+                    pltpu.make_async_copy(cells.at[n], dst, cell_recv.at[i_g * 3 + slot]).start()
 
                 @pl.when(owner != i_s)
-                def _(cell_n=cell_n, dst=dst, slot=slot, o_g=o_g, o_p=o_p, o_c=o_c):
+                def _(n=n, dst=dst, slot=slot, o_g=o_g, o_p=o_p, o_c=o_c):
                     pltpu.make_async_remote_copy(
-                        src_ref=cells.at[cell_n],
+                        src_ref=cells.at[n],
                         dst_ref=dst,
-                        send_sem=cell_send.at[cell_n],
+                        send_sem=cell_send.at[n],
                         recv_sem=cell_recv.at[i_g * 3 + slot],
                         device_id={"g": o_g, "p": o_p, "c": o_c},
                         device_id_type=pl.DeviceIdType.MESH,
                     ).start()
 
-                waits.append((cell_n, owner))
-                cell_n += 1
+                sent_cells.append(owner)
+
+    def arrived(image, at, value):
+        grad, _ = norm_back(inputs[image, at, :].astype(F32), gain[...], value)
+        home[image, at, :] = (grad_mid[image, at, :] + grad).astype(BF)
+
     for part in range(split):
         arrived(i_g, part_rows(part), over_pair(0, part))
-
-    vec_over_cores()
-    swapped()
-    vec_late[-1].wait_recv()
-    total[...] = sum_of(by_core, 2)
-
+    for copy in small:
+        copy.wait_recv()
+    vec_c[i_c] = sum_of(vec_z, chips)
+    tab_c[i_c] = sum_of(tab_z, chips)
+    small = [link(vec_c.at[i_c], vec_c.at[i_c], core), link(tab_c.at[i_c], tab_c.at[i_c], core)]
+    for copy in swaps:
+        copy.wait_recv()
+    for u in range(2):
+        place_fc2(u, 1 - i_c, got[u].astype(F32))
+    place_proj(1 - i_c, got_p[...].astype(F32))
+    for copy in small:
+        copy.wait_recv()
+    out_vec[...] = sum_of(vec_c, 2)
+    tab_all[i_dp] = sum_of(tab_c, 2)
+    small = [link(tab_all.at[i_dp], tab_all.at[i_dp], {"dp": i_dp ^ bit}) for bit in range(1, dp)]
     for part in range(split):
         at = part_rows(part)
         for bit_g in range(1, ng):
@@ -895,69 +896,93 @@
             term = taken[g, slot].astype(F32)
             value = term if value is None else value + term
         owned[:, slot * cell : (slot + 1) * cell] = value
-    for cell_n, owner in waits:
+    for copy in small:
+        copy.wait_recv()
+    for j in range(dp):
+        out_tab[j * tab_rows : (j + 1) * tab_rows, :] = tab_all[j]
+    for n, owner in enumerate(sent_cells):
 
         @pl.when(owner != i_s)
-        def _(cell_n=cell_n):
-            pltpu.make_async_copy(cells.at[cell_n], cells.at[cell_n], cell_send.at[cell_n]).wait()
+        def _(n=n):
+            pltpu.make_async_copy(cells.at[n], cells.at[n], cell_send.at[n]).wait()
 
     link.drain()
 
 
-def finish(rows_in, vec, vec_block, inputs, grad_mid, gain, grads, parts, sizes, part_w, split=3):
+def finish(raw, normed, dx, tables, w, inputs, grad_mid, gain, early, proj_in, parts, sizes, part_w, split=3):
     count = inputs.shape[1]
     dp, ng, np_ = sizes
     chips = ng * np_
-    pieces = len(grads)
-    width = rows_in.shape[1]
-    shard = grads[0].shape[0] // dp
+    pieces = len(dx)
+    seq_len, width = raw.shape
+    lanes = dx[0].shape[1]
+    shard = width // dp
     cell = width // (chips * 2)
     total_cells = pieces * 3 * (part_w // cell)
-    parts_a, parts_b, parts_p = parts
-    lanes = parts_a[0].shape[1]
+    parts_a, parts_b = parts
+    part_lanes = parts_a[0].shape[1]
     hidden_rows = parts_a[0].shape[0] - shard
-    piece_rows = parts_p[0].shape[0]
-    own_vec = vec.shape[0] - (dp - 1) * vec_block
-    copies = split * (chips + ng * (np_ - 1) + ng - 1) + (dp - 1) * pieces + 2 * (dp - 1) + chips + 3
+    piece_rows = proj_in.shape[0]
+    copies = chips + split * (ng * (np_ - 1) + ng - 1) + (chips - 1) + (dp - 1) * 4 + 2 * (chips - 1) + 5
     hbm = pl.BlockSpec(memory_space=pl.ANY)
     vmem = pl.BlockSpec(memory_space=pltpu.VMEM)
+    table = tables[0].shape
+    block = (table[0] // dp, table[1])
     return pl.pallas_call(
-        partial(finish_kernel, sizes, split, pieces, part_w, vec_block),
-        in_specs=[hbm] + [vmem] * 4 + [hbm] * pieces + [vmem] * (3 * chips),
-        out_specs=[vmem] * 6,
+        partial(finish_kernel, sizes, split, pieces, part_w),
+        in_specs=[hbm] * (2 + pieces) + [vmem] * (pieces + 6 + 2 * chips),
+        out_specs=[vmem] * 7,
         out_shape=[
             jax.ShapeDtypeStruct((ng, count, width), BF),
             jax.ShapeDtypeStruct((shard, 3 * cell), F32),
-            jax.ShapeDtypeStruct((own_vec, 128), F32),
-            jax.ShapeDtypeStruct((shard, 2 * lanes), F32),
-            jax.ShapeDtypeStruct((4 * hidden_rows, lanes // 2), F32),
-            jax.ShapeDtypeStruct((2 * piece_rows, lanes // 2), F32),
+            jax.ShapeDtypeStruct((16, shard), F32),
+            jax.ShapeDtypeStruct(table, F32),
+            jax.ShapeDtypeStruct((shard, 2 * part_lanes), F32),
+            jax.ShapeDtypeStruct((4 * hidden_rows, part_lanes // 2), F32),
+            jax.ShapeDtypeStruct((2 * piece_rows, part_lanes // 2), F32),
         ],
         scratch_shapes=[
+            pltpu.VMEM((pieces, seq_len, lanes), BF),
+            pltpu.VMEM((seq_len, width), BF),
+            pltpu.VMEM((2, pieces, count, lanes), BF),
+            pltpu.VMEM((2, count, width), BF),
+            pltpu.VMEM((chips, count, width), BF),
             pltpu.VMEM((chips, count, width), BF),
             pltpu.VMEM((chips, count, width), BF),
             pltpu.VMEM((ng, np_, count, width), BF),
             pltpu.VMEM((ng, count, width), BF),
-            pltpu.VMEM((dp, pieces, shard, 3 * part_w), BF),
+            pltpu.VMEM((dp, pieces, shard, lanes), BF),
+            pltpu.VMEM((dp, pieces, shard, lanes), BF),
             pltpu.VMEM((total_cells, shard, cell), BF),
             pltpu.VMEM((ng, 3, shard, cell), BF),
-            pltpu.VMEM((dp, own_vec, 128), F32),
-            pltpu.VMEM((chips, own_vec, 128), F32),
-            pltpu.VMEM((2, own_vec, 128), F32),
-            pltpu.VMEM((2, hidden_rows, lanes // 2), BF),
-            pltpu.VMEM((2, hidden_rows, lanes // 2), BF),
-            pltpu.VMEM((piece_rows, lanes // 2), BF),
-            pltpu.VMEM((piece_rows, lanes // 2), BF),
-            pltpu.SemaphoreType.DMA((split * chips + pieces,)),
+            pltpu.VMEM((8, width), F32),
+            pltpu.VMEM((8, lanes), F32),
+            pltpu.VMEM((16, width), F32),
+            pltpu.VMEM((dp, 16, shard), F32),
+            pltpu.VMEM((dp, 16, shard), F32),
+            pltpu.VMEM((chips, 16, shard), F32),
+            pltpu.VMEM((2, 16, shard), F32),
+            pltpu.VMEM(table, F32),
+            pltpu.VMEM((dp,) + block, F32),
+            pltpu.VMEM((chips,) + block, F32),
+            pltpu.VMEM((2,) + block, F32),
+            pltpu.VMEM((dp,) + block, F32),
+            pltpu.VMEM((2, hidden_rows, part_lanes // 2), BF),
+            pltpu.VMEM((2, hidden_rows, part_lanes // 2), BF),
+            pltpu.VMEM((piece_rows, part_lanes // 2), BF),
+            pltpu.VMEM((piece_rows, part_lanes // 2), BF),
+            pltpu.VMEM((chips, piece_rows, part_lanes), BF),
+            pltpu.VMEM((chips, piece_rows, part_lanes), BF),
+            pltpu.SemaphoreType.DMA((2 * (1 + pieces) + 1 + pieces,)),
             pltpu.SemaphoreType.DMA((copies,)),
             pltpu.SemaphoreType.DMA((copies,)),
             pltpu.SemaphoreType.DMA((total_cells,)),
             pltpu.SemaphoreType.DMA((3 * ng,)),
         ],
-        compiler_params=pltpu.CompilerParams(collective_id=1, has_side_effects=True, vmem_limit_bytes=56 << 20),
+        compiler_params=pltpu.CompilerParams(collective_id=1, has_side_effects=True, vmem_limit_bytes=63 << 20),
         cost_estimate=FREE,
         name="finish",
-    )(rows_in, vec, inputs, grad_mid, gain, *grads, *parts_a, *parts_b, *parts_p)
+    )(raw, normed, *dx, *tables, w, inputs, grad_mid, gain, early, proj_in, *parts_a, *parts_b)
 
 
 def places():
@@ -1342,7 +1367,7 @@
     grad_heads, sum_a = tie(grad_heads, sum_a)
     sum_a = pieces_over_chips(sum_a)
     dx = []
-    grad_tables = 0.0
+    grad_tables = []
     for q in range(pieces):
         rows, table = attend_back(
             q * core_heads, core_heads, query_a, key_rows, value_rows, att_f, grad_heads, tables, side
@@ -1354,49 +1379,34 @@
         elif q == 1:
             rows, *sum_b = tie(rows, *sum_b)
         dx.append(rows)
-        grad_tables = grad_tables + table
+        grad_tables.append(table)
     dx[-1], sum_p = tie(dx[-1], sum_p)
-    sum_p = pieces_over_chips(sum_p)
-
-    grad_rows, sums = rows_back(dx, raw, qkv_full)
-    grad_qkv = [lax.dot_general(normed, rows, TN, preferred_element_type=F32).astype(BF) for rows in dx]
-
-    def spread(part):
-        full = jnp.zeros((width,), F32)
-        for q in range(pieces):
-            block = sums[2 + q, part * piece : (part + 1) * piece]
-            full = lax.dynamic_update_slice_in_dim(full, block, starts[3 * q], 0)
-        return full
-
-    entries = rel_pos_h.shape[0]
-    rel = jnp.stack([grad_tables[:entries, :HD], grad_tables[128 : 128 + entries, :HD]])[:, ::-1]
+
     bias_half = jnp.stack([bias_a.reshape(dp, per, unit // 2), bias_b.reshape(dp, per, unit // 2)], 2)
     bias_half = bias_half.reshape(dp * per, 1, unit)
     bias_full = jnp.concatenate([bias_half] * nc, 1)
     core = lax.broadcasted_iota(jnp.int32, bias_full.shape, 1)
-    bias_full = jnp.where(core == i_c, bias_full, 0.0).reshape(dp, -1)
-    eight = jnp.concatenate([jnp.stack([sums[0], sums[1], spread(0), spread(2)]), early[:4]])
-    vectors = jnp.concatenate([eight.reshape(8, dp, shard).transpose(1, 0, 2).reshape(dp, -1), bias_full], 1)
-    block = -(-vectors.shape[1] // 1024) * 8
-    vectors = jnp.pad(vectors, ((0, 0), (0, block * 128 - vectors.shape[1])))
-    rel = rel.reshape(-1)
-    vectors = jnp.concatenate([vectors.reshape(-1), jnp.pad(rel, (0, -rel.shape[0] % 1024))]).reshape(-1, 128)
-    grad_patches, out_qkv, vectors, out_fc1, out_fc2, out_proj = finish(
-        grad_rows,
-        vectors,
-        block,
+    bias_full = jnp.where(core == i_c, bias_full, 0.0).reshape(dp, -1, shard)
+    early = jnp.concatenate([early[:4], bias_full.transpose(1, 0, 2).reshape(-1, width)])
+    grad_patches, out_qkv, vec, rel, out_fc1, out_fc2, out_proj = finish(
+        raw,
+        normed,
+        dx,
+        grad_tables,
+        qkv_full,
         patches,
         grad_middle,
         gain_one[None],
-        grad_qkv,
-        (sum_a, sum_b, sum_p),
+        early,
+        sum_p,
+        (sum_a, sum_b),
         sizes,
         piece,
     )
-    rel = vectors[block:].reshape(-1)[: 2 * entries * HD].reshape(2, entries, HD)
-    flat = vectors[:block].reshape(-1)
-    vec = [flat[n * shard : (n + 1) * shard] for n in range(8)]
-    fc1_vec = flat[8 * shard : 8 * shard + hidden // dp]
+    entries = rel_pos_h.shape[0]
+    rel = [rel[:entries, :HD][::-1], rel[128 : 128 + entries, :HD][::-1]]
+    fc1_vec = vec[8:12].reshape(-1)
+
     return (
         output,
         grad_patches,

time: 590 us -> 550 us (0.932)
  matrix products: 13.1 us -> 0 us
  Pallas kernels: 458 us -> 446 us
  local copies, waits for them, and re-layouts: 57.7 us -> 48.2 us
    dot_general x2 -> x0, matrix products: 13.1 us -> none  [on_device(): lax.dot_general(normed, rows, TN, preferred_element_type=F32).astype(BF)]
    pallas_call x1, Pallas kernels: 30.9 us -> 21.9 us  [middle_rows(): pl.pallas_call(partial(middle_kernel, sizes), in_specs=[pl.BlockSpec(memo...]
    ppermute x12 -> x9, waiting for transfers between devices: 13.6 us -> 17.7 us  [flip(): return lax.ppermute(value, axis, [(i, i ^ bit) for i in range(size)])]
    ppermute x12 -> x9, starting transfers between devices: 19.9 us -> 15.9 us  [flip(): return lax.ppermute(value, axis, [(i, i ^ bit) for i in range(size)])]
    pallas_call x2 -> x1, Pallas kernels: 96.1 us -> 93.1 us  [finish(): pl.pallas_call(partial(finish_kernel, sizes, split, pieces, part_w), in_s...]
    unnamed x87 -> x70, local copies, waits for them, and re-layouts: 21 us -> 21 us
  transfers between devices with their start and end apart: 17 -> 14, of which waited for: 3 -> 1; matrix products, arithmetic and copies ran while one was open for 6% -> 5% of each run, Pallas kernels for 62% -> 64%
where the time goes in v5:
time: 550 us; the launch traced here: 546 us
  Pallas kernels  446 us (81%)
  local copies, waits for them, and re-layouts  48.2 us (9%)
  waiting for transfers between devices  18.5 us (3%)
  starting transfers between devices  16.3 us (3%)
  between operations  14.6 us (3%)
    pallas_call x2, Pallas kernels, attend_back(): pl.pallas_call(partial(attend_back_kernel, count, first, side, uc), grid=...  95 us
    pallas_call x1, Pallas kernels, finish(): pl.pallas_call(partial(finish_kernel, sizes, split, pieces, part_w), in_s...  93.1 us
    pallas_call x2, Pallas kernels, mlp_half(): pl.pallas_call(partial(mlp_kernel, bool(old), per), grid=(steps + dp,), i...  67.7 us
    pallas_call x1, Pallas kernels, start_exchange(): pl.pallas_call(partial(start_kernel, sizes, split), in_specs=[hbm] * 3, o...  58.6 us
    pallas_call x1, Pallas kernels, turn(): pl.pallas_call(partial(turn_kernel, sizes), in_specs=[vmem, hbm, hbm] + [...  48.9 us
    pallas_call x2, Pallas kernels, attend(): pl.pallas_call(partial(attend_kernel, heads, side, bool(old), sub), grid_...  39.5 us
    pallas_call x1, Pallas kernels, middle_rows(): pl.pallas_call(partial(middle_kernel, sizes), in_specs=[pl.BlockSpec(memo...  21.9 us
    unnamed x70, local copies, waits for them, and re-layouts  21 us
  transfers between devices with their start and end apart: 14, of which 1 were waited for; matrix products, arithmetic and copies ran while one was open for 5% of the time, Pallas kernels for 64%

profile of v5, /device:TPU:0, one launch (start us, length us, event | category | flops | bytes accessed | tf_op | source)
XLA Modules:
  0.0 545.9 jit_solution(17304457853760300464)
XLA Ops:
  7.3 1.9 copy-done.1
  9.2 1.9 copy-done.2
  11.2 1.7 copy-done.3
  12.9 1.1 copy-done.5
  14.0 3.2 select.11
  17.2 0.8 copy-done.6
  18.2 0.7 all-gather.7.cloned.1.call-update
  19.0 0.5 collective-permute-start.2
  19.7 1.2 concatenate.17.vec
  20.9 58.6 %start_exchange.1 = (bf16[2304,1280]{1,0:T(8,128)(2,1)}, bf16[4,320,960]{2,1,0:T(8,128)(2,1)}, bf16[4,10,320]{2,1,0:T(8,128)(2,1)}) custom-call(bf16[2,288,1280]{2,1,0:T(8,128)(2,1)} %refs_7_.1, bf16[320,960]{1,0:T(8,128)(2,1)} %copy-done.6, bf16[10,320]{1,0:T(8,128)(2,1)} %concatenate.17.vec), custom_call_target="tpu_custom_call" | custom-call | flops 1 | bytes 1 | tf_op jit(solution)/shard_map/start_exchange/pallas_call | solution.py:574
  79.9 0.8 fusion.5
  80.9 0.7 unstack.43.gain.refs_9_
  81.6 0.7 unstack.45.shift
  82.5 0.7 concatenate.18
  83.2 0.6 fusion.2.tables
  83.8 18.3 %qkv_rows.1 = (bf16[2304,1280]{1,0:T(8,128)(2,1)}, bf16[4,2304,256]{2,1,0:T(8,128)(2,1)}, bf16[4,2304,256]{2,1,0:T(8,128)(2,1)}, bf16[4,2304,128]{2,1,0:T(8,128)(2,1)}) custom-call(bf16[2304,1280]{1,0:T(8,128)(2,1)} %get-tuple-element.81.raw.refs_0_, f32[1,1280]{1,0:T(1,128)} %unstack.43.gain.refs_9_, f32[1,1280]{1,0:T(1,128)} %unstack.45.shift, ...), custom_call_target="tpu_custom_call" | custom-call | flops 1 | bytes 1 | tf_op jit(solution)/shard_map/qkv_rows/pallas_call | solution.py:94
  102.1 19.6 %attend.2 = (bf16[1152,320]{1,0:T(8,128)(2,1)}, f32[2304,320]{1,0:T(8,128)}, bf16[4,2304,256]{2,1,0:T(8,128)(2,1)}) custom-call(s32[1]{0:T(128)} %bitcast.9.at, bf16[4,2304,256]{2,1,0:T(8,128)(2,1)} %get-tuple-element.84.qa, bf16[4,2304,256]{2,1,0:T(8,128)(2,1)} %get-tuple-element.114.kp, bf16[4,2304,128]{2,1,0:T(8,128)(2,1)} %get-tuple-element.86.vp), custom_call_target="tpu_custom_call" | custom-call | flops 20000000000 | bytes 1 | tf_op jit(solution)/shard_map/attend/pallas_call | solution.py:169
  121.7 2.1 dynamic-slice_bitcast_fusion
  123.8 2.2 collective-permute-start.1
  126.0 1.0 collective-permute-start
  127.0 19.9 %attend.3 = (bf16[1152,320]{1,0:T(8,128)(2,1)}, f32[2304,320]{1,0:T(8,128)}, bf16[4,2304,256]{2,1,0:T(8,128)(2,1)}) custom-call(s32[1]{0:T(128)} %bitcast.2.at, bf16[4,2304,256]{2,1,0:T(8,128)(2,1)} %get-tuple-element.84.qa, bf16[4,2304,256]{2,1,0:T(8,128)(2,1)} %get-tuple-element.114.kp, ...), custom_call_target="tpu_custom_call", output_to_operand_aliasing={{1}: (4, {}), {2}: (5, {})} | custom-call | flops 20000000000 | bytes 1 | tf_op jit(solution)/shard_map/attend/pallas_call | solution.py:169
  147.0 0.7 squeeze.67.b1
  147.9 17.7 %collective-permute-done.refs_0_ = bf16[576,320]{1,0:T(8,128)(2,1)S(1)} collective-permute-done((bf16[576,320]{1,0:T(8,128)(2,1)}, bf16[576,320]{1,0:T(8,128)(2,1)S(1)}, u32[]{:S(2)}, u32[]{:S(2)}) %collective-permute-start) | collective-permute-done | bytes 368672 | tf_op jit(solution)/shard_map/ppermute | solution.py:1214
  165.6 3.2 slice.84
  168.8 21.9 %middle_rows.1 = (f32[2,288,1280]{2,1,0:T(8,128)}, bf16[2,288,1280]{2,1,0:T(8,128)(2,1)S(1)}, bf16[2,288,1280]{2,1,0:T(8,128)(2,1)S(1)}, bf16[2,2,2,288,320]{4,3,2,1,0:T(8,128)(2,1)}) custom-call(bf16[2,576,320]{2,1,0:T(8,128)(2,1)S(1)} %bitcast.43, bf16[576,320]{1,0:T(8,128)(2,1)S(1)} %collective-permute-done.refs_0_, ...), custom_call_target="tpu_custom_call" | custom-call | flops 1 | bytes 1 | tf_op jit(solution)/shard_map/middle_rows/pallas_call | solution.py:1056
  190.8 1.1 copy-done.8
  191.9 1.1 copy-done.9
  193.0 32.9 %mlp_half.2 = (f32[1152,1280]{1,0:T(8,128)}, f32[1152,1280]{1,0:T(8,128)}, bf16[4,640,1280]{2,1,0:T(8,128)(2,1)}, f32[1,1280]{1,0:T(1,128)}) custom-call(bf16[576,1280]{1,0:T(8,128)(2,1)} %bitcast.44, bf16[576,1280]{1,0:T(8,128)(2,1)} %bitcast.46, bf16[576,1280]{1,0:T(8,128)(2,1)} %bitcast.18.g_own, bf16[576,1280]{1,0:T(8,128)(2,1)} %collective-permute-done.2.g_other, ...), custom_call_target="tpu_custom_call" | custom-call | flops 35000000512 | bytes 1 | tf_op jit(solution)/shard_map/mlp_half/pallas_call | solution.py:392
  225.9 0.7 squeeze.66.b1
  226.6 34.8 %mlp_half.3 = (f32[1152,1280]{1,0:T(8,128)}, f32[1152,1280]{1,0:T(8,128)}, bf16[4,640,1280]{2,1,0:T(8,128)(2,1)}, f32[1,1280]{1,0:T(1,128)}) custom-call(bf16[576,1280]{1,0:T(8,128)(2,1)} %bitcast.45, bf16[576,1280]{1,0:T(8,128)(2,1)} %bitcast.47, bf16[576,1280]{1,0:T(8,128)(2,1)} %bitcast.18.g_own, ...), custom_call_target="tpu_custom_call", output_to_operand_aliasing={{0}: (7, {}), {1}: (8, {})} | custom-call | flops 35000000512 | bytes 1 | tf_op jit(solution)/shard_map/mlp_half/pallas_call | solution.py:392
  261.9 0.7 unstack.57.shift
  262.6 48.9 %turn.1 = (bf16[2,288,1280]{2,1,0:T(8,128)(2,1)}, f32[2,288,1280]{2,1,0:T(8,128)}, bf16[2304,320]{1,0:T(8,128)(2,1)}, bf16[2,320,1280]{2,1,0:T(8,128)(2,1)}, f32[8,1280]{1,0:T(8,128)}) custom-call(f32[2,288,1280]{2,1,0:T(8,128)} %get-tuple-element.95.mid, f32[1152,1280]{1,0:T(8,128)} %get-tuple-element.101.gn, f32[1152,1280]{1,0:T(8,128)} %get-tuple-element.102.out, ...), custom_call_target="tpu_custom_call" | custom-call | flops 1 | bytes 1 | tf_op jit(solution)/shard_map/turn/pallas_call | solution.py:1184
  312.1 0.8 slice.72
  312.9 0.6 pad_maximum_fusion.refs_10_
  313.5 3.4 copy.85
  317.1 0.3 copy.70
  317.4 0.3 copy.69
  317.7 0.3 copy.68
  318.0 5.3 collective-permute-start.3
  323.3 2.4 collective-permute-start.5
  325.7 47.2 %attend_back.2 = (bf16[2304,480]{1,0:T(8,128)(2,1)}, f32[256,128]{1,0:T(8,128)}) custom-call(bf16[4,2304,256]{2,1,0:T(8,128)(2,1)} %get-tuple-element.106.qa_ref, bf16[4,2304,256]{2,1,0:T(8,128)(2,1)} %get-tuple-element.114.kp, bf16[4,2304,128]{2,1,0:T(8,128)(2,1)} %get-tuple-element.86.vp, f32[2304,320]{1,0:T(8,128)} %get-tuple-element.107.of, ...), custom_call_target="tpu_custom_call" | custom-call | flops 49999998976 | bytes 1 | tf_op jit(solution)/shard_map/attend_back/pallas_call | solution.py:303
  372.9 1.0 copy.67
  373.9 2.8 copy.87
  377.3 0.3 copy.74
  377.5 0.3 copy.73
  377.8 1.1 collective-permute-start.6
  378.9 0.8 collective-permute-start.7
  379.7 2.5 collective-permute-start.8
  382.3 47.8 %attend_back.3 = (bf16[2304,480]{1,0:T(8,128)(2,1)}, f32[256,128]{1,0:T(8,128)}) custom-call(bf16[4,2304,256]{2,1,0:T(8,128)(2,1)} %get-tuple-element.106.qa_ref, bf16[4,2304,256]{2,1,0:T(8,128)(2,1)} %get-tuple-element.114.kp, bf16[4,2304,128]{2,1,0:T(8,128)(2,1)} %get-tuple-element.86.vp, f32[2304,320]{1,0:T(8,128)} %get-tuple-element.107.of, ...), custom_call_target="tpu_custom_call" | custom-call | flops 49999998976 | bytes 1 | tf_op jit(solution)/shard_map/attend_back/pallas_call | solution.py:303
  430.1 1.0 copy.72
  431.1 0.9 copy-done.16
  432.2 93.1 %finish.1 = (bf16[2,288,1280]{2,1,0:T(8,128)(2,1)}, f32[320,480]{1,0:T(8,128)}, f32[16,320]{1,0:T(8,128)}, f32[256,128]{1,0:T(8,128)}, f32[320,640]{1,0:T(8,128)...) custom-call(bf16[2304,1280]{1,0:T(8,128)(2,1)} %get-tuple-element.81.raw.refs_0_, ...), custom_call_target="tpu_custom_call" | custom-call | flops 1 | bytes 1 | tf_op jit(solution)/shard_map/finish/pallas_call | solution.py:931
  525.3 0.8 slice.80
  526.1 1.6 slice_reduce_fusion.10
  527.7 0.7 reshape.130
  528.4 0.8 fusion.4
  529.3 0.7 copy.83
  530.0 0.7 copy.82
  530.7 1.8 copy.80
  532.5 2.7 copy.81
  535.2 1.1 copy.96
  536.3 1.1 copy.97
  537.5 0.8 copy.98
  538.3 0.9 copy.99
  (120 shorter events, 3.5 us)
Async XLA Ops:
  7.2 158.4 %all-gather.5.cloned.1.call-start = ((), (), s32[]{:S(2)}) async-start(), calls=%async_computation.4 | async-start | bytes 10240000 | tf_op jit(solution)/shard_map/all_gather | solution.py:1292
  7.3 1.9 copy-start.1
  9.2 1.9 copy-start.2
  11.2 1.7 copy-start.3
  12.9 1.1 copy-start.5
  17.2 0.8 copy-start.6
  18.0 1.4 copy-start.22
  18.0 1.4 copy-start.23
  18.0 1.4 copy-start.24
  18.0 1.4 copy-start.25
  18.1 1.5 copy-start.26
  18.1 1.5 copy-start.27
  18.1 1.5 copy-start.28
  18.1 1.5 copy-start.29
  18.1 1.5 copy-start.21
  18.1 61.4 %copy-start.17 = (bf16[95,80]{0,1:T(8,128)(2,1)S(1)}, bf16[95,80]{0,1:T(8,128)(2,1)}, u32[]{:S(2)}) copy-start(bf16[95,80]{0,1:T(8,128)(2,1)} %param.31) | copy-start | bytes 45604
  18.1 61.6 %copy-start.18 = (bf16[95,80]{0,1:T(8,128)(2,1)S(1)}, bf16[95,80]{0,1:T(8,128)(2,1)}, u32[]{:S(2)}) copy-start(bf16[95,80]{0,1:T(8,128)(2,1)} %param.32) | copy-start | bytes 45604
  18.2 208.4 %all-gather.7.cloned.1.call-start = ((), (), s32[]{:S(2)}) async-start(), calls=%async_computation.5 | async-start | bytes 8192000 | tf_op jit(solution)/shard_map/all_gather | solution.py:1293
  18.9 294.6 %reduce-scatter.10.cloned.1.call-start = ((), (), s32[]{:S(2)}) async-start(), calls=%async_computation.6 | async-start | bytes 8192000
  19.0 174.0 %collective-permute-start.2 = (bf16[576,1280]{1,0:T(8,128)(2,1)}, bf16[576,1280]{1,0:T(8,128)(2,1)}, u32[]{:S(2)}, u32[]{:S(2)}) collective-permute-start(bf16[576,1280]{1,0:T(8,128)(2,1)} %bitcast.18.g_own), channel_id=1, source_target_pairs={{0,1},{1,0},{2,3},{3,2},{4,5},{5,4},{6,7},{7,6},{8,9},{9,8},{10,11... | collective-permute-start | bytes 4423688 | tf_op jit(solution)/shard_map/ppermute | solution.py:1214
  123.8 24.1 %collective-permute-start.1 = (bf16[576,320]{1,0:T(8,128)(2,1)}, bf16[576,320]{1,0:T(8,128)(2,1)S(1)}, u32[]{:S(2)}, u32[]{:S(2)}) collective-permute-start(bf16[576,320]{1,0:T(8,128)(2,1)} %get-tuple-element.220), channel_id=1, source_target_pairs={{0,6},{2,4},{4,2},{6,0},{1,7},{3,5},{5,3},{7,1},{8,14},{10,12},{12... | collective-permute-start | bytes 1105928 | tf_op jit(solution)/shard_map/ppermute | solution.py:1214
  126.0 39.6 %collective-permute-start = (bf16[576,320]{1,0:T(8,128)(2,1)}, bf16[576,320]{1,0:T(8,128)(2,1)S(1)}, u32[]{:S(2)}, u32[]{:S(2)}) collective-permute-start(bf16[576,320]{1,0:T(8,128)(2,1)} %get-tuple-element.221), channel_id=1, source_target_pairs={{0,4},{2,6},{4,0},{6,2},{1,5},{3,7},{5,1},{7,3},{8,12},{10,14},{12... | collective-permute-start | bytes 1105928 | tf_op jit(solution)/shard_map/ppermute | solution.py:1214
  146.9 21.9 %copy-start = (bf16[2,288,1280]{2,1,0:T(8,128)(2,1)S(1)}, bf16[2,288,1280]{2,1,0:T(8,128)(2,1)}, u32[]{:S(2)}) copy-start(bf16[2,288,1280]{2,1,0:T(8,128)(2,1)} %refs_7_.1) | copy-start | bytes 4423684
  146.9 21.9 %copy-start.4 = (bf16[1152,320]{1,0:T(8,128)(2,1)S(1)}, bf16[1152,320]{1,0:T(8,128)(2,1)}, u32[]{:S(2)}) copy-start(bf16[1152,320]{1,0:T(8,128)(2,1)} %get-tuple-element.91) | copy-start | bytes 2211844
  147.7 43.0 %copy-start.7 = (f32[1,1280]{1,0:T(1,128)}, f32[1,1280]{1,0:T(1,128)S(1)}, u32[]{:S(2)}) copy-start(f32[1,1280]{1,0:T(1,128)S(1)} %unstack.53.refs_5_.gain) | copy-start | bytes 15364
  190.8 1.1 copy-start.8
  191.9 1.1 copy-start.9
  225.9 148.1 %reduce-scatter.12.cloned.1.call-start = ((), (), s32[]{:S(2)}) async-start(), calls=%async_computation.7 | async-start | bytes 8192000
  261.4 170.5 %reduce-scatter.8.cloned.1.call-start = ((), (), s32[]{:S(2)}) async-start(), calls=%async_computation.3 | async-start | bytes 2048000 | tf_op jit(solution)/shard_map/reduce_scatter | solution.py:1347
  262.6 48.9 %copy-start.20 = (f32[1,1280]{1,0:T(1,128)S(1)}, f32[1,1280]{1,0:T(1,128)}, u32[]{:S(2)}) copy-start(f32[1,1280]{1,0:T(1,128)} %get-tuple-element.126) | copy-start | bytes 15364
  262.6 49.0 %copy-start.19 = (f32[1,1280]{1,0:T(1,128)S(1)}, f32[1,1280]{1,0:T(1,128)}, u32[]{:S(2)}) copy-start(f32[1,1280]{1,0:T(1,128)} %get-tuple-element.125) | copy-start | bytes 15364
  318.0 58.8 %collective-permute-start.3 = (bf16[640,320]{1,0:T(8,128)(2,1)S(1)}, bf16[640,320]{1,0:T(8,128)(2,1)}, u32[]{:S(2)}, u32[]{:S(2)}) collective-permute-start(bf16[640,320]{1,0:T(8,128)(2,1)S(1)} %bitcast.64), channel_id=1, source_target_pairs={{0,2},{2,0},{4,6},{6,4},{1,3},{3,1},{5,7},{7,5},{8,10},{10,8},{12,... | collective-permute-start | bytes 1228808 | tf_op jit(solution)/shard_map/ppermute | solution.py:1214
  323.3 53.5 %collective-permute-start.4 = (bf16[640,320]{1,0:T(8,128)(2,1)S(1)}, bf16[640,320]{1,0:T(8,128)(2,1)}, u32[]{:S(2)}, u32[]{:S(2)}) collective-permute-start(bf16[640,320]{1,0:T(8,128)(2,1)S(1)} %bitcast.62), channel_id=1, source_target_pairs={{0,4},{2,6},{4,0},{6,2},{1,5},{3,7},{5,1},{7,3},{8,12},{10,14},{12... | collective-permute-start | bytes 1228808 | tf_op jit(solution)/shard_map/ppermute | solution.py:1214
  323.3 53.5 %collective-permute-start.5 = (bf16[640,320]{1,0:T(8,128)(2,1)S(1)}, bf16[640,320]{1,0:T(8,128)(2,1)}, u32[]{:S(2)}, u32[]{:S(2)}) collective-permute-start(bf16[640,320]{1,0:T(8,128)(2,1)S(1)} %bitcast.60), channel_id=1, source_target_pairs={{0,6},{2,4},{4,2},{6,0},{1,7},{3,5},{5,3},{7,1},{8,14},{10,12},{12... | collective-permute-start | bytes 1228808 | tf_op jit(solution)/shard_map/ppermute | solution.py:1214
  377.8 53.3 %collective-permute-start.6 = (bf16[640,320]{1,0:T(8,128)(2,1)S(1)}, bf16[640,320]{1,0:T(8,128)(2,1)S(1)}, u32[]{:S(2)}, u32[]{:S(2)}) collective-permute-start(bf16[640,320]{1,0:T(8,128)(2,1)S(1)} %bitcast.65), channel_id=1, source_target_pairs={{0,2},{2,0},{4,6},{6,4},{1,3},{3,1},{5,7},{7,5},{8,10},{10,8},{12,... | collective-permute-start | bytes 1228808 | tf_op jit(solution)/shard_map/ppermute | solution.py:1214
  378.9 52.2 %collective-permute-start.7 = (bf16[640,320]{1,0:T(8,128)(2,1)S(1)}, bf16[640,320]{1,0:T(8,128)(2,1)S(1)}, u32[]{:S(2)}, u32[]{:S(2)}) collective-permute-start(bf16[640,320]{1,0:T(8,128)(2,1)S(1)} %bitcast.63), channel_id=1, source_target_pairs={{0,4},{2,6},{4,0},{6,2},{1,5},{3,7},{5,1},{7,3},{8,12},{10,14},{12... | collective-permute-start | bytes 1228808 | tf_op jit(solution)/shard_map/ppermute | solution.py:1214
  379.7 51.4 %collective-permute-start.8 = (bf16[640,320]{1,0:T(8,128)(2,1)S(1)}, bf16[640,320]{1,0:T(8,128)(2,1)S(1)}, u32[]{:S(2)}, u32[]{:S(2)}) collective-permute-start(bf16[640,320]{1,0:T(8,128)(2,1)S(1)} %bitcast.61), channel_id=1, source_target_pairs={{0,6},{2,4},{4,2},{6,0},{1,7},{3,5},{5,3},{7,1},{8,14},{10,12},{12... | collective-permute-start | bytes 1228808 | tf_op jit(solution)/shard_map/ppermute | solution.py:1214
  431.1 0.9 copy-start.14
  431.1 1.1 copy-start.15
  431.1 0.9 copy-start.16
  525.3 10.0 %copy-start.10 = (bf16[2,288,1280]{2,1,0:T(8,128)(2,1)S(1)}, bf16[2,288,1280]{2,1,0:T(8,128)(2,1)}, u32[]{:S(2)}) copy-start(bf16[2,288,1280]{2,1,0:T(8,128)(2,1)} %get-tuple-element.249) | copy-start | bytes 4423684
  532.5 3.8 copy-start.11
  535.2 2.2 copy-start.13
  536.3 2.0 copy-start.12
Sparse Core Ops, SparseCore 0:
  18.3 110.5 all-gather.4
  130.7 72.3 all-gather.6
  226.0 70.5 reduce-scatter.9
  299.5 72.3 reduce-scatter.11
  374.7 31.3 reduce-scatter.7

commit v6 on v5

--- a/solution.py
+++ b/solution.py
@@ -50,49 +50,59 @@
     return center * lax.rsqrt(spread + EPSILON)
 
 
-def qkv_kernel(pieces, group_heads, side, raw, gain, shift, w, bias, tables, normed, qa, kp, vp):
-    rows = raw.shape[0]
-    rows_n = (normal_rows(raw[...].astype(F32)) * gain[...] + shift[...]).astype(BF)
-    normed[...] = rows_n
-    joined = (dot(rows_n, w[...]) + bias[...]).astype(BF)
-    first_row = pl.program_id(0) * (rows // side)
-    lane = lax.broadcasted_iota(jnp.int32, (rows, 128), 1)
+def qkv_kernel(pieces, group_heads, side, sub, raw, gain, shift, w, bias, tables, normed, qa, kp, vp):
+    count = raw.shape[0] // sub
+    width = group_heads * HD
+    lane = lax.broadcasted_iota(jnp.int32, (sub, 128), 1)
     group_lane = lax.broadcasted_iota(jnp.int32, (side, 128), 1)
     group_row = lax.broadcasted_iota(jnp.int32, (side, 128), 0)
     col_hot = (group_lane == group_row) | ((group_lane >= side) & (group_lane < side + 3))
     col_hot = jnp.where(col_hot, 1.0, 0.0).astype(BF)
-    hot = []
-    for i in range(rows // side):
-        hot.append(jnp.where(group_lane == first_row + (HD + i), 1.0, 0.0).astype(BF))
-    row_hot = jnp.concatenate(hot, 0)
-    col_hot = jnp.concatenate([col_hot] * (rows // side), 0)
-    width = group_heads * HD
-    for n in range(pieces * group_heads):
-        q_at = (n // group_heads) * 3 * width + (n % group_heads) * HD
-        q = joined[:, q_at : q_at + HD]
-        g = dot(q, tables[...], NT) * math.sqrt(HD)
-        gh = []
-        gw = []
-        for i in range(rows // side):
-            part = g[i * side : (i + 1) * side]
-            gh.append(pltpu.roll(part[:, :128], first_row + (33 + i), axis=1))
-            gw.append(pltpu.roll(part[:, 128:], 81, axis=1, stride=1, stride_axis=0))
-        qa[n, :, 0:128] = jnp.concatenate(gh, 0).astype(BF)
-        qa[n, :, 0:HD] = q
-        qa[n, :, 128:256] = jnp.where(lane < side, jnp.concatenate(gw, 0), 0.0).astype(BF)
-        kp[n, :, 0:128] = row_hot
-        kp[n, :, 128:256] = col_hot
-        kp[n, :, 0:HD] = joined[:, q_at + width : q_at + width + HD]
-        vp[n] = jnp.ones((rows, 128), BF)
-        vp[n, :, 0:HD] = joined[:, q_at + 2 * width : q_at + 2 * width + HD]
-
-
-def qkv_rows(raw, gain, shift, w, bias, tables, pieces, group_heads, side, rows=384):
+    col_hot = jnp.concatenate([col_hot] * (sub // side), 0)
+
+    def product(n):
+        part = slice(n * sub, (n + 1) * sub)
+        rows_n = (normal_rows(raw[part, :].astype(F32)) * gain[...] + shift[...]).astype(BF)
+        normed[part, :] = rows_n
+        return (dot(rows_n, w[...]) + bias[...]).astype(BF)
+
+    ahead = product(0)
+    for m in range(count):
+        joined = ahead
+        if m + 1 < count:
+            ahead = product(m + 1)
+        part = slice(m * sub, (m + 1) * sub)
+        first_row = (pl.program_id(0) * count + m) * (sub // side)
+        hot = []
+        for i in range(sub // side):
+            hot.append(jnp.where(group_lane == first_row + (HD + i), 1.0, 0.0).astype(BF))
+        row_hot = jnp.concatenate(hot, 0)
+        for n in range(pieces * group_heads):
+            q_at = (n // group_heads) * 3 * width + (n % group_heads) * HD
+            q = joined[:, q_at : q_at + HD]
+            g = dot(q, tables[...], NT) * math.sqrt(HD)
+            gh = []
+            gw = []
+            for i in range(sub // side):
+                rows = g[i * side : (i + 1) * side]
+                gh.append(pltpu.roll(rows[:, :128], first_row + (33 + i), axis=1))
+                gw.append(pltpu.roll(rows[:, 128:], 81, axis=1, stride=1, stride_axis=0))
+            qa[n, part, 0:128] = jnp.concatenate(gh, 0).astype(BF)
+            qa[n, part, 0:HD] = q
+            qa[n, part, 128:256] = jnp.where(lane < side, jnp.concatenate(gw, 0), 0.0).astype(BF)
+            kp[n, part, 0:128] = row_hot
+            kp[n, part, 128:256] = col_hot
+            kp[n, part, 0:HD] = joined[:, q_at + width : q_at + width + HD]
+            vp[n, part, :] = jnp.ones((sub, 128), BF)
+            vp[n, part, 0:HD] = joined[:, q_at + 2 * width : q_at + 2 * width + HD]
+
+
+def qkv_rows(raw, gain, shift, w, bias, tables, pieces, group_heads, side, rows=384, sub=192):
     seq_len, width = raw.shape
     lanes = w.shape[1]
     heads = pieces * group_heads
     return pl.pallas_call(
-        partial(qkv_kernel, pieces, group_heads, side),
+        partial(qkv_kernel, pieces, group_heads, side, sub),
         grid=(seq_len // rows,),
         in_specs=[
             pl.BlockSpec((rows, width), lambda i: (i, 0)),
@@ -195,7 +205,7 @@
     )(jnp.stack([group]), qa, kp, vp, *old)
 
 
-def attend_back_kernel(heads, first, side, uc, qa_ref, kp, vp, of, go, tables, dx, gt, kt, dop, dk, dv, dq):
+def attend_back_kernel(heads, first, side, uc, qa_ref, kp, vp, of, go, tables, hot, dx, gt, kt, dop, dk, dv, dq):
     seq_len = kp.shape[1]
     tb = qa_ref.shape[1]
     h = pl.program_id(0)
@@ -208,26 +218,38 @@
     def _():
         gt[...] = jnp.zeros_like(gt)
 
+        blocks, high, wide = go.shape
+        total_lanes = of.shape[1]
+        fold = wide // total_lanes
+        if fold == 1:
+            high = rows
+
         def prep(i, c):
-            part = pl.ds(pl.multiple_of(i * rows, rows), rows)
-            lane = lax.broadcasted_iota(jnp.int32, (rows, 128), 1)
-            for n in range(heads):
-                at = (first + n) * HD
-                rows_go = go[part, at : at + HD]
-                inner = jnp.sum(rows_go.astype(F32) * of[part, at : at + HD], -1, keepdims=True)
-                hi = inner.astype(BF).astype(F32)
-                tail = jnp.where(lane == HD, -hi, jnp.where(lane == HD + 1, hi - inner, 0.0))
-                dop[n, part, :] = tail.astype(BF)
-                dop[n, part, 0:HD] = rows_go
+            lane = lax.broadcasted_iota(jnp.int32, (high, 128), 1)
+            for s in range(fold):
+                part = pl.ds(pl.multiple_of((i * fold + s) * high, high), high)
+                for n in range(heads):
+                    at = (first + n) * HD
+                    if fold == 1:
+                        rows_go = flat_go[part, at : at + HD]
+                    else:
+                        rows_go = go[i, :, s * total_lanes + at : s * total_lanes + at + HD]
+                    inner = jnp.sum(rows_go.astype(F32) * of[part, at : at + HD], -1, keepdims=True)
+                    hi = inner.astype(BF).astype(F32)
+                    tail = jnp.where(lane == HD, -hi, jnp.where(lane == HD + 1, hi - inner, 0.0))
+                    dop[n, part, :] = tail.astype(BF)
+                    dop[n, part, 0:HD] = rows_go
             return c
 
-        lax.fori_loop(0, 9, prep, 0)
+        flat_go = go.at[0]
+        lax.fori_loop(0, seq_len // (fold * high), prep, 0)
 
     @pl.when(step == 0)
     def _():
         def prep(i, c):
             part = pl.ds(pl.multiple_of(i * rows, rows), rows)
-            kt[:, part] = kp[0, part, :].T[0 : HD + 2 * side]
+            kt[0:128, part] = kp[0, part, 0:128].T
+            kt[128 : 128 + side, part] = hot[:, part]
             dk[part, :] = jnp.zeros((rows, 128), F32)
             dv[part, :] = jnp.zeros((rows, 128), F32)
             return c
@@ -266,7 +288,7 @@
     for i in range(groups):
         part = slice(i * side, (i + 1) * side)
         back_h.append(pltpu.roll(rel_h[part], 256 - 33 - step * groups - i, axis=1))
-        back_w.append(stagger(rel_w[part], side))
+        back_w.append(pltpu.roll(rel_w[part], 0, axis=1, stride=1, stride_axis=0))
     both = jnp.concatenate([jnp.concatenate(back_h, 0), jnp.concatenate(back_w, 0)], 1).astype(BF)
     dq[base, :] = acc[:, :HD] * scale + dot(both, tables[...])
     gt[...] += dot(both, qa[:, 0:128], TN)
@@ -287,19 +309,11 @@
             lax.fori_loop(0, 9, post, 0)
 
 
-def stagger(val, side):
-    row = lax.broadcasted_iota(jnp.int32, val.shape, 0)
-    shift = side - 1 - row
-    bit = 1
-    while bit < side:
-        val = jnp.where((shift & bit) != 0, pltpu.roll(val, bit, axis=1), val)
-        bit *= 2
-    return val
-
-
-def attend_back(first, count, qa, kp, vp, of, go, tables, side, tb=768, uc=256):
+def attend_back(first, count, qa, kp, vp, of, go, tables, hot, side, tb=768, uc=256):
     heads, seq_len, _ = qa.shape
     lanes = heads * HD
+    if go.shape[2] == lanes:
+        go = go.reshape(1, seq_len, lanes)
     return pl.pallas_call(
         partial(attend_back_kernel, count, first, side, uc),
         grid=(count, seq_len // tb),
@@ -308,8 +322,9 @@
             pl.BlockSpec((1, seq_len, 256), lambda h, i: (first + h, 0, 0)),
             pl.BlockSpec((1, seq_len, 128), lambda h, i: (first + h, 0, 0)),
             whole(seq_len, lanes),
-            whole(seq_len, lanes),
+            whole(*go.shape),
             whole(256, HD),
+            whole(side, seq_len),
         ],
         out_specs=[whole(seq_len, 3 * count * HD), whole(256, 128)],
         out_shape=[
@@ -326,7 +341,7 @@
         compiler_params=params(2),
         cost_estimate=busy(50),
         name="attend_back",
-    )(qa, kp, vp, of, go, tables)
+    )(qa, kp, vp, of, go, tables, hot)
 
 
 def mlp_kernel(aliased, per, n_own, n_other, g_own, g_other, w1, b1, w2, *refs):
@@ -565,9 +580,10 @@
         copy.wait()
 
 
-def start_exchange(patches, own, vec, sizes, split=3):
+def start_exchange(patches, own, vec, sizes):
     dp, ng, np_ = sizes
     images, count, width = patches.shape
+    split = 6 if count % 48 == 0 else 3
     chunk_copies = ng * np_ + (ng - 1) + (np_ - 1) + (ng - 1) * (np_ - 1)
     copies = 2 * (dp - 1) + split * chunk_copies
     hbm = pl.BlockSpec(memory_space=pl.ANY)
@@ -837,7 +853,9 @@
             for u in range(part_w // cell):
                 n = len(sent_cells)
                 lane = t * part_w + u * cell
-                cells[n] = value[:, lane : lane + cell]
+                quarter = shard // 4
+                for i in range(4):
+                    cells[n, :, i * cell : (i + 1) * cell] = value[i * quarter : (i + 1) * quarter, lane : lane + cell]
                 unit = (t * width + (i_p * pieces + q) * shard + i_c * part_w) // cell + u
                 owner = unit // 3
                 slot = unit % 3
@@ -895,7 +913,10 @@
             pltpu.make_async_copy(cells.at[0], taken.at[g, slot], cell_recv.at[g * 3 + slot]).wait()
             term = taken[g, slot].astype(F32)
             value = term if value is None else value + term
-        owned[:, slot * cell : (slot + 1) * cell] = value
+        quarter = shard // 4
+        for i in range(4):
+            rows_at = slice(i * quarter, (i + 1) * quarter)
+            owned[rows_at, slot * cell : (slot + 1) * cell] = value[:, i * cell : (i + 1) * cell]
     for copy in small:
         copy.wait_recv()
     for j in range(dp):
@@ -953,8 +974,8 @@
             pltpu.VMEM((ng, count, width), BF),
             pltpu.VMEM((dp, pieces, shard, lanes), BF),
             pltpu.VMEM((dp, pieces, shard, lanes), BF),
-            pltpu.VMEM((total_cells, shard, cell), BF),
-            pltpu.VMEM((ng, 3, shard, cell), BF),
+            pltpu.VMEM((total_cells, shard // 4, 4 * cell), BF),
+            pltpu.VMEM((ng, 3, shard // 4, 4 * cell), BF),
             pltpu.VMEM((8, width), F32),
             pltpu.VMEM((8, lanes), F32),
             pltpu.VMEM((16, width), F32),
@@ -985,16 +1006,55 @@
     )(raw, normed, *dx, *tables, w, inputs, grad_mid, gain, early, proj_in, *parts_a, *parts_b)
 
 
+def split_kernel(chips, at, value, *outs):
+    for z in range(chips):
+
+        @pl.when(at[0] == z)
+        def _(z=z):
+            for n in range(chips):
+                lanes = outs[n].shape[1]
+                outs[n][...] = value[:, (z ^ n) * lanes : ((z ^ n) + 1) * lanes]
+
+
+def split_columns(value, index, chips):
+    rows, width = value.shape
+    vmem = pl.BlockSpec(memory_space=pltpu.VMEM)
+    return pl.pallas_call(
+        partial(split_kernel, chips),
+        in_specs=[pl.BlockSpec(memory_space=pltpu.SMEM), vmem],
+        out_specs=[vmem] * chips,
+        out_shape=[jax.ShapeDtypeStruct((rows, width // chips), value.dtype)] * chips,
+        cost_estimate=FREE,
+        name="split_columns",
+    )(jnp.stack([index]), value)
+
+
 def places():
     return tuple(lax.axis_index(name) for name in ("dp", "g", "p", "c"))
+
+
+def proj_copy(w, held, sem):
+    piece = held.shape[1]
+    copy = pltpu.make_async_copy(w.at[:, pl.ds(4 * piece, piece)], held, sem)
+    copy.start()
+    return copy
+
+
+def rows_of(w, p, np_):
+    dp, piece, width = w.shape
+    if dp >= np_:
+        each = dp // np_
+        return w[pl.ds(p * each, each)].reshape(each * piece, width)
+    raise NotImplementedError
 
 
 def middle_kernel(sizes, near, *refs):
     dp, ng, np_ = sizes
     far = refs[:np_]
-    (w, patches, bias, gain, shift, mid, two_own, two_other, mixed,
-     pieces, mine, away, came, sem, send, recv) = refs[np_:]
+    (w_all, patches, bias, gain, shift, mid, two_own, two_other, mixed,
+     w, pieces, mine, away, came, sem, send, recv) = refs[np_:]
     i_dp, i_g, i_p, i_c = places()
+    proj = proj_copy(w_all, w, sem.at[1])
     rows = patches.shape[1]
     core = {"c": 1 - i_c}
     meet([core] + [{"p": i_p ^ k} for k in range(1, np_)])
@@ -1014,11 +1074,12 @@
     def product(b, image):
         total = None
         for p in range(np_):
-            term = dot(mixed[p, b, image], w[p])
+            term = dot(mixed[p, b, image], rows_of(w, p, np_))
             total = term if total is None else total + term
         return total
 
     other = []
+    proj.wait()
     for bit in (1, 0):
         image = i_g ^ bit
         if bit:
@@ -1055,7 +1116,7 @@
     own = jax.ShapeDtypeStruct((images, rows, width), BF)
     return pl.pallas_call(
         partial(middle_kernel, sizes),
-        in_specs=[pl.BlockSpec(memory_space=pl.ANY)] + [vmem] * (len(far) + 5),
+        in_specs=[pl.BlockSpec(memory_space=pl.ANY)] + [vmem] * len(far) + [pl.BlockSpec(memory_space=pl.ANY)] + [vmem] * 4,
         out_specs=[vmem] * 4,
         out_shape=[
             jax.ShapeDtypeStruct((images, rows, width), F32),
@@ -1064,11 +1125,12 @@
             jax.ShapeDtypeStruct((np_, 2, images, rows, lanes), BF),
         ],
         scratch_shapes=[
+            pltpu.VMEM((dp, w.shape[1] // 5, width), BF),
             pltpu.VMEM((np_, 2 * rows, lanes), BF),
             pltpu.VMEM((images, rows, width), F32),
             pltpu.VMEM((images, rows, width), F32),
             pltpu.VMEM((images, rows, width), F32),
-            pltpu.SemaphoreType.DMA((1,)),
+            pltpu.SemaphoreType.DMA((2,)),
             pltpu.SemaphoreType.DMA((copies,)),
             pltpu.SemaphoreType.DMA((copies,)),
         ],
@@ -1088,11 +1150,12 @@
     return inverse * (scaled - jnp.mean(scaled, -1, keepdims=True) - normal * inner), normal
 
 
-def turn_kernel(sizes, mid, gn, out, branch, gain, shift, w, mixed, output, grad_mid, heads, grad_proj, sums,
-                back_own, back_other, gn_own, gn_came, out_own, out_came, stage, sem, send, recv):
+def turn_kernel(sizes, mid, gn, out, branch, gain, shift, w_all, mixed, output, grad_mid, heads, grad_proj, sums,
+                w, back_own, back_other, gn_own, gn_came, out_own, out_came, stage, sem, send, recv):
     dp, ng, np_ = sizes
     i_dp, i_g, i_p, i_c = places()
     images, rows, width = mid.shape
+    fold = rows // stage.shape[1]
     i_z = i_g * np_ + i_p
     core = {"c": 1 - i_c}
     peers = [core]
@@ -1101,6 +1164,7 @@
     meet(peers)
     link = Links(send, recv)
     turns = [i_g ^ 1, i_g]
+    proj = proj_copy(w_all, w, sem.at[2 * images + 2])
 
     def half(ref, b, image):
         start = (b * images + image) * rows
@@ -1120,9 +1184,11 @@
         source = (back_own if b == 0 else back_other)[image]
         for k in range(np_):
             slot = (n * np_ + k) * 2 + b
-            stage[slot] = dot(source, w[i_p ^ k], NT).astype(BF)
-            start = (i_z * 2 + (i_c ^ b)) * rows
-            dst = heads.at[pl.ds(pl.multiple_of(start, 8), rows)]
+            value = dot(source, rows_of(w, i_p ^ k, np_), NT).astype(BF)
+            lanes = value.shape[1]
+            for s in range(fold):
+                stage[slot, :, s * lanes : (s + 1) * lanes] = value[s * rows // fold : (s + 1) * rows // fold]
+            dst = heads.at[i_z * 2 + (i_c ^ b)]
             if n == 1 and k == 0:
                 locals_.append(pltpu.make_async_copy(stage.at[slot], dst, sem.at[2 * images + b]))
                 locals_[-1].start()
@@ -1145,6 +1211,8 @@
         sums[1:2, :] += jnp.sum(grad_two, 0, keepdims=True)
         sums[2:3, :] += jnp.sum(back_own[image].astype(F32), 0, keepdims=True)
         sums[3:4, :] += jnp.sum(grad_out, 0, keepdims=True)
+        if n == 0:
+            proj.wait()
         give(n, 0)
     outs = []
     for n, image in enumerate(turns):
@@ -1175,7 +1243,8 @@
 def turn(mid, gn, out, branch, gain, shift, w, mixed, sizes):
     dp, ng, np_ = sizes
     images, rows, width = mid.shape
-    lanes = w.shape[1]
+    lanes = mixed.shape[4]
+    fold = 2 if rows % 32 == 0 else 1
     chips = ng * np_
     vmem = pl.BlockSpec(memory_space=pltpu.VMEM)
     hbm = pl.BlockSpec(memory_space=pl.ANY)
@@ -1183,24 +1252,25 @@
     own = (images, rows, width)
     return pl.pallas_call(
         partial(turn_kernel, sizes),
-        in_specs=[vmem, hbm, hbm] + [vmem] * 5,
+        in_specs=[vmem, hbm, hbm, vmem, vmem, vmem, hbm, vmem],
         out_specs=[vmem, vmem, hbm, vmem, vmem],
         out_shape=[
             jax.ShapeDtypeStruct(own, BF),
             jax.ShapeDtypeStruct(own, F32),
-            jax.ShapeDtypeStruct((chips * 2 * rows, lanes), BF),
+            jax.ShapeDtypeStruct((chips * 2, rows // fold, lanes * fold), BF),
             jax.ShapeDtypeStruct((np_, lanes, width), BF),
             jax.ShapeDtypeStruct((8, width), F32),
         ],
         scratch_shapes=[
+            pltpu.VMEM((dp, w.shape[1] // 5, width), BF),
             pltpu.VMEM(own, BF),
             pltpu.VMEM(own, BF),
             pltpu.VMEM(own, F32),
             pltpu.VMEM(own, F32),
             pltpu.VMEM(own, F32),
             pltpu.VMEM(own, F32),
-            pltpu.VMEM((chips * 2, rows, lanes), BF),
-            pltpu.SemaphoreType.DMA((2 * images + 2,)),
+            pltpu.VMEM((chips * 2, rows // fold, lanes * fold), BF),
+            pltpu.SemaphoreType.DMA((2 * images + 3,)),
             pltpu.SemaphoreType.DMA((copies,)),
             pltpu.SemaphoreType.DMA((copies,)),
         ],
@@ -1291,7 +1361,6 @@
     qkv_own, slab_a, slab_b = select(spot, qkv_weight, fc1_weight, fc2_weight, proj_weight, ng, np_, nc, lanes)
     weights_a = lax.all_gather(slab_a, "dp", axis=0)
     weights_b = lax.all_gather(slab_b, "dp", axis=0)
-    proj_half = weights_a[:, 2 * shard :]
     raw, qkv_full, vectors = start_exchange(patches, qkv_own, packed, (dp, ng, np_))
     qkv_full = qkv_full.reshape(width, 3 * lanes)
     vectors = vectors.astype(F32)
@@ -1316,6 +1385,10 @@
     branch_other = flip(branch_own, "c", nc, 1)
 
     tables = flip_tables(rel_pos_h, rel_pos_w)
+    back_tables = flip_tables(rel_pos_h, rel_pos_w[::-1])
+    token = lax.broadcasted_iota(jnp.int32, (side, seq_len), 1)
+    column = lax.broadcasted_iota(jnp.int32, (side, seq_len), 0)
+    col_hot = (token % side == side - 1 - column).astype(BF)
     normed, query, key_rows, value_rows = qkv_rows(
         raw, gain_one[None], shift_one[None], qkv_full, qkv_shift, tables, pieces, core_heads, side
     )
@@ -1329,12 +1402,11 @@
     for k in range(np_):
         arrived[1, k] = pinned[k]
     near_att = near_att.reshape(np_, nc * row_count, lanes)
-    proj_rows = proj_half.reshape(np_, lanes, width)
     sizes = (dp, ng, np_)
     middle, two_own, two_other, mixed = middle_rows(
         near_att,
         [arrived[1, k] for k in range(np_)],
-        proj_rows,
+        weights_a,
         patches,
         proj_shift[None],
         gain_two[None],
@@ -1354,15 +1426,14 @@
         two_own, two_other, branch_own, branch_other, weights_b, fc1_shift[1], (out_a, back_a)
     )
     output, grad_middle, grad_heads, grad_proj, early = turn(
-        middle, back_b, out_b, cotangent, gain_two[None], fc2_shift[None], proj_rows, mixed, sizes
+        middle, back_b, out_b, cotangent, gain_two[None], fc2_shift[None], weights_a, mixed, sizes
     )
     sum_b = over_dp(grads_b)
     sum_p = over_dp(grad_proj.reshape(dp, piece, width))
 
     def pieces_over_chips(value):
-        split = value.reshape(value.shape[0], chips, width // chips).transpose(1, 0, 2)
-        sent = [flip(pick(split, i_z ^ bit), ("g", "p"), chips, bit) for bit in range(1, chips)]
-        return [pick(split, i_z)] + sent
+        blocks = split_columns(value, i_z, chips)
+        return [blocks[0]] + [flip(blocks[bit], ("g", "p"), chips, bit) for bit in range(1, chips)]
 
     grad_heads, sum_a = tie(grad_heads, sum_a)
     sum_a = pieces_over_chips(sum_a)
@@ -1370,7 +1441,7 @@
     grad_tables = []
     for q in range(pieces):
         rows, table = attend_back(
-            q * core_heads, core_heads, query_a, key_rows, value_rows, att_f, grad_heads, tables, side
+            q * core_heads, core_heads, query_a, key_rows, value_rows, att_f, grad_heads, back_tables, col_hot, side
         )
         if q == 0:
             rows, *sum_a = tie(rows, *sum_a)
@@ -1404,7 +1475,7 @@
         piece,
     )
     entries = rel_pos_h.shape[0]
-    rel = [rel[:entries, :HD][::-1], rel[128 : 128 + entries, :HD][::-1]]
+    rel = [rel[:entries, :HD][::-1], rel[128 : 128 + entries, :HD]]
     fc1_vec = vec[8:12].reshape(-1)
 
     return (

time: 550 us -> 538 us (0.978)
  local copies, waits for them, and re-layouts: 48.2 us -> 35.4 us
    ppermute x9, waiting for transfers between devices: 17.7 us -> 7.44 us  [flip(): return lax.ppermute(value, axis, [(i, i ^ bit) for i in range(size)])]
    pallas_call x1, Pallas kernels: 21.9 us -> 28.8 us  [middle_rows(): pl.pallas_call(partial(middle_kernel, sizes), in_specs=[pl.BlockSpec(memo...]
    optimization_barrier x2 -> x0, local copies, waits for them, and re-layouts: 6.27 us -> none  [tie(): return lax.optimization_barrier(values)]
    reduce_scatter x1 -> x3, waiting for transfers between devices: 0.01 us -> 5.76 us  [over_dp(): lax.psum_scatter(value.reshape(-1, value.shape[-1]), 'dp', scatter_dimens...]
    unnamed x70 -> x76, local copies, waits for them, and re-layouts: 21 us -> 23.4 us
    pallas_call x2 -> x4, Pallas kernels: 67.2 us -> 66.4 us  [the longest x1 42.7 us: turn(): pl.pallas_call(partial(turn_kernel, sizes), in_specs=[vmem, hbm, hbm, vme...]
  transfers between devices with their start and end apart: 14 -> 14, of which waited for: 1 -> 2; matrix products, arithmetic and copies ran while one was open for 5% -> 2% of each run, Pallas kernels for 64% -> 67%
where the time goes in v6:
time: 538 us; the launch traced here: 534 us
  Pallas kernels  451 us (84%)
  local copies, waits for them, and re-layouts  35.4 us (7%)
  starting transfers between devices  15.8 us (3%)
  between operations  14.5 us (3%)
  waiting for transfers between devices  14 us (3%)
    pallas_call x2, Pallas kernels, attend_back(): pl.pallas_call(partial(attend_back_kernel, count, first, side, uc), grid=...  95.4 us
    pallas_call x1, Pallas kernels, finish(): pl.pallas_call(partial(finish_kernel, sizes, split, pieces, part_w), in_s...  91.1 us
    pallas_call x2, Pallas kernels, mlp_half(): pl.pallas_call(partial(mlp_kernel, bool(old), per), grid=(steps + dp,), i...  67.7 us
    pallas_call x1, Pallas kernels, start_exchange(): pl.pallas_call(partial(start_kernel, sizes, split), in_specs=[hbm] * 3, o...  58.8 us
    pallas_call x1, Pallas kernels, turn(): pl.pallas_call(partial(turn_kernel, sizes), in_specs=[vmem, hbm, hbm, vme...  42.7 us
    pallas_call x2, Pallas kernels, attend(): pl.pallas_call(partial(attend_kernel, heads, side, bool(old), sub), grid_...  39.6 us
    pallas_call x1, Pallas kernels, middle_rows(): pl.pallas_call(partial(middle_kernel, sizes), in_specs=[pl.BlockSpec(memo...  28.8 us
    unnamed x76, local copies, waits for them, and re-layouts  23.4 us
  transfers between devices with their start and end apart: 14, of which 2 were waited for; matrix products, arithmetic and copies ran while one was open for 2% of the time, Pallas kernels for 67%

profile of v6, /device:TPU:0, one launch (start us, length us, event | category | flops | bytes accessed | tf_op | source)
XLA Modules:
  0.0 533.8 jit_solution(15657769264374675763)
XLA Ops:
  7.3 1.9 copy-done.1
  9.2 1.9 copy-done.2
  11.2 1.7 copy-done.3
  12.9 1.1 copy-done.5
  14.0 3.2 select.18
  17.2 0.8 copy-done.6
  18.2 0.7 all-gather.7.cloned.1.call-update
  19.2 1.2 concatenate.20.vec
  20.5 58.8 %start_exchange.1 = (bf16[2304,1280]{1,0:T(8,128)(2,1)}, bf16[4,320,960]{2,1,0:T(8,128)(2,1)}, bf16[4,10,320]{2,1,0:T(8,128)(2,1)}) custom-call(bf16[2,288,1280]{2,1,0:T(8,128)(2,1)} %refs_7_.1, bf16[320,960]{1,0:T(8,128)(2,1)} %copy-done.6, bf16[10,320]{1,0:T(8,128)(2,1)} %concatenate.20.vec), custom_call_target="tpu_custom_call" | custom-call | flops 1 | bytes 1 | tf_op jit(solution)/shard_map/start_exchange/pallas_call | solution.py:590
  79.3 0.8 fusion.11
  80.1 0.1 slice_reduce_fusion
  80.4 0.7 unstack.43.gain.refs_9_
  81.1 0.7 unstack.45.shift
  81.8 0.1 copy.46
  81.9 0.1 copy.45
  82.2 0.7 concatenate.21
  82.9 0.7 fusion.5
  83.5 16.9 %qkv_rows.1 = (bf16[2304,1280]{1,0:T(8,128)(2,1)}, bf16[4,2304,256]{2,1,0:T(8,128)(2,1)}, bf16[4,2304,256]{2,1,0:T(8,128)(2,1)}, bf16[4,2304,128]{2,1,0:T(8,128)(2,1)}) custom-call(bf16[2304,1280]{1,0:T(8,128)(2,1)} %get-tuple-element.89.raw.refs_0_, f32[1,1280]{1,0:T(1,128)} %unstack.43.gain.refs_9_, f32[1,1280]{1,0:T(1,128)} %unstack.45.shift, ...), custom_call_target="tpu_custom_call" | custom-call | flops 1 | bytes 1 | tf_op jit(solution)/shard_map/qkv_rows/pallas_call | solution.py:104
  100.4 19.6 %attend.2 = (bf16[1152,320]{1,0:T(8,128)(2,1)}, f32[2304,320]{1,0:T(8,128)}, bf16[4,2304,256]{2,1,0:T(8,128)(2,1)}) custom-call(s32[1]{0:T(128)} %bitcast.7.at, bf16[4,2304,256]{2,1,0:T(8,128)(2,1)} %get-tuple-element.92.qa, bf16[4,2304,256]{2,1,0:T(8,128)(2,1)} %get-tuple-element.126.kp, bf16[4,2304,128]{2,1,0:T(8,128)(2,1)} %get-tuple-element.94.vp), custom_call_target="tpu_custom_call" | custom-call | flops 20000000000 | bytes 1 | tf_op jit(solution)/shard_map/attend/pallas_call | solution.py:179
  120.0 1.2 dynamic-slice_bitcast_fusion
  121.2 2.2 collective-permute-start
  123.4 1.9 collective-permute-start.1
  125.4 20.0 %attend.3 = (bf16[1152,320]{1,0:T(8,128)(2,1)}, f32[2304,320]{1,0:T(8,128)}, bf16[4,2304,256]{2,1,0:T(8,128)(2,1)}) custom-call(s32[1]{0:T(128)} %bitcast.at, bf16[4,2304,256]{2,1,0:T(8,128)(2,1)} %get-tuple-element.92.qa, bf16[4,2304,256]{2,1,0:T(8,128)(2,1)} %get-tuple-element.126.kp, ...), custom_call_target="tpu_custom_call", output_to_operand_aliasing={{1}: (4, {}), {2}: (5, {})} | custom-call | flops 20000000000 | bytes 1 | tf_op jit(solution)/shard_map/attend/pallas_call | solution.py:179
  145.7 0.7 squeeze.42.b1
  146.4 7.4 %collective-permute-done.refs_0_ = bf16[576,320]{1,0:T(8,128)(2,1)S(1)} collective-permute-done((bf16[576,320]{1,0:T(8,128)(2,1)S(1)}, bf16[576,320]{1,0:T(8,128)(2,1)S(1)}, u32[]{:S(2)}, u32[]{:S(2)}) %collective-permute-start) | collective-permute-done | bytes 368672 | tf_op jit(solution)/shard_map/ppermute | solution.py:1284
  153.8 1.2 copy-done.4
  155.0 28.8 %middle_rows.1 = (f32[2,288,1280]{2,1,0:T(8,128)}, bf16[2,288,1280]{2,1,0:T(8,128)(2,1)S(1)}, bf16[2,288,1280]{2,1,0:T(8,128)(2,1)S(1)}, bf16[2,2,2,288,320]{4,3,2,1,0:T(8,128)(2,1)}) custom-call(bf16[2,576,320]{2,1,0:T(8,128)(2,1)S(1)} %bitcast.31, bf16[576,320]{1,0:T(8,128)(2,1)S(1)} %collective-permute-done.refs_0_, ...), custom_call_target="tpu_custom_call" | custom-call | flops 1 | bytes 1 | tf_op jit(solution)/shard_map/middle_rows/pallas_call | solution.py:1117
  183.9 1.1 copy-done.8
  185.0 1.1 copy-done.9
  186.1 32.8 %mlp_half.2 = (f32[1152,1280]{1,0:T(8,128)}, f32[1152,1280]{1,0:T(8,128)}, bf16[4,640,1280]{2,1,0:T(8,128)(2,1)}, f32[1,1280]{1,0:T(1,128)}) custom-call(bf16[576,1280]{1,0:T(8,128)(2,1)} %bitcast.32, bf16[576,1280]{1,0:T(8,128)(2,1)} %bitcast.34, bf16[576,1280]{1,0:T(8,128)(2,1)} %bitcast.15.g_own, bf16[576,1280]{1,0:T(8,128)(2,1)} %collective-permute-done.2.g_other, ...), custom_call_target="tpu_custom_call" | custom-call | flops 35000000512 | bytes 1 | tf_op jit(solution)/shard_map/mlp_half/pallas_call | solution.py:407
  219.0 0.7 squeeze.41.b1
  219.6 34.9 %mlp_half.3 = (f32[1152,1280]{1,0:T(8,128)}, f32[1152,1280]{1,0:T(8,128)}, bf16[4,640,1280]{2,1,0:T(8,128)(2,1)}, f32[1,1280]{1,0:T(1,128)}) custom-call(bf16[576,1280]{1,0:T(8,128)(2,1)} %bitcast.33, bf16[576,1280]{1,0:T(8,128)(2,1)} %bitcast.35, bf16[576,1280]{1,0:T(8,128)(2,1)} %bitcast.15.g_own, ...), custom_call_target="tpu_custom_call", output_to_operand_aliasing={{0}: (7, {}), {1}: (8, {})} | custom-call | flops 35000000512 | bytes 1 | tf_op jit(solution)/shard_map/mlp_half/pallas_call | solution.py:407
  254.5 0.3 reduce-scatter.8.cloned.1.call-start
  255.0 0.7 unstack.57.shift
  255.7 0.8 fusion.hot
  256.5 42.7 %turn.1 = (bf16[2,288,1280]{2,1,0:T(8,128)(2,1)}, f32[2,288,1280]{2,1,0:T(8,128)}, bf16[8,144,640]{2,1,0:T(8,128)(2,1)}, bf16[2,320,1280]{2,1,0:T(8,128)(2,1)}, f32[8,1280]{1,0:T(8,128)}) custom-call(f32[2,288,1280]{2,1,0:T(8,128)} %get-tuple-element.103.mid, f32[1152,1280]{1,0:T(8,128)} %get-tuple-element.109.gn, f32[1152,1280]{1,0:T(8,128)} %get-tuple-element.110.out, ...), custom_call_target="tpu_custom_call" | custom-call | flops 1 | bytes 1 | tf_op jit(solution)/shard_map/turn/pallas_call | solution.py:1253
  299.9 0.8 slice.68
  300.7 0.6 pad_maximum_fusion.refs_10_
  301.3 3.6 split_columns.2
  305.0 4.5 collective-permute-start.3
  309.5 0.4 collective-permute-start.4
  309.8 2.0 collective-permute-start.5
  311.8 47.2 %attend_back.2 = (bf16[2304,480]{1,0:T(8,128)(2,1)}, f32[256,128]{1,0:T(8,128)}) custom-call(bf16[4,2304,256]{2,1,0:T(8,128)(2,1)} %get-tuple-element.114.qa_ref, bf16[4,2304,256]{2,1,0:T(8,128)(2,1)} %get-tuple-element.126.kp, bf16[4,2304,128]{2,1,0:T(8,128)(2,1)} %get-tuple-element.94.vp, f32[2304,320]{1,0:T(8,128)} %get-tuple-element.115.of, ...), custom_call_target="tpu_custom_call" | custom-call | flops 49999998976 | bytes 1 | tf_op jit(solution)/shard_map/attend_back/pallas_call | solution.py:317
  359.1 5.7 %reduce-scatter.6.cloned.1.call-done.value = bf16[640,1280]{1,0:T(8,128)(2,1)} async-done(((bf16[2560,1280]{1,0:T(8,128)(2,1)}), bf16[640,1280]{1,0:T(8,128)(2,1)}) %reduce-scatter.6.cloned.1.call-update) | async-done | bytes 1638416 | tf_op jit(solution)/shard_map/reduce_scatter | solution.py:1419
  364.8 3.2 split_columns.3
  368.0 1.5 collective-permute-start.6
  369.4 2.4 collective-permute-start.7
  371.9 0.5 collective-permute-start.8
  372.4 48.2 %attend_back.3 = (bf16[2304,480]{1,0:T(8,128)(2,1)}, f32[256,128]{1,0:T(8,128)}) custom-call(bf16[4,2304,256]{2,1,0:T(8,128)(2,1)} %get-tuple-element.114.qa_ref, bf16[4,2304,256]{2,1,0:T(8,128)(2,1)} %get-tuple-element.126.kp, bf16[4,2304,128]{2,1,0:T(8,128)(2,1)} %get-tuple-element.94.vp, f32[2304,320]{1,0:T(8,128)} %get-tuple-element.115.of, ...), custom_call_target="tpu_custom_call" | custom-call | flops 49999998976 | bytes 1 | tf_op jit(solution)/shard_map/attend_back/pallas_call | solution.py:317
  420.6 0.8 copy-done.16
  421.4 0.8 copy-done.17
  422.2 0.8 copy-done.18
  423.0 91.1 %finish.1 = (bf16[2,288,1280]{2,1,0:T(8,128)(2,1)}, f32[320,480]{1,0:T(8,128)}, f32[16,320]{1,0:T(8,128)}, f32[256,128]{1,0:T(8,128)}, f32[320,640]{1,0:T(8,128)...) custom-call(bf16[2304,1280]{1,0:T(8,128)(2,1)} %get-tuple-element.89.raw.refs_0_, ...), custom_call_target="tpu_custom_call" | custom-call | flops 1 | bytes 1 | tf_op jit(solution)/shard_map/finish/pallas_call | solution.py:952
  514.1 1.6 slice_reduce_fusion.10
  515.8 0.7 slice.76
  516.5 2.7 copy.53
  519.2 1.8 copy.52
  521.0 0.7 copy.54
  521.7 0.7 copy.55
  522.4 0.7 reshape.102
  523.1 1.1 copy.64
  524.2 1.1 copy.65
  525.3 0.8 copy.66
  526.2 0.9 copy.67
  (118 shorter events, 2.1 us)
Async XLA Ops:
  7.2 146.6 %all-gather.5.cloned.1.call-start = ((), (), s32[]{:S(2)}) async-start(), calls=%async_computation.6 | async-start | bytes 10240000 | tf_op jit(solution)/shard_map/all_gather | solution.py:1362
  7.3 1.9 copy-start.1
  9.2 1.9 copy-start.2
  11.2 1.7 copy-start.3
  12.9 1.1 copy-start.5
  17.2 0.8 copy-start.6
  18.0 0.9 copy-start.24
  18.0 1.0 copy-start.25
  18.0 1.0 copy-start.26
  18.0 1.0 copy-start.27
  18.0 1.1 copy-start.28
  18.1 1.1 copy-start.29
  18.1 1.1 copy-start.30
  18.1 1.1 copy-start.31
  18.1 1.1 copy-start.32
  18.1 63.6 %copy-start.20 = (bf16[95,80]{0,1:T(8,128)(2,1)S(1)}, bf16[95,80]{0,1:T(8,128)(2,1)}, u32[]{:S(2)}) copy-start(bf16[95,80]{0,1:T(8,128)(2,1)} %param.32) | copy-start | bytes 45604
  18.1 63.8 %copy-start.21 = (bf16[95,80]{0,1:T(8,128)(2,1)S(1)}, bf16[95,80]{0,1:T(8,128)(2,1)}, u32[]{:S(2)}) copy-start(bf16[95,80]{0,1:T(8,128)(2,1)} %param.31) | copy-start | bytes 45604
  18.2 201.5 %all-gather.7.cloned.1.call-start = ((), (), s32[]{:S(2)}) async-start(), calls=%async_computation.7 | async-start | bytes 8192000 | tf_op jit(solution)/shard_map/all_gather | solution.py:1363
  18.9 282.4 %reduce-scatter.4.cloned.1.call-start = ((), (), s32[]{:S(2)}) async-start(), calls=%async_computation.3 | async-start | bytes 8192000 | tf_op jit(solution)/shard_map/reduce_scatter | solution.py:1419
  121.2 32.6 %collective-permute-start = (bf16[576,320]{1,0:T(8,128)(2,1)S(1)}, bf16[576,320]{1,0:T(8,128)(2,1)S(1)}, u32[]{:S(2)}, u32[]{:S(2)}) collective-permute-start(bf16[576,320]{1,0:T(8,128)(2,1)S(1)} %get-tuple-element.212), channel_id=1, source_target_pairs={{0,4},{2,6},{4,0},{6,2},{1,5},{3,7},{5,1},{7,3},{8,12},{10,14},{12... | collective-permute-start | bytes 1105928 | tf_op jit(solution)/shard_map/ppermute | solution.py:1284
  123.4 30.4 %collective-permute-start.1 = (bf16[576,320]{1,0:T(8,128)(2,1)S(1)}, bf16[576,320]{1,0:T(8,128)(2,1)S(1)}, u32[]{:S(2)}, u32[]{:S(2)}) collective-permute-start(bf16[576,320]{1,0:T(8,128)(2,1)S(1)} %get-tuple-element.211), channel_id=1, source_target_pairs={{0,6},{2,4},{4,2},{6,0},{1,7},{3,5},{5,3},{7,1},{8,14},{10,12},{12... | collective-permute-start | bytes 1105928 | tf_op jit(solution)/shard_map/ppermute | solution.py:1284
  125.4 60.7 %collective-permute-start.2 = (bf16[576,1280]{1,0:T(8,128)(2,1)}, bf16[576,1280]{1,0:T(8,128)(2,1)}, u32[]{:S(2)}, u32[]{:S(2)}) collective-permute-start(bf16[576,1280]{1,0:T(8,128)(2,1)} %bitcast.15.g_own), channel_id=1, source_target_pairs={{0,1},{1,0},{2,3},{3,2},{4,5},{5,4},{6,7},{7,6},{8,9},{9,8},{10,11... | collective-permute-start | bytes 4423688 | tf_op jit(solution)/shard_map/ppermute | solution.py:1284
  125.4 28.5 %copy-start = (bf16[2,288,1280]{2,1,0:T(8,128)(2,1)S(1)}, bf16[2,288,1280]{2,1,0:T(8,128)(2,1)}, u32[]{:S(2)}) copy-start(bf16[2,288,1280]{2,1,0:T(8,128)(2,1)} %refs_7_.1) | copy-start | bytes 4423684
  145.5 38.4 %copy-start.7 = (f32[1,1280]{1,0:T(1,128)}, f32[1,1280]{1,0:T(1,128)S(1)}, u32[]{:S(2)}) copy-start(f32[1,1280]{1,0:T(1,128)S(1)} %unstack.53.refs_5_.gain) | copy-start | bytes 15364
  153.8 1.2 copy-start.4
  183.8 1.1 copy-start.8
  185.0 1.1 copy-start.9
  218.9 145.9 %reduce-scatter.6.cloned.1.call-start = ((), (), s32[]{:S(2)}) async-start(), calls=%async_computation.4 | async-start | bytes 8192000 | tf_op jit(solution)/shard_map/reduce_scatter | solution.py:1419
  254.5 168.4 %reduce-scatter.8.cloned.1.call-start = ((), (), s32[]{:S(2)}) async-start(), calls=%async_computation.5 | async-start | bytes 2048000 | tf_op jit(solution)/shard_map/reduce_scatter | solution.py:1419
  256.5 42.7 %copy-start.23 = (f32[1,1280]{1,0:T(1,128)S(1)}, f32[1,1280]{1,0:T(1,128)}, u32[]{:S(2)}) copy-start(f32[1,1280]{1,0:T(1,128)} %get-tuple-element.142) | copy-start | bytes 15364
  256.5 42.9 %copy-start.22 = (f32[1,1280]{1,0:T(1,128)S(1)}, f32[1,1280]{1,0:T(1,128)}, u32[]{:S(2)}) copy-start(f32[1,1280]{1,0:T(1,128)} %get-tuple-element.141) | copy-start | bytes 15364
  305.0 54.1 %collective-permute-start.3 = (bf16[640,320]{1,0:T(8,128)(2,1)}, bf16[640,320]{1,0:T(8,128)(2,1)S(1)}, u32[]{:S(2)}, u32[]{:S(2)}) collective-permute-start(bf16[640,320]{1,0:T(8,128)(2,1)} %get-tuple-element.122), channel_id=1, source_target_pairs={{0,2},{2,0},{4,6},{6,4},{1,3},{3,1},{5,7},{7,5},{8,10},{10,8},{12,... | collective-permute-start | bytes 1228808 | tf_op jit(solution)/shard_map/ppermute | solution.py:1284
  309.5 49.6 %collective-permute-start.4 = (bf16[640,320]{1,0:T(8,128)(2,1)}, bf16[640,320]{1,0:T(8,128)(2,1)S(1)}, u32[]{:S(2)}, u32[]{:S(2)}) collective-permute-start(bf16[640,320]{1,0:T(8,128)(2,1)} %get-tuple-element.123), channel_id=1, source_target_pairs={{0,4},{2,6},{4,0},{6,2},{1,5},{3,7},{5,1},{7,3},{8,12},{10,14},{12... | collective-permute-start | bytes 1228808 | tf_op jit(solution)/shard_map/ppermute | solution.py:1284
  309.8 49.2 %collective-permute-start.5 = (bf16[640,320]{1,0:T(8,128)(2,1)}, bf16[640,320]{1,0:T(8,128)(2,1)}, u32[]{:S(2)}, u32[]{:S(2)}) collective-permute-start(bf16[640,320]{1,0:T(8,128)(2,1)} %get-tuple-element.124), channel_id=1, source_target_pairs={{0,6},{2,4},{4,2},{6,0},{1,7},{3,5},{5,3},{7,1},{8,14},{10,12},{12... | collective-permute-start | bytes 1228808 | tf_op jit(solution)/shard_map/ppermute | solution.py:1284
  359.0 61.5 %copy-start.14 = (bf16[640,320]{1,0:T(8,128)(2,1)}, bf16[640,320]{1,0:T(8,128)(2,1)S(1)}, u32[]{:S(2)}) copy-start(bf16[640,320]{1,0:T(8,128)(2,1)S(1)} %collective-permute-done.3.refs_13_) | copy-start | bytes 1228804
  359.1 61.5 %copy-start.15 = (bf16[640,320]{1,0:T(8,128)(2,1)}, bf16[640,320]{1,0:T(8,128)(2,1)S(1)}, u32[]{:S(2)}) copy-start(bf16[640,320]{1,0:T(8,128)(2,1)S(1)} %collective-permute-done.4.refs_14_) | copy-start | bytes 1228804
  368.0 52.6 %collective-permute-start.6 = (bf16[640,320]{1,0:T(8,128)(2,1)}, bf16[640,320]{1,0:T(8,128)(2,1)S(1)}, u32[]{:S(2)}, u32[]{:S(2)}) collective-permute-start(bf16[640,320]{1,0:T(8,128)(2,1)} %get-tuple-element.131), channel_id=1, source_target_pairs={{0,2},{2,0},{4,6},{6,4},{1,3},{3,1},{5,7},{7,5},{8,10},{10,8},{12,... | collective-permute-start | bytes 1228808 | tf_op jit(solution)/shard_map/ppermute | solution.py:1284
  369.4 52.0 %collective-permute-start.7 = (bf16[640,320]{1,0:T(8,128)(2,1)}, bf16[640,320]{1,0:T(8,128)(2,1)S(1)}, u32[]{:S(2)}, u32[]{:S(2)}) collective-permute-start(bf16[640,320]{1,0:T(8,128)(2,1)} %get-tuple-element.132), channel_id=1, source_target_pairs={{0,4},{2,6},{4,0},{6,2},{1,5},{3,7},{5,1},{7,3},{8,12},{10,14},{12... | collective-permute-start | bytes 1228808 | tf_op jit(solution)/shard_map/ppermute | solution.py:1284
  371.9 50.3 %collective-permute-start.8 = (bf16[640,320]{1,0:T(8,128)(2,1)}, bf16[640,320]{1,0:T(8,128)(2,1)S(1)}, u32[]{:S(2)}, u32[]{:S(2)}) collective-permute-start(bf16[640,320]{1,0:T(8,128)(2,1)} %get-tuple-element.133), channel_id=1, source_target_pairs={{0,6},{2,4},{4,2},{6,0},{1,7},{3,5},{5,3},{7,1},{8,14},{10,12},{12... | collective-permute-start | bytes 1228808 | tf_op jit(solution)/shard_map/ppermute | solution.py:1284
  420.6 0.8 copy-start.16
  421.4 0.8 copy-start.17
  422.2 0.8 copy-start.18
  514.1 6.9 %copy-start.19 = (f32[256,128]{1,0:T(8,128)S(1)}, f32[256,128]{1,0:T(8,128)}, u32[]{:S(2)}) copy-start(f32[256,128]{1,0:T(8,128)} %get-tuple-element.158) | copy-start | bytes 393220
  514.1 9.0 %copy-start.10 = (bf16[2,288,1280]{2,1,0:T(8,128)(2,1)S(1)}, bf16[2,288,1280]{2,1,0:T(8,128)(2,1)}, u32[]{:S(2)}) copy-start(bf16[2,288,1280]{2,1,0:T(8,128)(2,1)} %get-tuple-element.244) | copy-start | bytes 4423684
  516.5 7.8 %copy-start.11 = (bf16[2,288,1280]{2,1,0:T(8,128)(2,1)S(1)}, bf16[2,288,1280]{2,1,0:T(8,128)(2,1)}, u32[]{:S(2)}) copy-start(bf16[2,288,1280]{2,1,0:T(8,128)(2,1)} %get-tuple-element.245) | copy-start | bytes 4423684
  523.1 2.2 copy-start.13
  524.2 2.0 copy-start.12
Sparse Core Ops, SparseCore 0:
  18.2 109.8 all-gather.4
  129.9 72.3 all-gather.6
  219.0 70.4 reduce-scatter.3
  292.4 72.3 reduce-scatter.5
  367.7 31.3 reduce-scatter.7

commit v7 on v6

--- a/solution.py
+++ b/solution.py
@@ -242,7 +242,7 @@
             return c
 
         flat_go = go.at[0]
-        lax.fori_loop(0, seq_len // (fold * high), prep, 0)
+        lax.fori_loop(0, seq_len // (fold * high), prep, 0, unroll=2)
 
     @pl.when(step == 0)
     def _():
@@ -434,7 +434,13 @@
     )(n_own, n_other, g_own, g_other, weights, b1, weights, *old)
 
 
-def select_kernel(ng, np_, nc, at, qkv, fc1, fc2, proj, own, *slabs):
+def select_kernel(ng, np_, nc, at, qkv_in, fc1_in, fc2_in, proj_in, own, *refs):
+    slabs = refs[:2]
+    qkv, fc1, fc2, proj, sem = refs[2:]
+    loads = []
+    for n, (src, dst) in enumerate(((qkv_in, qkv), (proj_in, proj), (fc1_in, fc1), (fc2_in, fc2))):
+        loads.append(pltpu.make_async_copy(src, dst, sem.at[n]))
+        loads[-1].start()
     i_p, i_c = at[1], at[2]
     shard = fc1.shape[0]
     width = proj.shape[1]
@@ -447,6 +453,20 @@
     lanes = own.shape[1] // 3
     pieces = lanes // piece
     per = fc2.shape[0] // (nc * unit)
+    loads[0].wait()
+    for c in range(nc):
+        for p in range(np_):
+
+            @pl.when((i_c == c) & (i_p == p))
+            def _(c=c, p=p):
+                for q in range(pieces):
+                    for t in range(3):
+                        src = t * width + (p * pieces + q) * shard_lanes + c * piece
+                        dst = (3 * q + t) * piece
+                        own[:, dst : dst + piece] = qkv[:, src : src + piece]
+
+    for copy in loads[1:]:
+        copy.wait()
     for c in range(nc):
 
         @pl.when(i_c == c)
@@ -461,29 +481,21 @@
                     slabs[u][dst : dst + part, :] = fc2[src : src + part, :]
             slabs[0][2 * shard : 2 * shard + piece, :] = proj[c * piece : (c + 1) * piece, :]
 
-        for p in range(np_):
-
-            @pl.when((i_c == c) & (i_p == p))
-            def _(c=c, p=p):
-                for q in range(pieces):
-                    for t in range(3):
-                        src = t * width + (p * pieces + q) * shard_lanes + c * piece
-                        dst = (3 * q + t) * piece
-                        own[:, dst : dst + piece] = qkv[:, src : src + piece]
-
 
 def select(at, qkv, fc1, fc2, proj, ng, np_, nc, lanes):
     shard, width = proj.shape[0], proj.shape[1]
     return pl.pallas_call(
         partial(select_kernel, ng, np_, nc),
-        in_specs=[pl.BlockSpec(memory_space=pltpu.SMEM)] + [pl.BlockSpec(memory_space=pltpu.VMEM)] * 4,
+        in_specs=[pl.BlockSpec(memory_space=pltpu.SMEM)] + [pl.BlockSpec(memory_space=pltpu.HBM)] * 4,
         out_specs=[pl.BlockSpec(memory_space=pltpu.VMEM)] * 3,
+        scratch_shapes=[pltpu.VMEM(value.shape, BF) for value in (qkv, fc1, fc2, proj)]
+        + [pltpu.SemaphoreType.DMA((4,))],
         out_shape=[
             jax.ShapeDtypeStruct((shard, 3 * lanes), BF),
             jax.ShapeDtypeStruct((2 * shard + shard // nc, width), BF),
             jax.ShapeDtypeStruct((2 * shard, width), BF),
         ],
-        compiler_params=pltpu.CompilerParams(vmem_limit_bytes=40 << 20),
+        compiler_params=pltpu.CompilerParams(vmem_limit_bytes=63 << 20),
         cost_estimate=FREE,
         name="select",
     )(at, qkv, fc1, fc2, proj)
@@ -645,12 +657,19 @@
     dx = refs[2 : 2 + pieces]
     tables = refs[2 + pieces : 2 + 2 * pieces]
     refs = refs[2 + 2 * pieces :]
-    w, inputs, grad_mid, gain, early, proj_in = refs[:6]
-    parts_a, parts_b = refs[6 : 6 + chips], refs[6 + chips : 6 + 2 * chips]
+    w_in, inputs_in, grad_mid_in, gain, early, proj_in = refs[:6]
+    parts_in = refs[6 : 6 + 2 * chips]
     (home, owned, out_vec, out_tab, out_fc1, out_fc2, out_proj,
      dx_all, norm_all, dx_ring, raw_ring, keep, away, came, pair, far, slab_out, slabs, cells, taken,
      sums, lane_sums, vec, vec_out, vec_dp, vec_z, vec_c, tab, tab_dp, tab_z, tab_c, tab_all,
-     give, got, give_p, got_p, proj_out, proj_got, sem, send, recv, cell_send, cell_recv) = refs[6 + 2 * chips :]
+     give, got, give_p, got_p, proj_out, proj_got, w, inputs, grad_mid, parts, late, sem, send, recv, cell_send, cell_recv,
+     ) = refs[6 + 2 * chips :]
+    w_load = pltpu.make_async_copy(w_in, w, late.at[0])
+    w_load.start()
+    late_loads = [pltpu.make_async_copy(inputs_in, inputs, late.at[1])]
+    late_loads.append(pltpu.make_async_copy(grad_mid_in, grad_mid, late.at[2]))
+    for n, ref in enumerate(parts_in):
+        late_loads.append(pltpu.make_async_copy(ref, parts.at[n], late.at[3 + n]))
     i_dp, i_g, i_p, i_c = places()
     i_z = i_g * np_ + i_p
     i_s = i_z * 2 + i_c
@@ -693,6 +712,8 @@
     for q in range(pieces):
         whole_loads.append(pltpu.make_async_copy(dx[q], dx_all.at[q], sem.at[2 * (1 + pieces) + 1 + q]))
     for copy in whole_loads:
+        copy.start()
+    for copy in late_loads:
         copy.start()
     sums[...] = jnp.zeros_like(sums)
     lane_sums[...] = jnp.zeros_like(lane_sums)
@@ -740,10 +761,11 @@
         return value
 
     half = len(far_slots) * 2
+    w_load.wait()
     for n in range(half):
         rows(n)
 
-    part_lanes = parts_a[0].shape[1]
+    part_lanes = parts.shape[2]
     for z in range(chips):
         proj_out[z] = proj_in[:, z * part_lanes : (z + 1) * part_lanes]
     from_chip = [link(proj_out.at[z_of(k)], proj_got.at[k], chip_peer(k)) for k in range(1, chips)]
@@ -819,26 +841,39 @@
         there[...] = jnp.where(i_c == 0, value[:, cols:], value[:, :cols]).astype(BF)
         return mine
 
-    def place_fc2(u, c, value):
-        for b in range(hidden_rows // per_rows):
-            start = ((b * 2 + c) * 2 + u) * per_rows
-            out_fc2[pl.ds(pl.multiple_of(start, 8), per_rows), :] = value[b * per_rows : (b + 1) * per_rows, :]
-
-    def place_proj(c, value):
-        out_proj[pl.ds(pl.multiple_of(c * value.shape[0], 8), value.shape[0]), :] = value
-
-    for u, parts in ((0, parts_a), (1, parts_b)):
-        value = parts[0][...].astype(F32)
-        for ref in parts[1:]:
-            value = value + ref[...].astype(F32)
+    def place_fc2(u, flip_core, value):
+        value = value.T
+        for c in range(2):
+
+            @pl.when((i_c ^ flip_core) == c)
+            def _(c=c):
+                for b in range(hidden_rows // per_rows):
+                    start = ((b * 2 + c) * 2 + u) * per_rows
+                    out_fc2[:, start : start + per_rows] = value[:, b * per_rows : (b + 1) * per_rows]
+
+    def place_proj(flip_core, value):
+        value = value.T
+        n = value.shape[1]
+        for c in range(2):
+
+            @pl.when((i_c ^ flip_core) == c)
+            def _(c=c):
+                out_proj[:, c * n : (c + 1) * n] = value
+
+    for copy in late_loads:
+        copy.wait()
+    for u in range(2):
+        value = parts[u * chips].astype(F32)
+        for n in range(1, chips):
+            value = value + parts[u * chips + n].astype(F32)
         out_fc1[:, u * per_rows : (u + 1) * per_rows] = value[0:shard]
-        place_fc2(u, i_c, halves(value[shard:], give.at[u]))
+        place_fc2(u, 0, halves(value[shard:], give.at[u]))
         swaps.append(link(give.at[u], got.at[u], core))
     value = proj_out[i_z].astype(F32)
     for k in range(1, chips):
         from_chip[k - 1].wait_recv()
         value = value + proj_got[k].astype(F32)
-    place_proj(i_c, halves(value, give_p))
+    place_proj(0, halves(value, give_p))
     swaps.append(link(give_p, got_p, core))
 
     for copy in from_dp:
@@ -895,8 +930,8 @@
     for copy in swaps:
         copy.wait_recv()
     for u in range(2):
-        place_fc2(u, 1 - i_c, got[u].astype(F32))
-    place_proj(1 - i_c, got_p[...].astype(F32))
+        place_fc2(u, 1, got[u].astype(F32))
+    place_proj(1, got_p[...].astype(F32))
     for copy in small:
         copy.wait_recv()
     out_vec[...] = sum_of(vec_c, 2)
@@ -945,13 +980,13 @@
     hidden_rows = parts_a[0].shape[0] - shard
     piece_rows = proj_in.shape[0]
     copies = chips + split * (ng * (np_ - 1) + ng - 1) + (chips - 1) + (dp - 1) * 4 + 2 * (chips - 1) + 5
-    hbm = pl.BlockSpec(memory_space=pl.ANY)
+    hbm = pl.BlockSpec(memory_space=pltpu.HBM)
     vmem = pl.BlockSpec(memory_space=pltpu.VMEM)
     table = tables[0].shape
     block = (table[0] // dp, table[1])
     return pl.pallas_call(
         partial(finish_kernel, sizes, split, pieces, part_w),
-        in_specs=[hbm] * (2 + pieces) + [vmem] * (pieces + 6 + 2 * chips),
+        in_specs=[hbm] * (2 + pieces) + [vmem] * pieces + [hbm] * 3 + [vmem] * 3 + [hbm] * (2 * chips),
         out_specs=[vmem] * 7,
         out_shape=[
             jax.ShapeDtypeStruct((ng, count, width), BF),
@@ -959,8 +994,8 @@
             jax.ShapeDtypeStruct((16, shard), F32),
             jax.ShapeDtypeStruct(table, F32),
             jax.ShapeDtypeStruct((shard, 2 * part_lanes), F32),
-            jax.ShapeDtypeStruct((4 * hidden_rows, part_lanes // 2), F32),
-            jax.ShapeDtypeStruct((2 * piece_rows, part_lanes // 2), F32),
+            jax.ShapeDtypeStruct((part_lanes // 2, 4 * hidden_rows), F32),
+            jax.ShapeDtypeStruct((part_lanes // 2, 2 * piece_rows), F32),
         ],
         scratch_shapes=[
             pltpu.VMEM((pieces, seq_len, lanes), BF),
@@ -994,6 +1029,11 @@
             pltpu.VMEM((piece_rows, part_lanes // 2), BF),
             pltpu.VMEM((chips, piece_rows, part_lanes), BF),
             pltpu.VMEM((chips, piece_rows, part_lanes), BF),
+            pltpu.VMEM(w.shape, BF),
+            pltpu.VMEM((ng, count, width), BF),
+            pltpu.VMEM((ng, count, width), F32),
+            pltpu.VMEM((2 * chips,) + parts_a[0].shape, BF),
+            pltpu.SemaphoreType.DMA((3 + 2 * chips,)),
             pltpu.SemaphoreType.DMA((2 * (1 + pieces) + 1 + pieces,)),
             pltpu.SemaphoreType.DMA((copies,)),
             pltpu.SemaphoreType.DMA((copies,)),
@@ -1477,6 +1517,7 @@
     entries = rel_pos_h.shape[0]
     rel = [rel[:entries, :HD][::-1], rel[128 : 128 + entries, :HD]]
     fc1_vec = vec[8:12].reshape(-1)
+    out_fc2, out_proj = out_fc2.T, out_proj.T
 
     return (
         output,

time: 538 us -> 533 us (level)
  local copies, waits for them, and re-layouts: 35.4 us -> 27.3 us
    unnamed x76 -> x66, local copies, waits for them, and re-layouts: 23.4 us -> 14.5 us
where the time goes in v7:
time: 533 us; the launch traced here: 529 us
  Pallas kernels  454 us (85%)
  local copies, waits for them, and re-layouts  27.3 us (5%)
  starting transfers between devices  15.8 us (3%)
  between operations  14.5 us (3%)
  waiting for transfers between devices  14.2 us (3%)
    pallas_call x2, Pallas kernels, attend_back(): pl.pallas_call(partial(attend_back_kernel, count, first, side, uc), grid=...  95.1 us
    pallas_call x1, Pallas kernels, finish(): pl.pallas_call(partial(finish_kernel, sizes, split, pieces, part_w), in_s...  90 us
    pallas_call x2, Pallas kernels, mlp_half(): pl.pallas_call(partial(mlp_kernel, bool(old), per), grid=(steps + dp,), i...  67.7 us
    pallas_call x1, Pallas kernels, start_exchange(): pl.pallas_call(partial(start_kernel, sizes, split), in_specs=[hbm] * 3, o...  58.8 us
    pallas_call x1, Pallas kernels, turn(): pl.pallas_call(partial(turn_kernel, sizes), in_specs=[vmem, hbm, hbm, vme...  42.7 us
    pallas_call x2, Pallas kernels, attend(): pl.pallas_call(partial(attend_kernel, heads, side, bool(old), sub), grid_...  39.6 us
    pallas_call x1, Pallas kernels, middle_rows(): pl.pallas_call(partial(middle_kernel, sizes), in_specs=[pl.BlockSpec(memo...  28.9 us
    pallas_call x1, Pallas kernels, qkv_rows(): pl.pallas_call(partial(qkv_kernel, pieces, group_heads, side, sub), grid=...  16.9 us
  transfers between devices with their start and end apart: 14, of which 2 were waited for; matrix products, arithmetic and copies ran while one was open for 2% of the time, Pallas kernels for 67%

profile of v7, /device:TPU:0, one launch (start us, length us, event | category | flops | bytes accessed | tf_op | source)
XLA Modules:
  0.0 529.1 jit_solution(18151403985156995508)
XLA Ops:
  7.2 0.6 pad_add_fusion.at
  7.8 7.2 %select.18 = (bf16[320,960]{1,0:T(8,128)(2,1)}, bf16[800,1280]{1,0:T(8,128)(2,1)}, bf16[640,1280]{1,0:T(8,128)(2,1)}) custom-call(s32[3]{0:T(128)} %pad_add_fusion.at, bf16[320,3840]{1,0:T(8,128)(2,1)} %qkv_in.1, bf16[320,5120]{1,0:T(8,128)(2,1)} %fc1_in.1, bf16[1280,1280]{1,0:T(8,128)(2,1)} %fc2_in.1, bf16[320,1280]{1,0:T(8,128)(2,1)} %proj_in.1), custom_call_target="tpu_custom_call" | custom-call | flops 1 | bytes 1 | tf_op jit(solution)/shard_map/select/pallas_call | solution.py:487
  15.2 0.7 all-gather.7.cloned.1.call-update
  16.2 1.2 concatenate.20.vec
  17.5 58.8 %start_exchange.1 = (bf16[2304,1280]{1,0:T(8,128)(2,1)}, bf16[4,320,960]{2,1,0:T(8,128)(2,1)}, bf16[4,10,320]{2,1,0:T(8,128)(2,1)}) custom-call(bf16[2,288,1280]{2,1,0:T(8,128)(2,1)} %refs_7_.1, bf16[320,960]{1,0:T(8,128)(2,1)} %get-tuple-element.88.own, bf16[10,320]{1,0:T(8,128)(2,1)} %concatenate.20.vec), custom_call_target="tpu_custom_call" | custom-call | flops 1 | bytes 1 | tf_op jit(solution)/shard_map/start_exchange/pallas_call | solution.py:602
  76.3 0.8 fusion.11
  77.1 0.1 slice_reduce_fusion
  77.4 0.7 unstack.43.gain.refs_9_
  78.1 0.7 unstack.45.shift
  78.8 0.1 copy.44
  79.0 0.1 copy.43
  79.2 0.7 concatenate.21
  79.9 0.7 fusion.5
  80.6 16.9 %qkv_rows.1 = (bf16[2304,1280]{1,0:T(8,128)(2,1)}, bf16[4,2304,256]{2,1,0:T(8,128)(2,1)}, bf16[4,2304,256]{2,1,0:T(8,128)(2,1)}, bf16[4,2304,128]{2,1,0:T(8,128)(2,1)}) custom-call(bf16[2304,1280]{1,0:T(8,128)(2,1)} %get-tuple-element.89.raw.refs_0_, f32[1,1280]{1,0:T(1,128)} %unstack.43.gain.refs_9_, f32[1,1280]{1,0:T(1,128)} %unstack.45.shift, ...), custom_call_target="tpu_custom_call" | custom-call | flops 1 | bytes 1 | tf_op jit(solution)/shard_map/qkv_rows/pallas_call | solution.py:104
  97.5 19.5 %attend.2 = (bf16[1152,320]{1,0:T(8,128)(2,1)}, f32[2304,320]{1,0:T(8,128)}, bf16[4,2304,256]{2,1,0:T(8,128)(2,1)}) custom-call(s32[1]{0:T(128)} %bitcast.7.at, bf16[4,2304,256]{2,1,0:T(8,128)(2,1)} %get-tuple-element.92.qa, bf16[4,2304,256]{2,1,0:T(8,128)(2,1)} %get-tuple-element.126.kp, bf16[4,2304,128]{2,1,0:T(8,128)(2,1)} %get-tuple-element.94.vp), custom_call_target="tpu_custom_call" | custom-call | flops 20000000000 | bytes 1 | tf_op jit(solution)/shard_map/attend/pallas_call | solution.py:179
  117.0 1.2 dynamic-slice_bitcast_fusion
  118.3 2.2 collective-permute-start
  120.5 1.9 collective-permute-start.1
  122.4 20.0 %attend.3 = (bf16[1152,320]{1,0:T(8,128)(2,1)}, f32[2304,320]{1,0:T(8,128)}, bf16[4,2304,256]{2,1,0:T(8,128)(2,1)}) custom-call(s32[1]{0:T(128)} %bitcast.at, bf16[4,2304,256]{2,1,0:T(8,128)(2,1)} %get-tuple-element.92.qa, bf16[4,2304,256]{2,1,0:T(8,128)(2,1)} %get-tuple-element.126.kp, ...), custom_call_target="tpu_custom_call", output_to_operand_aliasing={{1}: (4, {}), {2}: (5, {})} | custom-call | flops 20000000000 | bytes 1 | tf_op jit(solution)/shard_map/attend/pallas_call | solution.py:179
  142.8 0.7 squeeze.42.b1
  143.4 7.5 %collective-permute-done.refs_0_ = bf16[576,320]{1,0:T(8,128)(2,1)S(1)} collective-permute-done((bf16[576,320]{1,0:T(8,128)(2,1)S(1)}, bf16[576,320]{1,0:T(8,128)(2,1)S(1)}, u32[]{:S(2)}, u32[]{:S(2)}) %collective-permute-start) | collective-permute-done | bytes 368672 | tf_op jit(solution)/shard_map/ppermute | solution.py:1324
  150.9 1.2 copy-done.1
  152.1 28.9 %middle_rows.1 = (f32[2,288,1280]{2,1,0:T(8,128)}, bf16[2,288,1280]{2,1,0:T(8,128)(2,1)S(1)}, bf16[2,288,1280]{2,1,0:T(8,128)(2,1)S(1)}, bf16[2,2,2,288,320]{4,3,2,1,0:T(8,128)(2,1)}) custom-call(bf16[2,576,320]{2,1,0:T(8,128)(2,1)S(1)} %bitcast.33, bf16[576,320]{1,0:T(8,128)(2,1)S(1)} %collective-permute-done.refs_0_, ...), custom_call_target="tpu_custom_call" | custom-call | flops 1 | bytes 1 | tf_op jit(solution)/shard_map/middle_rows/pallas_call | solution.py:1157
  181.0 1.1 copy-done.3
  182.1 1.1 copy-done.4
  183.2 32.8 %mlp_half.2 = (f32[1152,1280]{1,0:T(8,128)}, f32[1152,1280]{1,0:T(8,128)}, bf16[4,640,1280]{2,1,0:T(8,128)(2,1)}, f32[1,1280]{1,0:T(1,128)}) custom-call(bf16[576,1280]{1,0:T(8,128)(2,1)} %bitcast.34, bf16[576,1280]{1,0:T(8,128)(2,1)} %bitcast.36, bf16[576,1280]{1,0:T(8,128)(2,1)} %bitcast.15.g_own, bf16[576,1280]{1,0:T(8,128)(2,1)} %collective-permute-done.2.g_other, ...), custom_call_target="tpu_custom_call" | custom-call | flops 35000000512 | bytes 1 | tf_op jit(solution)/shard_map/mlp_half/pallas_call | solution.py:407
  216.1 0.7 squeeze.41.b1
  216.8 34.9 %mlp_half.3 = (f32[1152,1280]{1,0:T(8,128)}, f32[1152,1280]{1,0:T(8,128)}, bf16[4,640,1280]{2,1,0:T(8,128)(2,1)}, f32[1,1280]{1,0:T(1,128)}) custom-call(bf16[576,1280]{1,0:T(8,128)(2,1)} %bitcast.35, bf16[576,1280]{1,0:T(8,128)(2,1)} %bitcast.37, bf16[576,1280]{1,0:T(8,128)(2,1)} %bitcast.15.g_own, ...), custom_call_target="tpu_custom_call", output_to_operand_aliasing={{0}: (7, {}), {1}: (8, {})} | custom-call | flops 35000000512 | bytes 1 | tf_op jit(solution)/shard_map/mlp_half/pallas_call | solution.py:407
  251.7 0.3 reduce-scatter.8.cloned.1.call-start
  252.2 0.7 unstack.57.shift
  252.9 0.8 fusion.hot
  253.7 42.7 %turn.1 = (bf16[2,288,1280]{2,1,0:T(8,128)(2,1)}, f32[2,288,1280]{2,1,0:T(8,128)}, bf16[8,144,640]{2,1,0:T(8,128)(2,1)}, bf16[2,320,1280]{2,1,0:T(8,128)(2,1)}, f32[8,1280]{1,0:T(8,128)}) custom-call(f32[2,288,1280]{2,1,0:T(8,128)} %get-tuple-element.103.mid, f32[1152,1280]{1,0:T(8,128)} %get-tuple-element.109.gn, f32[1152,1280]{1,0:T(8,128)} %get-tuple-element.110.out, ...), custom_call_target="tpu_custom_call" | custom-call | flops 1 | bytes 1 | tf_op jit(solution)/shard_map/turn/pallas_call | solution.py:1293
  296.6 0.1 reshape.100
  296.7 0.1 concatenate.25
  296.9 0.1 reshape.101
  297.0 0.8 slice.68
  297.8 0.6 pad_maximum_fusion.refs_10_
  298.5 3.6 split_columns.2
  302.1 4.5 collective-permute-start.3
  306.6 0.4 collective-permute-start.4
  307.0 1.9 collective-permute-start.5
  309.0 47.0 %attend_back.2 = (bf16[2304,480]{1,0:T(8,128)(2,1)}, f32[256,128]{1,0:T(8,128)}) custom-call(bf16[4,2304,256]{2,1,0:T(8,128)(2,1)} %get-tuple-element.114.qa_ref, bf16[4,2304,256]{2,1,0:T(8,128)(2,1)} %get-tuple-element.126.kp, bf16[4,2304,128]{2,1,0:T(8,128)(2,1)} %get-tuple-element.94.vp, f32[2304,320]{1,0:T(8,128)} %get-tuple-element.115.of, ...), custom_call_target="tpu_custom_call" | custom-call | flops 49999998976 | bytes 1 | tf_op jit(solution)/shard_map/attend_back/pallas_call | solution.py:317
  356.1 5.9 %reduce-scatter.6.cloned.1.call-done.value = bf16[640,1280]{1,0:T(8,128)(2,1)} async-done(((bf16[2560,1280]{1,0:T(8,128)(2,1)}), bf16[640,1280]{1,0:T(8,128)(2,1)}) %reduce-scatter.6.cloned.1.call-update) | async-done | bytes 1638416 | tf_op jit(solution)/shard_map/reduce_scatter | solution.py:1459
  362.0 3.2 split_columns.3
  365.2 1.5 collective-permute-start.6
  366.6 2.4 collective-permute-start.7
  369.0 0.5 collective-permute-start.8
  369.6 48.0 %attend_back.3 = (bf16[2304,480]{1,0:T(8,128)(2,1)}, f32[256,128]{1,0:T(8,128)}) custom-call(bf16[4,2304,256]{2,1,0:T(8,128)(2,1)} %get-tuple-element.114.qa_ref, bf16[4,2304,256]{2,1,0:T(8,128)(2,1)} %get-tuple-element.126.kp, bf16[4,2304,128]{2,1,0:T(8,128)(2,1)} %get-tuple-element.94.vp, f32[2304,320]{1,0:T(8,128)} %get-tuple-element.115.of, ...), custom_call_target="tpu_custom_call" | custom-call | flops 49999998976 | bytes 1 | tf_op jit(solution)/shard_map/attend_back/pallas_call | solution.py:317
  417.6 0.8 copy-done.11
  418.4 0.8 copy-done.12
  419.2 0.8 copy-done.13
  420.0 90.0 %finish.1 = (bf16[2,288,1280]{2,1,0:T(8,128)(2,1)}, f32[320,480]{1,0:T(8,128)}, f32[16,320]{1,0:T(8,128)}, f32[256,128]{1,0:T(8,128)}, f32[320,640]{1,0:T(8,128)...) custom-call(bf16[2304,1280]{1,0:T(8,128)(2,1)} %get-tuple-element.89.raw.refs_0_, ...), custom_call_target="tpu_custom_call" | custom-call | flops 1 | bytes 1 | tf_op jit(solution)/shard_map/finish/pallas_call | solution.py:987
  510.0 1.6 slice_reduce_fusion.10
  511.6 0.7 slice.76
  512.3 0.8 fusion.10
  513.2 0.7 copy.50
  513.9 0.7 copy.51
  514.6 0.7 reshape.102
  515.3 2.6 copy.62
  517.9 1.1 copy.63
  519.1 0.8 copy.64
  519.9 0.7 copy.65
  520.6 0.9 copy.66
  521.5 0.9 copy.67
  (108 shorter events, 1.7 us)
Async XLA Ops:
  7.2 143.7 %all-gather.5.cloned.1.call-start = ((), (), s32[]{:S(2)}) async-start(), calls=%async_computation.6 | async-start | bytes 10240000 | tf_op jit(solution)/shard_map/all_gather | solution.py:1402
  15.0 1.0 copy-start.19
  15.0 1.0 copy-start.20
  15.0 1.0 copy-start.21
  15.0 1.1 copy-start.22
  15.1 1.1 copy-start.23
  15.1 1.1 copy-start.24
  15.1 1.1 copy-start.25
  15.1 1.1 copy-start.26
  15.1 1.1 copy-start.27
  15.1 63.7 %copy-start.15 = (bf16[95,80]{0,1:T(8,128)(2,1)S(1)}, bf16[95,80]{0,1:T(8,128)(2,1)}, u32[]{:S(2)}) copy-start(bf16[95,80]{0,1:T(8,128)(2,1)} %param.32) | copy-start | bytes 45604
  15.1 63.8 %copy-start.16 = (bf16[95,80]{0,1:T(8,128)(2,1)S(1)}, bf16[95,80]{0,1:T(8,128)(2,1)}, u32[]{:S(2)}) copy-start(bf16[95,80]{0,1:T(8,128)(2,1)} %param.31) | copy-start | bytes 45604
  15.2 201.7 %all-gather.7.cloned.1.call-start = ((), (), s32[]{:S(2)}) async-start(), calls=%async_computation.7 | async-start | bytes 8192000 | tf_op jit(solution)/shard_map/all_gather | solution.py:1403
  15.9 282.6 %reduce-scatter.4.cloned.1.call-start = ((), (), s32[]{:S(2)}) async-start(), calls=%async_computation.3 | async-start | bytes 8192000 | tf_op jit(solution)/shard_map/reduce_scatter | solution.py:1459
  118.3 32.6 %collective-permute-start = (bf16[576,320]{1,0:T(8,128)(2,1)S(1)}, bf16[576,320]{1,0:T(8,128)(2,1)S(1)}, u32[]{:S(2)}, u32[]{:S(2)}) collective-permute-start(bf16[576,320]{1,0:T(8,128)(2,1)S(1)} %get-tuple-element.212), channel_id=1, source_target_pairs={{0,4},{2,6},{4,0},{6,2},{1,5},{3,7},{5,1},{7,3},{8,12},{10,14},{12... | collective-permute-start | bytes 1105928 | tf_op jit(solution)/shard_map/ppermute | solution.py:1324
  120.5 30.4 %collective-permute-start.1 = (bf16[576,320]{1,0:T(8,128)(2,1)S(1)}, bf16[576,320]{1,0:T(8,128)(2,1)S(1)}, u32[]{:S(2)}, u32[]{:S(2)}) collective-permute-start(bf16[576,320]{1,0:T(8,128)(2,1)S(1)} %get-tuple-element.211), channel_id=1, source_target_pairs={{0,6},{2,4},{4,2},{6,0},{1,7},{3,5},{5,3},{7,1},{8,14},{10,12},{12... | collective-permute-start | bytes 1105928 | tf_op jit(solution)/shard_map/ppermute | solution.py:1324
  122.4 60.8 %collective-permute-start.2 = (bf16[576,1280]{1,0:T(8,128)(2,1)}, bf16[576,1280]{1,0:T(8,128)(2,1)}, u32[]{:S(2)}, u32[]{:S(2)}) collective-permute-start(bf16[576,1280]{1,0:T(8,128)(2,1)} %bitcast.15.g_own), channel_id=1, source_target_pairs={{0,1},{1,0},{2,3},{3,2},{4,5},{5,4},{6,7},{7,6},{8,9},{9,8},{10,11... | collective-permute-start | bytes 4423688 | tf_op jit(solution)/shard_map/ppermute | solution.py:1324
  122.4 28.5 %copy-start = (bf16[2,288,1280]{2,1,0:T(8,128)(2,1)S(1)}, bf16[2,288,1280]{2,1,0:T(8,128)(2,1)}, u32[]{:S(2)}) copy-start(bf16[2,288,1280]{2,1,0:T(8,128)(2,1)} %refs_7_.1) | copy-start | bytes 4423684
  142.5 38.5 %copy-start.2 = (f32[1,1280]{1,0:T(1,128)}, f32[1,1280]{1,0:T(1,128)S(1)}, u32[]{:S(2)}) copy-start(f32[1,1280]{1,0:T(1,128)S(1)} %unstack.53.refs_5_.gain) | copy-start | bytes 15364
  150.9 1.2 copy-start.1
  181.0 1.1 copy-start.3
  182.1 1.1 copy-start.4
  216.1 145.9 %reduce-scatter.6.cloned.1.call-start = ((), (), s32[]{:S(2)}) async-start(), calls=%async_computation.4 | async-start | bytes 8192000 | tf_op jit(solution)/shard_map/reduce_scatter | solution.py:1459
  251.7 168.2 %reduce-scatter.8.cloned.1.call-start = ((), (), s32[]{:S(2)}) async-start(), calls=%async_computation.5 | async-start | bytes 2048000 | tf_op jit(solution)/shard_map/reduce_scatter | solution.py:1459
  253.7 42.7 %copy-start.18 = (f32[1,1280]{1,0:T(1,128)S(1)}, f32[1,1280]{1,0:T(1,128)}, u32[]{:S(2)}) copy-start(f32[1,1280]{1,0:T(1,128)} %get-tuple-element.142) | copy-start | bytes 15364
  253.7 42.8 %copy-start.17 = (f32[1,1280]{1,0:T(1,128)S(1)}, f32[1,1280]{1,0:T(1,128)}, u32[]{:S(2)}) copy-start(f32[1,1280]{1,0:T(1,128)} %get-tuple-element.141) | copy-start | bytes 15364
  302.1 53.9 %collective-permute-start.3 = (bf16[640,320]{1,0:T(8,128)(2,1)}, bf16[640,320]{1,0:T(8,128)(2,1)S(1)}, u32[]{:S(2)}, u32[]{:S(2)}) collective-permute-start(bf16[640,320]{1,0:T(8,128)(2,1)} %get-tuple-element.122), channel_id=1, source_target_pairs={{0,2},{2,0},{4,6},{6,4},{1,3},{3,1},{5,7},{7,5},{8,10},{10,8},{12,... | collective-permute-start | bytes 1228808 | tf_op jit(solution)/shard_map/ppermute | solution.py:1324
  306.6 49.4 %collective-permute-start.4 = (bf16[640,320]{1,0:T(8,128)(2,1)}, bf16[640,320]{1,0:T(8,128)(2,1)S(1)}, u32[]{:S(2)}, u32[]{:S(2)}) collective-permute-start(bf16[640,320]{1,0:T(8,128)(2,1)} %get-tuple-element.123), channel_id=1, source_target_pairs={{0,4},{2,6},{4,0},{6,2},{1,5},{3,7},{5,1},{7,3},{8,12},{10,14},{12... | collective-permute-start | bytes 1228808 | tf_op jit(solution)/shard_map/ppermute | solution.py:1324
  307.0 49.0 %collective-permute-start.5 = (bf16[640,320]{1,0:T(8,128)(2,1)}, bf16[640,320]{1,0:T(8,128)(2,1)}, u32[]{:S(2)}, u32[]{:S(2)}) collective-permute-start(bf16[640,320]{1,0:T(8,128)(2,1)} %get-tuple-element.124), channel_id=1, source_target_pairs={{0,6},{2,4},{4,2},{6,0},{1,7},{3,5},{5,3},{7,1},{8,14},{10,12},{12... | collective-permute-start | bytes 1228808 | tf_op jit(solution)/shard_map/ppermute | solution.py:1324
  356.0 61.6 %copy-start.9 = (bf16[640,320]{1,0:T(8,128)(2,1)}, bf16[640,320]{1,0:T(8,128)(2,1)S(1)}, u32[]{:S(2)}) copy-start(bf16[640,320]{1,0:T(8,128)(2,1)S(1)} %collective-permute-done.3.refs_13_) | copy-start | bytes 1228804
  356.0 61.5 %copy-start.10 = (bf16[640,320]{1,0:T(8,128)(2,1)}, bf16[640,320]{1,0:T(8,128)(2,1)S(1)}, u32[]{:S(2)}) copy-start(bf16[640,320]{1,0:T(8,128)(2,1)S(1)} %collective-permute-done.4.refs_14_) | copy-start | bytes 1228804
  365.2 52.4 %collective-permute-start.6 = (bf16[640,320]{1,0:T(8,128)(2,1)}, bf16[640,320]{1,0:T(8,128)(2,1)S(1)}, u32[]{:S(2)}, u32[]{:S(2)}) collective-permute-start(bf16[640,320]{1,0:T(8,128)(2,1)} %get-tuple-element.131), channel_id=1, source_target_pairs={{0,2},{2,0},{4,6},{6,4},{1,3},{3,1},{5,7},{7,5},{8,10},{10,8},{12,... | collective-permute-start | bytes 1228808 | tf_op jit(solution)/shard_map/ppermute | solution.py:1324
  366.6 51.8 %collective-permute-start.7 = (bf16[640,320]{1,0:T(8,128)(2,1)}, bf16[640,320]{1,0:T(8,128)(2,1)S(1)}, u32[]{:S(2)}, u32[]{:S(2)}) collective-permute-start(bf16[640,320]{1,0:T(8,128)(2,1)} %get-tuple-element.132), channel_id=1, source_target_pairs={{0,4},{2,6},{4,0},{6,2},{1,5},{3,7},{5,1},{7,3},{8,12},{10,14},{12... | collective-permute-start | bytes 1228808 | tf_op jit(solution)/shard_map/ppermute | solution.py:1324
  369.0 50.2 %collective-permute-start.8 = (bf16[640,320]{1,0:T(8,128)(2,1)}, bf16[640,320]{1,0:T(8,128)(2,1)S(1)}, u32[]{:S(2)}, u32[]{:S(2)}) collective-permute-start(bf16[640,320]{1,0:T(8,128)(2,1)} %get-tuple-element.133), channel_id=1, source_target_pairs={{0,6},{2,4},{4,2},{6,0},{1,7},{3,5},{5,3},{7,1},{8,14},{10,12},{12... | collective-permute-start | bytes 1228808 | tf_op jit(solution)/shard_map/ppermute | solution.py:1324
  417.6 0.8 copy-start.11
  418.4 0.8 copy-start.12
  419.2 0.8 copy-start.13
  510.0 8.0 %copy-start.5 = (bf16[2,288,1280]{2,1,0:T(8,128)(2,1)S(1)}, bf16[2,288,1280]{2,1,0:T(8,128)(2,1)}, u32[]{:S(2)}) copy-start(bf16[2,288,1280]{2,1,0:T(8,128)(2,1)} %get-tuple-element.245) | copy-start | bytes 4423684
  515.3 3.8 copy-start.8
  517.9 2.0 copy-start.14
  517.9 2.7 copy-start.7
  517.9 3.5 copy-start.6
Sparse Core Ops, SparseCore 0:
  15.3 109.8 all-gather.4
  127.0 72.3 all-gather.6
  216.2 70.4 reduce-scatter.3
  289.6 72.3 reduce-scatter.5
  364.8 31.3 reduce-scatter.7

commit v8 on v7

--- a/solution.py
+++ b/solution.py
@@ -205,7 +205,7 @@
     )(jnp.stack([group]), qa, kp, vp, *old)
 
 
-def attend_back_kernel(heads, first, side, uc, qa_ref, kp, vp, of, go, tables, hot, dx, gt, kt, dop, dk, dv, dq):
+def attend_back_kernel(heads, first, side, uc, qa_ref, kp, vp, of, go, tables, hot, held, dx, gt, passed, kt, dop, dk, dv, dq, sem):
     seq_len = kp.shape[1]
     tb = qa_ref.shape[1]
     h = pl.program_id(0)
@@ -217,6 +217,7 @@
     @pl.when((h == 0) & (step == 0))
     def _():
         gt[...] = jnp.zeros_like(gt)
+        pltpu.make_async_copy(held, passed, sem.at[0]).start()
 
         blocks, high, wide = go.shape
         total_lanes = of.shape[1]
@@ -293,6 +294,10 @@
     dq[base, :] = acc[:, :HD] * scale + dot(both, tables[...])
     gt[...] += dot(both, qa[:, 0:128], TN)
 
+    @pl.when((h == heads - 1) & (step == last))
+    def _():
+        pltpu.make_async_copy(held, passed, sem.at[0]).wait()
+
     width = heads * HD
     for n in range(heads):
 
@@ -309,7 +314,7 @@
             lax.fori_loop(0, 9, post, 0)
 
 
-def attend_back(first, count, qa, kp, vp, of, go, tables, hot, side, tb=768, uc=256):
+def attend_back(first, count, qa, kp, vp, of, go, tables, hot, held, side, tb=768, uc=256):
     heads, seq_len, _ = qa.shape
     lanes = heads * HD
     if go.shape[2] == lanes:
@@ -325,11 +330,13 @@
             whole(*go.shape),
             whole(256, HD),
             whole(side, seq_len),
-        ],
-        out_specs=[whole(seq_len, 3 * count * HD), whole(256, 128)],
+            pl.BlockSpec(memory_space=pltpu.HBM),
+        ],
+        out_specs=[whole(seq_len, 3 * count * HD), whole(256, 128), pl.BlockSpec(memory_space=pltpu.HBM)],
         out_shape=[
             jax.ShapeDtypeStruct((seq_len, 3 * count * HD), BF),
             jax.ShapeDtypeStruct((256, 128), F32),
+            jax.ShapeDtypeStruct(held.shape, held.dtype),
         ],
         scratch_shapes=[
             pltpu.VMEM((HD + 2 * side, seq_len), BF),
@@ -337,11 +344,12 @@
             pltpu.VMEM((seq_len, 128), F32),
             pltpu.VMEM((seq_len, 128), F32),
             pltpu.VMEM((seq_len, HD), F32),
+            pltpu.SemaphoreType.DMA((1,)),
         ],
         compiler_params=params(2),
         cost_estimate=busy(50),
         name="attend_back",
-    )(qa, kp, vp, of, go, tables, hot)
+    )(qa, kp, vp, of, go, tables, hot, held)
 
 
 def mlp_kernel(aliased, per, n_own, n_other, g_own, g_other, w1, b1, w2, *refs):
@@ -1480,8 +1488,8 @@
     dx = []
     grad_tables = []
     for q in range(pieces):
-        rows, table = attend_back(
-            q * core_heads, core_heads, query_a, key_rows, value_rows, att_f, grad_heads, back_tables, col_hot, side
+        rows, table, output = attend_back(
+            q * core_heads, core_heads, query_a, key_rows, value_rows, att_f, grad_heads, back_tables, col_hot, output, side
         )
         if q == 0:
             rows, *sum_a = tie(rows, *sum_a)

time: 533 us -> 536 us (level)
  Pallas kernels: 454 us -> 463 us
    pallas_call x2, Pallas kernels: 95.1 us -> 104 us  [attend_back(): pl.pallas_call(partial(attend_back_kernel, count, first, side, uc), grid=...]
    unnamed x66 -> x63, local copies, waits for them, and re-layouts: 14.5 us -> 13.4 us
  transfers between devices with their start and end apart: 14 -> 14, of which waited for: 2 -> 2; matrix products, arithmetic and copies ran while one was open for 2% -> 2% of each run, Pallas kernels for 67% -> 69%
where the time goes in v8:
time: 536 us; the launch traced here: 532 us
  Pallas kernels  463 us (86%)
  local copies, waits for them, and re-layouts  26.3 us (5%)
  starting transfers between devices  15.8 us (3%)
  between operations  14.5 us (3%)
  waiting for transfers between devices  9.15 us (2%)
    pallas_call x2, Pallas kernels, attend_back(): pl.pallas_call(partial(attend_back_kernel, count, first, side, uc), grid=...  104 us
    pallas_call x1, Pallas kernels, finish(): pl.pallas_call(partial(finish_kernel, sizes, split, pieces, part_w), in_s...  89.9 us
    pallas_call x2, Pallas kernels, mlp_half(): pl.pallas_call(partial(mlp_kernel, bool(old), per), grid=(steps + dp,), i...  67.8 us
    pallas_call x1, Pallas kernels, start_exchange(): pl.pallas_call(partial(start_kernel, sizes, split), in_specs=[hbm] * 3, o...  58.8 us
    pallas_call x1, Pallas kernels, turn(): pl.pallas_call(partial(turn_kernel, sizes), in_specs=[vmem, hbm, hbm, vme...  42.7 us
    pallas_call x2, Pallas kernels, attend(): pl.pallas_call(partial(attend_kernel, heads, side, bool(old), sub), grid_...  39.5 us
    pallas_call x1, Pallas kernels, middle_rows(): pl.pallas_call(partial(middle_kernel, sizes), in_specs=[pl.BlockSpec(memo...  28.9 us
    pallas_call x1, Pallas kernels, qkv_rows(): pl.pallas_call(partial(qkv_kernel, pieces, group_heads, side, sub), grid=...  17 us
  transfers between devices with their start and end apart: 14, of which 2 were waited for; matrix products, arithmetic and copies ran while one was open for 2% of the time, Pallas kernels for 69%

profile of v8, /device:TPU:0, one launch (start us, length us, event | category | flops | bytes accessed | tf_op | source)
XLA Modules:
  0.0 532.3 jit_solution(2077243137429651920)
XLA Ops:
  7.2 0.6 pad_add_fusion.at
  7.8 7.2 %select.18 = (bf16[320,960]{1,0:T(8,128)(2,1)}, bf16[800,1280]{1,0:T(8,128)(2,1)}, bf16[640,1280]{1,0:T(8,128)(2,1)}) custom-call(s32[3]{0:T(128)} %pad_add_fusion.at, bf16[320,3840]{1,0:T(8,128)(2,1)} %qkv_in.1, bf16[320,5120]{1,0:T(8,128)(2,1)} %fc1_in.1, bf16[1280,1280]{1,0:T(8,128)(2,1)} %fc2_in.1, bf16[320,1280]{1,0:T(8,128)(2,1)} %proj_in.1), custom_call_target="tpu_custom_call" | custom-call | flops 1 | bytes 1 | tf_op jit(solution)/shard_map/select/pallas_call | solution.py:495
  15.2 0.7 all-gather.7.cloned.1.call-update
  16.2 1.2 concatenate.20.vec
  17.5 58.8 %start_exchange.1 = (bf16[2304,1280]{1,0:T(8,128)(2,1)}, bf16[4,320,960]{2,1,0:T(8,128)(2,1)}, bf16[4,10,320]{2,1,0:T(8,128)(2,1)}) custom-call(bf16[2,288,1280]{2,1,0:T(8,128)(2,1)} %refs_7_.1, bf16[320,960]{1,0:T(8,128)(2,1)} %get-tuple-element.90.own, bf16[10,320]{1,0:T(8,128)(2,1)} %concatenate.20.vec), custom_call_target="tpu_custom_call" | custom-call | flops 1 | bytes 1 | tf_op jit(solution)/shard_map/start_exchange/pallas_call | solution.py:610
  76.3 0.8 fusion.11
  77.1 0.1 slice_reduce_fusion
  77.3 0.7 unstack.43.gain.refs_9_
  78.0 0.7 unstack.45.shift
  78.8 0.1 copy.44
  78.9 0.1 copy.43
  79.1 0.1 fusion.12
  79.2 0.7 concatenate.21
  79.9 0.7 fusion.5
  80.6 17.0 %qkv_rows.1 = (bf16[2304,1280]{1,0:T(8,128)(2,1)}, bf16[4,2304,256]{2,1,0:T(8,128)(2,1)}, bf16[4,2304,256]{2,1,0:T(8,128)(2,1)}, bf16[4,2304,128]{2,1,0:T(8,128)(2,1)}) custom-call(bf16[2304,1280]{1,0:T(8,128)(2,1)} %get-tuple-element.91.raw.refs_0_, f32[1,1280]{1,0:T(1,128)} %unstack.43.gain.refs_9_, f32[1,1280]{1,0:T(1,128)} %unstack.45.shift, ...), custom_call_target="tpu_custom_call" | custom-call | flops 1 | bytes 1 | tf_op jit(solution)/shard_map/qkv_rows/pallas_call | solution.py:104
  97.5 19.5 %attend.2 = (bf16[1152,320]{1,0:T(8,128)(2,1)}, f32[2304,320]{1,0:T(8,128)}, bf16[4,2304,256]{2,1,0:T(8,128)(2,1)}) custom-call(s32[1]{0:T(128)} %bitcast.7.at, bf16[4,2304,256]{2,1,0:T(8,128)(2,1)} %get-tuple-element.94.qa, bf16[4,2304,256]{2,1,0:T(8,128)(2,1)} %get-tuple-element.127.kp, bf16[4,2304,128]{2,1,0:T(8,128)(2,1)} %get-tuple-element.96.vp), custom_call_target="tpu_custom_call" | custom-call | flops 20000000000 | bytes 1 | tf_op jit(solution)/shard_map/attend/pallas_call | solution.py:179
  117.1 1.2 dynamic-slice_bitcast_fusion
  118.3 2.2 collective-permute-start
  120.5 1.9 collective-permute-start.1
  122.5 20.0 %attend.3 = (bf16[1152,320]{1,0:T(8,128)(2,1)}, f32[2304,320]{1,0:T(8,128)}, bf16[4,2304,256]{2,1,0:T(8,128)(2,1)}) custom-call(s32[1]{0:T(128)} %bitcast.at, bf16[4,2304,256]{2,1,0:T(8,128)(2,1)} %get-tuple-element.94.qa, bf16[4,2304,256]{2,1,0:T(8,128)(2,1)} %get-tuple-element.127.kp, ...), custom_call_target="tpu_custom_call", output_to_operand_aliasing={{1}: (4, {}), {2}: (5, {})} | custom-call | flops 20000000000 | bytes 1 | tf_op jit(solution)/shard_map/attend/pallas_call | solution.py:179
  142.8 0.7 squeeze.42.b1
  143.5 7.5 %collective-permute-done.refs_0_ = bf16[576,320]{1,0:T(8,128)(2,1)S(1)} collective-permute-done((bf16[576,320]{1,0:T(8,128)(2,1)S(1)}, bf16[576,320]{1,0:T(8,128)(2,1)S(1)}, u32[]{:S(2)}, u32[]{:S(2)}) %collective-permute-start) | collective-permute-done | bytes 368672 | tf_op jit(solution)/shard_map/ppermute | solution.py:1332
  151.0 1.2 copy-done.1
  152.1 28.9 %middle_rows.1 = (f32[2,288,1280]{2,1,0:T(8,128)}, bf16[2,288,1280]{2,1,0:T(8,128)(2,1)S(1)}, bf16[2,288,1280]{2,1,0:T(8,128)(2,1)S(1)}, bf16[2,2,2,288,320]{4,3,2,1,0:T(8,128)(2,1)}) custom-call(bf16[2,576,320]{2,1,0:T(8,128)(2,1)S(1)} %bitcast.33, bf16[576,320]{1,0:T(8,128)(2,1)S(1)} %collective-permute-done.refs_0_, ...), custom_call_target="tpu_custom_call" | custom-call | flops 1 | bytes 1 | tf_op jit(solution)/shard_map/middle_rows/pallas_call | solution.py:1165
  181.0 1.1 copy-done.3
  182.1 1.1 copy-done.4
  183.2 32.8 %mlp_half.2 = (f32[1152,1280]{1,0:T(8,128)}, f32[1152,1280]{1,0:T(8,128)}, bf16[4,640,1280]{2,1,0:T(8,128)(2,1)}, f32[1,1280]{1,0:T(1,128)}) custom-call(bf16[576,1280]{1,0:T(8,128)(2,1)} %bitcast.34, bf16[576,1280]{1,0:T(8,128)(2,1)} %bitcast.36, bf16[576,1280]{1,0:T(8,128)(2,1)} %bitcast.15.g_own, bf16[576,1280]{1,0:T(8,128)(2,1)} %collective-permute-done.2.g_other, ...), custom_call_target="tpu_custom_call" | custom-call | flops 35000000512 | bytes 1 | tf_op jit(solution)/shard_map/mlp_half/pallas_call | solution.py:415
  216.2 0.7 squeeze.41.b1
  216.8 34.9 %mlp_half.3 = (f32[1152,1280]{1,0:T(8,128)}, f32[1152,1280]{1,0:T(8,128)}, bf16[4,640,1280]{2,1,0:T(8,128)(2,1)}, f32[1,1280]{1,0:T(1,128)}) custom-call(bf16[576,1280]{1,0:T(8,128)(2,1)} %bitcast.35, bf16[576,1280]{1,0:T(8,128)(2,1)} %bitcast.37, bf16[576,1280]{1,0:T(8,128)(2,1)} %bitcast.15.g_own, ...), custom_call_target="tpu_custom_call", output_to_operand_aliasing={{0}: (7, {}), {1}: (8, {})} | custom-call | flops 35000000512 | bytes 1 | tf_op jit(solution)/shard_map/mlp_half/pallas_call | solution.py:415
  251.8 0.3 reduce-scatter.8.cloned.1.call-start
  252.1 0.7 unstack.57.shift
  252.9 0.8 fusion.hot
  253.7 42.7 %turn.1 = (bf16[2,288,1280]{2,1,0:T(8,128)(2,1)}, f32[2,288,1280]{2,1,0:T(8,128)}, bf16[8,144,640]{2,1,0:T(8,128)(2,1)}, bf16[2,320,1280]{2,1,0:T(8,128)(2,1)}, f32[8,1280]{1,0:T(8,128)}) custom-call(f32[2,288,1280]{2,1,0:T(8,128)} %get-tuple-element.107.mid, f32[1152,1280]{1,0:T(8,128)} %get-tuple-element.113.gn, f32[1152,1280]{1,0:T(8,128)} %get-tuple-element.114.out, ...), custom_call_target="tpu_custom_call" | custom-call | flops 1 | bytes 1 | tf_op jit(solution)/shard_map/turn/pallas_call | solution.py:1301
  296.7 0.1 reshape.100
  296.8 0.1 concatenate.25
  297.0 0.1 reshape.101
  297.1 0.8 slice.68
  297.9 0.6 pad_maximum_fusion.refs_10_
  298.6 3.6 split_columns.2
  302.2 4.5 collective-permute-start.3
  306.7 0.3 collective-permute-start.4
  307.0 2.1 collective-permute-start.5
  309.0 52.0 %attend_back.2 = (bf16[2304,480]{1,0:T(8,128)(2,1)}, f32[256,128]{1,0:T(8,128)}, bf16[2,288,1280]{2,1,0:T(8,128)(2,1)}) custom-call(bf16[4,2304,256]{2,1,0:T(8,128)(2,1)} %get-tuple-element.99.qa_ref, bf16[4,2304,256]{2,1,0:T(8,128)(2,1)} %get-tuple-element.127.kp, bf16[4,2304,128]{2,1,0:T(8,128)(2,1)} %get-tuple-element.96.vp, ...), custom_call_target="tpu_custom_call" | custom-call | flops 49999998976 | bytes 1 | tf_op jit(solution)/shard_map/attend_back/pallas_call | solution.py:322
  361.1 0.9 reduce-scatter.6.cloned.1.call-done.value
  361.9 3.2 split_columns.3
  365.1 1.5 collective-permute-start.6
  366.6 2.4 collective-permute-start.7
  369.0 0.5 collective-permute-start.8
  369.5 52.3 %attend_back.3 = (bf16[2304,480]{1,0:T(8,128)(2,1)}, f32[256,128]{1,0:T(8,128)}, bf16[2,288,1280]{2,1,0:T(8,128)(2,1)}) custom-call(bf16[4,2304,256]{2,1,0:T(8,128)(2,1)} %get-tuple-element.99.qa_ref, bf16[4,2304,256]{2,1,0:T(8,128)(2,1)} %get-tuple-element.127.kp, bf16[4,2304,128]{2,1,0:T(8,128)(2,1)} %get-tuple-element.96.vp, ...), custom_call_target="tpu_custom_call" | custom-call | flops 49999998976 | bytes 1 | tf_op jit(solution)/shard_map/attend_back/pallas_call | solution.py:322
  421.9 0.8 copy-done.10
  422.6 0.8 copy-done.11
  423.4 0.8 copy-done.12
  424.2 89.9 %finish.1 = (bf16[2,288,1280]{2,1,0:T(8,128)(2,1)}, f32[320,480]{1,0:T(8,128)}, f32[16,320]{1,0:T(8,128)}, f32[256,128]{1,0:T(8,128)}, f32[320,640]{1,0:T(8,128)...) custom-call(bf16[2304,1280]{1,0:T(8,128)(2,1)} %get-tuple-element.91.raw.refs_0_, ...), custom_call_target="tpu_custom_call" | custom-call | flops 1 | bytes 1 | tf_op jit(solution)/shard_map/finish/pallas_call | solution.py:995
  514.1 1.6 slice_reduce_fusion.10
  515.8 0.7 slice.76
  516.5 0.7 reshape.102
  517.2 0.9 fusion.10
  518.1 0.7 copy.50
  518.8 0.7 copy.51
  519.5 2.7 copy.61
  522.2 0.8 copy.62
  523.0 0.7 copy.63
  523.7 0.9 copy.64
  524.6 0.9 copy.65
  (105 shorter events, 1.6 us)
Async XLA Ops:
  7.2 143.8 %all-gather.5.cloned.1.call-start = ((), (), s32[]{:S(2)}) async-start(), calls=%async_computation.6 | async-start | bytes 10240000 | tf_op jit(solution)/shard_map/all_gather | solution.py:1410
  15.0 1.0 copy-start.19
  15.0 1.0 copy-start.20
  15.0 1.0 copy-start.21
  15.0 1.0 copy-start.22
  15.1 1.0 copy-start.23
  15.1 1.0 copy-start.24
  15.1 1.0 copy-start.25
  15.1 1.0 copy-start.26
  15.1 1.0 copy-start.18
  15.1 63.7 %copy-start.14 = (bf16[95,80]{0,1:T(8,128)(2,1)S(1)}, bf16[95,80]{0,1:T(8,128)(2,1)}, u32[]{:S(2)}) copy-start(bf16[95,80]{0,1:T(8,128)(2,1)} %param.32) | copy-start | bytes 45604
  15.2 63.8 %copy-start.15 = (bf16[95,80]{0,1:T(8,128)(2,1)S(1)}, bf16[95,80]{0,1:T(8,128)(2,1)}, u32[]{:S(2)}) copy-start(bf16[95,80]{0,1:T(8,128)(2,1)} %param.31) | copy-start | bytes 45604
  15.2 201.7 %all-gather.7.cloned.1.call-start = ((), (), s32[]{:S(2)}) async-start(), calls=%async_computation.7 | async-start | bytes 8192000 | tf_op jit(solution)/shard_map/all_gather | solution.py:1411
  15.9 282.6 %reduce-scatter.4.cloned.1.call-start = ((), (), s32[]{:S(2)}) async-start(), calls=%async_computation.3 | async-start | bytes 8192000 | tf_op jit(solution)/shard_map/reduce_scatter | solution.py:1467
  118.3 32.6 %collective-permute-start = (bf16[576,320]{1,0:T(8,128)(2,1)S(1)}, bf16[576,320]{1,0:T(8,128)(2,1)S(1)}, u32[]{:S(2)}, u32[]{:S(2)}) collective-permute-start(bf16[576,320]{1,0:T(8,128)(2,1)S(1)} %get-tuple-element.216), channel_id=1, source_target_pairs={{0,4},{2,6},{4,0},{6,2},{1,5},{3,7},{5,1},{7,3},{8,12},{10,14},{12... | collective-permute-start | bytes 1105928 | tf_op jit(solution)/shard_map/ppermute | solution.py:1332
  120.5 30.4 %collective-permute-start.1 = (bf16[576,320]{1,0:T(8,128)(2,1)S(1)}, bf16[576,320]{1,0:T(8,128)(2,1)S(1)}, u32[]{:S(2)}, u32[]{:S(2)}) collective-permute-start(bf16[576,320]{1,0:T(8,128)(2,1)S(1)} %get-tuple-element.215), channel_id=1, source_target_pairs={{0,6},{2,4},{4,2},{6,0},{1,7},{3,5},{5,3},{7,1},{8,14},{10,12},{12... | collective-permute-start | bytes 1105928 | tf_op jit(solution)/shard_map/ppermute | solution.py:1332
  122.5 60.8 %collective-permute-start.2 = (bf16[576,1280]{1,0:T(8,128)(2,1)}, bf16[576,1280]{1,0:T(8,128)(2,1)}, u32[]{:S(2)}, u32[]{:S(2)}) collective-permute-start(bf16[576,1280]{1,0:T(8,128)(2,1)} %bitcast.15.g_own), channel_id=1, source_target_pairs={{0,1},{1,0},{2,3},{3,2},{4,5},{5,4},{6,7},{7,6},{8,9},{9,8},{10,11... | collective-permute-start | bytes 4423688 | tf_op jit(solution)/shard_map/ppermute | solution.py:1332
  122.5 28.5 %copy-start = (bf16[2,288,1280]{2,1,0:T(8,128)(2,1)S(1)}, bf16[2,288,1280]{2,1,0:T(8,128)(2,1)}, u32[]{:S(2)}) copy-start(bf16[2,288,1280]{2,1,0:T(8,128)(2,1)} %refs_7_.1) | copy-start | bytes 4423684
  142.6 38.4 %copy-start.2 = (f32[1,1280]{1,0:T(1,128)}, f32[1,1280]{1,0:T(1,128)S(1)}, u32[]{:S(2)}) copy-start(f32[1,1280]{1,0:T(1,128)S(1)} %unstack.53.refs_5_.gain) | copy-start | bytes 15364
  150.9 1.2 copy-start.1
  181.0 1.1 copy-start.3
  182.1 1.1 copy-start.4
  216.1 145.8 %reduce-scatter.6.cloned.1.call-start = ((), (), s32[]{:S(2)}) async-start(), calls=%async_computation.4 | async-start | bytes 8192000 | tf_op jit(solution)/shard_map/reduce_scatter | solution.py:1467
  251.8 172.4 %reduce-scatter.8.cloned.1.call-start = ((), (), s32[]{:S(2)}) async-start(), calls=%async_computation.5 | async-start | bytes 2048000 | tf_op jit(solution)/shard_map/reduce_scatter | solution.py:1467
  253.7 42.7 %copy-start.17 = (f32[1,1280]{1,0:T(1,128)S(1)}, f32[1,1280]{1,0:T(1,128)}, u32[]{:S(2)}) copy-start(f32[1,1280]{1,0:T(1,128)} %get-tuple-element.146) | copy-start | bytes 15364
  253.7 42.9 %copy-start.16 = (f32[1,1280]{1,0:T(1,128)S(1)}, f32[1,1280]{1,0:T(1,128)}, u32[]{:S(2)}) copy-start(f32[1,1280]{1,0:T(1,128)} %get-tuple-element.145) | copy-start | bytes 15364
  302.2 58.8 %collective-permute-start.3 = (bf16[640,320]{1,0:T(8,128)(2,1)}, bf16[640,320]{1,0:T(8,128)(2,1)S(1)}, u32[]{:S(2)}, u32[]{:S(2)}) collective-permute-start(bf16[640,320]{1,0:T(8,128)(2,1)} %get-tuple-element.123), channel_id=1, source_target_pairs={{0,2},{2,0},{4,6},{6,4},{1,3},{3,1},{5,7},{7,5},{8,10},{10,8},{12,... | collective-permute-start | bytes 1228808 | tf_op jit(solution)/shard_map/ppermute | solution.py:1332
  306.7 54.4 %collective-permute-start.4 = (bf16[640,320]{1,0:T(8,128)(2,1)}, bf16[640,320]{1,0:T(8,128)(2,1)S(1)}, u32[]{:S(2)}, u32[]{:S(2)}) collective-permute-start(bf16[640,320]{1,0:T(8,128)(2,1)} %get-tuple-element.124), channel_id=1, source_target_pairs={{0,4},{2,6},{4,0},{6,2},{1,5},{3,7},{5,1},{7,3},{8,12},{10,14},{12... | collective-permute-start | bytes 1228808 | tf_op jit(solution)/shard_map/ppermute | solution.py:1332
  307.0 54.1 %collective-permute-start.5 = (bf16[640,320]{1,0:T(8,128)(2,1)}, bf16[640,320]{1,0:T(8,128)(2,1)}, u32[]{:S(2)}, u32[]{:S(2)}) collective-permute-start(bf16[640,320]{1,0:T(8,128)(2,1)} %get-tuple-element.125), channel_id=1, source_target_pairs={{0,6},{2,4},{4,2},{6,0},{1,7},{3,5},{5,3},{7,1},{8,14},{10,12},{12... | collective-permute-start | bytes 1228808 | tf_op jit(solution)/shard_map/ppermute | solution.py:1332
  361.0 60.8 %copy-start.8 = (bf16[640,320]{1,0:T(8,128)(2,1)}, bf16[640,320]{1,0:T(8,128)(2,1)S(1)}, u32[]{:S(2)}) copy-start(bf16[640,320]{1,0:T(8,128)(2,1)S(1)} %collective-permute-done.3.refs_13_) | copy-start | bytes 1228804
  361.0 60.8 %copy-start.9 = (bf16[640,320]{1,0:T(8,128)(2,1)}, bf16[640,320]{1,0:T(8,128)(2,1)S(1)}, u32[]{:S(2)}) copy-start(bf16[640,320]{1,0:T(8,128)(2,1)S(1)} %collective-permute-done.4.refs_14_) | copy-start | bytes 1228804
  365.1 56.7 %collective-permute-start.6 = (bf16[640,320]{1,0:T(8,128)(2,1)}, bf16[640,320]{1,0:T(8,128)(2,1)S(1)}, u32[]{:S(2)}, u32[]{:S(2)}) collective-permute-start(bf16[640,320]{1,0:T(8,128)(2,1)} %get-tuple-element.135), channel_id=1, source_target_pairs={{0,2},{2,0},{4,6},{6,4},{1,3},{3,1},{5,7},{7,5},{8,10},{10,8},{12,... | collective-permute-start | bytes 1228808 | tf_op jit(solution)/shard_map/ppermute | solution.py:1332
  366.6 56.1 %collective-permute-start.7 = (bf16[640,320]{1,0:T(8,128)(2,1)}, bf16[640,320]{1,0:T(8,128)(2,1)S(1)}, u32[]{:S(2)}, u32[]{:S(2)}) collective-permute-start(bf16[640,320]{1,0:T(8,128)(2,1)} %get-tuple-element.136), channel_id=1, source_target_pairs={{0,4},{2,6},{4,0},{6,2},{1,5},{3,7},{5,1},{7,3},{8,12},{10,14},{12... | collective-permute-start | bytes 1228808 | tf_op jit(solution)/shard_map/ppermute | solution.py:1332
  369.0 54.5 %collective-permute-start.8 = (bf16[640,320]{1,0:T(8,128)(2,1)}, bf16[640,320]{1,0:T(8,128)(2,1)S(1)}, u32[]{:S(2)}, u32[]{:S(2)}) collective-permute-start(bf16[640,320]{1,0:T(8,128)(2,1)} %get-tuple-element.137), channel_id=1, source_target_pairs={{0,6},{2,4},{4,2},{6,0},{1,7},{3,5},{5,3},{7,1},{8,14},{10,12},{12... | collective-permute-start | bytes 1228808 | tf_op jit(solution)/shard_map/ppermute | solution.py:1332
  421.9 0.8 copy-start.10
  422.6 0.8 copy-start.11
  423.4 0.8 copy-start.12
  514.1 8.1 %copy-start.7 = (f32[320,480]{1,0:T(8,128)S(1)}, f32[320,480]{1,0:T(8,128)}, u32[]{:S(2)}) copy-start(f32[320,480]{1,0:T(8,128)} %get-tuple-element.252) | copy-start | bytes 1843204
  514.1 8.9 %copy-start.13 = (f32[160,320]{1,0:T(8,128)S(1)}, f32[160,320]{1,0:T(8,128)}, u32[]{:S(2)}) copy-start(f32[160,320]{1,0:T(8,128)} %get-tuple-element.159) | copy-start | bytes 614404
  517.2 6.5 %copy-start.6 = (f32[320,640]{1,0:T(8,128)S(1)}, f32[320,640]{1,0:T(8,128)}, u32[]{:S(2)}) copy-start(f32[320,640]{1,0:T(8,128)} %get-tuple-element.259) | copy-start | bytes 2457604
  519.5 5.1 copy-start.5
Sparse Core Ops, SparseCore 0:
  15.3 109.8 all-gather.4
  127.0 72.3 all-gather.6
  216.2 70.3 reduce-scatter.3
  289.5 72.3 reduce-scatter.5
  364.8 31.3 reduce-scatter.7
